TPU v7x, 32 devices: a whole 2x2x4 slice. The times are simulated.
32 devices in a mesh: gx: 8 (over z, x), gy: 4 (over y, core).
Axes of the slice: x: 2, y: 2, z: 4, core: 2. Of those that a mesh axis runs over, the one named last changes fastest.
Arguments:
- velocity: float32 [3, 128, 256, 256], P(None, 'gx', 'gy'), may hold values from -6 to 6
Outputs:
- details_one: float32 [7, 9, 64, 128, 128], P(None, None, 'gx', 'gy')
- stress_one: float32 [6, 64, 128, 128], P(None, 'gx', 'gy')
- details_two: float32 [7, 9, 32, 64, 64], P(None, None, 'gx', 'gy')
- stress_two: float32 [6, 32, 64, 64], P(None, 'gx', 'gy')
- details_three: float32 [7, 9, 16, 32, 32], P(None, None, 'gx', 'gy')
- stress_three: float32 [6, 16, 32, 32], P(None, 'gx', 'gy')
- coarse_velocity: float32 [3, 16, 32, 32], P(None, 'gx', 'gy')
All inputs are finite; a program needn't handle non-finite values.
Results may differ from a plain program's by a relative error of at most 0.0003.
Values sent between devices are 32-bit elements; how exact they have to be, the bound alone decides.
No kernel may reach another device: no remote copies, remote signals or barrier semaphores. Data moves between devices by JAX's collectives and lax.ppermute only.
A program may use at most 256 MiB of HBM per device.

v0:
```python
import jax
import jax.numpy as jnp
import numpy as np
from jax import lax
from jax.experimental import pallas as pl
from jax.experimental.pallas import tpu as pltpu
from jax.sharding import PartitionSpec as P

predict_one = -1.586134342
update_one = -0.05298011854
predict_two = 0.8829110762
update_two = 0.4435068522
scaling = 1.149604398
product_pairs = ((0, 0), (0, 1), (0, 2), (1, 1), (1, 2), (2, 2))
BEFORE = 4
AFTER = 3
MIB = 1 << 20


def shifted(block, axis, distance):
    size = lax.axis_size(axis)
    return lax.ppermute(block, axis, [(i, (i + distance) % size) for i in range(size)])


def third_table(length, lanes):
    eye = np.eye(length)
    e, o = eye[:, 0::2], eye[:, 1::2]
    following = lambda t: np.concatenate([t[:, 1:], t[:, -1:]], 1)
    preceding = lambda t: np.concatenate([t[:, :1], t[:, :-1]], 1)
    o = o + predict_one * (e + following(e))
    e = e + update_one * (o + preceding(o))
    o = o + predict_two * (e + following(e))
    e = e + update_two * (o + preceding(o))
    table = np.zeros((lanes, lanes))
    table[:length, : length // 2] = e * scaling
    table[:length, lanes // 2 : lanes // 2 + length // 2] = o / scaling
    return table.astype(np.float32)


def band_scale(by, bx):
    return float(scaling ** ((1 - 2 * by) + (1 - 2 * bx)))


def dot(a, b):
    return jnp.dot(a, b, precision=lax.Precision.HIGHEST, preferred_element_type=jnp.float32)


def ring_lift(e, o):
    n = e.shape[0]
    up = lambda t: pltpu.roll(t, n - 1, 0)
    down = lambda t: pltpu.roll(t, 1, 0)
    o = o + predict_one * (e + up(e))
    e = e + update_one * (o + down(o))
    o = o + predict_two * (e + up(e))
    e = e + update_two * (o + down(o))
    return e, o


def halo_lift(e, o, p, q, r, s, following, preceding, first, last):
    o1 = o + predict_one * (e + following(e, r))
    o1_before = p + predict_one * first(e)
    e1 = e + update_one * (preceding(o1, o1_before) + o1)
    e1_before = q + update_one * o1_before
    e1_after = r + update_one * (last(o1) + s)
    o2 = o1 + predict_two * (e1 + following(e1, e1_after))
    o2_before = o1_before + predict_two * (e1_before + first(e1))
    e2 = e1 + update_two * (preceding(o2, o2_before) + o2)
    return e2, o2


def lead_lift(e, o, p, q, r, s):
    return halo_lift_list(e, o, p, q, r, s)


def halo_lift_list(e, o, p, q, r, s):
    m = len(e)
    e = list(e) + [r]
    o1 = [p + predict_one * e[0]]
    o1 += [o[i] + predict_one * (e[i] + e[i + 1]) for i in range(m)] + [s]
    e1 = [q + update_one * o1[0]]
    e1 += [e[i] + update_one * (o1[i] + o1[i + 1]) for i in range(m + 1)]
    o2 = [o1[i] + predict_two * (e1[i] + e1[i + 1]) for i in range(m + 1)]
    e2 = [e1[i + 1] + update_two * (o2[i] + o2[i + 1]) for i in range(m)]
    return e2, o2[1:]


def sublane_lift(e, o, p, q, r, s):
    n = e.shape[0]
    row = lax.broadcasted_iota(jnp.int32, e.shape, 0)
    following = lambda t, edge: jnp.where(row == n - 1, edge, pltpu.roll(t, n - 1, 0))
    preceding = lambda t, edge: jnp.where(row == 0, edge, pltpu.roll(t, 1, 0))
    return halo_lift(e, o, p, q, r, s, following, preceding, lambda t: t[0:1], lambda t: t[n - 1 : n])


def parts_for_next(c):
    p = c[-1] + predict_one * c[-2]
    q = c[-2] + update_one * (c[-3] + predict_one * (c[-4] + c[-2]))
    return p, q


def parts_for_previous(c):
    return c[0], c[1] + predict_one * (c[0] + c[2])


def row_parts(layer):
    rows = layer.shape[0]
    tail = [layer[rows - 4 + i : rows - 3 + i] for i in range(4)]
    head = [layer[i : i + 1] for i in range(3)]
    return parts_for_next(tail) + parts_for_previous(head)


def local_kernel(v_ref, before_ref, after_ref, table_ref, low_ref, rest_ref, rows_ref, stack_ref):
    ny = v_ref.shape[2]
    half = ny // 2
    lanes = v_ref.shape[3] // 2
    even, odd = [], []
    for c in range(3):
        for h in range(2):
            cut = pl.ds(h * lanes, lanes)
            rows_ref[c, h, 12:16, :] = before_ref[c, 0, :, cut]
            rows_ref[c, h, 16 : 16 + ny, :] = v_ref[c, 0, :, cut]
            rows_ref[c, h, 16 + ny : 16 + ny + AFTER, :] = after_ref[c, 0, :, cut]
    count = half + 16
    for h in range(2):
        even = [rows_ref[c, h, pl.ds(0, count, stride=2), :] for c in range(3)]
        odd = [rows_ref[c, h, pl.ds(1, count, stride=2), :] for c in range(3)]
        for f in range(9):
            if f < 3:
                e, o = even[f], odd[f]
            else:
                i, j = product_pairs[f - 3]
                e, o = even[i] * even[j], odd[i] * odd[j]
            e, o = ring_lift(e, o)
            stack_ref[f * ny : f * ny + half, h * lanes : (h + 1) * lanes] = e[8 : 8 + half]
            stack_ref[f * ny + half : (f + 1) * ny, h * lanes : (h + 1) * lanes] = o[8 : 8 + half]
    out = dot(stack_ref[...], table_ref[...])
    for f in range(9):
        low_ref[f, 0] = out[f * ny : f * ny + half, :lanes]
        rest_ref[0, f, 0] = out[f * ny + half : (f + 1) * ny, :lanes]
        rest_ref[1, f, 0] = out[f * ny : f * ny + half, lanes:]
        rest_ref[2, f, 0] = out[f * ny + half : (f + 1) * ny, lanes:]


def local_pass(velocity, before, after, table):
    _, nx, ny, nz = velocity.shape
    half, lanes = ny // 2, nz // 2
    return pl.pallas_call(
        local_kernel,
        grid=(nx,),
        in_specs=[
            pl.BlockSpec((3, 1, ny, nz), lambda i: (0, i, 0, 0)),
            pl.BlockSpec((3, 1, BEFORE, nz), lambda i: (0, i + BEFORE, 0, 0)),
            pl.BlockSpec((3, 1, AFTER, nz), lambda i: (0, i + BEFORE, 0, 0)),
            pl.BlockSpec((nz, nz), lambda i: (0, 0)),
        ],
        out_specs=[
            pl.BlockSpec((9, 1, half, lanes), lambda i: (0, i, 0, 0)),
            pl.BlockSpec((3, 9, 1, half, lanes), lambda i: (0, 0, i, 0, 0)),
        ],
        out_shape=[
            jax.ShapeDtypeStruct((9, nx, half, lanes), jnp.float32),
            jax.ShapeDtypeStruct((3, 9, nx, half, lanes), jnp.float32),
        ],
        scratch_shapes=[pltpu.VMEM((3, 2, ny + 32, lanes), jnp.float32), pltpu.VMEM((9 * ny, nz), jnp.float32)],
        compiler_params=pltpu.CompilerParams(vmem_limit_bytes=24 * MIB),
        cost_estimate=pl.CostEstimate(flops=9 * nx * ny * nz * 512, bytes_accessed=9 * nx * ny * nz * 6, transcendentals=0),
        name="local_pass",
    )(velocity, before, after, table)


def pair_of(f):
    k = f - 3
    one = jnp.where(k < 3, 0, jnp.where(k < 5, 1, 2))
    two = jnp.where(k < 3, k, jnp.where(k < 5, k - 2, 2))
    return jnp.where(f < 3, f, one), jnp.where(f < 3, 3, two)


def gather_rows(refs, rows_ref, even_ref, odd_ref):
    edge_before, mid_before, edge_after, mid_after, row_before, row_after = refs
    mid = mid_before.shape[2]
    ny = mid + 16
    nx = row_before.shape[1] - BEFORE - AFTER
    lanes = rows_ref.shape[2]
    count = ny // 2 + 16
    even_ref[3] = jnp.ones(even_ref.shape[1:], jnp.float32)
    odd_ref[3] = jnp.ones(odd_ref.shape[1:], jnp.float32)
    for c in range(3):
        for layer in range(BEFORE + AFTER):
            if layer < BEFORE:
                edge, middle, at, line = edge_before, mid_before, layer, layer
            else:
                edge, middle, at, line = edge_after, mid_after, layer - BEFORE, layer + nx
            for h in range(2):
                cut = pl.ds(h * lanes, lanes)
                rows_ref[h, 12:16, :] = row_before[c, line, :, cut]
                rows_ref[h, 16:24, :] = edge[c, at, 0:8, cut]
                rows_ref[h, 24 : 24 + mid, :] = middle[c, at, :, cut]
                rows_ref[h, 24 + mid : 32 + mid, :] = edge[c, at, 8:16, cut]
                rows_ref[h, 16 + ny : 16 + ny + AFTER, :] = row_after[c, line, :, cut]
                even_ref[c, layer, :, cut] = rows_ref[h, pl.ds(0, count, stride=2), :]
                odd_ref[c, layer, :, cut] = rows_ref[h, pl.ds(1, count, stride=2), :]


def halo_parts(ref, i, j):
    g = [ref[i, layer] * ref[j, layer] for layer in range(BEFORE + AFTER)]
    return parts_for_next(g[:BEFORE]) + parts_for_previous(g[BEFORE:])


def lift_first(layers, halo):
    return halo_lift_list(layers[0::2], layers[1::2], *halo)


def send_parts(layers, f, next_ref, prev_ref, next_edge_ref, prev_edge_ref, down_ref, up_ref):
    for part, value in enumerate(parts_for_next(layers)):
        next_ref[f, part] = value
        for at, row in enumerate(row_parts(value)):
            next_edge_ref[f, part, at : at + 1, :] = row
    for part, value in enumerate(parts_for_previous(layers)):
        prev_ref[f, part] = value
        for at, row in enumerate(row_parts(value)):
            prev_edge_ref[f, part, at : at + 1, :] = row
    for at, layer in enumerate(layers):
        p, q, r, s = row_parts(layer)
        down_ref[f, at, 0:1, :] = p
        down_ref[f, at, 1:2, :] = q
        up_ref[f, at, 0:1, :] = r
        up_ref[f, at, 1:2, :] = s


def approx_kernel(*refs):
    low_ref, table_ref = refs[:2]
    halo_refs = refs[2:8]
    approx_ref, high_ref, stress_ref = refs[8:11]
    sends = refs[11:17]
    rows_ref, even_ref, odd_ref, kept_ref, stack_ref = refs[17:]
    f = pl.program_id(0)
    nx, half, lanes = low_ref.shape[1:]

    @pl.when(f == 0)
    def _():
        gather_rows(halo_refs, rows_ref, even_ref, odd_ref)

    i, j = pair_of(f)
    even = halo_parts(even_ref, i, j)
    odd = halo_parts(odd_ref, i, j)
    for k in range(4):
        e, _ = ring_lift(even[k], odd[k])
        stack_ref[k * half : (k + 1) * half, :] = e[8 : 8 + half]
    out = dot(stack_ref[...], table_ref[:, :lanes])
    halo = [out[k * half : (k + 1) * half] for k in range(4)]
    e, o = lift_first([low_ref[0, x] for x in range(nx)], halo)
    e = [t * band_scale(0, 0) for t in e]
    for x in range(nx // 2):
        approx_ref[0, x] = e[x]
        high_ref[0, x] = o[x] * band_scale(0, 1)

    @pl.when(f < 3)
    def _():
        for x in range(nx // 2):
            kept_ref[f, x] = e[x]

    @pl.when(f >= 3)
    def _():
        for x in range(nx // 2):
            stress_ref[0, x] = e[x] - kept_ref[i, x] * kept_ref[j, x]

    send_parts(e, 0, *sends)


def whole(shape):
    return pl.BlockSpec(shape, lambda f: (0,) * len(shape))


def per_field(shape):
    return pl.BlockSpec((1,) + shape, lambda f: (f,) + (0,) * len(shape))


def approx_pass(low, halo, table):
    _, nx, half, lanes = low.shape
    nz, count, mx = 2 * lanes, half + 16, nx // 2
    f32 = lambda *shape: jax.ShapeDtypeStruct(shape, jnp.float32)
    sends = [(2, half, lanes), (2, half, lanes), (2, 4, lanes), (2, 4, lanes), (mx, 2, lanes), (mx, 2, lanes)]
    return pl.pallas_call(
        approx_kernel,
        grid=(9,),
        in_specs=[per_field((nx, half, lanes)), whole((nz, nz))] + [whole(h.shape) for h in halo],
        out_specs=[
            per_field((mx, half, lanes)),
            per_field((mx, half, lanes)),
            pl.BlockSpec((1, mx, half, lanes), lambda f: (jnp.maximum(f - 3, 0), 0, 0, 0)),
        ]
        + [per_field(s) for s in sends],
        out_shape=[f32(9, mx, half, lanes), f32(9, mx, half, lanes), f32(6, mx, half, lanes)] + [f32(9, *s) for s in sends],
        scratch_shapes=[
            pltpu.VMEM((2, 2 * half + 32, lanes), jnp.float32),
            pltpu.VMEM((4, BEFORE + AFTER, count, nz), jnp.float32),
            pltpu.VMEM((4, BEFORE + AFTER, count, nz), jnp.float32),
            pltpu.VMEM((3, mx, half, lanes), jnp.float32),
            pltpu.VMEM((4 * half, nz), jnp.float32),
        ],
        compiler_params=pltpu.CompilerParams(vmem_limit_bytes=24 * MIB),
        name="approx_pass",
    )(low, table, *halo)


def detail_kernel(*refs):
    rest_ref, high_ref, table_ref = refs[:3]
    halo_refs = refs[3:9]
    out_ref, rows_ref, even_ref, odd_ref, stack_ref = refs[9:]
    f = pl.program_id(0)
    nx, half, lanes = rest_ref.shape[2:]

    @pl.when(f == 0)
    def _():
        gather_rows(halo_refs, rows_ref, even_ref, odd_ref)

    i, j = pair_of(f)
    even = halo_parts(even_ref, i, j)
    odd = halo_parts(odd_ref, i, j)
    for k in range(4):
        e, o = ring_lift(even[k], odd[k])
        stack_ref[k * half : (k + 1) * half, :] = e[8 : 8 + half]
        stack_ref[(4 + k) * half : (5 + k) * half, :] = o[8 : 8 + half]
    out = dot(stack_ref[...], table_ref[...])
    for x in range(nx // 2):
        out_ref[0, 0, x] = high_ref[0, x]
    for band, (bz, by) in enumerate(((0, 1), (1, 0), (1, 1))):
        halo = [out[(4 * by + k) * half : (4 * by + k + 1) * half, bz * lanes : (bz + 1) * lanes] for k in range(4)]
        e, o = lift_first([rest_ref[band, 0, x] for x in range(nx)], halo)
        at = 4 * bz + 2 * by - 1
        for x in range(nx // 2):
            out_ref[at, 0, x] = e[x] * band_scale(by, 0)
            out_ref[at + 1, 0, x] = o[x] * band_scale(by, 1)


def detail_pass(rest, high, halo, table):
    _, _, nx, half, lanes = rest.shape
    nz, count, mx = 2 * lanes, half + 16, nx // 2
    return pl.pallas_call(
        detail_kernel,
        grid=(9,),
        in_specs=[
            pl.BlockSpec((3, 1, nx, half, lanes), lambda f: (0, f, 0, 0, 0)),
            per_field((mx, half, lanes)),
            whole((nz, nz)),
        ]
        + [whole(h.shape) for h in halo],
        out_specs=pl.BlockSpec((7, 1, mx, half, lanes), lambda f: (0, f, 0, 0, 0)),
        out_shape=jax.ShapeDtypeStruct((7, 9, mx, half, lanes), jnp.float32),
        scratch_shapes=[
            pltpu.VMEM((2, 2 * half + 32, lanes), jnp.float32),
            pltpu.VMEM((4, BEFORE + AFTER, count, nz), jnp.float32),
            pltpu.VMEM((4, BEFORE + AFTER, count, nz), jnp.float32),
            pltpu.VMEM((8 * half, nz), jnp.float32),
        ],
        compiler_params=pltpu.CompilerParams(vmem_limit_bytes=24 * MIB),
        cost_estimate=pl.CostEstimate(flops=9 * nx * half * nz * 200, bytes_accessed=9 * nx * half * nz * 16, transcendentals=0),
        name="detail_pass",
    )(rest, high, table, *halo)


def level_kernel(last, nz, *refs):
    a_ref, before_ref, after_ref, down_ref, up_ref, table_ref = refs[:6]
    detail_ref, stress_ref, approx_ref = refs[6:9]
    sends = refs[9:15] if not last else ()
    pad_ref, stack_ref, out_ref, kept_ref = refs[-4:]
    nx, ny = a_ref.shape[1:3]
    half, lanes = ny // 2, nz // 2
    wide = table_ref.shape[0]
    if nz < wide:
        pad_ref[...] = jnp.zeros_like(pad_ref)
    for f in range(9):
        for layer in range(nx + 4):
            if layer < nx:
                source = a_ref.at[f, layer]
            elif layer < nx + 2:
                source = before_ref.at[f, layer - nx]
            else:
                source = after_ref.at[f, layer - nx - 2]
            pad_ref[layer, :, :nz] = source[...]
            e = pad_ref[layer, pl.ds(0, half, stride=2), :]
            o = pad_ref[layer, pl.ds(1, half, stride=2), :]
            rows = [down_ref[f, layer, 0:1, :], down_ref[f, layer, 1:2, :], up_ref[f, layer, 0:1, :], up_ref[f, layer, 1:2, :]]
            if nz < wide:
                rows = [jnp.concatenate([row, jnp.zeros((1, wide - nz), jnp.float32)], axis=1) for row in rows]
            e, o = sublane_lift(e, o, *rows)
            stack_ref[layer * ny : layer * ny + half, :] = e
            stack_ref[layer * ny + half : (layer + 1) * ny, :] = o
        out_ref[...] = dot(stack_ref[...], table_ref[...])
        layers = [out_ref[layer * ny : (layer + 1) * ny, :] for layer in range(nx + 4)]
        low, high = lift_first(layers[:nx], layers[nx:])
        approx = []
        for x in range(nx // 2):
            for bx, value in enumerate((low[x], high[x])):
                for by in range(2):
                    t = value[by * half : (by + 1) * half] * band_scale(by, bx)
                    for bz in range(2):
                        band = 4 * bz + 2 * by + bx
                        piece = t[:, bz * (wide // 2) : bz * (wide // 2) + lanes]
                        if band:
                            detail_ref[band - 1, f, x] = piece
                        else:
                            approx.append(piece)
        for x in range(nx // 2):
            if f < 3:
                kept_ref[f, x] = approx[x]
            else:
                i, j = product_pairs[f - 3]
                stress_ref[f - 3, x] = approx[x] - kept_ref[i, x] * kept_ref[j, x]
            if not last or f < 3:
                approx_ref[f, x] = approx[x]
        if not last:
            send_parts(approx, f, *sends)


def level_pass(approx, halo, last):
    _, nx, ny, nz = approx.shape
    mx, half, lanes = nx // 2, ny // 2, nz // 2
    wide = max(nz, 128)
    f32 = lambda *shape: jax.ShapeDtypeStruct(shape, jnp.float32)
    out = [f32(7, 9, mx, half, lanes), f32(6, mx, half, lanes), f32(3 if last else 9, mx, half, lanes)]
    if not last:
        out += [f32(9, *s) for s in ((2, half, lanes), (2, half, lanes), (2, 4, lanes), (2, 4, lanes), (mx, 2, lanes), (mx, 2, lanes))]
    vmem = pl.BlockSpec(memory_space=pltpu.VMEM)
    return pl.pallas_call(
        lambda *refs: level_kernel(last, nz, *refs),
        in_specs=[vmem] * 6,
        out_specs=[vmem] * len(out),
        out_shape=out,
        scratch_shapes=[
            pltpu.VMEM((nx + 4, ny, wide), jnp.float32),
            pltpu.VMEM(((nx + 4) * ny, wide), jnp.float32),
            pltpu.VMEM(((nx + 4) * ny, wide), jnp.float32),
            pltpu.VMEM((3, mx, half, lanes), jnp.float32),
        ],
        compiler_params=pltpu.CompilerParams(vmem_limit_bytes=24 * MIB),
        name="last_level" if last else "second_level",
    )(approx, *halo, jnp.asarray(third_table(nz, wide)))


def exchange(to_next, to_prev, edge_next, edge_prev, down, up):
    from_prev_edge = shifted(edge_next, "gx", 1)
    from_next_edge = shifted(edge_prev, "gx", -1)
    before = shifted(to_next, "gx", 1)
    after = shifted(to_prev, "gx", -1)
    down = jnp.concatenate([down, from_prev_edge[:, :, 0:2], from_next_edge[:, :, 0:2]], axis=1)
    up = jnp.concatenate([up, from_prev_edge[:, :, 2:4], from_next_edge[:, :, 2:4]], axis=1)
    return before, after, shifted(down, "gy", 1), shifted(up, "gy", -1)


def body(velocity):
    _, nx, ny, nz = velocity.shape
    table = jnp.asarray(third_table(nz, nz))
    tail, head = velocity[:, nx - BEFORE :], velocity[:, :AFTER]
    edges = lambda t: jnp.concatenate([t[:, :, :8], t[:, :, ny - 8 :]], axis=2)
    edge_before = shifted(edges(tail), "gx", 1)
    edge_after = shifted(edges(head), "gx", -1)
    mid_before = shifted(tail[:, :, 8 : ny - 8], "gx", 1)
    mid_after = shifted(head[:, :, 8 : ny - 8], "gx", -1)
    down = jnp.concatenate([edge_before[:, :, 12:], velocity[:, :, ny - BEFORE :], edge_after[:, :, 12:]], axis=1)
    up = jnp.concatenate([edge_before[:, :, :AFTER], velocity[:, :, :AFTER], edge_after[:, :, :AFTER]], axis=1)
    row_before = shifted(down, "gy", 1)
    row_after = shifted(up, "gy", -1)
    low, rest = local_pass(velocity, row_before, row_after, table)
    halo = (edge_before, mid_before, edge_after, mid_after, row_before, row_after)
    approx, high, stress_one, *sends = approx_pass(low, halo, table)
    second_halo = exchange(*sends)
    details_one = detail_pass(rest, high, halo, table)
    details_two, stress_two, approx, *sends = level_pass(approx, second_halo, False)
    details_three, stress_three, coarse = level_pass(approx, exchange(*sends), True)
    return details_one, stress_one, details_two, stress_two, details_three, stress_three, coarse


def solution(mesh):
    in_specs = (P(None, "gx", "gy", None),)
    out_specs = (
        P(None, None, "gx", "gy", None),
        P(None, "gx", "gy", None),
        P(None, None, "gx", "gy", None),
        P(None, "gx", "gy", None),
        P(None, None, "gx", "gy", None),
        P(None, "gx", "gy", None),
        P(None, "gx", "gy", None),
    )
    return jax.shard_map(body, mesh=mesh, in_specs=in_specs, out_specs=out_specs, check_vma=False)
```

profile of v0, /device:TPU:0, one launch (start us, length us, event | category | flops | bytes accessed | tf_op | source)
XLA Modules:
  0.0 104.5 jit_solution(234761487874810775)
XLA Ops:
  0.6 0.0 copy-start
  0.6 0.0 copy-start.1
  0.7 1.1 %fusion = (f32[3,4,8,256]{3,2,1,0:T(8,128)S(1)}, f32[3,4,8,256]{3,2,1,0:T(8,128)S(1)}) fusion(f32[3,16,64,256]{3,2,1,0:T(8,128)} %v_ref.1), kind=kLoop, calls=%fused_computation.8 | loop fusion | bytes 393216 | tf_op jit(solution)/shard_map/slice | solution.py:455
  1.8 3.0 %collective-permute-start = (f32[3,4,16,256]{3,2,1,0:T(8,128)S(1)}, f32[3,4,16,256]{3,2,1,0:T(8,128)S(1)}, u32[]{:S(2)}, u32[]{:S(2)}) collective-permute-start(f32[3,4,16,256]{3,2,1,0:T(8,128)S(1)} %pad_maximum_fusion.2), channel_id=1, source_target_pairs={{0,4},{4,8},{8,12},{12,16},{16,20},{20,24},{24,28},{28,0},{1,5},{5... | collective-permute-start | bytes 589832 | tf_op jit(solution)/shard_map/ppermute | solution.py:22
  4.8 0.9 fusion.1
  5.8 3.1 %collective-permute-start.1 = (f32[3,3,16,256]{3,2,1,0:T(8,128)S(1)}, f32[3,3,16,256]{3,2,1,0:T(8,128)S(1)}, u32[]{:S(2)}, u32[]{:S(2)}) collective-permute-start(f32[3,3,16,256]{3,2,1,0:T(8,128)S(1)} %pad_maximum_fusion.3), channel_id=1, source_target_pairs={{0,28},{4,0},{8,4},{12,8},{16,12},{20,16},{24,20},{28,24},{1,29},{... | collective-permute-start | bytes 442376 | tf_op jit(solution)/shard_map/ppermute | solution.py:22
  8.9 1.1 %slice.78 = f32[3,4,48,256]{3,2,1,0:T(8,128)S(1)} slice(f32[3,16,64,256]{3,2,1,0:T(8,128)} %v_ref.1), slice={[0:3], [12:16], [8:56], [0:256]} | slice | bytes 1179648 | tf_op jit(solution)/shard_map/slice | solution.py:458
  10.0 0.1 collective-permute-start.4
  10.1 1.1 %slice.79 = f32[3,3,48,256]{3,2,1,0:T(8,128)S(1)} slice(f32[3,16,64,256]{3,2,1,0:T(8,128)} %v_ref.1), slice={[0:3], [0:3], [8:56], [0:256]} | slice | bytes 884736 | tf_op jit(solution)/shard_map/slice | solution.py:459
  11.1 4.8 %collective-permute-start.5 = (f32[3,3,48,256]{3,2,1,0:T(8,128)S(1)}, f32[3,3,48,256]{3,2,1,0:T(8,128)S(1)}, u32[]{:S(2)}, u32[]{:S(2)}) collective-permute-start(f32[3,3,48,256]{3,2,1,0:T(8,128)S(1)} %slice.79), channel_id=1, source_target_pairs={{0,28},{4,0},{8,4},{12,8},{16,12},{20,16},{24,20},{28,24},{1,29},{... | collective-permute-start | bytes 1327112 | tf_op jit(solution)/shard_map/ppermute | solution.py:22
  15.9 0.1 slice.71
  16.0 12.7 %collective-permute-done.1.refs_4_.refs_5_ = f32[3,3,16,256]{3,2,1,0:T(8,128)S(1)} collective-permute-done((f32[3,3,16,256]{3,2,1,0:T(8,128)S(1)}, f32[3,3,16,256]{3,2,1,0:T(8,128)S(1)}, u32[]{:S(2)}, u32[]{:S(2)}) %collective-permute-start.1) | collective-permute-done | bytes 147488 | tf_op jit(solution)/shard_map/ppermute | solution.py:22
  28.7 0.0 collective-permute-done.refs_2_.refs_3_
  28.7 0.1 pad_maximum_fusion
  28.8 0.1 collective-permute-start.2
  28.9 0.1 pad_maximum_fusion.1
  28.9 1.8 %collective-permute-start.3 = (f32[3,23,3,256]{3,2,1,0:T(4,128)S(1)}, f32[3,23,3,256]{3,2,1,0:T(4,128)S(1)}, u32[]{:S(2)}, u32[]{:S(2)}) collective-permute-start(f32[3,23,3,256]{3,2,1,0:T(4,128)S(1)} %pad_maximum_fusion.1), channel_id=1, source_target_pairs={{0,3},{1,0},{2,1},{3,2},{4,7},{5,4},{6,5},{7,6},{8,11},{9,8},{10,9... | collective-permute-start | bytes 635912 | tf_op jit(solution)/shard_map/ppermute | solution.py:22
  30.7 6.2 %collective-permute-done.3.after_ref.refs_7_.refs_8_ = f32[3,23,3,256]{3,2,1,0:T(4,128)S(1)} collective-permute-done((f32[3,23,3,256]{3,2,1,0:T(4,128)S(1)}, f32[3,23,3,256]{3,2,1,0:T(4,128)S(1)}, u32[]{:S(2)}, u32[]{:S(2)}) %collective-permute-start.3) | collective-permute-done | bytes 212000 | tf_op jit(solution)/shard_map/ppermute | solution.py:22
  36.9 0.0 collective-permute-done.2.before_ref.refs_6_.refs_7_
  36.9 15.7 %local_pass.1 = (f32[9,16,32,128]{3,2,1,0:T(8,128)S(1)}, f32[3,9,16,32,128]{4,3,2,1,0:T(8,128)S(1)}) custom-call(f32[3,16,64,256]{3,2,1,0:T(8,128)S(1)} %copy-done.1, f32[3,23,4,256]{3,2,1,0:T(4,128)S(1)} %collective-permute-done.2.before_ref.refs_6_.refs_7_, f32[3,23,3,256]{3,2,1,0:T(4,128)S(1)} %collective-permute-done.3.after_ref.refs_7_.refs_8_, ...), custom_call_target="tpu_custom_call" | custom-call | flops 1207959552 | bytes 14155776 | tf_op jit(solution)/shard_map/local_pass/pallas_call | solution.py:147
  52.6 0.0 copy-start.3
  52.6 0.0 collective-permute-done.5.refs_5_.refs_6_
  52.6 0.0 collective-permute-done.4.refs_3_.refs_4_
  52.6 6.0 %approx_pass.1 = (f32[9,8,32,128]{3,2,1,0:T(8,128)S(1)}, f32[9,8,32,128]{3,2,1,0:T(8,128)S(1)}, f32[6,8,32,128]{3,2,1,0:T(8,128)}, f32[9,2,32,128]{3,2,1,0:T(8,1...) custom-call(f32[9,16,32,128]{3,2,1,0:T(8,128)S(1)} %get-tuple-elemen, ...), custom_call_target="tpu_custom_call" | custom-call | tf_op jit(solution)/shard_map/approx_pass/pallas_call | solution.py:283
  58.6 0.0 collective-permute-start.8
  58.6 4.7 %collective-permute-start.9 = (f32[9,2,4,128]{3,2,1,0:T(4,128)S(1)}, f32[9,2,4,128]{3,2,1,0:T(4,128)S(1)}, u32[]{:S(2)}, u32[]{:S(2)}) collective-permute-start(f32[9,2,4,128]{3,2,1,0:T(4,128)S(1)} %get-tuple-element.39), channel_id=1, source_target_pairs={{0,28},{4,0},{8,4},{12,8},{16,12},{20,16},{24,20},{28,24},{1,29},{... | collective-permute-start | bytes 110600 | tf_op jit(solution)/shard_map/ppermute | solution.py:22
  63.3 4.7 %collective-permute-start.7 = (f32[9,2,32,128]{3,2,1,0:T(8,128)S(1)}, f32[9,2,32,128]{3,2,1,0:T(8,128)S(1)}, u32[]{:S(2)}, u32[]{:S(2)}) collective-permute-start(f32[9,2,32,128]{3,2,1,0:T(8,128)S(1)} %get-tuple-element.36), channel_id=1, source_target_pairs={{0,28},{4,0},{8,4},{12,8},{16,12},{20,16},{24,20},{28,24},{1,29},{... | collective-permute-start | bytes 884744 | tf_op jit(solution)/shard_map/ppermute | solution.py:22
  68.1 0.0 collective-permute-done.8
  68.1 0.1 pad_maximum_fusion.4
  68.2 0.1 collective-permute-start.10
  68.2 0.1 pad_maximum_fusion.5
  68.3 1.8 %collective-permute-start.11 = (f32[9,12,2,128]{3,2,1,0:T(2,128)S(1)}, f32[9,12,2,128]{3,2,1,0:T(2,128)S(1)}, u32[]{:S(2)}, u32[]{:S(2)}) collective-permute-start(f32[9,12,2,128]{3,2,1,0:T(2,128)S(1)} %pad_maximum_fusion.5), channel_id=1, source_target_pairs={{0,3},{1,0},{2,1},{3,2},{4,7},{5,4},{6,5},{7,6},{8,11},{9,8},{10,9... | collective-permute-start | bytes 331784 | tf_op jit(solution)/shard_map/ppermute | solution.py:22
  70.1 2.3 %collective-permute-done.10.refs_3_ = f32[9,12,2,128]{3,2,1,0:T(2,128)S(1)} collective-permute-done((f32[9,12,2,128]{3,2,1,0:T(2,128)S(1)}, f32[9,12,2,128]{3,2,1,0:T(2,128)S(1)}, u32[]{:S(2)}, u32[]{:S(2)}) %collective-permute-start.10) | collective-permute-done | bytes 110624 | tf_op jit(solution)/shard_map/ppermute | solution.py:22
  72.4 0.2 collective-permute-done.11.refs_4_
  72.6 4.0 %collective-permute-done.6.refs_1_ = f32[9,2,32,128]{3,2,1,0:T(8,128)S(1)} collective-permute-done((f32[9,2,32,128]{3,2,1,0:T(8,128)S(1)}, f32[9,2,32,128]{3,2,1,0:T(8,128)S(1)}, u32[]{:S(2)}, u32[]{:S(2)}) %collective-permute-start.6) | collective-permute-done | bytes 294944 | tf_op jit(solution)/shard_map/ppermute | solution.py:22
  76.6 2.2 %collective-permute-done.7.refs_2_ = f32[9,2,32,128]{3,2,1,0:T(8,128)S(1)} collective-permute-done((f32[9,2,32,128]{3,2,1,0:T(8,128)S(1)}, f32[9,2,32,128]{3,2,1,0:T(8,128)S(1)}, u32[]{:S(2)}, u32[]{:S(2)}) %collective-permute-start.7) | collective-permute-done | bytes 294944 | tf_op jit(solution)/shard_map/ppermute | solution.py:22
  78.8 3.9 %second_level.1 = (f32[7,9,4,16,64]{4,3,2,1,0:T(8,128)}, f32[6,4,16,64]{3,2,1,0:T(8,128)}, f32[9,4,16,64]{3,2,1,0:T(8,128)S(1)}, f32[9,2,16,64]{3,2,1,0:T(8,128)...) custom-call(f32[9,8,32,128]{3,2,1,0:T(8,128)S(1)} %get-tuple-element, ...), custom_call_target="tpu_custom_call" | custom-call | tf_op jit(solution)/shard_map/second_level/pallas_call | solution.py:425
  82.7 0.3 collective-permute-start.14
  83.0 4.5 %collective-permute-start.15 = (f32[9,2,4,64]{3,2,1,0:T(4,128)S(1)}, f32[9,2,4,64]{3,2,1,0:T(4,128)S(1)}, u32[]{:S(2)}, u32[]{:S(2)}) collective-permute-start(f32[9,2,4,64]{3,2,1,0:T(4,128)S(1)} %get-tuple-element.48), channel_id=1, source_target_pairs={{0,28},{4,0},{8,4},{12,8},{16,12},{20,16},{24,20},{28,24},{1,29},{... | collective-permute-start | bytes 55304 | tf_op jit(solution)/shard_map/ppermute | solution.py:22
  87.5 0.0 collective-permute-start.12
  87.5 4.7 %collective-permute-start.13 = (f32[9,2,16,64]{3,2,1,0:T(8,128)S(1)}, f32[9,2,16,64]{3,2,1,0:T(8,128)S(1)}, u32[]{:S(2)}, u32[]{:S(2)}) collective-permute-start(f32[9,2,16,64]{3,2,1,0:T(8,128)S(1)} %get-tuple-element.45), channel_id=1, source_target_pairs={{0,28},{4,0},{8,4},{12,8},{16,12},{20,16},{24,20},{28,24},{1,29},{... | collective-permute-start | bytes 221192 | tf_op jit(solution)/shard_map/ppermute | solution.py:22
  92.2 0.0 collective-permute-done.14
  92.3 0.1 collective-permute-start.16
  92.4 1.8 %collective-permute-start.17 = (f32[9,8,2,64]{3,2,1,0:T(2,128)S(1)}, f32[9,8,2,64]{3,2,1,0:T(2,128)S(1)}, u32[]{:S(2)}, u32[]{:S(2)}) collective-permute-start(f32[9,8,2,64]{3,2,1,0:T(2,128)S(1)} %pad_maximum_fusion.7), channel_id=1, source_target_pairs={{0,3},{1,0},{2,1},{3,2},{4,7},{5,4},{6,5},{7,6},{8,11},{9,8},{10,9... | collective-permute-start | bytes 110600 | tf_op jit(solution)/shard_map/ppermute | solution.py:22
  94.2 8.5 %detail_pass.1 = f32[7,9,8,32,128]{4,3,2,1,0:T(8,128)} custom-call(f32[3,9,16,32,128]{4,3,2,1,0:T(8,128)S(1)} %get-tuple-element.30.refs_0_, f32[9,8,32,128]{3,2,1,0:T(8,128)S(1)} %get-tuple-element.32.refs_1_, f32[256,256]{1,0:T(8,128)S(1)} %copy-done, f32[3,4,16,256]{3,2,1,0:T(8,128)S(1)} %collective-permute-done.refs_2_.refs_3_, ...), custom_call_target="tpu_custom_call" | custom-call | flops 235929600 | bytes 18874368 | tf_op jit(solution)/shard_map/detail_pass/pallas_call | solution.py:339
  102.7 0.0 collective-permute-done.16.refs_3_
  102.7 0.0 collective-permute-done.13.refs_2_
  102.7 1.8 %last_level.1 = (f32[7,9,2,8,32]{4,3,2,1,0:T(8,128)}, f32[6,2,8,32]{3,2,1,0:T(8,128)}, f32[3,2,8,32]{3,2,1,0:T(8,128)}) custom-call(f32[9,4,16,64]{3,2,1,0:T(8,128)S(1)} %get-tuple-element.43.refs_0_, f32[9,2,16,64]{3,2,1,0:T(8,128)S(1)} %collective-permute-done.12.refs_1_, f32[9,2,16,64]{3,2,1,0:T(8,128)S(1)} %collective-permute-done.13.refs_2_, ...), custom_call_target="tpu_custom_call" | custom-call | tf_op jit(solution)/shard_map/last_level/pallas_call | solution.py:425
  (23 shorter events, 0.3 us)
Async XLA Ops:
  0.6 36.3 %copy-start = (f32[256,256]{1,0:T(8,128)S(1)}, f32[256,256]{1,0:T(8,128)}, u32[]{:S(2)}) copy-start(f32[256,256]{1,0:T(8,128)} %constant.6.clone.table_ref.refs_1_.refs_2_) | copy-start | bytes 786436
  0.6 15.2 %copy-start.1 = (f32[3,16,64,256]{3,2,1,0:T(8,128)S(1)}, f32[3,16,64,256]{3,2,1,0:T(8,128)}, u32[]{:S(2)}) copy-start(f32[3,16,64,256]{3,2,1,0:T(8,128)} %v_ref.1) | copy-start | bytes 9437188
  1.8 26.9 %collective-permute-start = (f32[3,4,16,256]{3,2,1,0:T(8,128)S(1)}, f32[3,4,16,256]{3,2,1,0:T(8,128)S(1)}, u32[]{:S(2)}, u32[]{:S(2)}) collective-permute-start(f32[3,4,16,256]{3,2,1,0:T(8,128)S(1)} %pad_maximum_fusion.2), channel_id=1, source_target_pairs={{0,4},{4,8},{8,12},{12,16},{16,20},{20,24},{24,28},{28,0},{1,5},{5... | collective-permute-start | bytes 589832 | tf_op jit(solution)/shard_map/ppermute | solution.py:22
  5.8 22.9 %collective-permute-start.1 = (f32[3,3,16,256]{3,2,1,0:T(8,128)S(1)}, f32[3,3,16,256]{3,2,1,0:T(8,128)S(1)}, u32[]{:S(2)}, u32[]{:S(2)}) collective-permute-start(f32[3,3,16,256]{3,2,1,0:T(8,128)S(1)} %pad_maximum_fusion.3), channel_id=1, source_target_pairs={{0,28},{4,0},{8,4},{12,8},{16,12},{20,16},{24,20},{28,24},{1,29},{... | collective-permute-start | bytes 442376 | tf_op jit(solution)/shard_map/ppermute | solution.py:22
  10.0 42.6 %collective-permute-start.4 = (f32[3,4,48,256]{3,2,1,0:T(8,128)S(1)}, f32[3,4,48,256]{3,2,1,0:T(8,128)S(1)}, u32[]{:S(2)}, u32[]{:S(2)}) collective-permute-start(f32[3,4,48,256]{3,2,1,0:T(8,128)S(1)} %slice.78), channel_id=1, source_target_pairs={{0,4},{4,8},{8,12},{12,16},{16,20},{20,24},{24,28},{28,0},{1,5},{5... | collective-permute-start | bytes 1769480 | tf_op jit(solution)/shard_map/ppermute | solution.py:22
  11.1 41.5 %collective-permute-start.5 = (f32[3,3,48,256]{3,2,1,0:T(8,128)S(1)}, f32[3,3,48,256]{3,2,1,0:T(8,128)S(1)}, u32[]{:S(2)}, u32[]{:S(2)}) collective-permute-start(f32[3,3,48,256]{3,2,1,0:T(8,128)S(1)} %slice.79), channel_id=1, source_target_pairs={{0,28},{4,0},{8,4},{12,8},{16,12},{20,16},{24,20},{28,24},{1,29},{... | collective-permute-start | bytes 1327112 | tf_op jit(solution)/shard_map/ppermute | solution.py:22
  28.8 8.1 %collective-permute-start.2 = (f32[3,23,4,256]{3,2,1,0:T(4,128)S(1)}, f32[3,23,4,256]{3,2,1,0:T(4,128)S(1)}, u32[]{:S(2)}, u32[]{:S(2)}) collective-permute-start(f32[3,23,4,256]{3,2,1,0:T(4,128)S(1)} %pad_maximum_fusion), channel_id=1, source_target_pairs={{0,1},{1,2},{2,3},{3,0},{4,5},{5,6},{6,7},{7,4},{8,9},{9,10},{10,1... | collective-permute-start | bytes 847880 | tf_op jit(solution)/shard_map/ppermute | solution.py:22
  28.9 8.0 %collective-permute-start.3 = (f32[3,23,3,256]{3,2,1,0:T(4,128)S(1)}, f32[3,23,3,256]{3,2,1,0:T(4,128)S(1)}, u32[]{:S(2)}, u32[]{:S(2)}) collective-permute-start(f32[3,23,3,256]{3,2,1,0:T(4,128)S(1)} %pad_maximum_fusion.1), channel_id=1, source_target_pairs={{0,3},{1,0},{2,1},{3,2},{4,7},{5,4},{6,5},{7,6},{8,11},{9,8},{10,9... | collective-permute-start | bytes 635912 | tf_op jit(solution)/shard_map/ppermute | solution.py:22
  52.6 26.2 %copy-start.3 = (f32[128,128]{1,0:T(8,128)S(1)}, f32[128,128]{1,0:T(8,128)}, u32[]{:S(2)}) copy-start(f32[128,128]{1,0:T(8,128)} %constant.7.clone.refs_5_) | copy-start | bytes 196612
  58.6 9.4 %collective-permute-start.8 = (f32[9,2,4,128]{3,2,1,0:T(4,128)S(1)}, f32[9,2,4,128]{3,2,1,0:T(4,128)S(1)}, u32[]{:S(2)}, u32[]{:S(2)}) collective-permute-start(f32[9,2,4,128]{3,2,1,0:T(4,128)S(1)} %get-tuple-element.38), channel_id=1, source_target_pairs={{0,4},{4,8},{8,12},{12,16},{16,20},{20,24},{24,28},{28,0},{1,5},{5... | collective-permute-start | bytes 110600 | tf_op jit(solution)/shard_map/ppermute | solution.py:22
  58.6 9.5 %collective-permute-start.9 = (f32[9,2,4,128]{3,2,1,0:T(4,128)S(1)}, f32[9,2,4,128]{3,2,1,0:T(4,128)S(1)}, u32[]{:S(2)}, u32[]{:S(2)}) collective-permute-start(f32[9,2,4,128]{3,2,1,0:T(4,128)S(1)} %get-tuple-element.39), channel_id=1, source_target_pairs={{0,28},{4,0},{8,4},{12,8},{16,12},{20,16},{24,20},{28,24},{1,29},{... | collective-permute-start | bytes 110600 | tf_op jit(solution)/shard_map/ppermute | solution.py:22
  63.3 13.3 %collective-permute-start.6 = (f32[9,2,32,128]{3,2,1,0:T(8,128)S(1)}, f32[9,2,32,128]{3,2,1,0:T(8,128)S(1)}, u32[]{:S(2)}, u32[]{:S(2)}) collective-permute-start(f32[9,2,32,128]{3,2,1,0:T(8,128)S(1)} %get-tuple-element.35), channel_id=1, source_target_pairs={{0,4},{4,8},{8,12},{12,16},{16,20},{20,24},{24,28},{28,0},{1,5},{5... | collective-permute-start | bytes 884744 | tf_op jit(solution)/shard_map/ppermute | solution.py:22
  63.3 15.5 %collective-permute-start.7 = (f32[9,2,32,128]{3,2,1,0:T(8,128)S(1)}, f32[9,2,32,128]{3,2,1,0:T(8,128)S(1)}, u32[]{:S(2)}, u32[]{:S(2)}) collective-permute-start(f32[9,2,32,128]{3,2,1,0:T(8,128)S(1)} %get-tuple-element.36), channel_id=1, source_target_pairs={{0,28},{4,0},{8,4},{12,8},{16,12},{20,16},{24,20},{28,24},{1,29},{... | collective-permute-start | bytes 884744 | tf_op jit(solution)/shard_map/ppermute | solution.py:22
  68.2 4.2 %collective-permute-start.10 = (f32[9,12,2,128]{3,2,1,0:T(2,128)S(1)}, f32[9,12,2,128]{3,2,1,0:T(2,128)S(1)}, u32[]{:S(2)}, u32[]{:S(2)}) collective-permute-start(f32[9,12,2,128]{3,2,1,0:T(2,128)S(1)} %pad_maximum_fusion.4), channel_id=1, source_target_pairs={{0,1},{1,2},{2,3},{3,0},{4,5},{5,6},{6,7},{7,4},{8,9},{9,10},{10,1... | collective-permute-start | bytes 331784 | tf_op jit(solution)/shard_map/ppermute | solution.py:22
  68.3 4.3 %collective-permute-start.11 = (f32[9,12,2,128]{3,2,1,0:T(2,128)S(1)}, f32[9,12,2,128]{3,2,1,0:T(2,128)S(1)}, u32[]{:S(2)}, u32[]{:S(2)}) collective-permute-start(f32[9,12,2,128]{3,2,1,0:T(2,128)S(1)} %pad_maximum_fusion.5), channel_id=1, source_target_pairs={{0,3},{1,0},{2,1},{3,2},{4,7},{5,4},{6,5},{7,6},{8,11},{9,8},{10,9... | collective-permute-start | bytes 331784 | tf_op jit(solution)/shard_map/ppermute | solution.py:22
  82.7 9.4 %collective-permute-start.14 = (f32[9,2,4,64]{3,2,1,0:T(4,128)S(1)}, f32[9,2,4,64]{3,2,1,0:T(4,128)S(1)}, u32[]{:S(2)}, u32[]{:S(2)}) collective-permute-start(f32[9,2,4,64]{3,2,1,0:T(4,128)S(1)} %get-tuple-element.47), channel_id=1, source_target_pairs={{0,4},{4,8},{8,12},{12,16},{16,20},{20,24},{24,28},{28,0},{1,5},{5... | collective-permute-start | bytes 55304 | tf_op jit(solution)/shard_map/ppermute | solution.py:22
  83.0 9.2 %collective-permute-start.15 = (f32[9,2,4,64]{3,2,1,0:T(4,128)S(1)}, f32[9,2,4,64]{3,2,1,0:T(4,128)S(1)}, u32[]{:S(2)}, u32[]{:S(2)}) collective-permute-start(f32[9,2,4,64]{3,2,1,0:T(4,128)S(1)} %get-tuple-element.48), channel_id=1, source_target_pairs={{0,28},{4,0},{8,4},{12,8},{16,12},{20,16},{24,20},{28,24},{1,29},{... | collective-permute-start | bytes 55304 | tf_op jit(solution)/shard_map/ppermute | solution.py:22
  87.5 15.2 %collective-permute-start.12 = (f32[9,2,16,64]{3,2,1,0:T(8,128)S(1)}, f32[9,2,16,64]{3,2,1,0:T(8,128)S(1)}, u32[]{:S(2)}, u32[]{:S(2)}) collective-permute-start(f32[9,2,16,64]{3,2,1,0:T(8,128)S(1)} %get-tuple-element.44), channel_id=1, source_target_pairs={{0,4},{4,8},{8,12},{12,16},{16,20},{20,24},{24,28},{28,0},{1,5},{5... | collective-permute-start | bytes 221192 | tf_op jit(solution)/shard_map/ppermute | solution.py:22
  87.5 15.2 %collective-permute-start.13 = (f32[9,2,16,64]{3,2,1,0:T(8,128)S(1)}, f32[9,2,16,64]{3,2,1,0:T(8,128)S(1)}, u32[]{:S(2)}, u32[]{:S(2)}) collective-permute-start(f32[9,2,16,64]{3,2,1,0:T(8,128)S(1)} %get-tuple-element.45), channel_id=1, source_target_pairs={{0,28},{4,0},{8,4},{12,8},{16,12},{20,16},{24,20},{28,24},{1,29},{... | collective-permute-start | bytes 221192 | tf_op jit(solution)/shard_map/ppermute | solution.py:22
  92.3 10.4 %collective-permute-start.16 = (f32[9,8,2,64]{3,2,1,0:T(2,128)S(1)}, f32[9,8,2,64]{3,2,1,0:T(2,128)S(1)}, u32[]{:S(2)}, u32[]{:S(2)}) collective-permute-start(f32[9,8,2,64]{3,2,1,0:T(2,128)S(1)} %pad_maximum_fusion.6), channel_id=1, source_target_pairs={{0,1},{1,2},{2,3},{3,0},{4,5},{5,6},{6,7},{7,4},{8,9},{9,10},{10,1... | collective-permute-start | bytes 110600 | tf_op jit(solution)/shard_map/ppermute | solution.py:22
  92.4 10.3 %collective-permute-start.17 = (f32[9,8,2,64]{3,2,1,0:T(2,128)S(1)}, f32[9,8,2,64]{3,2,1,0:T(2,128)S(1)}, u32[]{:S(2)}, u32[]{:S(2)}) collective-permute-start(f32[9,8,2,64]{3,2,1,0:T(2,128)S(1)} %pad_maximum_fusion.7), channel_id=1, source_target_pairs={{0,3},{1,0},{2,1},{3,2},{4,7},{5,4},{6,5},{7,6},{8,11},{9,8},{10,9... | collective-permute-start | bytes 110600 | tf_op jit(solution)/shard_map/ppermute | solution.py:22
  94.2 8.5 %copy-start.2 = (f32[128,128]{1,0:T(8,128)S(1)}, f32[128,128]{1,0:T(8,128)}, u32[]{:S(2)}) copy-start(f32[128,128]{1,0:T(8,128)} %constant.8.clone.refs_5_) | copy-start | bytes 196612
where the time goes:
time: 105 us
  Pallas kernels  35.9 us (34%)
  starting transfers between devices  35.3 us (34%)
  waiting for transfers between devices  27.6 us (26%)
  local copies, waits for them, and re-layouts  4.4 us (4%)
    ppermute x18, starting transfers between devices, shifted(): lax.ppermute(block, axis, [(i, (i + distance) % size) for i in range(size)])  35.3 us
    ppermute x18, waiting for transfers between devices, shifted(): lax.ppermute(block, axis, [(i, (i + distance) % size) for i in range(size)])  27.6 us
    pallas_call x1, Pallas kernels, local_pass(): pl.pallas_call(local_kernel, grid=(nx,), in_specs=[pl.BlockSpec((3, 1, ny...  15.7 us
    pallas_call x1, Pallas kernels, detail_pass(): pl.pallas_call(detail_kernel, grid=(9,), in_specs=[pl.BlockSpec((3, 1, nx...  8.46 us
    pallas_call x1, Pallas kernels, approx_pass(): pl.pallas_call(approx_kernel, grid=(9,), in_specs=[per_field((nx, half, l...  5.99 us
    pallas_call x2, Pallas kernels, level_pass(): pl.pallas_call(lambda *refs: level_kernel(last, nz, *refs), in_specs=[vme...  5.79 us
  transfers between devices with their start and end apart: 18, of which 6 were waited for; matrix products, arithmetic and copies ran while one was open for 3% of the time, Pallas kernels for 23%

commit v1 on v0

--- a/solution.py
+++ b/solution.py
@@ -149,8 +149,8 @@
         grid=(nx,),
         in_specs=[
             pl.BlockSpec((3, 1, ny, nz), lambda i: (0, i, 0, 0)),
-            pl.BlockSpec((3, 1, BEFORE, nz), lambda i: (0, i + BEFORE, 0, 0)),
-            pl.BlockSpec((3, 1, AFTER, nz), lambda i: (0, i + BEFORE, 0, 0)),
+            pl.BlockSpec((3, 1, BEFORE, nz), lambda i: (0, i, 0, 0)),
+            pl.BlockSpec((3, 1, AFTER, nz), lambda i: (0, i, 0, 0)),
             pl.BlockSpec((nz, nz), lambda i: (0, 0)),
         ],
         out_specs=[
@@ -179,7 +179,6 @@
     edge_before, mid_before, edge_after, mid_after, row_before, row_after = refs
     mid = mid_before.shape[2]
     ny = mid + 16
-    nx = row_before.shape[1] - BEFORE - AFTER
     lanes = rows_ref.shape[2]
     count = ny // 2 + 16
     even_ref[3] = jnp.ones(even_ref.shape[1:], jnp.float32)
@@ -187,16 +186,16 @@
     for c in range(3):
         for layer in range(BEFORE + AFTER):
             if layer < BEFORE:
-                edge, middle, at, line = edge_before, mid_before, layer, layer
+                edge, middle, at = edge_before, mid_before, layer
             else:
-                edge, middle, at, line = edge_after, mid_after, layer - BEFORE, layer + nx
+                edge, middle, at = edge_after, mid_after, layer - BEFORE
             for h in range(2):
                 cut = pl.ds(h * lanes, lanes)
-                rows_ref[h, 12:16, :] = row_before[c, line, :, cut]
+                rows_ref[h, 12:16, :] = row_before[c, layer, :, cut]
                 rows_ref[h, 16:24, :] = edge[c, at, 0:8, cut]
                 rows_ref[h, 24 : 24 + mid, :] = middle[c, at, :, cut]
                 rows_ref[h, 24 + mid : 32 + mid, :] = edge[c, at, 8:16, cut]
-                rows_ref[h, 16 + ny : 16 + ny + AFTER, :] = row_after[c, line, :, cut]
+                rows_ref[h, 16 + ny : 16 + ny + AFTER, :] = row_after[c, layer, :, cut]
                 even_ref[c, layer, :, cut] = rows_ref[h, pl.ds(0, count, stride=2), :]
                 odd_ref[c, layer, :, cut] = rows_ref[h, pl.ds(1, count, stride=2), :]
 
@@ -457,15 +456,19 @@
     edge_after = shifted(edges(head), "gx", -1)
     mid_before = shifted(tail[:, :, 8 : ny - 8], "gx", 1)
     mid_after = shifted(head[:, :, 8 : ny - 8], "gx", -1)
-    down = jnp.concatenate([edge_before[:, :, 12:], velocity[:, :, ny - BEFORE :], edge_after[:, :, 12:]], axis=1)
-    up = jnp.concatenate([edge_before[:, :, :AFTER], velocity[:, :, :AFTER], edge_after[:, :, :AFTER]], axis=1)
+    own_before = shifted(velocity[:, :, ny - BEFORE :], "gy", 1)
+    own_after = shifted(velocity[:, :, :AFTER], "gy", -1)
+    low, rest = local_pass(velocity, own_before, own_after, table)
+    edge_before, edge_after, low = lax.optimization_barrier((edge_before, edge_after, low))
+    down = jnp.concatenate([edge_before[:, :, 12:], edge_after[:, :, 12:]], axis=1)
+    up = jnp.concatenate([edge_before[:, :, :AFTER], edge_after[:, :, :AFTER]], axis=1)
     row_before = shifted(down, "gy", 1)
     row_after = shifted(up, "gy", -1)
-    low, rest = local_pass(velocity, row_before, row_after, table)
     halo = (edge_before, mid_before, edge_after, mid_after, row_before, row_after)
     approx, high, stress_one, *sends = approx_pass(low, halo, table)
     second_halo = exchange(*sends)
     details_one = detail_pass(rest, high, halo, table)
+    approx, details_one = lax.optimization_barrier((approx, details_one))
     details_two, stress_two, approx, *sends = level_pass(approx, second_halo, False)
     details_three, stress_three, coarse = level_pass(approx, exchange(*sends), True)
     return details_one, stress_one, details_two, stress_two, details_three, stress_three, coarse

time: 105 us -> 88.9 us (0.85)
  waiting for transfers between devices: 27.6 us -> 9.05 us
  starting transfers between devices: 35.3 us -> 36.4 us
  local copies, waits for them, and re-layouts: 4.4 us -> 5.46 us
    ppermute x18 -> x20, waiting for transfers between devices: 27.6 us -> 9.05 us  [shifted(): lax.ppermute(block, axis, [(i, (i + distance) % size) for i in range(size)])]
    slice x2, local copies, waits for them, and re-layouts: 0.08 us -> 2.06 us  [the longest x1 1.04 us: body(): own_before = shifted(velocity[:, :, ny - BEFORE:], 'gy', 1)]
    ppermute x18 -> x20, starting transfers between devices: 35.3 us -> 36.4 us  [shifted(): lax.ppermute(block, axis, [(i, (i + distance) % size) for i in range(size)])]
  transfers between devices with their start and end apart: 18 -> 20, of which waited for: 6 -> 4; matrix products, arithmetic and copies ran while one was open for 3% -> 5% of each run, Pallas kernels for 23% -> 28%
where the time goes in v1:
time: 88.9 us; the launch traced here: 88.1 us
  starting transfers between devices  36.4 us (41%)
  Pallas kernels  36 us (40%)
  waiting for transfers between devices  9.05 us (10%)
  local copies, waits for them, and re-layouts  5.46 us (6%)
    ppermute x20, starting transfers between devices, shifted(): lax.ppermute(block, axis, [(i, (i + distance) % size) for i in range(size)])  36.4 us
    pallas_call x1, Pallas kernels, local_pass(): pl.pallas_call(local_kernel, grid=(nx,), in_specs=[pl.BlockSpec((3, 1, ny...  15.8 us
    ppermute x20, waiting for transfers between devices, shifted(): lax.ppermute(block, axis, [(i, (i + distance) % size) for i in range(size)])  9.05 us
    pallas_call x1, Pallas kernels, detail_pass(): pl.pallas_call(detail_kernel, grid=(9,), in_specs=[pl.BlockSpec((3, 1, nx...  8.46 us
    pallas_call x1, Pallas kernels, approx_pass(): pl.pallas_call(approx_kernel, grid=(9,), in_specs=[per_field((nx, half, l...  6 us
    pallas_call x2, Pallas kernels, level_pass(): pl.pallas_call(lambda *refs: level_kernel(last, nz, *refs), in_specs=[vme...  5.77 us
  transfers between devices with their start and end apart: 20, of which 4 were waited for; matrix products, arithmetic and copies ran while one was open for 5% of the time, Pallas kernels for 28%

profile of v1, /device:TPU:0, one launch (start us, length us, event | category | flops | bytes accessed | tf_op | source)
XLA Modules:
  0.0 88.1 jit_solution(9736079272649826811)
XLA Ops:
  0.6 0.0 copy-start
  0.6 0.0 copy-start.1
  0.7 1.1 %fusion.1 = (f32[3,4,8,256]{3,2,1,0:T(8,128)S(1)}, f32[3,4,8,256]{3,2,1,0:T(8,128)S(1)}) fusion(f32[3,16,64,256]{3,2,1,0:T(8,128)} %v_ref.1), kind=kLoop, calls=%fused_computation.9 | loop fusion | bytes 393216 | tf_op jit(solution)/shard_map/slice | solution.py:454
  1.8 3.0 %collective-permute-start = (f32[3,4,16,256]{3,2,1,0:T(8,128)S(1)}, f32[3,4,16,256]{3,2,1,0:T(8,128)S(1)}, u32[]{:S(2)}, u32[]{:S(2)}) collective-permute-start(f32[3,4,16,256]{3,2,1,0:T(8,128)S(1)} %pad_maximum_fusion), channel_id=1, source_target_pairs={{0,4},{4,8},{8,12},{12,16},{16,20},{20,24},{24,28},{28,0},{1,5},{5... | collective-permute-start | bytes 589832 | tf_op jit(solution)/shard_map/ppermute | solution.py:22
  4.8 1.0 %slice.73 = f32[3,16,3,256]{3,2,1,0:T(4,128)S(1)} slice(f32[3,16,64,256]{3,2,1,0:T(8,128)} %v_ref.1), slice={[0:3], [0:16], [0:3], [0:256]} | slice | bytes 294912 | tf_op jit(solution)/shard_map/slice | solution.py:460
  5.8 0.7 collective-permute-start.3
  6.6 1.0 %slice.72 = f32[3,16,4,256]{3,2,1,0:T(4,128)S(1)} slice(f32[3,16,64,256]{3,2,1,0:T(8,128)} %v_ref.1), slice={[0:3], [0:16], [60:64], [0:256]} | slice | bytes 393216 | tf_op jit(solution)/shard_map/slice | solution.py:459
  7.6 0.1 collective-permute-start.2
  7.7 1.1 %slice.75 = f32[3,3,48,256]{3,2,1,0:T(8,128)S(1)} slice(f32[3,16,64,256]{3,2,1,0:T(8,128)} %v_ref.1), slice={[0:3], [0:3], [8:56], [0:256]} | slice | bytes 884736 | tf_op jit(solution)/shard_map/slice | solution.py:458
  8.7 3.4 %collective-permute-start.5 = (f32[3,3,48,256]{3,2,1,0:T(8,128)S(1)}, f32[3,3,48,256]{3,2,1,0:T(8,128)S(1)}, u32[]{:S(2)}, u32[]{:S(2)}) collective-permute-start(f32[3,3,48,256]{3,2,1,0:T(8,128)S(1)} %slice.75), channel_id=1, source_target_pairs={{0,28},{4,0},{8,4},{12,8},{16,12},{20,16},{24,20},{28,24},{1,29},{... | collective-permute-start | bytes 1327112 | tf_op jit(solution)/shard_map/ppermute | solution.py:22
  12.1 1.1 %slice.74 = f32[3,4,48,256]{3,2,1,0:T(8,128)S(1)} slice(f32[3,16,64,256]{3,2,1,0:T(8,128)} %v_ref.1), slice={[0:3], [12:16], [8:56], [0:256]} | slice | bytes 1179648 | tf_op jit(solution)/shard_map/slice | solution.py:457
  13.2 0.1 collective-permute-start.4
  13.4 0.0 collective-permute-done.3.after_ref
  13.4 4.7 %collective-permute-start.1 = (f32[3,3,16,256]{3,2,1,0:T(8,128)S(1)}, f32[3,3,16,256]{3,2,1,0:T(8,128)S(1)}, u32[]{:S(2)}, u32[]{:S(2)}) collective-permute-start(f32[3,3,16,256]{3,2,1,0:T(8,128)S(1)} %pad_maximum_fusion.1), channel_id=1, source_target_pairs={{0,28},{4,0},{8,4},{12,8},{16,12},{20,16},{24,20},{28,24},{1,29},{... | collective-permute-start | bytes 442376 | tf_op jit(solution)/shard_map/ppermute | solution.py:22
  18.1 0.0 collective-permute-done.2.before_ref
  18.1 15.8 %local_pass.1 = (f32[9,16,32,128]{3,2,1,0:T(8,128)S(1)}, f32[3,9,16,32,128]{4,3,2,1,0:T(8,128)S(1)}) custom-call(f32[3,16,64,256]{3,2,1,0:T(8,128)S(1)} %copy-done.1, f32[3,16,4,256]{3,2,1,0:T(4,128)S(1)} %collective-permute-done.2.before_ref, f32[3,16,3,256]{3,2,1,0:T(4,128)S(1)} %collective-permute-done.3.after_ref, f32[256,256]{1,0:T(8,128)S(1)} %copy-done), custom_call_target="tpu_custom_call" | custom-call | flops 1207959552 | bytes 14155776 | tf_op jit(solution)/shard_map/local_pass/pallas_call | solution.py:147
  33.9 4.1 %collective-permute-done.1.refs_4_.refs_5_ = f32[3,3,16,256]{3,2,1,0:T(8,128)S(1)} collective-permute-done((f32[3,3,16,256]{3,2,1,0:T(8,128)S(1)}, f32[3,3,16,256]{3,2,1,0:T(8,128)S(1)}, u32[]{:S(2)}, u32[]{:S(2)}) %collective-permute-start.1) | collective-permute-done | bytes 147488 | tf_op jit(solution)/shard_map/ppermute | solution.py:22
  38.0 0.0 collective-permute-done.refs_2_.refs_3_
  38.1 0.2 collective-permute-start.6
  38.3 1.7 %collective-permute-start.7 = (f32[3,7,3,256]{3,2,1,0:T(4,128)S(1)}, f32[3,7,3,256]{3,2,1,0:T(4,128)S(1)}, u32[]{:S(2)}, u32[]{:S(2)}) collective-permute-start(f32[3,7,3,256]{3,2,1,0:T(4,128)S(1)} %pad_maximum_fusion.5), channel_id=1, source_target_pairs={{0,3},{1,0},{2,1},{3,2},{4,7},{5,4},{6,5},{7,6},{8,11},{9,8},{10,9... | collective-permute-start | bytes 193544 | tf_op jit(solution)/shard_map/ppermute | solution.py:22
  40.0 2.1 %collective-permute-done.7.refs_7_.refs_8_ = f32[3,7,3,256]{3,2,1,0:T(4,128)S(1)} collective-permute-done((f32[3,7,3,256]{3,2,1,0:T(4,128)S(1)}, f32[3,7,3,256]{3,2,1,0:T(4,128)S(1)}, u32[]{:S(2)}, u32[]{:S(2)}) %collective-permute-start.7) | collective-permute-done | bytes 64544 | tf_op jit(solution)/shard_map/ppermute | solution.py:22
  42.1 0.0 collective-permute-done.6.refs_6_.refs_7_
  42.1 0.0 collective-permute-done.5.refs_5_.refs_6_
  42.1 0.0 collective-permute-done.4.refs_3_.refs_4_
  42.1 6.0 %approx_pass.1 = (f32[9,8,32,128]{3,2,1,0:T(8,128)S(1)}, f32[9,8,32,128]{3,2,1,0:T(8,128)S(1)}, f32[6,8,32,128]{3,2,1,0:T(8,128)}, f32[9,2,32,128]{3,2,1,0:T(8,1...) custom-call(f32[9,16,32,128]{3,2,1,0:T(8,128)S(1)} %get-tuple-elemen, ...), custom_call_target="tpu_custom_call" | custom-call | tf_op jit(solution)/shard_map/approx_pass/pallas_call | solution.py:282
  48.1 0.0 collective-permute-start.10
  48.1 4.7 %collective-permute-start.11 = (f32[9,2,4,128]{3,2,1,0:T(4,128)S(1)}, f32[9,2,4,128]{3,2,1,0:T(4,128)S(1)}, u32[]{:S(2)}, u32[]{:S(2)}) collective-permute-start(f32[9,2,4,128]{3,2,1,0:T(4,128)S(1)} %get-tuple-element.49), channel_id=1, source_target_pairs={{0,28},{4,0},{8,4},{12,8},{16,12},{20,16},{24,20},{28,24},{1,29},{... | collective-permute-start | bytes 110600 | tf_op jit(solution)/shard_map/ppermute | solution.py:22
  52.8 0.0 collective-permute-start.8
  52.8 4.7 %collective-permute-start.9 = (f32[9,2,32,128]{3,2,1,0:T(8,128)S(1)}, f32[9,2,32,128]{3,2,1,0:T(8,128)S(1)}, u32[]{:S(2)}, u32[]{:S(2)}) collective-permute-start(f32[9,2,32,128]{3,2,1,0:T(8,128)S(1)} %get-tuple-element.46), channel_id=1, source_target_pairs={{0,28},{4,0},{8,4},{12,8},{16,12},{20,16},{24,20},{28,24},{1,29},{... | collective-permute-start | bytes 884744 | tf_op jit(solution)/shard_map/ppermute | solution.py:22
  57.6 0.0 collective-permute-done.10
  57.6 0.0 collective-permute-done.11
  57.6 0.1 pad_maximum_fusion.2
  57.7 0.6 collective-permute-start.12
  58.4 1.2 %collective-permute-start.13 = (f32[9,12,2,128]{3,2,1,0:T(2,128)S(1)}, f32[9,12,2,128]{3,2,1,0:T(2,128)S(1)}, u32[]{:S(2)}, u32[]{:S(2)}) collective-permute-start(f32[9,12,2,128]{3,2,1,0:T(2,128)S(1)} %pad_maximum_fusion.3), channel_id=1, source_target_pairs={{0,3},{1,0},{2,1},{3,2},{4,7},{5,4},{6,5},{7,6},{8,11},{9,8},{10,9... | collective-permute-start | bytes 331784 | tf_op jit(solution)/shard_map/ppermute | solution.py:22
  59.6 8.5 %detail_pass.1 = f32[7,9,8,32,128]{4,3,2,1,0:T(8,128)} custom-call(f32[3,9,16,32,128]{4,3,2,1,0:T(8,128)S(1)} %get-tuple-element.40.refs_0_, f32[9,8,32,128]{3,2,1,0:T(8,128)S(1)} %get-tuple-element.41.refs_1_, f32[256,256]{1,0:T(8,128)S(1)} %copy-done, f32[3,4,16,256]{3,2,1,0:T(8,128)S(1)} %collective-permute-done.refs_2_.refs_3_, ...), custom_call_target="tpu_custom_call" | custom-call | flops 235929600 | bytes 18874368 | tf_op jit(solution)/shard_map/detail_pass/pallas_call | solution.py:338
  68.0 0.0 collective-permute-done.12.refs_3_
  68.0 0.8 collective-permute-done.9.refs_2_
  68.9 3.9 %second_level.1 = (f32[7,9,4,16,64]{4,3,2,1,0:T(8,128)}, f32[6,4,16,64]{3,2,1,0:T(8,128)}, f32[9,4,16,64]{3,2,1,0:T(8,128)S(1)}, f32[9,2,16,64]{3,2,1,0:T(8,128)...) custom-call(f32[9,8,32,128]{3,2,1,0:T(8,128)S(1)} %get-tuple-element, ...), custom_call_target="tpu_custom_call" | custom-call | tf_op jit(solution)/shard_map/second_level/pallas_call | solution.py:424
  72.8 0.0 collective-permute-start.16
  72.8 4.7 %collective-permute-start.17 = (f32[9,2,4,64]{3,2,1,0:T(4,128)S(1)}, f32[9,2,4,64]{3,2,1,0:T(4,128)S(1)}, u32[]{:S(2)}, u32[]{:S(2)}) collective-permute-start(f32[9,2,4,64]{3,2,1,0:T(4,128)S(1)} %get-tuple-element.58), channel_id=1, source_target_pairs={{0,28},{4,0},{8,4},{12,8},{16,12},{20,16},{24,20},{28,24},{1,29},{... | collective-permute-start | bytes 55304 | tf_op jit(solution)/shard_map/ppermute | solution.py:22
  77.5 0.0 collective-permute-start.14
  77.5 4.7 %collective-permute-start.15 = (f32[9,2,16,64]{3,2,1,0:T(8,128)S(1)}, f32[9,2,16,64]{3,2,1,0:T(8,128)S(1)}, u32[]{:S(2)}, u32[]{:S(2)}) collective-permute-start(f32[9,2,16,64]{3,2,1,0:T(8,128)S(1)} %get-tuple-element.55), channel_id=1, source_target_pairs={{0,28},{4,0},{8,4},{12,8},{16,12},{20,16},{24,20},{28,24},{1,29},{... | collective-permute-start | bytes 221192 | tf_op jit(solution)/shard_map/ppermute | solution.py:22
  82.3 0.0 collective-permute-done.17
  82.3 0.1 collective-permute-start.18
  82.5 1.8 %collective-permute-start.19 = (f32[9,8,2,64]{3,2,1,0:T(2,128)S(1)}, f32[9,8,2,64]{3,2,1,0:T(2,128)S(1)}, u32[]{:S(2)}, u32[]{:S(2)}) collective-permute-start(f32[9,8,2,64]{3,2,1,0:T(2,128)S(1)} %pad_maximum_fusion.7), channel_id=1, source_target_pairs={{0,3},{1,0},{2,1},{3,2},{4,7},{5,4},{6,5},{7,6},{8,11},{9,8},{10,9... | collective-permute-start | bytes 110600 | tf_op jit(solution)/shard_map/ppermute | solution.py:22
  84.2 1.9 %collective-permute-done.18.refs_3_ = f32[9,8,2,64]{3,2,1,0:T(2,128)S(1)} collective-permute-done((f32[9,8,2,64]{3,2,1,0:T(2,128)S(1)}, f32[9,8,2,64]{3,2,1,0:T(2,128)S(1)}, u32[]{:S(2)}, u32[]{:S(2)}) %collective-permute-start.18) | collective-permute-done | bytes 36896 | tf_op jit(solution)/shard_map/ppermute | solution.py:22
  86.2 0.0 collective-permute-done.19.refs_4_
  86.2 1.8 %last_level.1 = (f32[7,9,2,8,32]{4,3,2,1,0:T(8,128)}, f32[6,2,8,32]{3,2,1,0:T(8,128)}, f32[3,2,8,32]{3,2,1,0:T(8,128)}) custom-call(f32[9,4,16,64]{3,2,1,0:T(8,128)S(1)} %get-tuple-element.53.refs_0_, f32[9,2,16,64]{3,2,1,0:T(8,128)S(1)} %collective-permute-done.14.refs_1_, f32[9,2,16,64]{3,2,1,0:T(8,128)S(1)} %collective-permute-done.15.refs_2_, ...), custom_call_target="tpu_custom_call" | custom-call | tf_op jit(solution)/shard_map/last_level/pallas_call | solution.py:424
  (27 shorter events, 0.3 us)
Async XLA Ops:
  0.6 17.5 %copy-start = (f32[256,256]{1,0:T(8,128)S(1)}, f32[256,256]{1,0:T(8,128)}, u32[]{:S(2)}) copy-start(f32[256,256]{1,0:T(8,128)} %constant.6.clone.table_ref.refs_1_.refs_2_) | copy-start | bytes 786436
  0.6 12.7 %copy-start.1 = (f32[3,16,64,256]{3,2,1,0:T(8,128)S(1)}, f32[3,16,64,256]{3,2,1,0:T(8,128)}, u32[]{:S(2)}) copy-start(f32[3,16,64,256]{3,2,1,0:T(8,128)} %v_ref.1) | copy-start | bytes 9437188
  1.8 36.2 %collective-permute-start = (f32[3,4,16,256]{3,2,1,0:T(8,128)S(1)}, f32[3,4,16,256]{3,2,1,0:T(8,128)S(1)}, u32[]{:S(2)}, u32[]{:S(2)}) collective-permute-start(f32[3,4,16,256]{3,2,1,0:T(8,128)S(1)} %pad_maximum_fusion), channel_id=1, source_target_pairs={{0,4},{4,8},{8,12},{12,16},{16,20},{20,24},{24,28},{28,0},{1,5},{5... | collective-permute-start | bytes 589832 | tf_op jit(solution)/shard_map/ppermute | solution.py:22
  5.8 7.5 %collective-permute-start.3 = (f32[3,16,3,256]{3,2,1,0:T(4,128)S(1)}, f32[3,16,3,256]{3,2,1,0:T(4,128)S(1)}, u32[]{:S(2)}, u32[]{:S(2)}) collective-permute-start(f32[3,16,3,256]{3,2,1,0:T(4,128)S(1)} %slice.73), channel_id=1, source_target_pairs={{0,3},{1,0},{2,1},{3,2},{4,7},{5,4},{6,5},{7,6},{8,11},{9,8},{10,9... | collective-permute-start | bytes 442376 | tf_op jit(solution)/shard_map/ppermute | solution.py:22
  7.6 10.5 %collective-permute-start.2 = (f32[3,16,4,256]{3,2,1,0:T(4,128)S(1)}, f32[3,16,4,256]{3,2,1,0:T(4,128)S(1)}, u32[]{:S(2)}, u32[]{:S(2)}) collective-permute-start(f32[3,16,4,256]{3,2,1,0:T(4,128)S(1)} %slice.72), channel_id=1, source_target_pairs={{0,1},{1,2},{2,3},{3,0},{4,5},{5,6},{6,7},{7,4},{8,9},{9,10},{10,1... | collective-permute-start | bytes 589832 | tf_op jit(solution)/shard_map/ppermute | solution.py:22
  8.7 33.4 %collective-permute-start.5 = (f32[3,3,48,256]{3,2,1,0:T(8,128)S(1)}, f32[3,3,48,256]{3,2,1,0:T(8,128)S(1)}, u32[]{:S(2)}, u32[]{:S(2)}) collective-permute-start(f32[3,3,48,256]{3,2,1,0:T(8,128)S(1)} %slice.75), channel_id=1, source_target_pairs={{0,28},{4,0},{8,4},{12,8},{16,12},{20,16},{24,20},{28,24},{1,29},{... | collective-permute-start | bytes 1327112 | tf_op jit(solution)/shard_map/ppermute | solution.py:22
  13.2 28.9 %collective-permute-start.4 = (f32[3,4,48,256]{3,2,1,0:T(8,128)S(1)}, f32[3,4,48,256]{3,2,1,0:T(8,128)S(1)}, u32[]{:S(2)}, u32[]{:S(2)}) collective-permute-start(f32[3,4,48,256]{3,2,1,0:T(8,128)S(1)} %slice.74), channel_id=1, source_target_pairs={{0,4},{4,8},{8,12},{12,16},{16,20},{20,24},{24,28},{28,0},{1,5},{5... | collective-permute-start | bytes 1769480 | tf_op jit(solution)/shard_map/ppermute | solution.py:22
  13.4 24.7 %collective-permute-start.1 = (f32[3,3,16,256]{3,2,1,0:T(8,128)S(1)}, f32[3,3,16,256]{3,2,1,0:T(8,128)S(1)}, u32[]{:S(2)}, u32[]{:S(2)}) collective-permute-start(f32[3,3,16,256]{3,2,1,0:T(8,128)S(1)} %pad_maximum_fusion.1), channel_id=1, source_target_pairs={{0,28},{4,0},{8,4},{12,8},{16,12},{20,16},{24,20},{28,24},{1,29},{... | collective-permute-start | bytes 442376 | tf_op jit(solution)/shard_map/ppermute | solution.py:22
  38.1 4.0 %collective-permute-start.6 = (f32[3,7,4,256]{3,2,1,0:T(4,128)S(1)}, f32[3,7,4,256]{3,2,1,0:T(4,128)S(1)}, u32[]{:S(2)}, u32[]{:S(2)}) collective-permute-start(f32[3,7,4,256]{3,2,1,0:T(4,128)S(1)} %pad_maximum_fusion.4), channel_id=1, source_target_pairs={{0,1},{1,2},{2,3},{3,0},{4,5},{5,6},{6,7},{7,4},{8,9},{9,10},{10,1... | collective-permute-start | bytes 258056 | tf_op jit(solution)/shard_map/ppermute | solution.py:22
  38.3 3.8 %collective-permute-start.7 = (f32[3,7,3,256]{3,2,1,0:T(4,128)S(1)}, f32[3,7,3,256]{3,2,1,0:T(4,128)S(1)}, u32[]{:S(2)}, u32[]{:S(2)}) collective-permute-start(f32[3,7,3,256]{3,2,1,0:T(4,128)S(1)} %pad_maximum_fusion.5), channel_id=1, source_target_pairs={{0,3},{1,0},{2,1},{3,2},{4,7},{5,4},{6,5},{7,6},{8,11},{9,8},{10,9... | collective-permute-start | bytes 193544 | tf_op jit(solution)/shard_map/ppermute | solution.py:22
  48.1 9.4 %collective-permute-start.10 = (f32[9,2,4,128]{3,2,1,0:T(4,128)S(1)}, f32[9,2,4,128]{3,2,1,0:T(4,128)S(1)}, u32[]{:S(2)}, u32[]{:S(2)}) collective-permute-start(f32[9,2,4,128]{3,2,1,0:T(4,128)S(1)} %get-tuple-element.48), channel_id=1, source_target_pairs={{0,4},{4,8},{8,12},{12,16},{16,20},{20,24},{24,28},{28,0},{1,5},{5... | collective-permute-start | bytes 110600 | tf_op jit(solution)/shard_map/ppermute | solution.py:22
  48.1 9.5 %collective-permute-start.11 = (f32[9,2,4,128]{3,2,1,0:T(4,128)S(1)}, f32[9,2,4,128]{3,2,1,0:T(4,128)S(1)}, u32[]{:S(2)}, u32[]{:S(2)}) collective-permute-start(f32[9,2,4,128]{3,2,1,0:T(4,128)S(1)} %get-tuple-element.49), channel_id=1, source_target_pairs={{0,28},{4,0},{8,4},{12,8},{16,12},{20,16},{24,20},{28,24},{1,29},{... | collective-permute-start | bytes 110600 | tf_op jit(solution)/shard_map/ppermute | solution.py:22
  52.8 15.2 %collective-permute-start.8 = (f32[9,2,32,128]{3,2,1,0:T(8,128)S(1)}, f32[9,2,32,128]{3,2,1,0:T(8,128)S(1)}, u32[]{:S(2)}, u32[]{:S(2)}) collective-permute-start(f32[9,2,32,128]{3,2,1,0:T(8,128)S(1)} %get-tuple-element.45), channel_id=1, source_target_pairs={{0,4},{4,8},{8,12},{12,16},{16,20},{20,24},{24,28},{28,0},{1,5},{5... | collective-permute-start | bytes 884744 | tf_op jit(solution)/shard_map/ppermute | solution.py:22
  52.8 16.0 %collective-permute-start.9 = (f32[9,2,32,128]{3,2,1,0:T(8,128)S(1)}, f32[9,2,32,128]{3,2,1,0:T(8,128)S(1)}, u32[]{:S(2)}, u32[]{:S(2)}) collective-permute-start(f32[9,2,32,128]{3,2,1,0:T(8,128)S(1)} %get-tuple-element.46), channel_id=1, source_target_pairs={{0,28},{4,0},{8,4},{12,8},{16,12},{20,16},{24,20},{28,24},{1,29},{... | collective-permute-start | bytes 884744 | tf_op jit(solution)/shard_map/ppermute | solution.py:22
  57.7 10.4 %collective-permute-start.12 = (f32[9,12,2,128]{3,2,1,0:T(2,128)S(1)}, f32[9,12,2,128]{3,2,1,0:T(2,128)S(1)}, u32[]{:S(2)}, u32[]{:S(2)}) collective-permute-start(f32[9,12,2,128]{3,2,1,0:T(2,128)S(1)} %pad_maximum_fusion.2), channel_id=1, source_target_pairs={{0,1},{1,2},{2,3},{3,0},{4,5},{5,6},{6,7},{7,4},{8,9},{9,10},{10,1... | collective-permute-start | bytes 331784 | tf_op jit(solution)/shard_map/ppermute | solution.py:22
  58.4 9.7 %collective-permute-start.13 = (f32[9,12,2,128]{3,2,1,0:T(2,128)S(1)}, f32[9,12,2,128]{3,2,1,0:T(2,128)S(1)}, u32[]{:S(2)}, u32[]{:S(2)}) collective-permute-start(f32[9,12,2,128]{3,2,1,0:T(2,128)S(1)} %pad_maximum_fusion.3), channel_id=1, source_target_pairs={{0,3},{1,0},{2,1},{3,2},{4,7},{5,4},{6,5},{7,6},{8,11},{9,8},{10,9... | collective-permute-start | bytes 331784 | tf_op jit(solution)/shard_map/ppermute | solution.py:22
  59.6 9.3 %copy-start.3 = (f32[128,128]{1,0:T(8,128)S(1)}, f32[128,128]{1,0:T(8,128)}, u32[]{:S(2)}) copy-start(f32[128,128]{1,0:T(8,128)} %constant.7.clone.refs_5_) | copy-start | bytes 196612
  59.6 26.7 %copy-start.2 = (f32[128,128]{1,0:T(8,128)S(1)}, f32[128,128]{1,0:T(8,128)}, u32[]{:S(2)}) copy-start(f32[128,128]{1,0:T(8,128)} %constant.8.clone.refs_5_) | copy-start | bytes 196612
  72.8 9.4 %collective-permute-start.16 = (f32[9,2,4,64]{3,2,1,0:T(4,128)S(1)}, f32[9,2,4,64]{3,2,1,0:T(4,128)S(1)}, u32[]{:S(2)}, u32[]{:S(2)}) collective-permute-start(f32[9,2,4,64]{3,2,1,0:T(4,128)S(1)} %get-tuple-element.57), channel_id=1, source_target_pairs={{0,4},{4,8},{8,12},{12,16},{16,20},{20,24},{24,28},{28,0},{1,5},{5... | collective-permute-start | bytes 55304 | tf_op jit(solution)/shard_map/ppermute | solution.py:22
  72.8 9.5 %collective-permute-start.17 = (f32[9,2,4,64]{3,2,1,0:T(4,128)S(1)}, f32[9,2,4,64]{3,2,1,0:T(4,128)S(1)}, u32[]{:S(2)}, u32[]{:S(2)}) collective-permute-start(f32[9,2,4,64]{3,2,1,0:T(4,128)S(1)} %get-tuple-element.58), channel_id=1, source_target_pairs={{0,28},{4,0},{8,4},{12,8},{16,12},{20,16},{24,20},{28,24},{1,29},{... | collective-permute-start | bytes 55304 | tf_op jit(solution)/shard_map/ppermute | solution.py:22
  77.5 8.7 %collective-permute-start.14 = (f32[9,2,16,64]{3,2,1,0:T(8,128)S(1)}, f32[9,2,16,64]{3,2,1,0:T(8,128)S(1)}, u32[]{:S(2)}, u32[]{:S(2)}) collective-permute-start(f32[9,2,16,64]{3,2,1,0:T(8,128)S(1)} %get-tuple-element.54), channel_id=1, source_target_pairs={{0,4},{4,8},{8,12},{12,16},{16,20},{20,24},{24,28},{28,0},{1,5},{5... | collective-permute-start | bytes 221192 | tf_op jit(solution)/shard_map/ppermute | solution.py:22
  77.5 8.7 %collective-permute-start.15 = (f32[9,2,16,64]{3,2,1,0:T(8,128)S(1)}, f32[9,2,16,64]{3,2,1,0:T(8,128)S(1)}, u32[]{:S(2)}, u32[]{:S(2)}) collective-permute-start(f32[9,2,16,64]{3,2,1,0:T(8,128)S(1)} %get-tuple-element.55), channel_id=1, source_target_pairs={{0,28},{4,0},{8,4},{12,8},{16,12},{20,16},{24,20},{28,24},{1,29},{... | collective-permute-start | bytes 221192 | tf_op jit(solution)/shard_map/ppermute | solution.py:22
  82.3 3.8 %collective-permute-start.18 = (f32[9,8,2,64]{3,2,1,0:T(2,128)S(1)}, f32[9,8,2,64]{3,2,1,0:T(2,128)S(1)}, u32[]{:S(2)}, u32[]{:S(2)}) collective-permute-start(f32[9,8,2,64]{3,2,1,0:T(2,128)S(1)} %pad_maximum_fusion.6), channel_id=1, source_target_pairs={{0,1},{1,2},{2,3},{3,0},{4,5},{5,6},{6,7},{7,4},{8,9},{9,10},{10,1... | collective-permute-start | bytes 110600 | tf_op jit(solution)/shard_map/ppermute | solution.py:22
  82.5 3.8 %collective-permute-start.19 = (f32[9,8,2,64]{3,2,1,0:T(2,128)S(1)}, f32[9,8,2,64]{3,2,1,0:T(2,128)S(1)}, u32[]{:S(2)}, u32[]{:S(2)}) collective-permute-start(f32[9,8,2,64]{3,2,1,0:T(2,128)S(1)} %pad_maximum_fusion.7), channel_id=1, source_target_pairs={{0,3},{1,0},{2,1},{3,2},{4,7},{5,4},{6,5},{7,6},{8,11},{9,8},{10,9... | collective-permute-start | bytes 110600 | tf_op jit(solution)/shard_map/ppermute | solution.py:22

commit v2 on v1

--- a/solution.py
+++ b/solution.py
@@ -14,6 +14,7 @@
 product_pairs = ((0, 0), (0, 1), (0, 2), (1, 1), (1, 2), (2, 2))
 BEFORE = 4
 AFTER = 3
+GROUP = 3
 MIB = 1 << 20
 
 
@@ -66,10 +67,6 @@
     o2_before = o1_before + predict_two * (e1_before + first(e1))
     e2 = e1 + update_two * (preceding(o2, o2_before) + o2)
     return e2, o2
-
-
-def lead_lift(e, o, p, q, r, s):
-    return halo_lift_list(e, o, p, q, r, s)
 
 
 def halo_lift_list(e, o, p, q, r, s):
@@ -239,31 +236,37 @@
     def _():
         gather_rows(halo_refs, rows_ref, even_ref, odd_ref)
 
-    i, j = pair_of(f)
-    even = halo_parts(even_ref, i, j)
-    odd = halo_parts(odd_ref, i, j)
-    for k in range(4):
-        e, _ = ring_lift(even[k], odd[k])
-        stack_ref[k * half : (k + 1) * half, :] = e[8 : 8 + half]
+    pairs = [pair_of(f * GROUP + k) for k in range(GROUP)]
+    for n, (i, j) in enumerate(pairs):
+        even = halo_parts(even_ref, i, j)
+        odd = halo_parts(odd_ref, i, j)
+        for k in range(4):
+            e, _ = ring_lift(even[k], odd[k])
+            at = (4 * n + k) * half
+            stack_ref[at : at + half, :] = e[8 : 8 + half]
     out = dot(stack_ref[...], table_ref[:, :lanes])
-    halo = [out[k * half : (k + 1) * half] for k in range(4)]
-    e, o = lift_first([low_ref[0, x] for x in range(nx)], halo)
-    e = [t * band_scale(0, 0) for t in e]
-    for x in range(nx // 2):
-        approx_ref[0, x] = e[x]
-        high_ref[0, x] = o[x] * band_scale(0, 1)
-
-    @pl.when(f < 3)
+    fields = []
+    for n in range(GROUP):
+        halo = [out[(4 * n + k) * half : (4 * n + k + 1) * half] for k in range(4)]
+        e, o = lift_first([low_ref[n, x] for x in range(nx)], halo)
+        e = [t * band_scale(0, 0) for t in e]
+        for x in range(nx // 2):
+            approx_ref[n, x] = e[x]
+            high_ref[n, x] = o[x] * band_scale(0, 1)
+        send_parts(e, n, *sends)
+        fields.append(e)
+
+    @pl.when(f == 0)
     def _():
-        for x in range(nx // 2):
-            kept_ref[f, x] = e[x]
-
-    @pl.when(f >= 3)
+        for n in range(GROUP):
+            for x in range(nx // 2):
+                kept_ref[n, x] = fields[n][x]
+
+    @pl.when(f > 0)
     def _():
-        for x in range(nx // 2):
-            stress_ref[0, x] = e[x] - kept_ref[i, x] * kept_ref[j, x]
-
-    send_parts(e, 0, *sends)
+        for n, (i, j) in enumerate(pairs):
+            for x in range(nx // 2):
+                stress_ref[n, x] = approx_ref[n, x] - kept_ref[i, x] * kept_ref[j, x]
 
 
 def whole(shape):
@@ -271,7 +274,7 @@
 
 
 def per_field(shape):
-    return pl.BlockSpec((1,) + shape, lambda f: (f,) + (0,) * len(shape))
+    return pl.BlockSpec((GROUP,) + shape, lambda f: (f,) + (0,) * len(shape))
 
 
 def approx_pass(low, halo, table):
@@ -281,12 +284,12 @@
     sends = [(2, half, lanes), (2, half, lanes), (2, 4, lanes), (2, 4, lanes), (mx, 2, lanes), (mx, 2, lanes)]
     return pl.pallas_call(
         approx_kernel,
-        grid=(9,),
+        grid=(9 // GROUP,),
         in_specs=[per_field((nx, half, lanes)), whole((nz, nz))] + [whole(h.shape) for h in halo],
         out_specs=[
             per_field((mx, half, lanes)),
             per_field((mx, half, lanes)),
-            pl.BlockSpec((1, mx, half, lanes), lambda f: (jnp.maximum(f - 3, 0), 0, 0, 0)),
+            pl.BlockSpec((GROUP, mx, half, lanes), lambda f: (jnp.maximum(f - 1, 0), 0, 0, 0)),
         ]
         + [per_field(s) for s in sends],
         out_shape=[f32(9, mx, half, lanes), f32(9, mx, half, lanes), f32(6, mx, half, lanes)] + [f32(9, *s) for s in sends],
@@ -295,7 +298,7 @@
             pltpu.VMEM((4, BEFORE + AFTER, count, nz), jnp.float32),
             pltpu.VMEM((4, BEFORE + AFTER, count, nz), jnp.float32),
             pltpu.VMEM((3, mx, half, lanes), jnp.float32),
-            pltpu.VMEM((4 * half, nz), jnp.float32),
+            pltpu.VMEM((GROUP * 4 * half, nz), jnp.float32),
         ],
         compiler_params=pltpu.CompilerParams(vmem_limit_bytes=24 * MIB),
         name="approx_pass",
@@ -313,23 +316,30 @@
     def _():
         gather_rows(halo_refs, rows_ref, even_ref, odd_ref)
 
-    i, j = pair_of(f)
-    even = halo_parts(even_ref, i, j)
-    odd = halo_parts(odd_ref, i, j)
-    for k in range(4):
-        e, o = ring_lift(even[k], odd[k])
-        stack_ref[k * half : (k + 1) * half, :] = e[8 : 8 + half]
-        stack_ref[(4 + k) * half : (5 + k) * half, :] = o[8 : 8 + half]
-    out = dot(stack_ref[...], table_ref[...])
-    for x in range(nx // 2):
-        out_ref[0, 0, x] = high_ref[0, x]
-    for band, (bz, by) in enumerate(((0, 1), (1, 0), (1, 1))):
-        halo = [out[(4 * by + k) * half : (4 * by + k + 1) * half, bz * lanes : (bz + 1) * lanes] for k in range(4)]
-        e, o = lift_first([rest_ref[band, 0, x] for x in range(nx)], halo)
-        at = 4 * bz + 2 * by - 1
+    for n in range(GROUP):
+        i, j = pair_of(f * GROUP + n)
+        even = halo_parts(even_ref, i, j)
+        odd = halo_parts(odd_ref, i, j)
+        for k in range(4):
+            e, o = ring_lift(even[k], odd[k])
+            at = (8 * n + k) * half
+            stack_ref[at : at + half, :] = e[8 : 8 + half]
+            at += 4 * half
+            stack_ref[at : at + half, :] = o[8 : 8 + half]
+    stack_ref[...] = dot(stack_ref[...], table_ref[...])
+    for n in range(GROUP):
         for x in range(nx // 2):
-            out_ref[at, 0, x] = e[x] * band_scale(by, 0)
-            out_ref[at + 1, 0, x] = o[x] * band_scale(by, 1)
+            out_ref[0, n, x] = high_ref[n, x]
+        for band, (bz, by) in enumerate(((0, 1), (1, 0), (1, 1))):
+            halo = []
+            for k in range(4):
+                at = (8 * n + 4 * by + k) * half
+                halo.append(stack_ref[at : at + half, bz * lanes : (bz + 1) * lanes])
+            e, o = lift_first([rest_ref[band, n, x] for x in range(nx)], halo)
+            at = 4 * bz + 2 * by - 1
+            for x in range(nx // 2):
+                out_ref[at, n, x] = e[x] * band_scale(by, 0)
+                out_ref[at + 1, n, x] = o[x] * band_scale(by, 1)
 
 
 def detail_pass(rest, high, halo, table):
@@ -337,20 +347,20 @@
     nz, count, mx = 2 * lanes, half + 16, nx // 2
     return pl.pallas_call(
         detail_kernel,
-        grid=(9,),
+        grid=(9 // GROUP,),
         in_specs=[
-            pl.BlockSpec((3, 1, nx, half, lanes), lambda f: (0, f, 0, 0, 0)),
+            pl.BlockSpec((3, GROUP, nx, half, lanes), lambda f: (0, f, 0, 0, 0)),
             per_field((mx, half, lanes)),
             whole((nz, nz)),
         ]
         + [whole(h.shape) for h in halo],
-        out_specs=pl.BlockSpec((7, 1, mx, half, lanes), lambda f: (0, f, 0, 0, 0)),
+        out_specs=pl.BlockSpec((7, GROUP, mx, half, lanes), lambda f: (0, f, 0, 0, 0)),
         out_shape=jax.ShapeDtypeStruct((7, 9, mx, half, lanes), jnp.float32),
         scratch_shapes=[
             pltpu.VMEM((2, 2 * half + 32, lanes), jnp.float32),
             pltpu.VMEM((4, BEFORE + AFTER, count, nz), jnp.float32),
             pltpu.VMEM((4, BEFORE + AFTER, count, nz), jnp.float32),
-            pltpu.VMEM((8 * half, nz), jnp.float32),
+            pltpu.VMEM((GROUP * 8 * half, nz), jnp.float32),
         ],
         compiler_params=pltpu.CompilerParams(vmem_limit_bytes=24 * MIB),
         cost_estimate=pl.CostEstimate(flops=9 * nx * half * nz * 200, bytes_accessed=9 * nx * half * nz * 16, transcendentals=0),
@@ -368,6 +378,7 @@
     wide = table_ref.shape[0]
     if nz < wide:
         pad_ref[...] = jnp.zeros_like(pad_ref)
+    lines = (nx + 4) * ny
     for f in range(9):
         for layer in range(nx + 4):
             if layer < nx:
@@ -376,17 +387,21 @@
                 source = before_ref.at[f, layer - nx]
             else:
                 source = after_ref.at[f, layer - nx - 2]
-            pad_ref[layer, :, :nz] = source[...]
-            e = pad_ref[layer, pl.ds(0, half, stride=2), :]
-            o = pad_ref[layer, pl.ds(1, half, stride=2), :]
+            pad_ref[f, layer, :, :nz] = source[...]
+    for f in range(9):
+        for layer in range(nx + 4):
+            e = pad_ref[f, layer, pl.ds(0, half, stride=2), :]
+            o = pad_ref[f, layer, pl.ds(1, half, stride=2), :]
             rows = [down_ref[f, layer, 0:1, :], down_ref[f, layer, 1:2, :], up_ref[f, layer, 0:1, :], up_ref[f, layer, 1:2, :]]
             if nz < wide:
                 rows = [jnp.concatenate([row, jnp.zeros((1, wide - nz), jnp.float32)], axis=1) for row in rows]
             e, o = sublane_lift(e, o, *rows)
-            stack_ref[layer * ny : layer * ny + half, :] = e
-            stack_ref[layer * ny + half : (layer + 1) * ny, :] = o
-        out_ref[...] = dot(stack_ref[...], table_ref[...])
-        layers = [out_ref[layer * ny : (layer + 1) * ny, :] for layer in range(nx + 4)]
+            at = f * lines + layer * ny
+            stack_ref[at : at + half, :] = e
+            stack_ref[at + half : at + ny, :] = o
+    out_ref[...] = dot(stack_ref[...], table_ref[...])
+    for f in range(9):
+        layers = [out_ref[f * lines + layer * ny : f * lines + (layer + 1) * ny, :] for layer in range(nx + 4)]
         low, high = lift_first(layers[:nx], layers[nx:])
         approx = []
         for x in range(nx // 2):
@@ -427,9 +442,9 @@
         out_specs=[vmem] * len(out),
         out_shape=out,
         scratch_shapes=[
-            pltpu.VMEM((nx + 4, ny, wide), jnp.float32),
-            pltpu.VMEM(((nx + 4) * ny, wide), jnp.float32),
-            pltpu.VMEM(((nx + 4) * ny, wide), jnp.float32),
+            pltpu.VMEM((9, nx + 4, ny, wide), jnp.float32),
+            pltpu.VMEM((9 * (nx + 4) * ny, wide), jnp.float32),
+            pltpu.VMEM((9 * (nx + 4) * ny, wide), jnp.float32),
             pltpu.VMEM((3, mx, half, lanes), jnp.float32),
         ],
         compiler_params=pltpu.CompilerParams(vmem_limit_bytes=24 * MIB),

time: 88.9 us -> 87.8 us (0.988)
  Pallas kernels: 36 us -> 33.9 us
  waiting for transfers between devices: 9.05 us -> 10.1 us
    pallas_call x2, Pallas kernels: 14.5 us -> 12.2 us  [the longest x1 7.43 us: detail_pass(): pl.pallas_call(detail_kernel, grid=(9 // GROUP,), in_specs=[pl.BlockSpec(...]
    ppermute x20, waiting for transfers between devices: 9.05 us -> 10.1 us  [shifted(): lax.ppermute(block, axis, [(i, (i + distance) % size) for i in range(size)])]
  transfers between devices with their start and end apart: 20 -> 20, of which waited for: 4 -> 4; matrix products, arithmetic and copies ran while one was open for 5% -> 5% of each run, Pallas kernels for 28% -> 27%
where the time goes in v2:
time: 87.8 us; the launch traced here: 87 us
  starting transfers between devices  36.4 us (41%)
  Pallas kernels  33.9 us (39%)
  waiting for transfers between devices  10.1 us (12%)
  local copies, waits for them, and re-layouts  5.46 us (6%)
    ppermute x20, starting transfers between devices, shifted(): lax.ppermute(block, axis, [(i, (i + distance) % size) for i in range(size)])  36.4 us
    pallas_call x1, Pallas kernels, local_pass(): pl.pallas_call(local_kernel, grid=(nx,), in_specs=[pl.BlockSpec((3, 1, ny...  15.8 us
    ppermute x20, waiting for transfers between devices, shifted(): lax.ppermute(block, axis, [(i, (i + distance) % size) for i in range(size)])  10.1 us
    pallas_call x1, Pallas kernels, detail_pass(): pl.pallas_call(detail_kernel, grid=(9 // GROUP,), in_specs=[pl.BlockSpec(...  7.43 us
    pallas_call x2, Pallas kernels, level_pass(): pl.pallas_call(lambda *refs: level_kernel(last, nz, *refs), in_specs=[vme...  5.86 us
    pallas_call x1, Pallas kernels, approx_pass(): pl.pallas_call(approx_kernel, grid=(9 // GROUP,), in_specs=[per_field((nx...  4.81 us
  transfers between devices with their start and end apart: 20, of which 4 were waited for; matrix products, arithmetic and copies ran while one was open for 5% of the time, Pallas kernels for 27%

profile of v2, /device:TPU:0, one launch (start us, length us, event | category | flops | bytes accessed | tf_op | source)
XLA Modules:
  0.0 87.0 jit_solution(14072070892012157887)
XLA Ops:
  0.6 0.0 copy-start
  0.6 0.0 copy-start.1
  0.7 1.1 %fusion.1 = (f32[3,4,8,256]{3,2,1,0:T(8,128)S(1)}, f32[3,4,8,256]{3,2,1,0:T(8,128)S(1)}) fusion(f32[3,16,64,256]{3,2,1,0:T(8,128)} %v_ref.1), kind=kLoop, calls=%fused_computation.9 | loop fusion | bytes 393216 | tf_op jit(solution)/shard_map/slice | solution.py:469
  1.8 3.0 %collective-permute-start = (f32[3,4,16,256]{3,2,1,0:T(8,128)S(1)}, f32[3,4,16,256]{3,2,1,0:T(8,128)S(1)}, u32[]{:S(2)}, u32[]{:S(2)}) collective-permute-start(f32[3,4,16,256]{3,2,1,0:T(8,128)S(1)} %pad_maximum_fusion), channel_id=1, source_target_pairs={{0,4},{4,8},{8,12},{12,16},{16,20},{20,24},{24,28},{28,0},{1,5},{5... | collective-permute-start | bytes 589832 | tf_op jit(solution)/shard_map/ppermute | solution.py:23
  4.8 1.0 %slice.73 = f32[3,16,3,256]{3,2,1,0:T(4,128)S(1)} slice(f32[3,16,64,256]{3,2,1,0:T(8,128)} %v_ref.1), slice={[0:3], [0:16], [0:3], [0:256]} | slice | bytes 294912 | tf_op jit(solution)/shard_map/slice | solution.py:475
  5.8 0.7 collective-permute-start.3
  6.6 1.0 %slice.72 = f32[3,16,4,256]{3,2,1,0:T(4,128)S(1)} slice(f32[3,16,64,256]{3,2,1,0:T(8,128)} %v_ref.1), slice={[0:3], [0:16], [60:64], [0:256]} | slice | bytes 393216 | tf_op jit(solution)/shard_map/slice | solution.py:474
  7.6 0.1 collective-permute-start.2
  7.7 1.1 %slice.75 = f32[3,3,48,256]{3,2,1,0:T(8,128)S(1)} slice(f32[3,16,64,256]{3,2,1,0:T(8,128)} %v_ref.1), slice={[0:3], [0:3], [8:56], [0:256]} | slice | bytes 884736 | tf_op jit(solution)/shard_map/slice | solution.py:473
  8.7 3.4 %collective-permute-start.5 = (f32[3,3,48,256]{3,2,1,0:T(8,128)S(1)}, f32[3,3,48,256]{3,2,1,0:T(8,128)S(1)}, u32[]{:S(2)}, u32[]{:S(2)}) collective-permute-start(f32[3,3,48,256]{3,2,1,0:T(8,128)S(1)} %slice.75), channel_id=1, source_target_pairs={{0,28},{4,0},{8,4},{12,8},{16,12},{20,16},{24,20},{28,24},{1,29},{... | collective-permute-start | bytes 1327112 | tf_op jit(solution)/shard_map/ppermute | solution.py:23
  12.1 1.1 %slice.74 = f32[3,4,48,256]{3,2,1,0:T(8,128)S(1)} slice(f32[3,16,64,256]{3,2,1,0:T(8,128)} %v_ref.1), slice={[0:3], [12:16], [8:56], [0:256]} | slice | bytes 1179648 | tf_op jit(solution)/shard_map/slice | solution.py:472
  13.2 0.1 collective-permute-start.4
  13.4 0.0 collective-permute-done.3.after_ref
  13.4 4.7 %collective-permute-start.1 = (f32[3,3,16,256]{3,2,1,0:T(8,128)S(1)}, f32[3,3,16,256]{3,2,1,0:T(8,128)S(1)}, u32[]{:S(2)}, u32[]{:S(2)}) collective-permute-start(f32[3,3,16,256]{3,2,1,0:T(8,128)S(1)} %pad_maximum_fusion.1), channel_id=1, source_target_pairs={{0,28},{4,0},{8,4},{12,8},{16,12},{20,16},{24,20},{28,24},{1,29},{... | collective-permute-start | bytes 442376 | tf_op jit(solution)/shard_map/ppermute | solution.py:23
  18.1 0.0 collective-permute-done.2.before_ref
  18.1 15.8 %local_pass.1 = (f32[9,16,32,128]{3,2,1,0:T(8,128)S(1)}, f32[3,9,16,32,128]{4,3,2,1,0:T(8,128)S(1)}) custom-call(f32[3,16,64,256]{3,2,1,0:T(8,128)S(1)} %copy-done.1, f32[3,16,4,256]{3,2,1,0:T(4,128)S(1)} %collective-permute-done.2.before_ref, f32[3,16,3,256]{3,2,1,0:T(4,128)S(1)} %collective-permute-done.3.after_ref, f32[256,256]{1,0:T(8,128)S(1)} %copy-done), custom_call_target="tpu_custom_call" | custom-call | flops 1207959552 | bytes 14155776 | tf_op jit(solution)/shard_map/local_pass/pallas_call | solution.py:144
  33.9 4.1 %collective-permute-done.1.refs_4_.refs_5_ = f32[3,3,16,256]{3,2,1,0:T(8,128)S(1)} collective-permute-done((f32[3,3,16,256]{3,2,1,0:T(8,128)S(1)}, f32[3,3,16,256]{3,2,1,0:T(8,128)S(1)}, u32[]{:S(2)}, u32[]{:S(2)}) %collective-permute-start.1) | collective-permute-done | bytes 147488 | tf_op jit(solution)/shard_map/ppermute | solution.py:23
  38.1 0.2 collective-permute-start.6
  38.3 1.7 %collective-permute-start.7 = (f32[3,7,3,256]{3,2,1,0:T(4,128)S(1)}, f32[3,7,3,256]{3,2,1,0:T(4,128)S(1)}, u32[]{:S(2)}, u32[]{:S(2)}) collective-permute-start(f32[3,7,3,256]{3,2,1,0:T(4,128)S(1)} %pad_maximum_fusion.5), channel_id=1, source_target_pairs={{0,3},{1,0},{2,1},{3,2},{4,7},{5,4},{6,5},{7,6},{8,11},{9,8},{10,9... | collective-permute-start | bytes 193544 | tf_op jit(solution)/shard_map/ppermute | solution.py:23
  40.0 2.1 %collective-permute-done.7.refs_7_.refs_8_ = f32[3,7,3,256]{3,2,1,0:T(4,128)S(1)} collective-permute-done((f32[3,7,3,256]{3,2,1,0:T(4,128)S(1)}, f32[3,7,3,256]{3,2,1,0:T(4,128)S(1)}, u32[]{:S(2)}, u32[]{:S(2)}) %collective-permute-start.7) | collective-permute-done | bytes 64544 | tf_op jit(solution)/shard_map/ppermute | solution.py:23
  42.1 0.0 collective-permute-done.6.refs_6_.refs_7_
  42.1 0.0 collective-permute-done.5.refs_5_.refs_6_
  42.1 0.0 collective-permute-done.4.refs_3_.refs_4_
  42.1 4.8 %approx_pass.1 = (f32[9,8,32,128]{3,2,1,0:T(8,128)S(1)}, f32[9,8,32,128]{3,2,1,0:T(8,128)S(1)}, f32[6,8,32,128]{3,2,1,0:T(8,128)}, f32[9,2,32,128]{3,2,1,0:T(8,1...) custom-call(f32[9,16,32,128]{3,2,1,0:T(8,128)S(1)} %get-tuple-elemen, ...), custom_call_target="tpu_custom_call" | custom-call | tf_op jit(solution)/shard_map/approx_pass/pallas_call | solution.py:285
  46.9 0.0 collective-permute-start.10
  46.9 4.7 %collective-permute-start.11 = (f32[9,2,4,128]{3,2,1,0:T(4,128)S(1)}, f32[9,2,4,128]{3,2,1,0:T(4,128)S(1)}, u32[]{:S(2)}, u32[]{:S(2)}) collective-permute-start(f32[9,2,4,128]{3,2,1,0:T(4,128)S(1)} %get-tuple-element.49), channel_id=1, source_target_pairs={{0,28},{4,0},{8,4},{12,8},{16,12},{20,16},{24,20},{28,24},{1,29},{... | collective-permute-start | bytes 110600 | tf_op jit(solution)/shard_map/ppermute | solution.py:23
  51.7 4.7 %collective-permute-start.9 = (f32[9,2,32,128]{3,2,1,0:T(8,128)S(1)}, f32[9,2,32,128]{3,2,1,0:T(8,128)S(1)}, u32[]{:S(2)}, u32[]{:S(2)}) collective-permute-start(f32[9,2,32,128]{3,2,1,0:T(8,128)S(1)} %get-tuple-element.46), channel_id=1, source_target_pairs={{0,28},{4,0},{8,4},{12,8},{16,12},{20,16},{24,20},{28,24},{1,29},{... | collective-permute-start | bytes 884744 | tf_op jit(solution)/shard_map/ppermute | solution.py:23
  56.4 0.0 collective-permute-done.11
  56.4 0.1 pad_maximum_fusion.2
  56.5 0.6 collective-permute-start.12
  57.2 1.2 %collective-permute-start.13 = (f32[9,12,2,128]{3,2,1,0:T(2,128)S(1)}, f32[9,12,2,128]{3,2,1,0:T(2,128)S(1)}, u32[]{:S(2)}, u32[]{:S(2)}) collective-permute-start(f32[9,12,2,128]{3,2,1,0:T(2,128)S(1)} %pad_maximum_fusion.3), channel_id=1, source_target_pairs={{0,3},{1,0},{2,1},{3,2},{4,7},{5,4},{6,5},{7,6},{8,11},{9,8},{10,9... | collective-permute-start | bytes 331784 | tf_op jit(solution)/shard_map/ppermute | solution.py:23
  58.4 7.4 %detail_pass.1 = f32[7,9,8,32,128]{4,3,2,1,0:T(8,128)} custom-call(f32[3,9,16,32,128]{4,3,2,1,0:T(8,128)S(1)} %get-tuple-element.40.refs_0_, f32[9,8,32,128]{3,2,1,0:T(8,128)S(1)} %get-tuple-element.41.refs_1_, f32[256,256]{1,0:T(8,128)S(1)} %copy-done, f32[3,4,16,256]{3,2,1,0:T(8,128)S(1)} %collective-permute-done.refs_2_.refs_3_, ...), custom_call_target="tpu_custom_call" | custom-call | flops 235929600 | bytes 18874368 | tf_op jit(solution)/shard_map/detail_pass/pallas_call | solution.py:348
  65.8 0.0 collective-permute-done.12.refs_3_
  65.8 0.0 collective-permute-done.13.refs_4_
  65.8 0.0 collective-permute-done.8.refs_1_
  65.8 1.8 %collective-permute-done.9.refs_2_ = f32[9,2,32,128]{3,2,1,0:T(8,128)S(1)} collective-permute-done((f32[9,2,32,128]{3,2,1,0:T(8,128)S(1)}, f32[9,2,32,128]{3,2,1,0:T(8,128)S(1)}, u32[]{:S(2)}, u32[]{:S(2)}) %collective-permute-start.9) | collective-permute-done | bytes 294944 | tf_op jit(solution)/shard_map/ppermute | solution.py:23
  67.7 4.0 %second_level.1 = (f32[7,9,4,16,64]{4,3,2,1,0:T(8,128)}, f32[6,4,16,64]{3,2,1,0:T(8,128)}, f32[9,4,16,64]{3,2,1,0:T(8,128)S(1)}, f32[9,2,16,64]{3,2,1,0:T(8,128)...) custom-call(f32[9,8,32,128]{3,2,1,0:T(8,128)S(1)} %get-tuple-element, ...), custom_call_target="tpu_custom_call" | custom-call | tf_op jit(solution)/shard_map/second_level/pallas_call | solution.py:439
  71.7 4.7 %collective-permute-start.17 = (f32[9,2,4,64]{3,2,1,0:T(4,128)S(1)}, f32[9,2,4,64]{3,2,1,0:T(4,128)S(1)}, u32[]{:S(2)}, u32[]{:S(2)}) collective-permute-start(f32[9,2,4,64]{3,2,1,0:T(4,128)S(1)} %get-tuple-element.58), channel_id=1, source_target_pairs={{0,28},{4,0},{8,4},{12,8},{16,12},{20,16},{24,20},{28,24},{1,29},{... | collective-permute-start | bytes 55304 | tf_op jit(solution)/shard_map/ppermute | solution.py:23
  76.4 0.0 collective-permute-start.14
  76.4 4.7 %collective-permute-start.15 = (f32[9,2,16,64]{3,2,1,0:T(8,128)S(1)}, f32[9,2,16,64]{3,2,1,0:T(8,128)S(1)}, u32[]{:S(2)}, u32[]{:S(2)}) collective-permute-start(f32[9,2,16,64]{3,2,1,0:T(8,128)S(1)} %get-tuple-element.55), channel_id=1, source_target_pairs={{0,28},{4,0},{8,4},{12,8},{16,12},{20,16},{24,20},{28,24},{1,29},{... | collective-permute-start | bytes 221192 | tf_op jit(solution)/shard_map/ppermute | solution.py:23
  81.1 0.0 collective-permute-done.16
  81.2 0.1 collective-permute-start.18
  81.3 1.8 %collective-permute-start.19 = (f32[9,8,2,64]{3,2,1,0:T(2,128)S(1)}, f32[9,8,2,64]{3,2,1,0:T(2,128)S(1)}, u32[]{:S(2)}, u32[]{:S(2)}) collective-permute-start(f32[9,8,2,64]{3,2,1,0:T(2,128)S(1)} %pad_maximum_fusion.7), channel_id=1, source_target_pairs={{0,3},{1,0},{2,1},{3,2},{4,7},{5,4},{6,5},{7,6},{8,11},{9,8},{10,9... | collective-permute-start | bytes 110600 | tf_op jit(solution)/shard_map/ppermute | solution.py:23
  83.1 1.9 %collective-permute-done.18.refs_3_ = f32[9,8,2,64]{3,2,1,0:T(2,128)S(1)} collective-permute-done((f32[9,8,2,64]{3,2,1,0:T(2,128)S(1)}, f32[9,8,2,64]{3,2,1,0:T(2,128)S(1)}, u32[]{:S(2)}, u32[]{:S(2)}) %collective-permute-start.18) | collective-permute-done | bytes 36896 | tf_op jit(solution)/shard_map/ppermute | solution.py:23
  85.1 0.0 collective-permute-done.19.refs_4_
  85.1 0.0 collective-permute-done.14.refs_1_
  85.1 0.0 collective-permute-done.15.refs_2_
  85.1 1.9 %last_level.1 = (f32[7,9,2,8,32]{4,3,2,1,0:T(8,128)}, f32[6,2,8,32]{3,2,1,0:T(8,128)}, f32[3,2,8,32]{3,2,1,0:T(8,128)}) custom-call(f32[9,4,16,64]{3,2,1,0:T(8,128)S(1)} %get-tuple-element.53.refs_0_, f32[9,2,16,64]{3,2,1,0:T(8,128)S(1)} %collective-permute-done.14.refs_1_, f32[9,2,16,64]{3,2,1,0:T(8,128)S(1)} %collective-permute-done.15.refs_2_, ...), custom_call_target="tpu_custom_call" | custom-call | tf_op jit(solution)/shard_map/last_level/pallas_call | solution.py:439
  (27 shorter events, 0.3 us)
Async XLA Ops:
  0.6 17.5 %copy-start = (f32[256,256]{1,0:T(8,128)S(1)}, f32[256,256]{1,0:T(8,128)}, u32[]{:S(2)}) copy-start(f32[256,256]{1,0:T(8,128)} %constant.6.clone.table_ref.refs_1_.refs_2_) | copy-start | bytes 786436
  0.6 12.7 %copy-start.1 = (f32[3,16,64,256]{3,2,1,0:T(8,128)S(1)}, f32[3,16,64,256]{3,2,1,0:T(8,128)}, u32[]{:S(2)}) copy-start(f32[3,16,64,256]{3,2,1,0:T(8,128)} %v_ref.1) | copy-start | bytes 9437188
  1.8 36.2 %collective-permute-start = (f32[3,4,16,256]{3,2,1,0:T(8,128)S(1)}, f32[3,4,16,256]{3,2,1,0:T(8,128)S(1)}, u32[]{:S(2)}, u32[]{:S(2)}) collective-permute-start(f32[3,4,16,256]{3,2,1,0:T(8,128)S(1)} %pad_maximum_fusion), channel_id=1, source_target_pairs={{0,4},{4,8},{8,12},{12,16},{16,20},{20,24},{24,28},{28,0},{1,5},{5... | collective-permute-start | bytes 589832 | tf_op jit(solution)/shard_map/ppermute | solution.py:23
  5.8 7.5 %collective-permute-start.3 = (f32[3,16,3,256]{3,2,1,0:T(4,128)S(1)}, f32[3,16,3,256]{3,2,1,0:T(4,128)S(1)}, u32[]{:S(2)}, u32[]{:S(2)}) collective-permute-start(f32[3,16,3,256]{3,2,1,0:T(4,128)S(1)} %slice.73), channel_id=1, source_target_pairs={{0,3},{1,0},{2,1},{3,2},{4,7},{5,4},{6,5},{7,6},{8,11},{9,8},{10,9... | collective-permute-start | bytes 442376 | tf_op jit(solution)/shard_map/ppermute | solution.py:23
  7.6 10.5 %collective-permute-start.2 = (f32[3,16,4,256]{3,2,1,0:T(4,128)S(1)}, f32[3,16,4,256]{3,2,1,0:T(4,128)S(1)}, u32[]{:S(2)}, u32[]{:S(2)}) collective-permute-start(f32[3,16,4,256]{3,2,1,0:T(4,128)S(1)} %slice.72), channel_id=1, source_target_pairs={{0,1},{1,2},{2,3},{3,0},{4,5},{5,6},{6,7},{7,4},{8,9},{9,10},{10,1... | collective-permute-start | bytes 589832 | tf_op jit(solution)/shard_map/ppermute | solution.py:23
  8.7 33.4 %collective-permute-start.5 = (f32[3,3,48,256]{3,2,1,0:T(8,128)S(1)}, f32[3,3,48,256]{3,2,1,0:T(8,128)S(1)}, u32[]{:S(2)}, u32[]{:S(2)}) collective-permute-start(f32[3,3,48,256]{3,2,1,0:T(8,128)S(1)} %slice.75), channel_id=1, source_target_pairs={{0,28},{4,0},{8,4},{12,8},{16,12},{20,16},{24,20},{28,24},{1,29},{... | collective-permute-start | bytes 1327112 | tf_op jit(solution)/shard_map/ppermute | solution.py:23
  13.2 28.9 %collective-permute-start.4 = (f32[3,4,48,256]{3,2,1,0:T(8,128)S(1)}, f32[3,4,48,256]{3,2,1,0:T(8,128)S(1)}, u32[]{:S(2)}, u32[]{:S(2)}) collective-permute-start(f32[3,4,48,256]{3,2,1,0:T(8,128)S(1)} %slice.74), channel_id=1, source_target_pairs={{0,4},{4,8},{8,12},{12,16},{16,20},{20,24},{24,28},{28,0},{1,5},{5... | collective-permute-start | bytes 1769480 | tf_op jit(solution)/shard_map/ppermute | solution.py:23
  13.4 24.7 %collective-permute-start.1 = (f32[3,3,16,256]{3,2,1,0:T(8,128)S(1)}, f32[3,3,16,256]{3,2,1,0:T(8,128)S(1)}, u32[]{:S(2)}, u32[]{:S(2)}) collective-permute-start(f32[3,3,16,256]{3,2,1,0:T(8,128)S(1)} %pad_maximum_fusion.1), channel_id=1, source_target_pairs={{0,28},{4,0},{8,4},{12,8},{16,12},{20,16},{24,20},{28,24},{1,29},{... | collective-permute-start | bytes 442376 | tf_op jit(solution)/shard_map/ppermute | solution.py:23
  38.1 4.0 %collective-permute-start.6 = (f32[3,7,4,256]{3,2,1,0:T(4,128)S(1)}, f32[3,7,4,256]{3,2,1,0:T(4,128)S(1)}, u32[]{:S(2)}, u32[]{:S(2)}) collective-permute-start(f32[3,7,4,256]{3,2,1,0:T(4,128)S(1)} %pad_maximum_fusion.4), channel_id=1, source_target_pairs={{0,1},{1,2},{2,3},{3,0},{4,5},{5,6},{6,7},{7,4},{8,9},{9,10},{10,1... | collective-permute-start | bytes 258056 | tf_op jit(solution)/shard_map/ppermute | solution.py:23
  38.3 3.8 %collective-permute-start.7 = (f32[3,7,3,256]{3,2,1,0:T(4,128)S(1)}, f32[3,7,3,256]{3,2,1,0:T(4,128)S(1)}, u32[]{:S(2)}, u32[]{:S(2)}) collective-permute-start(f32[3,7,3,256]{3,2,1,0:T(4,128)S(1)} %pad_maximum_fusion.5), channel_id=1, source_target_pairs={{0,3},{1,0},{2,1},{3,2},{4,7},{5,4},{6,5},{7,6},{8,11},{9,8},{10,9... | collective-permute-start | bytes 193544 | tf_op jit(solution)/shard_map/ppermute | solution.py:23
  46.9 9.4 %collective-permute-start.10 = (f32[9,2,4,128]{3,2,1,0:T(4,128)S(1)}, f32[9,2,4,128]{3,2,1,0:T(4,128)S(1)}, u32[]{:S(2)}, u32[]{:S(2)}) collective-permute-start(f32[9,2,4,128]{3,2,1,0:T(4,128)S(1)} %get-tuple-element.48), channel_id=1, source_target_pairs={{0,4},{4,8},{8,12},{12,16},{16,20},{20,24},{24,28},{28,0},{1,5},{5... | collective-permute-start | bytes 110600 | tf_op jit(solution)/shard_map/ppermute | solution.py:23
  46.9 9.5 %collective-permute-start.11 = (f32[9,2,4,128]{3,2,1,0:T(4,128)S(1)}, f32[9,2,4,128]{3,2,1,0:T(4,128)S(1)}, u32[]{:S(2)}, u32[]{:S(2)}) collective-permute-start(f32[9,2,4,128]{3,2,1,0:T(4,128)S(1)} %get-tuple-element.49), channel_id=1, source_target_pairs={{0,28},{4,0},{8,4},{12,8},{16,12},{20,16},{24,20},{28,24},{1,29},{... | collective-permute-start | bytes 110600 | tf_op jit(solution)/shard_map/ppermute | solution.py:23
  51.6 14.2 %collective-permute-start.8 = (f32[9,2,32,128]{3,2,1,0:T(8,128)S(1)}, f32[9,2,32,128]{3,2,1,0:T(8,128)S(1)}, u32[]{:S(2)}, u32[]{:S(2)}) collective-permute-start(f32[9,2,32,128]{3,2,1,0:T(8,128)S(1)} %get-tuple-element.45), channel_id=1, source_target_pairs={{0,4},{4,8},{8,12},{12,16},{16,20},{20,24},{24,28},{28,0},{1,5},{5... | collective-permute-start | bytes 884744 | tf_op jit(solution)/shard_map/ppermute | solution.py:23
  51.7 16.0 %collective-permute-start.9 = (f32[9,2,32,128]{3,2,1,0:T(8,128)S(1)}, f32[9,2,32,128]{3,2,1,0:T(8,128)S(1)}, u32[]{:S(2)}, u32[]{:S(2)}) collective-permute-start(f32[9,2,32,128]{3,2,1,0:T(8,128)S(1)} %get-tuple-element.46), channel_id=1, source_target_pairs={{0,28},{4,0},{8,4},{12,8},{16,12},{20,16},{24,20},{28,24},{1,29},{... | collective-permute-start | bytes 884744 | tf_op jit(solution)/shard_map/ppermute | solution.py:23
  56.5 9.3 %collective-permute-start.12 = (f32[9,12,2,128]{3,2,1,0:T(2,128)S(1)}, f32[9,12,2,128]{3,2,1,0:T(2,128)S(1)}, u32[]{:S(2)}, u32[]{:S(2)}) collective-permute-start(f32[9,12,2,128]{3,2,1,0:T(2,128)S(1)} %pad_maximum_fusion.2), channel_id=1, source_target_pairs={{0,1},{1,2},{2,3},{3,0},{4,5},{5,6},{6,7},{7,4},{8,9},{9,10},{10,1... | collective-permute-start | bytes 331784 | tf_op jit(solution)/shard_map/ppermute | solution.py:23
  57.2 8.7 %collective-permute-start.13 = (f32[9,12,2,128]{3,2,1,0:T(2,128)S(1)}, f32[9,12,2,128]{3,2,1,0:T(2,128)S(1)}, u32[]{:S(2)}, u32[]{:S(2)}) collective-permute-start(f32[9,12,2,128]{3,2,1,0:T(2,128)S(1)} %pad_maximum_fusion.3), channel_id=1, source_target_pairs={{0,3},{1,0},{2,1},{3,2},{4,7},{5,4},{6,5},{7,6},{8,11},{9,8},{10,9... | collective-permute-start | bytes 331784 | tf_op jit(solution)/shard_map/ppermute | solution.py:23
  58.4 9.3 %copy-start.3 = (f32[128,128]{1,0:T(8,128)S(1)}, f32[128,128]{1,0:T(8,128)}, u32[]{:S(2)}) copy-start(f32[128,128]{1,0:T(8,128)} %constant.7.clone.refs_5_) | copy-start | bytes 196612
  58.4 26.7 %copy-start.2 = (f32[128,128]{1,0:T(8,128)S(1)}, f32[128,128]{1,0:T(8,128)}, u32[]{:S(2)}) copy-start(f32[128,128]{1,0:T(8,128)} %constant.8.clone.refs_5_) | copy-start | bytes 196612
  71.7 9.4 %collective-permute-start.16 = (f32[9,2,4,64]{3,2,1,0:T(4,128)S(1)}, f32[9,2,4,64]{3,2,1,0:T(4,128)S(1)}, u32[]{:S(2)}, u32[]{:S(2)}) collective-permute-start(f32[9,2,4,64]{3,2,1,0:T(4,128)S(1)} %get-tuple-element.57), channel_id=1, source_target_pairs={{0,4},{4,8},{8,12},{12,16},{16,20},{20,24},{24,28},{28,0},{1,5},{5... | collective-permute-start | bytes 55304 | tf_op jit(solution)/shard_map/ppermute | solution.py:23
  71.7 9.5 %collective-permute-start.17 = (f32[9,2,4,64]{3,2,1,0:T(4,128)S(1)}, f32[9,2,4,64]{3,2,1,0:T(4,128)S(1)}, u32[]{:S(2)}, u32[]{:S(2)}) collective-permute-start(f32[9,2,4,64]{3,2,1,0:T(4,128)S(1)} %get-tuple-element.58), channel_id=1, source_target_pairs={{0,28},{4,0},{8,4},{12,8},{16,12},{20,16},{24,20},{28,24},{1,29},{... | collective-permute-start | bytes 55304 | tf_op jit(solution)/shard_map/ppermute | solution.py:23
  76.4 8.7 %collective-permute-start.14 = (f32[9,2,16,64]{3,2,1,0:T(8,128)S(1)}, f32[9,2,16,64]{3,2,1,0:T(8,128)S(1)}, u32[]{:S(2)}, u32[]{:S(2)}) collective-permute-start(f32[9,2,16,64]{3,2,1,0:T(8,128)S(1)} %get-tuple-element.54), channel_id=1, source_target_pairs={{0,4},{4,8},{8,12},{12,16},{16,20},{20,24},{24,28},{28,0},{1,5},{5... | collective-permute-start | bytes 221192 | tf_op jit(solution)/shard_map/ppermute | solution.py:23
  76.4 8.7 %collective-permute-start.15 = (f32[9,2,16,64]{3,2,1,0:T(8,128)S(1)}, f32[9,2,16,64]{3,2,1,0:T(8,128)S(1)}, u32[]{:S(2)}, u32[]{:S(2)}) collective-permute-start(f32[9,2,16,64]{3,2,1,0:T(8,128)S(1)} %get-tuple-element.55), channel_id=1, source_target_pairs={{0,28},{4,0},{8,4},{12,8},{16,12},{20,16},{24,20},{28,24},{1,29},{... | collective-permute-start | bytes 221192 | tf_op jit(solution)/shard_map/ppermute | solution.py:23
  81.2 3.8 %collective-permute-start.18 = (f32[9,8,2,64]{3,2,1,0:T(2,128)S(1)}, f32[9,8,2,64]{3,2,1,0:T(2,128)S(1)}, u32[]{:S(2)}, u32[]{:S(2)}) collective-permute-start(f32[9,8,2,64]{3,2,1,0:T(2,128)S(1)} %pad_maximum_fusion.6), channel_id=1, source_target_pairs={{0,1},{1,2},{2,3},{3,0},{4,5},{5,6},{6,7},{7,4},{8,9},{9,10},{10,1... | collective-permute-start | bytes 110600 | tf_op jit(solution)/shard_map/ppermute | solution.py:23
  81.3 3.8 %collective-permute-start.19 = (f32[9,8,2,64]{3,2,1,0:T(2,128)S(1)}, f32[9,8,2,64]{3,2,1,0:T(2,128)S(1)}, u32[]{:S(2)}, u32[]{:S(2)}) collective-permute-start(f32[9,8,2,64]{3,2,1,0:T(2,128)S(1)} %pad_maximum_fusion.7), channel_id=1, source_target_pairs={{0,3},{1,0},{2,1},{3,2},{4,7},{5,4},{6,5},{7,6},{8,11},{9,8},{10,9... | collective-permute-start | bytes 110600 | tf_op jit(solution)/shard_map/ppermute | solution.py:23

commit v3 on v2

--- a/solution.py
+++ b/solution.py
@@ -368,17 +368,14 @@
     )(rest, high, table, *halo)
 
 
-def level_kernel(last, nz, *refs):
-    a_ref, before_ref, after_ref, down_ref, up_ref, table_ref = refs[:6]
-    detail_ref, stress_ref, approx_ref = refs[6:9]
-    sends = refs[9:15] if not last else ()
-    pad_ref, stack_ref, out_ref, kept_ref = refs[-4:]
+def level_rows(refs, nz, lows, pad_ref, stack_ref):
+    a_ref, before_ref, after_ref, down_ref, up_ref = refs
     nx, ny = a_ref.shape[1:3]
-    half, lanes = ny // 2, nz // 2
-    wide = table_ref.shape[0]
+    half = ny // 2
+    wide = stack_ref.shape[1]
+    kept = half if lows else ny
     if nz < wide:
         pad_ref[...] = jnp.zeros_like(pad_ref)
-    lines = (nx + 4) * ny
     for f in range(9):
         for layer in range(nx + 4):
             if layer < nx:
@@ -396,14 +393,55 @@
             if nz < wide:
                 rows = [jnp.concatenate([row, jnp.zeros((1, wide - nz), jnp.float32)], axis=1) for row in rows]
             e, o = sublane_lift(e, o, *rows)
-            at = f * lines + layer * ny
+            at = (f * (nx + 4) + layer) * kept
             stack_ref[at : at + half, :] = e
-            stack_ref[at + half : at + ny, :] = o
+            if not lows:
+                stack_ref[at + half : at + ny, :] = o
+
+
+def level_approx_kernel(nz, *refs):
+    table_ref, approx_ref, stress_ref = refs[5:8]
+    sends, (pad_ref, stack_ref, out_ref, kept_ref) = refs[8:-4], refs[-4:]
+    nx, ny = refs[0].shape[1:3]
+    half, lanes = ny // 2, nz // 2
+    level_rows(refs[:5], nz, True, pad_ref, stack_ref)
     out_ref[...] = dot(stack_ref[...], table_ref[...])
     for f in range(9):
-        layers = [out_ref[f * lines + layer * ny : f * lines + (layer + 1) * ny, :] for layer in range(nx + 4)]
+        at = f * (nx + 4) * half
+        layers = [out_ref[at + layer * half : at + (layer + 1) * half, :] for layer in range(nx + 4)]
+        low, _ = lift_first(layers[:nx], layers[nx:])
+        approx = [(t * band_scale(0, 0))[:, :lanes] for t in low]
+        for x in range(nx // 2):
+            if f < 3:
+                kept_ref[f, x] = approx[x]
+            else:
+                i, j = product_pairs[f - 3]
+                stress_ref[f - 3, x] = approx[x] - kept_ref[i, x] * kept_ref[j, x]
+            approx_ref[f, x] = approx[x]
+        for part, value in enumerate(parts_for_next(approx)):
+            sends[0][f, part] = value
+        for part, value in enumerate(parts_for_previous(approx)):
+            sends[1][f, part] = value
+        for at, layer in enumerate(approx):
+            p, q, r, s = row_parts(layer)
+            sends[2][f, at, 0:1, :] = p
+            sends[2][f, at, 1:2, :] = q
+            sends[3][f, at, 0:1, :] = r
+            sends[3][f, at, 1:2, :] = s
+
+
+def level_detail_kernel(nz, last, *refs):
+    table_ref, detail_ref = refs[5:7]
+    pad_ref, stack_ref, out_ref, kept_ref = refs[-4:]
+    nx, ny = refs[0].shape[1:3]
+    half, lanes = ny // 2, nz // 2
+    wide = stack_ref.shape[1]
+    level_rows(refs[:5], nz, False, pad_ref, stack_ref)
+    out_ref[...] = dot(stack_ref[...], table_ref[...])
+    for f in range(9):
+        at = f * (nx + 4) * ny
+        layers = [out_ref[at + layer * ny : at + (layer + 1) * ny, :] for layer in range(nx + 4)]
         low, high = lift_first(layers[:nx], layers[nx:])
-        approx = []
         for x in range(nx // 2):
             for bx, value in enumerate((low[x], high[x])):
                 for by in range(2):
@@ -413,43 +451,64 @@
                         piece = t[:, bz * (wide // 2) : bz * (wide // 2) + lanes]
                         if band:
                             detail_ref[band - 1, f, x] = piece
-                        else:
-                            approx.append(piece)
-        for x in range(nx // 2):
-            if f < 3:
-                kept_ref[f, x] = approx[x]
-            else:
-                i, j = product_pairs[f - 3]
-                stress_ref[f - 3, x] = approx[x] - kept_ref[i, x] * kept_ref[j, x]
-            if not last or f < 3:
-                approx_ref[f, x] = approx[x]
-        if not last:
-            send_parts(approx, f, *sends)
-
-
-def level_pass(approx, halo, last):
+                        elif last:
+                            stress_ref, approx_ref = refs[7:9]
+                            if f < 3:
+                                kept_ref[f, x] = piece
+                                approx_ref[f, x] = piece
+                            else:
+                                i, j = product_pairs[f - 3]
+                                stress_ref[f - 3, x] = piece - kept_ref[i, x] * kept_ref[j, x]
+
+
+def level_call(kernel, approx, halo, out, kept):
     _, nx, ny, nz = approx.shape
-    mx, half, lanes = nx // 2, ny // 2, nz // 2
     wide = max(nz, 128)
-    f32 = lambda *shape: jax.ShapeDtypeStruct(shape, jnp.float32)
-    out = [f32(7, 9, mx, half, lanes), f32(6, mx, half, lanes), f32(3 if last else 9, mx, half, lanes)]
-    if not last:
-        out += [f32(9, *s) for s in ((2, half, lanes), (2, half, lanes), (2, 4, lanes), (2, 4, lanes), (mx, 2, lanes), (mx, 2, lanes))]
     vmem = pl.BlockSpec(memory_space=pltpu.VMEM)
     return pl.pallas_call(
-        lambda *refs: level_kernel(last, nz, *refs),
+        kernel,
         in_specs=[vmem] * 6,
         out_specs=[vmem] * len(out),
         out_shape=out,
         scratch_shapes=[
             pltpu.VMEM((9, nx + 4, ny, wide), jnp.float32),
-            pltpu.VMEM((9 * (nx + 4) * ny, wide), jnp.float32),
-            pltpu.VMEM((9 * (nx + 4) * ny, wide), jnp.float32),
-            pltpu.VMEM((3, mx, half, lanes), jnp.float32),
+            pltpu.VMEM((9 * (nx + 4) * kept, wide), jnp.float32),
+            pltpu.VMEM((9 * (nx + 4) * kept, wide), jnp.float32),
+            pltpu.VMEM((3, nx // 2, ny // 2, nz // 2), jnp.float32),
         ],
         compiler_params=pltpu.CompilerParams(vmem_limit_bytes=24 * MIB),
-        name="last_level" if last else "second_level",
     )(approx, *halo, jnp.asarray(third_table(nz, wide)))
+
+
+def level_approx(approx, halo):
+    _, nx, ny, nz = approx.shape
+    mx, half, lanes = nx // 2, ny // 2, nz // 2
+    f32 = lambda *shape: jax.ShapeDtypeStruct(shape, jnp.float32)
+    sends = ((2, half, lanes), (2, half, lanes), (mx, 2, lanes), (mx, 2, lanes))
+    out = [f32(9, mx, half, lanes), f32(6, mx, half, lanes)] + [f32(9, *s) for s in sends]
+    return level_call(lambda *refs: level_approx_kernel(nz, *refs), approx, halo, out, half)
+
+
+def level_details(approx, halo, last):
+    _, nx, ny, nz = approx.shape
+    mx, half, lanes = nx // 2, ny // 2, nz // 2
+    f32 = lambda *shape: jax.ShapeDtypeStruct(shape, jnp.float32)
+    out = [f32(7, 9, mx, half, lanes)]
+    if last:
+        out += [f32(6, mx, half, lanes), f32(3, mx, half, lanes)]
+    return level_call(lambda *refs: level_detail_kernel(nz, last, *refs), approx, halo, out, ny)
+
+
+def exchange_small(to_next, to_prev, down, up):
+    before = shifted(to_next, "gx", 1)
+    after = shifted(to_prev, "gx", -1)
+    rows = before.shape[2]
+    cell = lambda at: jnp.concatenate([before[:, :, at : at + 1], after[:, :, at : at + 1]], axis=1)
+    tail = jnp.concatenate(parts_for_next([cell(rows - 4 + i) for i in range(4)]), axis=2)
+    head = jnp.concatenate(parts_for_previous([cell(i) for i in range(3)]), axis=2)
+    down = jnp.concatenate([down, tail], axis=1)
+    up = jnp.concatenate([up, head], axis=1)
+    return before, after, shifted(down, "gy", 1), shifted(up, "gy", -1)
 
 
 def exchange(to_next, to_prev, edge_next, edge_prev, down, up):
@@ -484,8 +543,12 @@
     second_halo = exchange(*sends)
     details_one = detail_pass(rest, high, halo, table)
     approx, details_one = lax.optimization_barrier((approx, details_one))
-    details_two, stress_two, approx, *sends = level_pass(approx, second_halo, False)
-    details_three, stress_three, coarse = level_pass(approx, exchange(*sends), True)
+    second = approx
+    approx, stress_two, *sends = level_approx(second, second_halo)
+    third_halo = exchange_small(*sends)
+    details_two, = level_details(second, second_halo, False)
+    approx, details_two = lax.optimization_barrier((approx, details_two))
+    details_three, stress_three, coarse = level_details(approx, third_halo, True)
     return details_one, stress_one, details_two, stress_two, details_three, stress_three, coarse
 
 

time: 87.8 us -> 87.4 us (level)
  starting transfers between devices: 36.4 us -> 31.9 us
  waiting for transfers between devices: 10.1 us -> 12.3 us
  Pallas kernels: 33.9 us -> 36 us
    ppermute x20 -> x18, starting transfers between devices: 36.4 us -> 31.9 us  [shifted(): lax.ppermute(block, axis, [(i, (i + distance) % size) for i in range(size)])]
    ppermute x20 -> x18, waiting for transfers between devices: 10.1 us -> 12.3 us  [shifted(): lax.ppermute(block, axis, [(i, (i + distance) % size) for i in range(size)])]
    pallas_call x2 -> x3, Pallas kernels: 5.86 us -> 7.99 us  [level_call(): pl.pallas_call(kernel, in_specs=[vmem] * 6, out_specs=[vmem] * len(out),...]
  transfers between devices with their start and end apart: 20 -> 18, of which waited for: 4 -> 5; matrix products, arithmetic and copies ran while one was open for 5% -> 5% of each run, Pallas kernels for 27% -> 31%
where the time goes in v3:
time: 87.4 us; the launch traced here: 87.1 us
  Pallas kernels  36 us (41%)
  starting transfers between devices  31.9 us (36%)
  waiting for transfers between devices  12.3 us (14%)
  local copies, waits for them, and re-layouts  5.52 us (6%)
    ppermute x18, starting transfers between devices, shifted(): lax.ppermute(block, axis, [(i, (i + distance) % size) for i in range(size)])  31.9 us
    pallas_call x1, Pallas kernels, local_pass(): pl.pallas_call(local_kernel, grid=(nx,), in_specs=[pl.BlockSpec((3, 1, ny...  15.8 us
    ppermute x18, waiting for transfers between devices, shifted(): lax.ppermute(block, axis, [(i, (i + distance) % size) for i in range(size)])  12.3 us
    pallas_call x3, Pallas kernels, level_call(): pl.pallas_call(kernel, in_specs=[vmem] * 6, out_specs=[vmem] * len(out),...  7.99 us
    pallas_call x1, Pallas kernels, detail_pass(): pl.pallas_call(detail_kernel, grid=(9 // GROUP,), in_specs=[pl.BlockSpec(...  7.43 us
    pallas_call x1, Pallas kernels, approx_pass(): pl.pallas_call(approx_kernel, grid=(9 // GROUP,), in_specs=[per_field((nx...  4.81 us
  transfers between devices with their start and end apart: 18, of which 5 were waited for; matrix products, arithmetic and copies ran while one was open for 5% of the time, Pallas kernels for 31%

profile of v3, /device:TPU:0, one launch (start us, length us, event | category | flops | bytes accessed | tf_op | source)
XLA Modules:
  0.0 87.1 jit_solution(6490756765283786698)
XLA Ops:
  0.6 0.0 copy-start
  0.6 0.0 copy-start.1
  0.7 1.1 %fusion.6 = (f32[3,4,8,256]{3,2,1,0:T(8,128)S(1)}, f32[3,4,8,256]{3,2,1,0:T(8,128)S(1)}) fusion(f32[3,16,64,256]{3,2,1,0:T(8,128)} %v_ref.1), kind=kLoop, calls=%fused_computation.19 | loop fusion | bytes 393216 | tf_op jit(solution)/shard_map/slice | solution.py:528
  1.8 3.0 %collective-permute-start = (f32[3,4,16,256]{3,2,1,0:T(8,128)S(1)}, f32[3,4,16,256]{3,2,1,0:T(8,128)S(1)}, u32[]{:S(2)}, u32[]{:S(2)}) collective-permute-start(f32[3,4,16,256]{3,2,1,0:T(8,128)S(1)} %pad_maximum_fusion), channel_id=1, source_target_pairs={{0,4},{4,8},{8,12},{12,16},{16,20},{20,24},{24,28},{28,0},{1,5},{5... | collective-permute-start | bytes 589832 | tf_op jit(solution)/shard_map/ppermute | solution.py:23
  4.8 1.0 %slice.103 = f32[3,16,3,256]{3,2,1,0:T(4,128)S(1)} slice(f32[3,16,64,256]{3,2,1,0:T(8,128)} %v_ref.1), slice={[0:3], [0:16], [0:3], [0:256]} | slice | bytes 294912 | tf_op jit(solution)/shard_map/slice | solution.py:534
  5.8 0.7 collective-permute-start.3
  6.6 1.0 %slice.102 = f32[3,16,4,256]{3,2,1,0:T(4,128)S(1)} slice(f32[3,16,64,256]{3,2,1,0:T(8,128)} %v_ref.1), slice={[0:3], [0:16], [60:64], [0:256]} | slice | bytes 393216 | tf_op jit(solution)/shard_map/slice | solution.py:533
  7.6 0.1 collective-permute-start.2
  7.7 1.1 %slice.105 = f32[3,3,48,256]{3,2,1,0:T(8,128)S(1)} slice(f32[3,16,64,256]{3,2,1,0:T(8,128)} %v_ref.1), slice={[0:3], [0:3], [8:56], [0:256]} | slice | bytes 884736 | tf_op jit(solution)/shard_map/slice | solution.py:532
  8.7 3.4 %collective-permute-start.5 = (f32[3,3,48,256]{3,2,1,0:T(8,128)S(1)}, f32[3,3,48,256]{3,2,1,0:T(8,128)S(1)}, u32[]{:S(2)}, u32[]{:S(2)}) collective-permute-start(f32[3,3,48,256]{3,2,1,0:T(8,128)S(1)} %slice.105), channel_id=1, source_target_pairs={{0,28},{4,0},{8,4},{12,8},{16,12},{20,16},{24,20},{28,24},{1,29},{... | collective-permute-start | bytes 1327112 | tf_op jit(solution)/shard_map/ppermute | solution.py:23
  12.1 1.1 %slice.104 = f32[3,4,48,256]{3,2,1,0:T(8,128)S(1)} slice(f32[3,16,64,256]{3,2,1,0:T(8,128)} %v_ref.1), slice={[0:3], [12:16], [8:56], [0:256]} | slice | bytes 1179648 | tf_op jit(solution)/shard_map/slice | solution.py:531
  13.2 0.1 collective-permute-start.4
  13.3 0.0 collective-permute-done.3.after_ref
  13.4 4.7 %collective-permute-start.1 = (f32[3,3,16,256]{3,2,1,0:T(8,128)S(1)}, f32[3,3,16,256]{3,2,1,0:T(8,128)S(1)}, u32[]{:S(2)}, u32[]{:S(2)}) collective-permute-start(f32[3,3,16,256]{3,2,1,0:T(8,128)S(1)} %pad_maximum_fusion.1), channel_id=1, source_target_pairs={{0,28},{4,0},{8,4},{12,8},{16,12},{20,16},{24,20},{28,24},{1,29},{... | collective-permute-start | bytes 442376 | tf_op jit(solution)/shard_map/ppermute | solution.py:23
  18.1 15.8 %local_pass.1 = (f32[9,16,32,128]{3,2,1,0:T(8,128)S(1)}, f32[3,9,16,32,128]{4,3,2,1,0:T(8,128)S(1)}) custom-call(f32[3,16,64,256]{3,2,1,0:T(8,128)S(1)} %copy-done.1, f32[3,16,4,256]{3,2,1,0:T(4,128)S(1)} %collective-permute-done.2.before_ref, f32[3,16,3,256]{3,2,1,0:T(4,128)S(1)} %collective-permute-done.3.after_ref, f32[256,256]{1,0:T(8,128)S(1)} %copy-done), custom_call_target="tpu_custom_call" | custom-call | flops 1207959552 | bytes 14155776 | tf_op jit(solution)/shard_map/local_pass/pallas_call | solution.py:144
  33.9 4.1 %collective-permute-done.1.refs_4_.refs_5_ = f32[3,3,16,256]{3,2,1,0:T(8,128)S(1)} collective-permute-done((f32[3,3,16,256]{3,2,1,0:T(8,128)S(1)}, f32[3,3,16,256]{3,2,1,0:T(8,128)S(1)}, u32[]{:S(2)}, u32[]{:S(2)}) %collective-permute-start.1) | collective-permute-done | bytes 147488 | tf_op jit(solution)/shard_map/ppermute | solution.py:23
  38.1 0.2 collective-permute-start.6
  38.3 1.7 %collective-permute-start.7 = (f32[3,7,3,256]{3,2,1,0:T(4,128)S(1)}, f32[3,7,3,256]{3,2,1,0:T(4,128)S(1)}, u32[]{:S(2)}, u32[]{:S(2)}) collective-permute-start(f32[3,7,3,256]{3,2,1,0:T(4,128)S(1)} %pad_maximum_fusion.5), channel_id=1, source_target_pairs={{0,3},{1,0},{2,1},{3,2},{4,7},{5,4},{6,5},{7,6},{8,11},{9,8},{10,9... | collective-permute-start | bytes 193544 | tf_op jit(solution)/shard_map/ppermute | solution.py:23
  40.0 2.1 %collective-permute-done.7.refs_7_.refs_8_ = f32[3,7,3,256]{3,2,1,0:T(4,128)S(1)} collective-permute-done((f32[3,7,3,256]{3,2,1,0:T(4,128)S(1)}, f32[3,7,3,256]{3,2,1,0:T(4,128)S(1)}, u32[]{:S(2)}, u32[]{:S(2)}) %collective-permute-start.7) | collective-permute-done | bytes 64544 | tf_op jit(solution)/shard_map/ppermute | solution.py:23
  42.1 0.0 collective-permute-done.6.refs_6_.refs_7_
  42.1 0.0 collective-permute-done.5.refs_5_.refs_6_
  42.1 0.0 collective-permute-done.4.refs_3_.refs_4_
  42.1 4.8 %approx_pass.1 = (f32[9,8,32,128]{3,2,1,0:T(8,128)S(1)}, f32[9,8,32,128]{3,2,1,0:T(8,128)S(1)}, f32[6,8,32,128]{3,2,1,0:T(8,128)}, f32[9,2,32,128]{3,2,1,0:T(8,1...) custom-call(f32[9,16,32,128]{3,2,1,0:T(8,128)S(1)} %get-tuple-elemen, ...), custom_call_target="tpu_custom_call" | custom-call | tf_op jit(solution)/shard_map/approx_pass/pallas_call | solution.py:285
  46.9 0.0 collective-permute-start.10
  46.9 4.7 %collective-permute-start.11 = (f32[9,2,4,128]{3,2,1,0:T(4,128)S(1)}, f32[9,2,4,128]{3,2,1,0:T(4,128)S(1)}, u32[]{:S(2)}, u32[]{:S(2)}) collective-permute-start(f32[9,2,4,128]{3,2,1,0:T(4,128)S(1)} %get-tuple-element.48), channel_id=1, source_target_pairs={{0,28},{4,0},{8,4},{12,8},{16,12},{20,16},{24,20},{28,24},{1,29},{... | collective-permute-start | bytes 110600 | tf_op jit(solution)/shard_map/ppermute | solution.py:23
  51.6 0.0 collective-permute-start.8
  51.7 4.7 %collective-permute-start.9 = (f32[9,2,32,128]{3,2,1,0:T(8,128)S(1)}, f32[9,2,32,128]{3,2,1,0:T(8,128)S(1)}, u32[]{:S(2)}, u32[]{:S(2)}) collective-permute-start(f32[9,2,32,128]{3,2,1,0:T(8,128)S(1)} %get-tuple-element.45), channel_id=1, source_target_pairs={{0,28},{4,0},{8,4},{12,8},{16,12},{20,16},{24,20},{28,24},{1,29},{... | collective-permute-start | bytes 884744 | tf_op jit(solution)/shard_map/ppermute | solution.py:23
  56.4 0.0 collective-permute-done.11
  56.4 0.1 pad_maximum_fusion.2
  56.5 0.6 collective-permute-start.12
  57.2 1.2 %collective-permute-start.13 = (f32[9,12,2,128]{3,2,1,0:T(2,128)S(1)}, f32[9,12,2,128]{3,2,1,0:T(2,128)S(1)}, u32[]{:S(2)}, u32[]{:S(2)}) collective-permute-start(f32[9,12,2,128]{3,2,1,0:T(2,128)S(1)} %pad_maximum_fusion.3), channel_id=1, source_target_pairs={{0,3},{1,0},{2,1},{3,2},{4,7},{5,4},{6,5},{7,6},{8,11},{9,8},{10,9... | collective-permute-start | bytes 331784 | tf_op jit(solution)/shard_map/ppermute | solution.py:23
  58.4 7.4 %detail_pass.1 = f32[7,9,8,32,128]{4,3,2,1,0:T(8,128)} custom-call(f32[3,9,16,32,128]{4,3,2,1,0:T(8,128)S(1)} %get-tuple-element.39.refs_0_, f32[9,8,32,128]{3,2,1,0:T(8,128)S(1)} %get-tuple-element.40.refs_1_, f32[256,256]{1,0:T(8,128)S(1)} %copy-done, f32[3,4,16,256]{3,2,1,0:T(8,128)S(1)} %collective-permute-done.refs_2_.refs_3_, ...), custom_call_target="tpu_custom_call" | custom-call | flops 235929600 | bytes 18874368 | tf_op jit(solution)/shard_map/detail_pass/pallas_call | solution.py:348
  65.8 0.0 collective-permute-done.8.refs_1_
  65.8 1.8 %collective-permute-done.9.refs_2_ = f32[9,2,32,128]{3,2,1,0:T(8,128)S(1)} collective-permute-done((f32[9,2,32,128]{3,2,1,0:T(8,128)S(1)}, f32[9,2,32,128]{3,2,1,0:T(8,128)S(1)}, u32[]{:S(2)}, u32[]{:S(2)}) %collective-permute-start.9) | collective-permute-done | bytes 294944 | tf_op jit(solution)/shard_map/ppermute | solution.py:23
  67.7 2.4 %shard_map.108 = (f32[9,4,16,64]{3,2,1,0:T(8,128)S(1)}, f32[6,4,16,64]{3,2,1,0:T(8,128)}, f32[9,2,16,64]{3,2,1,0:T(8,128)S(1)}, f32[9,2,16,64]{3,2,1,0:T(8,128)S...) custom-call(f32[9,8,32,128]{3,2,1,0:T(8,128)S(1)} %get-tuple-element.43.refs_0_, ...), custom_call_target="tpu_custom_call" | custom-call | tf_op jit(solution)/shard_map/pallas_call | solution.py:468
  70.1 4.7 %collective-permute-start.15 = (f32[9,2,16,64]{3,2,1,0:T(8,128)S(1)}, f32[9,2,16,64]{3,2,1,0:T(8,128)S(1)}, u32[]{:S(2)}, u32[]{:S(2)}) collective-permute-start(f32[9,2,16,64]{3,2,1,0:T(8,128)S(1)} %get-tuple-element.55), channel_id=1, source_target_pairs={{0,28},{4,0},{8,4},{12,8},{16,12},{20,16},{24,20},{28,24},{1,29},{... | collective-permute-start | bytes 221192 | tf_op jit(solution)/shard_map/ppermute | solution.py:23
  74.8 3.9 %collective-permute-done.14.refs_1_ = f32[9,2,16,64]{3,2,1,0:T(8,128)S(1)} collective-permute-done((f32[9,2,16,64]{3,2,1,0:T(8,128)S(1)}, f32[9,2,16,64]{3,2,1,0:T(8,128)S(1)}, u32[]{:S(2)}, u32[]{:S(2)}) %collective-permute-start.14) | collective-permute-done | bytes 73760 | tf_op jit(solution)/shard_map/ppermute | solution.py:23
  78.8 0.3 collective-permute-done.15.refs_2_
  79.2 0.1 maximum_add_fusion
  79.3 0.1 maximum_maximum_fusion
  79.3 0.1 collective-permute-start.16
  79.4 0.1 fusion.4
  79.5 0.1 maximum_maximum_fusion.1
  79.5 2.0 %collective-permute-start.17 = (f32[9,8,2,64]{3,2,1,0:T(2,128)S(1)}, f32[9,8,2,64]{3,2,1,0:T(2,128)S(1)}, u32[]{:S(2)}, u32[]{:S(2)}) collective-permute-start(f32[9,8,2,64]{3,2,1,0:T(2,128)S(1)} %maximum_maximum_fusion.1), channel_id=1, source_target_pairs={{0,3},{1,0},{2,1},{3,2},{4,7},{5,4},{6,5},{7,6},{8,11},{9,8},{10,9... | collective-permute-start | bytes 110600 | tf_op jit(solution)/shard_map/ppermute | solution.py:23
  81.5 3.7 %shard_map.109 = f32[7,9,4,16,64]{4,3,2,1,0:T(8,128)} custom-call(f32[9,8,32,128]{3,2,1,0:T(8,128)S(1)} %get-tuple-element.43.refs_0_, f32[9,2,32,128]{3,2,1,0:T(8,128)S(1)} %collective-permute-done.8.refs_1_, f32[9,2,32,128]{3,2,1,0:T(8,128)S(1)} %collective-permute-done.9.refs_2_, f32[9,12,2,128]{3,2,1,0:T(2,128)S(1)} %collective-permute-done.12.refs_3_, ...), custom_call_target="tpu_custom_call" | custom-call | tf_op jit(solution)/shard_map/pallas_call | solution.py:468
  85.2 0.0 collective-permute-done.16.refs_3_
  85.2 0.0 collective-permute-done.17.refs_4_
  85.2 1.9 %shard_map.110 = (f32[7,9,2,8,32]{4,3,2,1,0:T(8,128)}, f32[6,2,8,32]{3,2,1,0:T(8,128)}, f32[3,2,8,32]{3,2,1,0:T(8,128)}) custom-call(f32[9,4,16,64]{3,2,1,0:T(8,128)S(1)} %get-tuple-element.53.refs_0_, f32[9,2,16,64]{3,2,1,0:T(8,128)S(1)} %collective-permute-done.14.refs_1_, f32[9,2,16,64]{3,2,1,0:T(8,128)S(1)} %collective-permute-done.15.refs_2_, ...), custom_call_target="tpu_custom_call" | custom-call | tf_op jit(solution)/shard_map/pallas_call | solution.py:468
  (26 shorter events, 0.3 us)
Async XLA Ops:
  0.6 17.5 %copy-start = (f32[256,256]{1,0:T(8,128)S(1)}, f32[256,256]{1,0:T(8,128)}, u32[]{:S(2)}) copy-start(f32[256,256]{1,0:T(8,128)} %constant.10.clone.table_ref.refs_1_.refs_2_) | copy-start | bytes 786436
  0.6 12.7 %copy-start.1 = (f32[3,16,64,256]{3,2,1,0:T(8,128)S(1)}, f32[3,16,64,256]{3,2,1,0:T(8,128)}, u32[]{:S(2)}) copy-start(f32[3,16,64,256]{3,2,1,0:T(8,128)} %v_ref.1) | copy-start | bytes 9437188
  1.8 36.2 %collective-permute-start = (f32[3,4,16,256]{3,2,1,0:T(8,128)S(1)}, f32[3,4,16,256]{3,2,1,0:T(8,128)S(1)}, u32[]{:S(2)}, u32[]{:S(2)}) collective-permute-start(f32[3,4,16,256]{3,2,1,0:T(8,128)S(1)} %pad_maximum_fusion), channel_id=1, source_target_pairs={{0,4},{4,8},{8,12},{12,16},{16,20},{20,24},{24,28},{28,0},{1,5},{5... | collective-permute-start | bytes 589832 | tf_op jit(solution)/shard_map/ppermute | solution.py:23
  5.8 7.5 %collective-permute-start.3 = (f32[3,16,3,256]{3,2,1,0:T(4,128)S(1)}, f32[3,16,3,256]{3,2,1,0:T(4,128)S(1)}, u32[]{:S(2)}, u32[]{:S(2)}) collective-permute-start(f32[3,16,3,256]{3,2,1,0:T(4,128)S(1)} %slice.103), channel_id=1, source_target_pairs={{0,3},{1,0},{2,1},{3,2},{4,7},{5,4},{6,5},{7,6},{8,11},{9,8},{10,9... | collective-permute-start | bytes 442376 | tf_op jit(solution)/shard_map/ppermute | solution.py:23
  7.6 10.5 %collective-permute-start.2 = (f32[3,16,4,256]{3,2,1,0:T(4,128)S(1)}, f32[3,16,4,256]{3,2,1,0:T(4,128)S(1)}, u32[]{:S(2)}, u32[]{:S(2)}) collective-permute-start(f32[3,16,4,256]{3,2,1,0:T(4,128)S(1)} %slice.102), channel_id=1, source_target_pairs={{0,1},{1,2},{2,3},{3,0},{4,5},{5,6},{6,7},{7,4},{8,9},{9,10},{10,1... | collective-permute-start | bytes 589832 | tf_op jit(solution)/shard_map/ppermute | solution.py:23
  8.7 33.4 %collective-permute-start.5 = (f32[3,3,48,256]{3,2,1,0:T(8,128)S(1)}, f32[3,3,48,256]{3,2,1,0:T(8,128)S(1)}, u32[]{:S(2)}, u32[]{:S(2)}) collective-permute-start(f32[3,3,48,256]{3,2,1,0:T(8,128)S(1)} %slice.105), channel_id=1, source_target_pairs={{0,28},{4,0},{8,4},{12,8},{16,12},{20,16},{24,20},{28,24},{1,29},{... | collective-permute-start | bytes 1327112 | tf_op jit(solution)/shard_map/ppermute | solution.py:23
  13.2 28.9 %collective-permute-start.4 = (f32[3,4,48,256]{3,2,1,0:T(8,128)S(1)}, f32[3,4,48,256]{3,2,1,0:T(8,128)S(1)}, u32[]{:S(2)}, u32[]{:S(2)}) collective-permute-start(f32[3,4,48,256]{3,2,1,0:T(8,128)S(1)} %slice.104), channel_id=1, source_target_pairs={{0,4},{4,8},{8,12},{12,16},{16,20},{20,24},{24,28},{28,0},{1,5},{5... | collective-permute-start | bytes 1769480 | tf_op jit(solution)/shard_map/ppermute | solution.py:23
  13.4 24.7 %collective-permute-start.1 = (f32[3,3,16,256]{3,2,1,0:T(8,128)S(1)}, f32[3,3,16,256]{3,2,1,0:T(8,128)S(1)}, u32[]{:S(2)}, u32[]{:S(2)}) collective-permute-start(f32[3,3,16,256]{3,2,1,0:T(8,128)S(1)} %pad_maximum_fusion.1), channel_id=1, source_target_pairs={{0,28},{4,0},{8,4},{12,8},{16,12},{20,16},{24,20},{28,24},{1,29},{... | collective-permute-start | bytes 442376 | tf_op jit(solution)/shard_map/ppermute | solution.py:23
  38.1 4.0 %collective-permute-start.6 = (f32[3,7,4,256]{3,2,1,0:T(4,128)S(1)}, f32[3,7,4,256]{3,2,1,0:T(4,128)S(1)}, u32[]{:S(2)}, u32[]{:S(2)}) collective-permute-start(f32[3,7,4,256]{3,2,1,0:T(4,128)S(1)} %pad_maximum_fusion.4), channel_id=1, source_target_pairs={{0,1},{1,2},{2,3},{3,0},{4,5},{5,6},{6,7},{7,4},{8,9},{9,10},{10,1... | collective-permute-start | bytes 258056 | tf_op jit(solution)/shard_map/ppermute | solution.py:23
  38.3 3.8 %collective-permute-start.7 = (f32[3,7,3,256]{3,2,1,0:T(4,128)S(1)}, f32[3,7,3,256]{3,2,1,0:T(4,128)S(1)}, u32[]{:S(2)}, u32[]{:S(2)}) collective-permute-start(f32[3,7,3,256]{3,2,1,0:T(4,128)S(1)} %pad_maximum_fusion.5), channel_id=1, source_target_pairs={{0,3},{1,0},{2,1},{3,2},{4,7},{5,4},{6,5},{7,6},{8,11},{9,8},{10,9... | collective-permute-start | bytes 193544 | tf_op jit(solution)/shard_map/ppermute | solution.py:23
  46.9 9.4 %collective-permute-start.10 = (f32[9,2,4,128]{3,2,1,0:T(4,128)S(1)}, f32[9,2,4,128]{3,2,1,0:T(4,128)S(1)}, u32[]{:S(2)}, u32[]{:S(2)}) collective-permute-start(f32[9,2,4,128]{3,2,1,0:T(4,128)S(1)} %get-tuple-element.47), channel_id=1, source_target_pairs={{0,4},{4,8},{8,12},{12,16},{16,20},{20,24},{24,28},{28,0},{1,5},{5... | collective-permute-start | bytes 110600 | tf_op jit(solution)/shard_map/ppermute | solution.py:23
  46.9 9.5 %collective-permute-start.11 = (f32[9,2,4,128]{3,2,1,0:T(4,128)S(1)}, f32[9,2,4,128]{3,2,1,0:T(4,128)S(1)}, u32[]{:S(2)}, u32[]{:S(2)}) collective-permute-start(f32[9,2,4,128]{3,2,1,0:T(4,128)S(1)} %get-tuple-element.48), channel_id=1, source_target_pairs={{0,28},{4,0},{8,4},{12,8},{16,12},{20,16},{24,20},{28,24},{1,29},{... | collective-permute-start | bytes 110600 | tf_op jit(solution)/shard_map/ppermute | solution.py:23
  51.6 14.2 %collective-permute-start.8 = (f32[9,2,32,128]{3,2,1,0:T(8,128)S(1)}, f32[9,2,32,128]{3,2,1,0:T(8,128)S(1)}, u32[]{:S(2)}, u32[]{:S(2)}) collective-permute-start(f32[9,2,32,128]{3,2,1,0:T(8,128)S(1)} %get-tuple-element.44), channel_id=1, source_target_pairs={{0,4},{4,8},{8,12},{12,16},{16,20},{20,24},{24,28},{28,0},{1,5},{5... | collective-permute-start | bytes 884744 | tf_op jit(solution)/shard_map/ppermute | solution.py:23
  51.7 16.0 %collective-permute-start.9 = (f32[9,2,32,128]{3,2,1,0:T(8,128)S(1)}, f32[9,2,32,128]{3,2,1,0:T(8,128)S(1)}, u32[]{:S(2)}, u32[]{:S(2)}) collective-permute-start(f32[9,2,32,128]{3,2,1,0:T(8,128)S(1)} %get-tuple-element.45), channel_id=1, source_target_pairs={{0,28},{4,0},{8,4},{12,8},{16,12},{20,16},{24,20},{28,24},{1,29},{... | collective-permute-start | bytes 884744 | tf_op jit(solution)/shard_map/ppermute | solution.py:23
  56.5 9.3 %collective-permute-start.12 = (f32[9,12,2,128]{3,2,1,0:T(2,128)S(1)}, f32[9,12,2,128]{3,2,1,0:T(2,128)S(1)}, u32[]{:S(2)}, u32[]{:S(2)}) collective-permute-start(f32[9,12,2,128]{3,2,1,0:T(2,128)S(1)} %pad_maximum_fusion.2), channel_id=1, source_target_pairs={{0,1},{1,2},{2,3},{3,0},{4,5},{5,6},{6,7},{7,4},{8,9},{9,10},{10,1... | collective-permute-start | bytes 331784 | tf_op jit(solution)/shard_map/ppermute | solution.py:23
  57.2 8.7 %collective-permute-start.13 = (f32[9,12,2,128]{3,2,1,0:T(2,128)S(1)}, f32[9,12,2,128]{3,2,1,0:T(2,128)S(1)}, u32[]{:S(2)}, u32[]{:S(2)}) collective-permute-start(f32[9,12,2,128]{3,2,1,0:T(2,128)S(1)} %pad_maximum_fusion.3), channel_id=1, source_target_pairs={{0,3},{1,0},{2,1},{3,2},{4,7},{5,4},{6,5},{7,6},{8,11},{9,8},{10,9... | collective-permute-start | bytes 331784 | tf_op jit(solution)/shard_map/ppermute | solution.py:23
  58.4 9.3 %copy-start.2 = (f32[128,128]{1,0:T(8,128)S(1)}, f32[128,128]{1,0:T(8,128)}, u32[]{:S(2)}) copy-start(f32[128,128]{1,0:T(8,128)} %constant.11.clone.refs_5_) | copy-start | bytes 196612
  65.8 19.4 %copy-start.3 = (f32[128,128]{1,0:T(8,128)S(1)}, f32[128,128]{1,0:T(8,128)}, u32[]{:S(2)}) copy-start(f32[128,128]{1,0:T(8,128)} %constant.12.clone.refs_5_) | copy-start | bytes 196612
  70.1 8.7 %collective-permute-start.14 = (f32[9,2,16,64]{3,2,1,0:T(8,128)S(1)}, f32[9,2,16,64]{3,2,1,0:T(8,128)S(1)}, u32[]{:S(2)}, u32[]{:S(2)}) collective-permute-start(f32[9,2,16,64]{3,2,1,0:T(8,128)S(1)} %get-tuple-element.54), channel_id=1, source_target_pairs={{0,4},{4,8},{8,12},{12,16},{16,20},{20,24},{24,28},{28,0},{1,5},{5... | collective-permute-start | bytes 221192 | tf_op jit(solution)/shard_map/ppermute | solution.py:23
  70.1 9.0 %collective-permute-start.15 = (f32[9,2,16,64]{3,2,1,0:T(8,128)S(1)}, f32[9,2,16,64]{3,2,1,0:T(8,128)S(1)}, u32[]{:S(2)}, u32[]{:S(2)}) collective-permute-start(f32[9,2,16,64]{3,2,1,0:T(8,128)S(1)} %get-tuple-element.55), channel_id=1, source_target_pairs={{0,28},{4,0},{8,4},{12,8},{16,12},{20,16},{24,20},{28,24},{1,29},{... | collective-permute-start | bytes 221192 | tf_op jit(solution)/shard_map/ppermute | solution.py:23
  79.3 5.9 %collective-permute-start.16 = (f32[9,8,2,64]{3,2,1,0:T(2,128)S(1)}, f32[9,8,2,64]{3,2,1,0:T(2,128)S(1)}, u32[]{:S(2)}, u32[]{:S(2)}) collective-permute-start(f32[9,8,2,64]{3,2,1,0:T(2,128)S(1)} %maximum_maximum_fusion), channel_id=1, source_target_pairs={{0,1},{1,2},{2,3},{3,0},{4,5},{5,6},{6,7},{7,4},{8,9},{9,10},{10,1... | collective-permute-start | bytes 110600 | tf_op jit(solution)/shard_map/ppermute | solution.py:23
  79.5 5.7 %collective-permute-start.17 = (f32[9,8,2,64]{3,2,1,0:T(2,128)S(1)}, f32[9,8,2,64]{3,2,1,0:T(2,128)S(1)}, u32[]{:S(2)}, u32[]{:S(2)}) collective-permute-start(f32[9,8,2,64]{3,2,1,0:T(2,128)S(1)} %maximum_maximum_fusion.1), channel_id=1, source_target_pairs={{0,3},{1,0},{2,1},{3,2},{4,7},{5,4},{6,5},{7,6},{8,11},{9,8},{10,9... | collective-permute-start | bytes 110600 | tf_op jit(solution)/shard_map/ppermute | solution.py:23

commit v4 on v3

--- a/solution.py
+++ b/solution.py
@@ -99,11 +99,28 @@
     return c[0], c[1] + predict_one * (c[0] + c[2])
 
 
-def row_parts(layer):
-    rows = layer.shape[0]
-    tail = [layer[rows - 4 + i : rows - 3 + i] for i in range(4)]
-    head = [layer[i : i + 1] for i in range(3)]
-    return parts_for_next(tail) + parts_for_previous(head)
+def row_parts(load, rows):
+    tail, head = load(rows - 8), load(0)
+    row = lax.broadcasted_iota(jnp.int32, tail.shape, 0)
+    inner = tail + predict_one * (pltpu.roll(tail, 1, 0) + pltpu.roll(tail, 7, 0))
+    p = tail + predict_one * pltpu.roll(tail, 1, 0)
+    q = tail + update_one * pltpu.roll(inner, 1, 0)
+    s = head + predict_one * (pltpu.roll(head, 1, 0) + pltpu.roll(head, 7, 0))
+    return jnp.where(row == 7, p, q)[6:8], jnp.where(row == 0, head, s)[0:2]
+
+
+def send_layers(layers, f, at, next_ref, prev_ref):
+    for part, value in enumerate(parts_for_next(layers)):
+        next_ref[f, part, at : at + 8, :] = value
+    for part, value in enumerate(parts_for_previous(layers)):
+        prev_ref[f, part, at : at + 8, :] = value
+
+
+def send_rows(ref, f, down_ref, up_ref):
+    for at in range(ref.shape[1]):
+        tail, head = row_parts(lambda row: ref[f, at, row : row + 8, :], ref.shape[2])
+        down_ref[f, at] = tail
+        up_ref[f, at] = head
 
 
 def local_kernel(v_ref, before_ref, after_ref, table_ref, low_ref, rest_ref, rows_ref, stack_ref):
@@ -138,16 +155,17 @@
         rest_ref[2, f, 0] = out[f * ny + half : (f + 1) * ny, lanes:]
 
 
-def local_pass(velocity, before, after, table):
+def local_pass(velocity, before, after, table, start):
     _, nx, ny, nz = velocity.shape
+    nx = nx // 2
     half, lanes = ny // 2, nz // 2
     return pl.pallas_call(
         local_kernel,
         grid=(nx,),
         in_specs=[
-            pl.BlockSpec((3, 1, ny, nz), lambda i: (0, i, 0, 0)),
-            pl.BlockSpec((3, 1, BEFORE, nz), lambda i: (0, i, 0, 0)),
-            pl.BlockSpec((3, 1, AFTER, nz), lambda i: (0, i, 0, 0)),
+            pl.BlockSpec((3, 1, ny, nz), lambda i: (0, i + start, 0, 0)),
+            pl.BlockSpec((3, 1, BEFORE, nz), lambda i: (0, i + start, 0, 0)),
+            pl.BlockSpec((3, 1, AFTER, nz), lambda i: (0, i + start, 0, 0)),
             pl.BlockSpec((nz, nz), lambda i: (0, 0)),
         ],
         out_specs=[
@@ -197,75 +215,78 @@
                 odd_ref[c, layer, :, cut] = rows_ref[h, pl.ds(1, count, stride=2), :]
 
 
-def halo_parts(ref, i, j):
-    g = [ref[i, layer] * ref[j, layer] for layer in range(BEFORE + AFTER)]
-    return parts_for_next(g[:BEFORE]) + parts_for_previous(g[BEFORE:])
-
-
 def lift_first(layers, halo):
     return halo_lift_list(layers[0::2], layers[1::2], *halo)
 
 
-def send_parts(layers, f, next_ref, prev_ref, next_edge_ref, prev_edge_ref, down_ref, up_ref):
-    for part, value in enumerate(parts_for_next(layers)):
-        next_ref[f, part] = value
-        for at, row in enumerate(row_parts(value)):
-            next_edge_ref[f, part, at : at + 1, :] = row
-    for part, value in enumerate(parts_for_previous(layers)):
-        prev_ref[f, part] = value
-        for at, row in enumerate(row_parts(value)):
-            prev_edge_ref[f, part, at : at + 1, :] = row
-    for at, layer in enumerate(layers):
-        p, q, r, s = row_parts(layer)
-        down_ref[f, at, 0:1, :] = p
-        down_ref[f, at, 1:2, :] = q
-        up_ref[f, at, 0:1, :] = r
-        up_ref[f, at, 1:2, :] = s
+def halo_stack(pairs, both, even_ref, odd_ref, part_ref, stack_ref):
+    count, nz = even_ref.shape[2:]
+    half, lanes = count - 16, nz // 2
+    kinds = 8 if both else 4
+    for n, (i, j) in enumerate(pairs):
+        for h in range(2):
+            cut = slice(h * lanes, (h + 1) * lanes)
+            for parity, ref in enumerate((even_ref, odd_ref)):
+                for r in range(0, count, 16):
+                    rows = slice(r, r + 16)
+                    g = [ref[i, layer, rows, cut] * ref[j, layer, rows, cut] for layer in range(BEFORE + AFTER)]
+                    for k, value in enumerate(parts_for_next(g[:BEFORE]) + parts_for_previous(g[BEFORE:])):
+                        part_ref[parity, k, rows, :] = value
+            for k in range(4):
+                e, o = ring_lift(part_ref[0, k], part_ref[1, k])
+                at = (kinds * n + k) * half
+                stack_ref[at : at + half, cut] = e[8 : 8 + half]
+                if both:
+                    at += 4 * half
+                    stack_ref[at : at + half, cut] = o[8 : 8 + half]
+
+
+def layer_list(refs, index, rows):
+    return [ref[index + (x, rows)] for ref in refs for x in range(ref.shape[len(index)])]
 
 
 def approx_kernel(*refs):
-    low_ref, table_ref = refs[:2]
-    halo_refs = refs[2:8]
-    approx_ref, high_ref, stress_ref = refs[8:11]
-    sends = refs[11:17]
-    rows_ref, even_ref, odd_ref, kept_ref, stack_ref = refs[17:]
+    low_refs, table_ref = refs[:2], refs[2]
+    halo_refs = refs[3:9]
+    approx_ref, high_ref, stress_ref = refs[9:12]
+    next_ref, prev_ref, next_edge_ref, prev_edge_ref, down_ref, up_ref = refs[12:18]
+    rows_ref, even_ref, odd_ref, kept_ref, part_ref, stack_ref, out_ref = refs[18:]
     f = pl.program_id(0)
-    nx, half, lanes = low_ref.shape[1:]
+    half, lanes = low_refs[0].shape[2:]
+    mx = approx_ref.shape[1]
 
     @pl.when(f == 0)
     def _():
         gather_rows(halo_refs, rows_ref, even_ref, odd_ref)
 
-    pairs = [pair_of(f * GROUP + k) for k in range(GROUP)]
-    for n, (i, j) in enumerate(pairs):
-        even = halo_parts(even_ref, i, j)
-        odd = halo_parts(odd_ref, i, j)
-        for k in range(4):
-            e, _ = ring_lift(even[k], odd[k])
-            at = (4 * n + k) * half
-            stack_ref[at : at + half, :] = e[8 : 8 + half]
-    out = dot(stack_ref[...], table_ref[:, :lanes])
-    fields = []
+    pairs = [pair_of(f * GROUP + n) for n in range(GROUP)]
+    halo_stack(pairs, False, even_ref, odd_ref, part_ref, stack_ref)
+    out_ref[...] = dot(stack_ref[...], table_ref[:, :lanes])
     for n in range(GROUP):
-        halo = [out[(4 * n + k) * half : (4 * n + k + 1) * half] for k in range(4)]
-        e, o = lift_first([low_ref[n, x] for x in range(nx)], halo)
-        e = [t * band_scale(0, 0) for t in e]
-        for x in range(nx // 2):
-            approx_ref[n, x] = e[x]
-            high_ref[n, x] = o[x] * band_scale(0, 1)
-        send_parts(e, n, *sends)
-        fields.append(e)
+        for r in range(0, half, 8):
+            rows = slice(r, r + 8)
+            halo = [out_ref[(4 * n + k) * half + r : (4 * n + k) * half + r + 8, :] for k in range(4)]
+            e, o = lift_first(layer_list(low_refs, (n,), rows), halo)
+            e = [t * band_scale(0, 0) for t in e]
+            for x in range(mx):
+                approx_ref[n, x, rows, :] = e[x]
+                high_ref[n, x, rows, :] = o[x] * band_scale(0, 1)
+            send_layers(e, n, r, next_ref, prev_ref)
+        send_rows(approx_ref, n, down_ref, up_ref)
+        for ref, edge_ref in ((next_ref, next_edge_ref), (prev_ref, prev_edge_ref)):
+            for part in range(2):
+                tail, head = row_parts(lambda row: ref[n, part, row : row + 8, :], half)
+                edge_ref[n, part, 0:2, :] = tail
+                edge_ref[n, part, 2:4, :] = head
 
     @pl.when(f == 0)
     def _():
-        for n in range(GROUP):
-            for x in range(nx // 2):
-                kept_ref[n, x] = fields[n][x]
+        kept_ref[...] = approx_ref[...]
 
     @pl.when(f > 0)
     def _():
         for n, (i, j) in enumerate(pairs):
-            for x in range(nx // 2):
+            for x in range(mx):
                 stress_ref[n, x] = approx_ref[n, x] - kept_ref[i, x] * kept_ref[j, x]
 
 
@@ -277,15 +298,15 @@
     return pl.BlockSpec((GROUP,) + shape, lambda f: (f,) + (0,) * len(shape))
 
 
-def approx_pass(low, halo, table):
-    _, nx, half, lanes = low.shape
-    nz, count, mx = 2 * lanes, half + 16, nx // 2
+def approx_pass(lows, halo, table):
+    _, nx, half, lanes = lows[0].shape
+    nz, count, mx = 2 * lanes, half + 16, nx
     f32 = lambda *shape: jax.ShapeDtypeStruct(shape, jnp.float32)
     sends = [(2, half, lanes), (2, half, lanes), (2, 4, lanes), (2, 4, lanes), (mx, 2, lanes), (mx, 2, lanes)]
     return pl.pallas_call(
         approx_kernel,
         grid=(9 // GROUP,),
-        in_specs=[per_field((nx, half, lanes)), whole((nz, nz))] + [whole(h.shape) for h in halo],
+        in_specs=[per_field((nx, half, lanes))] * 2 + [whole((nz, nz))] + [whole(h.shape) for h in halo],
         out_specs=[
             per_field((mx, half, lanes)),
             per_field((mx, half, lanes)),
@@ -293,79 +314,75 @@
         ]
         + [per_field(s) for s in sends],
         out_shape=[f32(9, mx, half, lanes), f32(9, mx, half, lanes), f32(6, mx, half, lanes)] + [f32(9, *s) for s in sends],
-        scratch_shapes=[
-            pltpu.VMEM((2, 2 * half + 32, lanes), jnp.float32),
-            pltpu.VMEM((4, BEFORE + AFTER, count, nz), jnp.float32),
-            pltpu.VMEM((4, BEFORE + AFTER, count, nz), jnp.float32),
+        scratch_shapes=halo_scratch(half, lanes)
+        + [
             pltpu.VMEM((3, mx, half, lanes), jnp.float32),
+            pltpu.VMEM((2, 4, count, lanes), jnp.float32),
             pltpu.VMEM((GROUP * 4 * half, nz), jnp.float32),
+            pltpu.VMEM((GROUP * 4 * half, lanes), jnp.float32),
         ],
         compiler_params=pltpu.CompilerParams(vmem_limit_bytes=24 * MIB),
         name="approx_pass",
-    )(low, table, *halo)
+    )(*lows, table, *halo)
+
+
+def halo_scratch(half, lanes):
+    return [
+        pltpu.VMEM((2, 2 * half + 32, lanes), jnp.float32),
+        pltpu.VMEM((4, BEFORE + AFTER, half + 16, 2 * lanes), jnp.float32),
+        pltpu.VMEM((4, BEFORE + AFTER, half + 16, 2 * lanes), jnp.float32),
+    ]
 
 
 def detail_kernel(*refs):
-    rest_ref, high_ref, table_ref = refs[:3]
-    halo_refs = refs[3:9]
-    out_ref, rows_ref, even_ref, odd_ref, stack_ref = refs[9:]
+    rest_refs, high_ref, table_ref = refs[:2], refs[2], refs[3]
+    halo_refs = refs[4:10]
+    out_ref, rows_ref, even_ref, odd_ref, part_ref, stack_ref = refs[10:]
     f = pl.program_id(0)
-    nx, half, lanes = rest_ref.shape[2:]
+    half, lanes = high_ref.shape[2:]
+    mx = high_ref.shape[1]
 
     @pl.when(f == 0)
     def _():
         gather_rows(halo_refs, rows_ref, even_ref, odd_ref)
 
-    for n in range(GROUP):
-        i, j = pair_of(f * GROUP + n)
-        even = halo_parts(even_ref, i, j)
-        odd = halo_parts(odd_ref, i, j)
-        for k in range(4):
-            e, o = ring_lift(even[k], odd[k])
-            at = (8 * n + k) * half
-            stack_ref[at : at + half, :] = e[8 : 8 + half]
-            at += 4 * half
-            stack_ref[at : at + half, :] = o[8 : 8 + half]
+    pairs = [pair_of(f * GROUP + n) for n in range(GROUP)]
+    halo_stack(pairs, True, even_ref, odd_ref, part_ref, stack_ref)
     stack_ref[...] = dot(stack_ref[...], table_ref[...])
     for n in range(GROUP):
-        for x in range(nx // 2):
+        for x in range(mx):
             out_ref[0, n, x] = high_ref[n, x]
         for band, (bz, by) in enumerate(((0, 1), (1, 0), (1, 1))):
-            halo = []
-            for k in range(4):
-                at = (8 * n + 4 * by + k) * half
-                halo.append(stack_ref[at : at + half, bz * lanes : (bz + 1) * lanes])
-            e, o = lift_first([rest_ref[band, n, x] for x in range(nx)], halo)
-            at = 4 * bz + 2 * by - 1
-            for x in range(nx // 2):
-                out_ref[at, n, x] = e[x] * band_scale(by, 0)
-                out_ref[at + 1, n, x] = o[x] * band_scale(by, 1)
-
-
-def detail_pass(rest, high, halo, table):
-    _, _, nx, half, lanes = rest.shape
-    nz, count, mx = 2 * lanes, half + 16, nx // 2
+            plane = 4 * bz + 2 * by - 1
+            for r in range(0, half, 8):
+                rows = slice(r, r + 8)
+                halo = []
+                for k in range(4):
+                    at = (8 * n + 4 * by + k) * half + r
+                    halo.append(stack_ref[at : at + 8, bz * lanes : (bz + 1) * lanes])
+                e, o = lift_first(layer_list(rest_refs, (band, n), rows), halo)
+                for x in range(mx):
+                    out_ref[plane, n, x, rows, :] = e[x] * band_scale(by, 0)
+                    out_ref[plane + 1, n, x, rows, :] = o[x] * band_scale(by, 1)
+
+
+def detail_pass(rests, high, halo, table):
+    _, mx, half, lanes = high.shape
+    nz, count = 2 * lanes, half + 16
     return pl.pallas_call(
         detail_kernel,
         grid=(9 // GROUP,),
-        in_specs=[
-            pl.BlockSpec((3, GROUP, nx, half, lanes), lambda f: (0, f, 0, 0, 0)),
-            per_field((mx, half, lanes)),
-            whole((nz, nz)),
-        ]
+        in_specs=[pl.BlockSpec((3, GROUP, mx, half, lanes), lambda f: (0, f, 0, 0, 0))] * 2
+        + [per_field((mx, half, lanes)), whole((nz, nz))]
         + [whole(h.shape) for h in halo],
         out_specs=pl.BlockSpec((7, GROUP, mx, half, lanes), lambda f: (0, f, 0, 0, 0)),
         out_shape=jax.ShapeDtypeStruct((7, 9, mx, half, lanes), jnp.float32),
-        scratch_shapes=[
-            pltpu.VMEM((2, 2 * half + 32, lanes), jnp.float32),
-            pltpu.VMEM((4, BEFORE + AFTER, count, nz), jnp.float32),
-            pltpu.VMEM((4, BEFORE + AFTER, count, nz), jnp.float32),
-            pltpu.VMEM((GROUP * 8 * half, nz), jnp.float32),
-        ],
+        scratch_shapes=halo_scratch(half, lanes)
+        + [pltpu.VMEM((2, 4, count, lanes), jnp.float32), pltpu.VMEM((GROUP * 8 * half, nz), jnp.float32)],
         compiler_params=pltpu.CompilerParams(vmem_limit_bytes=24 * MIB),
-        cost_estimate=pl.CostEstimate(flops=9 * nx * half * nz * 200, bytes_accessed=9 * nx * half * nz * 16, transcendentals=0),
+        cost_estimate=pl.CostEstimate(flops=18 * mx * half * nz * 200, bytes_accessed=18 * mx * half * nz * 16, transcendentals=0),
         name="detail_pass",
-    )(rest, high, table, *halo)
+    )(*rests, high, table, *halo)
 
 
 def level_rows(refs, nz, lows, pad_ref, stack_ref):
@@ -379,17 +396,17 @@
     for f in range(9):
         for layer in range(nx + 4):
             if layer < nx:
-                source = a_ref.at[f, layer]
+                source, at = a_ref, layer
             elif layer < nx + 2:
-                source = before_ref.at[f, layer - nx]
+                source, at = before_ref, layer - nx
             else:
-                source = after_ref.at[f, layer - nx - 2]
-            pad_ref[f, layer, :, :nz] = source[...]
-    for f in range(9):
-        for layer in range(nx + 4):
-            e = pad_ref[f, layer, pl.ds(0, half, stride=2), :]
-            o = pad_ref[f, layer, pl.ds(1, half, stride=2), :]
-            rows = [down_ref[f, layer, 0:1, :], down_ref[f, layer, 1:2, :], up_ref[f, layer, 0:1, :], up_ref[f, layer, 1:2, :]]
+                source, at = after_ref, layer - nx - 2
+            if nz < wide:
+                pad_ref[f, layer, :, :nz] = source[f, at]
+                source, at = pad_ref, layer
+            e = source[f, at, pl.ds(0, half, stride=2), :]
+            o = source[f, at, pl.ds(1, half, stride=2), :]
+            rows = [down_ref[f, layer, 1:2, :], down_ref[f, layer, 0:1, :], up_ref[f, layer, 0:1, :], up_ref[f, layer, 1:2, :]]
             if nz < wide:
                 rows = [jnp.concatenate([row, jnp.zeros((1, wide - nz), jnp.float32)], axis=1) for row in rows]
             e, o = sublane_lift(e, o, *rows)
@@ -406,28 +423,25 @@
     half, lanes = ny // 2, nz // 2
     level_rows(refs[:5], nz, True, pad_ref, stack_ref)
     out_ref[...] = dot(stack_ref[...], table_ref[...])
+    mx = nx // 2
     for f in range(9):
-        at = f * (nx + 4) * half
-        layers = [out_ref[at + layer * half : at + (layer + 1) * half, :] for layer in range(nx + 4)]
-        low, _ = lift_first(layers[:nx], layers[nx:])
-        approx = [(t * band_scale(0, 0))[:, :lanes] for t in low]
-        for x in range(nx // 2):
-            if f < 3:
-                kept_ref[f, x] = approx[x]
-            else:
-                i, j = product_pairs[f - 3]
-                stress_ref[f - 3, x] = approx[x] - kept_ref[i, x] * kept_ref[j, x]
-            approx_ref[f, x] = approx[x]
-        for part, value in enumerate(parts_for_next(approx)):
-            sends[0][f, part] = value
-        for part, value in enumerate(parts_for_previous(approx)):
-            sends[1][f, part] = value
-        for at, layer in enumerate(approx):
-            p, q, r, s = row_parts(layer)
-            sends[2][f, at, 0:1, :] = p
-            sends[2][f, at, 1:2, :] = q
-            sends[3][f, at, 0:1, :] = r
-            sends[3][f, at, 1:2, :] = s
+        for r in range(0, half, 8):
+            rows = slice(r, r + 8)
+            layers = []
+            for layer in range(nx + 4):
+                at = (f * (nx + 4) + layer) * half + r
+                layers.append(out_ref[at : at + 8, :])
+            low, _ = lift_first(layers[:nx], layers[nx:])
+            approx = [(t * band_scale(0, 0))[:, :lanes] for t in low]
+            for x in range(mx):
+                if f < 3:
+                    kept_ref[f, x, rows, :] = approx[x]
+                else:
+                    i, j = product_pairs[f - 3]
+                    stress_ref[f - 3, x, rows, :] = approx[x] - kept_ref[i, x, rows, :] * kept_ref[j, x, rows, :]
+                approx_ref[f, x, rows, :] = approx[x]
+            send_layers(approx, f, r, sends[0], sends[1])
+        send_rows(approx_ref, f, sends[2], sends[3])
 
 
 def level_detail_kernel(nz, last, *refs):
@@ -439,26 +453,30 @@
     level_rows(refs[:5], nz, False, pad_ref, stack_ref)
     out_ref[...] = dot(stack_ref[...], table_ref[...])
     for f in range(9):
-        at = f * (nx + 4) * ny
-        layers = [out_ref[at + layer * ny : at + (layer + 1) * ny, :] for layer in range(nx + 4)]
-        low, high = lift_first(layers[:nx], layers[nx:])
-        for x in range(nx // 2):
-            for bx, value in enumerate((low[x], high[x])):
-                for by in range(2):
-                    t = value[by * half : (by + 1) * half] * band_scale(by, bx)
-                    for bz in range(2):
-                        band = 4 * bz + 2 * by + bx
-                        piece = t[:, bz * (wide // 2) : bz * (wide // 2) + lanes]
-                        if band:
-                            detail_ref[band - 1, f, x] = piece
-                        elif last:
-                            stress_ref, approx_ref = refs[7:9]
-                            if f < 3:
-                                kept_ref[f, x] = piece
-                                approx_ref[f, x] = piece
-                            else:
-                                i, j = product_pairs[f - 3]
-                                stress_ref[f - 3, x] = piece - kept_ref[i, x] * kept_ref[j, x]
+        for by in range(2):
+            for r in range(0, half, 8):
+                rows = slice(r, r + 8)
+                layers = []
+                for layer in range(nx + 4):
+                    at = (f * (nx + 4) + layer) * ny + by * half + r
+                    layers.append(out_ref[at : at + 8, :])
+                low, high = lift_first(layers[:nx], layers[nx:])
+                for x in range(nx // 2):
+                    for bx, value in enumerate((low[x], high[x])):
+                        t = value * band_scale(by, bx)
+                        for bz in range(2):
+                            band = 4 * bz + 2 * by + bx
+                            piece = t[:, bz * (wide // 2) : bz * (wide // 2) + lanes]
+                            if band:
+                                detail_ref[band - 1, f, x, rows, :] = piece
+                            elif last:
+                                stress_ref, approx_ref = refs[7:9]
+                                if f < 3:
+                                    kept_ref[f, x, rows, :] = piece
+                                    approx_ref[f, x, rows, :] = piece
+                                else:
+                                    i, j = product_pairs[f - 3]
+                                    stress_ref[f - 3, x, rows, :] = piece - kept_ref[i, x, rows, :] * kept_ref[j, x, rows, :]
 
 
 def level_call(kernel, approx, halo, out, kept):
@@ -499,16 +517,14 @@
     return level_call(lambda *refs: level_detail_kernel(nz, last, *refs), approx, halo, out, ny)
 
 
-def exchange_small(to_next, to_prev, down, up):
-    before = shifted(to_next, "gx", 1)
-    after = shifted(to_prev, "gx", -1)
+def halo_rows(before, after, down, up):
     rows = before.shape[2]
     cell = lambda at: jnp.concatenate([before[:, :, at : at + 1], after[:, :, at : at + 1]], axis=1)
-    tail = jnp.concatenate(parts_for_next([cell(rows - 4 + i) for i in range(4)]), axis=2)
+    p, q = parts_for_next([cell(rows - 4 + i) for i in range(4)])
+    down = jnp.concatenate([down, jnp.concatenate([q, p], axis=2)], axis=1)
     head = jnp.concatenate(parts_for_previous([cell(i) for i in range(3)]), axis=2)
-    down = jnp.concatenate([down, tail], axis=1)
     up = jnp.concatenate([up, head], axis=1)
-    return before, after, shifted(down, "gy", 1), shifted(up, "gy", -1)
+    return shifted(down, "gy", 1), shifted(up, "gy", -1)
 
 
 def exchange(to_next, to_prev, edge_next, edge_prev, down, up):
@@ -532,22 +548,25 @@
     mid_after = shifted(head[:, :, 8 : ny - 8], "gx", -1)
     own_before = shifted(velocity[:, :, ny - BEFORE :], "gy", 1)
     own_after = shifted(velocity[:, :, :AFTER], "gy", -1)
-    low, rest = local_pass(velocity, own_before, own_after, table)
-    edge_before, edge_after, low = lax.optimization_barrier((edge_before, edge_after, low))
+    low_one, rest_one = local_pass(velocity, own_before, own_after, table, 0)
+    edge_before, edge_after, low_one = lax.optimization_barrier((edge_before, edge_after, low_one))
     down = jnp.concatenate([edge_before[:, :, 12:], edge_after[:, :, 12:]], axis=1)
     up = jnp.concatenate([edge_before[:, :, :AFTER], edge_after[:, :, :AFTER]], axis=1)
     row_before = shifted(down, "gy", 1)
     row_after = shifted(up, "gy", -1)
+    low_two, rest_two = local_pass(velocity, own_before, own_after, table, nx // 2)
     halo = (edge_before, mid_before, edge_after, mid_after, row_before, row_after)
-    approx, high, stress_one, *sends = approx_pass(low, halo, table)
+    approx, high, stress_one, *sends = approx_pass((low_one, low_two), halo, table)
     second_halo = exchange(*sends)
-    details_one = detail_pass(rest, high, halo, table)
+    details_one = detail_pass((rest_one, rest_two), high, halo, table)
     approx, details_one = lax.optimization_barrier((approx, details_one))
     second = approx
     approx, stress_two, *sends = level_approx(second, second_halo)
-    third_halo = exchange_small(*sends)
-    details_two, = level_details(second, second_halo, False)
-    approx, details_two = lax.optimization_barrier((approx, details_two))
+    before = shifted(sends[0], "gx", 1)
+    after = shifted(sends[1], "gx", -1)
+    (details_two,) = level_details(second, second_halo, False)
+    before, after, details_two = lax.optimization_barrier((before, after, details_two))
+    third_halo = (before, after) + halo_rows(before, after, *sends[2:])
     details_three, stress_three, coarse = level_details(approx, third_halo, True)
     return details_one, stress_one, details_two, stress_two, details_three, stress_three, coarse
 

time: 87.4 us -> 91.6 us (1.048)
  waiting for transfers between devices: 12.3 us -> 15.8 us
    ppermute x18, waiting for transfers between devices: 12.3 us -> 15.8 us  [shifted(): lax.ppermute(block, axis, [(i, (i + distance) % size) for i in range(size)])]
    pallas_call x1 -> x2, Pallas kernels: 15.8 us -> 15.8 us  [local_pass(): pl.pallas_call(local_kernel, grid=(nx,), in_specs=[pl.BlockSpec((3, 1, ny...]
  transfers between devices with their start and end apart: 18 -> 18, of which waited for: 5 -> 4; matrix products, arithmetic and copies ran while one was open for 5% -> 5% of each run, Pallas kernels for 31% -> 30%
where the time goes in v4:
time: 91.6 us; the launch traced here: 91.3 us
  Pallas kernels  36.1 us (39%)
  starting transfers between devices  32.5 us (35%)
  waiting for transfers between devices  15.8 us (17%)
  local copies, waits for them, and re-layouts  5.52 us (6%)
  between operations  0.93 us (1%)
    ppermute x18, starting transfers between devices, shifted(): lax.ppermute(block, axis, [(i, (i + distance) % size) for i in range(size)])  32.5 us
    ppermute x18, waiting for transfers between devices, shifted(): lax.ppermute(block, axis, [(i, (i + distance) % size) for i in range(size)])  15.8 us
    pallas_call x2, Pallas kernels, local_pass(): pl.pallas_call(local_kernel, grid=(nx,), in_specs=[pl.BlockSpec((3, 1, ny...  15.8 us
    pallas_call x3, Pallas kernels, level_call(): pl.pallas_call(kernel, in_specs=[vmem] * 6, out_specs=[vmem] * len(out),...  8 us
    pallas_call x1, Pallas kernels, detail_pass(): pl.pallas_call(detail_kernel, grid=(9 // GROUP,), in_specs=[pl.BlockSpec(...  7.46 us
    pallas_call x1, Pallas kernels, approx_pass(): pl.pallas_call(approx_kernel, grid=(9 // GROUP,), in_specs=[per_field((nx...  4.82 us
  transfers between devices with their start and end apart: 18, of which 4 were waited for; matrix products, arithmetic and copies ran while one was open for 5% of the time, Pallas kernels for 30%

profile of v4, /device:TPU:0, one launch (start us, length us, event | category | flops | bytes accessed | tf_op | source)
XLA Modules:
  0.0 91.3 jit_solution(6573934450484118691)
XLA Ops:
  0.6 0.0 copy-start.1
  0.6 0.0 copy-start
  0.7 1.1 %fusion.6 = (f32[3,4,8,256]{3,2,1,0:T(8,128)S(1)}, f32[3,4,8,256]{3,2,1,0:T(8,128)S(1)}) fusion(f32[3,16,64,256]{3,2,1,0:T(8,128)} %v_ref.3), kind=kLoop, calls=%fused_computation.19 | loop fusion | bytes 393216 | tf_op jit(solution)/shard_map/slice | solution.py:544
  1.8 3.0 %collective-permute-start = (f32[3,4,16,256]{3,2,1,0:T(8,128)S(1)}, f32[3,4,16,256]{3,2,1,0:T(8,128)S(1)}, u32[]{:S(2)}, u32[]{:S(2)}) collective-permute-start(f32[3,4,16,256]{3,2,1,0:T(8,128)S(1)} %pad_maximum_fusion), channel_id=1, source_target_pairs={{0,4},{4,8},{8,12},{12,16},{16,20},{20,24},{24,28},{28,0},{1,5},{5... | collective-permute-start | bytes 589832 | tf_op jit(solution)/shard_map/ppermute | solution.py:23
  4.8 1.0 %slice.102 = f32[3,16,4,256]{3,2,1,0:T(4,128)S(1)} slice(f32[3,16,64,256]{3,2,1,0:T(8,128)} %v_ref.3), slice={[0:3], [0:16], [60:64], [0:256]} | slice | bytes 393216 | tf_op jit(solution)/shard_map/slice | solution.py:549
  5.9 0.1 collective-permute-start.2
  5.9 1.0 %slice.103 = f32[3,16,3,256]{3,2,1,0:T(4,128)S(1)} slice(f32[3,16,64,256]{3,2,1,0:T(8,128)} %v_ref.3), slice={[0:3], [0:16], [0:3], [0:256]} | slice | bytes 294912 | tf_op jit(solution)/shard_map/slice | solution.py:550
  6.9 1.8 %collective-permute-start.3 = (f32[3,16,3,256]{3,2,1,0:T(4,128)S(1)}, f32[3,16,3,256]{3,2,1,0:T(4,128)S(1)}, u32[]{:S(2)}, u32[]{:S(2)}) collective-permute-start(f32[3,16,3,256]{3,2,1,0:T(4,128)S(1)} %slice.103), channel_id=1, source_target_pairs={{0,3},{1,0},{2,1},{3,2},{4,7},{5,4},{6,5},{7,6},{8,11},{9,8},{10,9... | collective-permute-start | bytes 442376 | tf_op jit(solution)/shard_map/ppermute | solution.py:23
  8.7 1.0 %slice.105 = f32[3,3,48,256]{3,2,1,0:T(8,128)S(1)} slice(f32[3,16,64,256]{3,2,1,0:T(8,128)} %v_ref.3), slice={[0:3], [0:3], [8:56], [0:256]} | slice | bytes 884736 | tf_op jit(solution)/shard_map/slice | solution.py:548
  9.8 3.1 %collective-permute-start.5 = (f32[3,3,48,256]{3,2,1,0:T(8,128)S(1)}, f32[3,3,48,256]{3,2,1,0:T(8,128)S(1)}, u32[]{:S(2)}, u32[]{:S(2)}) collective-permute-start(f32[3,3,48,256]{3,2,1,0:T(8,128)S(1)} %slice.105), channel_id=1, source_target_pairs={{0,28},{4,0},{8,4},{12,8},{16,12},{20,16},{24,20},{28,24},{1,29},{... | collective-permute-start | bytes 1327112 | tf_op jit(solution)/shard_map/ppermute | solution.py:23
  12.9 1.1 %slice.104 = f32[3,4,48,256]{3,2,1,0:T(8,128)S(1)} slice(f32[3,16,64,256]{3,2,1,0:T(8,128)} %v_ref.3), slice={[0:3], [12:16], [8:56], [0:256]} | slice | bytes 1179648 | tf_op jit(solution)/shard_map/slice | solution.py:547
  14.0 0.1 collective-permute-start.4
  14.1 0.0 collective-permute-done.3.after_ref
  14.1 4.7 %collective-permute-start.1 = (f32[3,3,16,256]{3,2,1,0:T(8,128)S(1)}, f32[3,3,16,256]{3,2,1,0:T(8,128)S(1)}, u32[]{:S(2)}, u32[]{:S(2)}) collective-permute-start(f32[3,3,16,256]{3,2,1,0:T(8,128)S(1)} %pad_maximum_fusion.1), channel_id=1, source_target_pairs={{0,28},{4,0},{8,4},{12,8},{16,12},{20,16},{24,20},{28,24},{1,29},{... | collective-permute-start | bytes 442376 | tf_op jit(solution)/shard_map/ppermute | solution.py:23
  18.9 0.0 collective-permute-done.2.before_ref
  18.9 7.9 %local_pass.2 = (f32[9,8,32,128]{3,2,1,0:T(8,128)S(1)}, f32[3,9,8,32,128]{4,3,2,1,0:T(8,128)S(1)}) custom-call(f32[3,16,64,256]{3,2,1,0:T(8,128)S(1)} %copy-done, f32[3,16,4,256]{3,2,1,0:T(4,128)S(1)} %collective-permute-done.2.before_ref, f32[3,16,3,256]{3,2,1,0:T(4,128)S(1)} %collective-permute-done.3.after_ref, f32[256,256]{1,0:T(8,128)S(1)} %copy-done.1), custom_call_target="tpu_custom_call" | custom-call | flops 603979776 | bytes 7077888 | tf_op jit(solution)/shard_map/local_pass/pallas_call | solution.py:162
  26.8 11.2 %collective-permute-done.1.refs_5_.refs_6_ = f32[3,3,16,256]{3,2,1,0:T(8,128)S(1)} collective-permute-done((f32[3,3,16,256]{3,2,1,0:T(8,128)S(1)}, f32[3,3,16,256]{3,2,1,0:T(8,128)S(1)}, u32[]{:S(2)}, u32[]{:S(2)}) %collective-permute-start.1) | collective-permute-done | bytes 147488 | tf_op jit(solution)/shard_map/ppermute | solution.py:23
  38.0 0.0 collective-permute-done.refs_3_.refs_4_
  38.1 0.1 collective-permute-start.6
  38.2 1.8 %collective-permute-start.7 = (f32[3,7,3,256]{3,2,1,0:T(4,128)S(1)}, f32[3,7,3,256]{3,2,1,0:T(4,128)S(1)}, u32[]{:S(2)}, u32[]{:S(2)}) collective-permute-start(f32[3,7,3,256]{3,2,1,0:T(4,128)S(1)} %pad_maximum_fusion.5), channel_id=1, source_target_pairs={{0,3},{1,0},{2,1},{3,2},{4,7},{5,4},{6,5},{7,6},{8,11},{9,8},{10,9... | collective-permute-start | bytes 193544 | tf_op jit(solution)/shard_map/ppermute | solution.py:23
  40.0 7.9 %local_pass.3 = (f32[9,8,32,128]{3,2,1,0:T(8,128)S(1)}, f32[3,9,8,32,128]{4,3,2,1,0:T(8,128)S(1)}) custom-call(f32[3,16,64,256]{3,2,1,0:T(8,128)S(1)} %copy-done, f32[3,16,4,256]{3,2,1,0:T(4,128)S(1)} %collective-permute-done.2.before_ref, f32[3,16,3,256]{3,2,1,0:T(4,128)S(1)} %collective-permute-done.3.after_ref, f32[256,256]{1,0:T(8,128)S(1)} %copy-done.1), custom_call_target="tpu_custom_call" | custom-call | flops 603979776 | bytes 7077888 | tf_op jit(solution)/shard_map/local_pass/pallas_call | solution.py:162
  47.9 0.0 collective-permute-done.7.refs_8_.refs_9_
  48.0 0.0 collective-permute-done.5.refs_6_.refs_7_
  48.0 0.0 collective-permute-done.4.refs_4_.refs_5_
  48.0 4.8 %approx_pass.1 = (f32[9,8,32,128]{3,2,1,0:T(8,128)S(1)}, f32[9,8,32,128]{3,2,1,0:T(8,128)S(1)}, f32[6,8,32,128]{3,2,1,0:T(8,128)}, f32[9,2,32,128]{3,2,1,0:T(8,1...) custom-call(f32[9,8,32,128]{3,2,1,0:T(8,128)S(1)} %get-tuple-element, ...), custom_call_target="tpu_custom_call" | custom-call | tf_op jit(solution)/shard_map/approx_pass/pallas_call | solution.py:306
  52.8 4.7 %collective-permute-start.11 = (f32[9,2,4,128]{3,2,1,0:T(4,128)S(1)}, f32[9,2,4,128]{3,2,1,0:T(4,128)S(1)}, u32[]{:S(2)}, u32[]{:S(2)}) collective-permute-start(f32[9,2,4,128]{3,2,1,0:T(4,128)S(1)} %get-tuple-element.53), channel_id=1, source_target_pairs={{0,28},{4,0},{8,4},{12,8},{16,12},{20,16},{24,20},{28,24},{1,29},{... | collective-permute-start | bytes 110600 | tf_op jit(solution)/shard_map/ppermute | solution.py:23
  57.5 4.7 %collective-permute-start.9 = (f32[9,2,32,128]{3,2,1,0:T(8,128)S(1)}, f32[9,2,32,128]{3,2,1,0:T(8,128)S(1)}, u32[]{:S(2)}, u32[]{:S(2)}) collective-permute-start(f32[9,2,32,128]{3,2,1,0:T(8,128)S(1)} %get-tuple-element.50), channel_id=1, source_target_pairs={{0,28},{4,0},{8,4},{12,8},{16,12},{20,16},{24,20},{28,24},{1,29},{... | collective-permute-start | bytes 884744 | tf_op jit(solution)/shard_map/ppermute | solution.py:23
  62.2 0.0 collective-permute-done.10
  62.3 0.1 pad_maximum_fusion.2
  62.4 0.1 collective-permute-start.12
  62.4 0.1 pad_maximum_fusion.3
  62.5 1.8 %collective-permute-start.13 = (f32[9,12,2,128]{3,2,1,0:T(2,128)S(1)}, f32[9,12,2,128]{3,2,1,0:T(2,128)S(1)}, u32[]{:S(2)}, u32[]{:S(2)}) collective-permute-start(f32[9,12,2,128]{3,2,1,0:T(2,128)S(1)} %pad_maximum_fusion.3), channel_id=1, source_target_pairs={{0,3},{1,0},{2,1},{3,2},{4,7},{5,4},{6,5},{7,6},{8,11},{9,8},{10,9... | collective-permute-start | bytes 331784 | tf_op jit(solution)/shard_map/ppermute | solution.py:23
  64.3 7.5 %detail_pass.1 = f32[7,9,8,32,128]{4,3,2,1,0:T(8,128)} custom-call(f32[3,9,8,32,128]{4,3,2,1,0:T(8,128)S(1)} %get-tuple-element.43.refs_0_, f32[3,9,8,32,128]{4,3,2,1,0:T(8,128)S(1)} %get-tuple-element.44.refs_1_, f32[9,8,32,128]{3,2,1,0:T(8,128)S(1)} %get-tuple-element.45.refs_2_, f32[256,256]{1,0:T(8,128)S(1)} %copy-done.1, ...), custom_call_target="tpu_custom_call" | custom-call | flops 235929600 | bytes 18874368 | tf_op jit(solution)/shard_map/detail_pass/pallas_call | solution.py:372
  71.7 0.4 collective-permute-done.9.refs_2_
  72.1 2.4 %shard_map.108 = (f32[9,4,16,64]{3,2,1,0:T(8,128)S(1)}, f32[6,4,16,64]{3,2,1,0:T(8,128)}, f32[9,2,16,64]{3,2,1,0:T(8,128)S(1)}, f32[9,2,16,64]{3,2,1,0:T(8,128)S...) custom-call(f32[9,8,32,128]{3,2,1,0:T(8,128)S(1)} %get-tuple-element.48.refs_0_, ...), custom_call_target="tpu_custom_call" | custom-call | tf_op jit(solution)/shard_map/pallas_call | solution.py:486
  74.5 0.7 collective-permute-start.14
  75.2 4.0 %collective-permute-start.15 = (f32[9,2,16,64]{3,2,1,0:T(8,128)S(1)}, f32[9,2,16,64]{3,2,1,0:T(8,128)S(1)}, u32[]{:S(2)}, u32[]{:S(2)}) collective-permute-start(f32[9,2,16,64]{3,2,1,0:T(8,128)S(1)} %get-tuple-element.56), channel_id=1, source_target_pairs={{0,28},{4,0},{8,4},{12,8},{16,12},{20,16},{24,20},{28,24},{1,29},{... | collective-permute-start | bytes 221192 | tf_op jit(solution)/shard_map/ppermute | solution.py:23
  79.3 3.7 %shard_map.109 = f32[7,9,4,16,64]{4,3,2,1,0:T(8,128)} custom-call(f32[9,8,32,128]{3,2,1,0:T(8,128)S(1)} %get-tuple-element.48.refs_0_, f32[9,2,32,128]{3,2,1,0:T(8,128)S(1)} %collective-permute-done.8.refs_1_, f32[9,2,32,128]{3,2,1,0:T(8,128)S(1)} %collective-permute-done.9.refs_2_, f32[9,12,2,128]{3,2,1,0:T(2,128)S(1)} %collective-permute-done.12.refs_3_, ...), custom_call_target="tpu_custom_call" | custom-call | tf_op jit(solution)/shard_map/pallas_call | solution.py:486
  83.0 2.0 %collective-permute-done.15.refs_2_ = f32[9,2,16,64]{3,2,1,0:T(8,128)S(1)} collective-permute-done((f32[9,2,16,64]{3,2,1,0:T(8,128)S(1)}, f32[9,2,16,64]{3,2,1,0:T(8,128)S(1)}, u32[]{:S(2)}, u32[]{:S(2)}) %collective-permute-start.15) | collective-permute-done | bytes 73760 | tf_op jit(solution)/shard_map/ppermute | solution.py:23
  84.9 0.1 fusion.7
  85.0 0.1 fusion.1
  85.1 0.1 maximum_maximum_fusion
  85.2 0.1 collective-permute-start.16
  85.3 0.1 fusion.4
  85.3 0.1 maximum_maximum_fusion.1
  85.4 1.8 %collective-permute-start.17 = (f32[9,8,2,64]{3,2,1,0:T(2,128)S(1)}, f32[9,8,2,64]{3,2,1,0:T(2,128)S(1)}, u32[]{:S(2)}, u32[]{:S(2)}) collective-permute-start(f32[9,8,2,64]{3,2,1,0:T(2,128)S(1)} %maximum_maximum_fusion.1), channel_id=1, source_target_pairs={{0,3},{1,0},{2,1},{3,2},{4,7},{5,4},{6,5},{7,6},{8,11},{9,8},{10,9... | collective-permute-start | bytes 110600 | tf_op jit(solution)/shard_map/ppermute | solution.py:23
  87.2 2.2 %collective-permute-done.16.refs_3_ = f32[9,8,2,64]{3,2,1,0:T(2,128)S(1)} collective-permute-done((f32[9,8,2,64]{3,2,1,0:T(2,128)S(1)}, f32[9,8,2,64]{3,2,1,0:T(2,128)S(1)}, u32[]{:S(2)}, u32[]{:S(2)}) %collective-permute-start.16) | collective-permute-done | bytes 36896 | tf_op jit(solution)/shard_map/ppermute | solution.py:23
  89.4 1.9 %shard_map.110 = (f32[7,9,2,8,32]{4,3,2,1,0:T(8,128)}, f32[6,2,8,32]{3,2,1,0:T(8,128)}, f32[3,2,8,32]{3,2,1,0:T(8,128)}) custom-call(f32[9,4,16,64]{3,2,1,0:T(8,128)S(1)} %get-tuple-element.59.refs_0_, f32[9,2,16,64]{3,2,1,0:T(8,128)S(1)} %collective-permute-done.14.refs_1_, f32[9,2,16,64]{3,2,1,0:T(8,128)S(1)} %collective-permute-done.15.refs_2_, ...), custom_call_target="tpu_custom_call" | custom-call | tf_op jit(solution)/shard_map/pallas_call | solution.py:486
  (26 shorter events, 0.2 us)
Async XLA Ops:
  0.6 18.3 %copy-start.1 = (f32[256,256]{1,0:T(8,128)S(1)}, f32[256,256]{1,0:T(8,128)}, u32[]{:S(2)}) copy-start(f32[256,256]{1,0:T(8,128)} %constant.10.clone.table_ref.refs_2_.refs_3_) | copy-start | bytes 786436
  0.6 13.4 %copy-start = (f32[3,16,64,256]{3,2,1,0:T(8,128)S(1)}, f32[3,16,64,256]{3,2,1,0:T(8,128)}, u32[]{:S(2)}) copy-start(f32[3,16,64,256]{3,2,1,0:T(8,128)} %v_ref.3) | copy-start | bytes 9437188
  1.8 36.2 %collective-permute-start = (f32[3,4,16,256]{3,2,1,0:T(8,128)S(1)}, f32[3,4,16,256]{3,2,1,0:T(8,128)S(1)}, u32[]{:S(2)}, u32[]{:S(2)}) collective-permute-start(f32[3,4,16,256]{3,2,1,0:T(8,128)S(1)} %pad_maximum_fusion), channel_id=1, source_target_pairs={{0,4},{4,8},{8,12},{12,16},{16,20},{20,24},{24,28},{28,0},{1,5},{5... | collective-permute-start | bytes 589832 | tf_op jit(solution)/shard_map/ppermute | solution.py:23
  5.9 13.0 %collective-permute-start.2 = (f32[3,16,4,256]{3,2,1,0:T(4,128)S(1)}, f32[3,16,4,256]{3,2,1,0:T(4,128)S(1)}, u32[]{:S(2)}, u32[]{:S(2)}) collective-permute-start(f32[3,16,4,256]{3,2,1,0:T(4,128)S(1)} %slice.102), channel_id=1, source_target_pairs={{0,1},{1,2},{2,3},{3,0},{4,5},{5,6},{6,7},{7,4},{8,9},{9,10},{10,1... | collective-permute-start | bytes 589832 | tf_op jit(solution)/shard_map/ppermute | solution.py:23
  6.9 7.2 %collective-permute-start.3 = (f32[3,16,3,256]{3,2,1,0:T(4,128)S(1)}, f32[3,16,3,256]{3,2,1,0:T(4,128)S(1)}, u32[]{:S(2)}, u32[]{:S(2)}) collective-permute-start(f32[3,16,3,256]{3,2,1,0:T(4,128)S(1)} %slice.103), channel_id=1, source_target_pairs={{0,3},{1,0},{2,1},{3,2},{4,7},{5,4},{6,5},{7,6},{8,11},{9,8},{10,9... | collective-permute-start | bytes 442376 | tf_op jit(solution)/shard_map/ppermute | solution.py:23
  9.8 38.2 %collective-permute-start.5 = (f32[3,3,48,256]{3,2,1,0:T(8,128)S(1)}, f32[3,3,48,256]{3,2,1,0:T(8,128)S(1)}, u32[]{:S(2)}, u32[]{:S(2)}) collective-permute-start(f32[3,3,48,256]{3,2,1,0:T(8,128)S(1)} %slice.105), channel_id=1, source_target_pairs={{0,28},{4,0},{8,4},{12,8},{16,12},{20,16},{24,20},{28,24},{1,29},{... | collective-permute-start | bytes 1327112 | tf_op jit(solution)/shard_map/ppermute | solution.py:23
  14.0 34.0 %collective-permute-start.4 = (f32[3,4,48,256]{3,2,1,0:T(8,128)S(1)}, f32[3,4,48,256]{3,2,1,0:T(8,128)S(1)}, u32[]{:S(2)}, u32[]{:S(2)}) collective-permute-start(f32[3,4,48,256]{3,2,1,0:T(8,128)S(1)} %slice.104), channel_id=1, source_target_pairs={{0,4},{4,8},{8,12},{12,16},{16,20},{20,24},{24,28},{28,0},{1,5},{5... | collective-permute-start | bytes 1769480 | tf_op jit(solution)/shard_map/ppermute | solution.py:23
  14.1 23.9 %collective-permute-start.1 = (f32[3,3,16,256]{3,2,1,0:T(8,128)S(1)}, f32[3,3,16,256]{3,2,1,0:T(8,128)S(1)}, u32[]{:S(2)}, u32[]{:S(2)}) collective-permute-start(f32[3,3,16,256]{3,2,1,0:T(8,128)S(1)} %pad_maximum_fusion.1), channel_id=1, source_target_pairs={{0,28},{4,0},{8,4},{12,8},{16,12},{20,16},{24,20},{28,24},{1,29},{... | collective-permute-start | bytes 442376 | tf_op jit(solution)/shard_map/ppermute | solution.py:23
  38.1 9.8 %collective-permute-start.6 = (f32[3,7,4,256]{3,2,1,0:T(4,128)S(1)}, f32[3,7,4,256]{3,2,1,0:T(4,128)S(1)}, u32[]{:S(2)}, u32[]{:S(2)}) collective-permute-start(f32[3,7,4,256]{3,2,1,0:T(4,128)S(1)} %pad_maximum_fusion.4), channel_id=1, source_target_pairs={{0,1},{1,2},{2,3},{3,0},{4,5},{5,6},{6,7},{7,4},{8,9},{9,10},{10,1... | collective-permute-start | bytes 258056 | tf_op jit(solution)/shard_map/ppermute | solution.py:23
  38.2 9.7 %collective-permute-start.7 = (f32[3,7,3,256]{3,2,1,0:T(4,128)S(1)}, f32[3,7,3,256]{3,2,1,0:T(4,128)S(1)}, u32[]{:S(2)}, u32[]{:S(2)}) collective-permute-start(f32[3,7,3,256]{3,2,1,0:T(4,128)S(1)} %pad_maximum_fusion.5), channel_id=1, source_target_pairs={{0,3},{1,0},{2,1},{3,2},{4,7},{5,4},{6,5},{7,6},{8,11},{9,8},{10,9... | collective-permute-start | bytes 193544 | tf_op jit(solution)/shard_map/ppermute | solution.py:23
  52.8 9.4 %collective-permute-start.10 = (f32[9,2,4,128]{3,2,1,0:T(4,128)S(1)}, f32[9,2,4,128]{3,2,1,0:T(4,128)S(1)}, u32[]{:S(2)}, u32[]{:S(2)}) collective-permute-start(f32[9,2,4,128]{3,2,1,0:T(4,128)S(1)} %get-tuple-element.52), channel_id=1, source_target_pairs={{0,4},{4,8},{8,12},{12,16},{16,20},{20,24},{24,28},{28,0},{1,5},{5... | collective-permute-start | bytes 110600 | tf_op jit(solution)/shard_map/ppermute | solution.py:23
  52.8 9.5 %collective-permute-start.11 = (f32[9,2,4,128]{3,2,1,0:T(4,128)S(1)}, f32[9,2,4,128]{3,2,1,0:T(4,128)S(1)}, u32[]{:S(2)}, u32[]{:S(2)}) collective-permute-start(f32[9,2,4,128]{3,2,1,0:T(4,128)S(1)} %get-tuple-element.53), channel_id=1, source_target_pairs={{0,28},{4,0},{8,4},{12,8},{16,12},{20,16},{24,20},{28,24},{1,29},{... | collective-permute-start | bytes 110600 | tf_op jit(solution)/shard_map/ppermute | solution.py:23
  57.5 14.2 %collective-permute-start.8 = (f32[9,2,32,128]{3,2,1,0:T(8,128)S(1)}, f32[9,2,32,128]{3,2,1,0:T(8,128)S(1)}, u32[]{:S(2)}, u32[]{:S(2)}) collective-permute-start(f32[9,2,32,128]{3,2,1,0:T(8,128)S(1)} %get-tuple-element.49), channel_id=1, source_target_pairs={{0,4},{4,8},{8,12},{12,16},{16,20},{20,24},{24,28},{28,0},{1,5},{5... | collective-permute-start | bytes 884744 | tf_op jit(solution)/shard_map/ppermute | solution.py:23
  57.5 14.6 %collective-permute-start.9 = (f32[9,2,32,128]{3,2,1,0:T(8,128)S(1)}, f32[9,2,32,128]{3,2,1,0:T(8,128)S(1)}, u32[]{:S(2)}, u32[]{:S(2)}) collective-permute-start(f32[9,2,32,128]{3,2,1,0:T(8,128)S(1)} %get-tuple-element.50), channel_id=1, source_target_pairs={{0,28},{4,0},{8,4},{12,8},{16,12},{20,16},{24,20},{28,24},{1,29},{... | collective-permute-start | bytes 884744 | tf_op jit(solution)/shard_map/ppermute | solution.py:23
  62.4 9.4 %collective-permute-start.12 = (f32[9,12,2,128]{3,2,1,0:T(2,128)S(1)}, f32[9,12,2,128]{3,2,1,0:T(2,128)S(1)}, u32[]{:S(2)}, u32[]{:S(2)}) collective-permute-start(f32[9,12,2,128]{3,2,1,0:T(2,128)S(1)} %pad_maximum_fusion.2), channel_id=1, source_target_pairs={{0,1},{1,2},{2,3},{3,0},{4,5},{5,6},{6,7},{7,4},{8,9},{9,10},{10,1... | collective-permute-start | bytes 331784 | tf_op jit(solution)/shard_map/ppermute | solution.py:23
  62.5 9.3 %collective-permute-start.13 = (f32[9,12,2,128]{3,2,1,0:T(2,128)S(1)}, f32[9,12,2,128]{3,2,1,0:T(2,128)S(1)}, u32[]{:S(2)}, u32[]{:S(2)}) collective-permute-start(f32[9,12,2,128]{3,2,1,0:T(2,128)S(1)} %pad_maximum_fusion.3), channel_id=1, source_target_pairs={{0,3},{1,0},{2,1},{3,2},{4,7},{5,4},{6,5},{7,6},{8,11},{9,8},{10,9... | collective-permute-start | bytes 331784 | tf_op jit(solution)/shard_map/ppermute | solution.py:23
  64.3 7.8 %copy-start.2 = (f32[128,128]{1,0:T(8,128)S(1)}, f32[128,128]{1,0:T(8,128)}, u32[]{:S(2)}) copy-start(f32[128,128]{1,0:T(8,128)} %constant.11.clone.refs_5_) | copy-start | bytes 196612
  71.7 17.7 %copy-start.3 = (f32[128,128]{1,0:T(8,128)S(1)}, f32[128,128]{1,0:T(8,128)}, u32[]{:S(2)}) copy-start(f32[128,128]{1,0:T(8,128)} %constant.12.clone.refs_5_) | copy-start | bytes 196612
  74.5 8.4 %collective-permute-start.14 = (f32[9,2,16,64]{3,2,1,0:T(8,128)S(1)}, f32[9,2,16,64]{3,2,1,0:T(8,128)S(1)}, u32[]{:S(2)}, u32[]{:S(2)}) collective-permute-start(f32[9,2,16,64]{3,2,1,0:T(8,128)S(1)} %get-tuple-element.55), channel_id=1, source_target_pairs={{0,4},{4,8},{8,12},{12,16},{16,20},{20,24},{24,28},{28,0},{1,5},{5... | collective-permute-start | bytes 221192 | tf_op jit(solution)/shard_map/ppermute | solution.py:23
  75.2 9.7 %collective-permute-start.15 = (f32[9,2,16,64]{3,2,1,0:T(8,128)S(1)}, f32[9,2,16,64]{3,2,1,0:T(8,128)S(1)}, u32[]{:S(2)}, u32[]{:S(2)}) collective-permute-start(f32[9,2,16,64]{3,2,1,0:T(8,128)S(1)} %get-tuple-element.56), channel_id=1, source_target_pairs={{0,28},{4,0},{8,4},{12,8},{16,12},{20,16},{24,20},{28,24},{1,29},{... | collective-permute-start | bytes 221192 | tf_op jit(solution)/shard_map/ppermute | solution.py:23
  85.2 4.2 %collective-permute-start.16 = (f32[9,8,2,64]{3,2,1,0:T(2,128)S(1)}, f32[9,8,2,64]{3,2,1,0:T(2,128)S(1)}, u32[]{:S(2)}, u32[]{:S(2)}) collective-permute-start(f32[9,8,2,64]{3,2,1,0:T(2,128)S(1)} %maximum_maximum_fusion), channel_id=1, source_target_pairs={{0,1},{1,2},{2,3},{3,0},{4,5},{5,6},{6,7},{7,4},{8,9},{9,10},{10,1... | collective-permute-start | bytes 110600 | tf_op jit(solution)/shard_map/ppermute | solution.py:23
  85.4 4.0 %collective-permute-start.17 = (f32[9,8,2,64]{3,2,1,0:T(2,128)S(1)}, f32[9,8,2,64]{3,2,1,0:T(2,128)S(1)}, u32[]{:S(2)}, u32[]{:S(2)}) collective-permute-start(f32[9,8,2,64]{3,2,1,0:T(2,128)S(1)} %maximum_maximum_fusion.1), channel_id=1, source_target_pairs={{0,3},{1,0},{2,1},{3,2},{4,7},{5,4},{6,5},{7,6},{8,11},{9,8},{10,9... | collective-permute-start | bytes 110600 | tf_op jit(solution)/shard_map/ppermute | solution.py:23

commit v5 on v4

--- a/solution.py
+++ b/solution.py
@@ -43,7 +43,11 @@
 
 
 def dot(a, b):
-    return jnp.dot(a, b, precision=lax.Precision.HIGHEST, preferred_element_type=jnp.float32)
+    a_high, b_high = a.astype(jnp.bfloat16), b.astype(jnp.bfloat16)
+    a_low = (a - a_high.astype(jnp.float32)).astype(jnp.bfloat16)
+    b_low = (b - b_high.astype(jnp.float32)).astype(jnp.bfloat16)
+    part = lambda x, y: jnp.dot(x, y, preferred_element_type=jnp.float32)
+    return part(a_high, b_high) + (part(a_high, b_low) + part(a_low, b_high))
 
 
 def ring_lift(e, o):

time: 91.6 us -> 87.4 us (0.954); the launches traced: 91.3 us -> 86.1 us
  Pallas kernels: 36.1 us -> 27.9 us
  waiting for transfers between devices: 15.8 us -> 18.9 us
    pallas_call x2, Pallas kernels: 15.8 us -> 10.9 us  [local_pass(): pl.pallas_call(local_kernel, grid=(nx,), in_specs=[pl.BlockSpec((3, 1, ny...]
    ppermute x18, waiting for transfers between devices: 15.8 us -> 18.9 us  [shifted(): lax.ppermute(block, axis, [(i, (i + distance) % size) for i in range(size)])]
    pallas_call x3, Pallas kernels: 8 us -> 6.46 us  [level_call(): pl.pallas_call(kernel, in_specs=[vmem] * 6, out_specs=[vmem] * len(out),...]
    pallas_call x1, Pallas kernels: 7.46 us -> 6.39 us  [detail_pass(): pl.pallas_call(detail_kernel, grid=(9 // GROUP,), in_specs=[pl.BlockSpec(...]
  transfers between devices with their start and end apart: 18 -> 18, of which waited for: 4 -> 6; matrix products, arithmetic and copies ran while one was open for 5% -> 5% of each run, Pallas kernels for 30% -> 23%
where the time goes in v5:
time: 87.4 us; the launch traced here: 86.1 us
  starting transfers between devices  32.5 us (37%)
  Pallas kernels  27.9 us (32%)
  waiting for transfers between devices  18.9 us (22%)
  local copies, waits for them, and re-layouts  5.52 us (6%)
  between operations  0.93 us (1%)
    ppermute x18, starting transfers between devices, shifted(): lax.ppermute(block, axis, [(i, (i + distance) % size) for i in range(size)])  32.5 us
    ppermute x18, waiting for transfers between devices, shifted(): lax.ppermute(block, axis, [(i, (i + distance) % size) for i in range(size)])  18.9 us
    pallas_call x2, Pallas kernels, local_pass(): pl.pallas_call(local_kernel, grid=(nx,), in_specs=[pl.BlockSpec((3, 1, ny...  10.9 us
    pallas_call x3, Pallas kernels, level_call(): pl.pallas_call(kernel, in_specs=[vmem] * 6, out_specs=[vmem] * len(out),...  6.46 us
    pallas_call x1, Pallas kernels, detail_pass(): pl.pallas_call(detail_kernel, grid=(9 // GROUP,), in_specs=[pl.BlockSpec(...  6.39 us
    pallas_call x1, Pallas kernels, approx_pass(): pl.pallas_call(approx_kernel, grid=(9 // GROUP,), in_specs=[per_field((nx...  4.18 us
  transfers between devices with their start and end apart: 18, of which 6 were waited for; matrix products, arithmetic and copies ran while one was open for 5% of the time, Pallas kernels for 23%

profile of v5, /device:TPU:0, one launch (start us, length us, event | category | flops | bytes accessed | tf_op | source)
XLA Modules:
  0.0 86.1 jit_solution(3876537354870823452)
XLA Ops:
  0.6 0.0 copy-start.1
  0.6 0.0 copy-start
  0.7 1.1 %fusion.6 = (f32[3,4,8,256]{3,2,1,0:T(8,128)S(1)}, f32[3,4,8,256]{3,2,1,0:T(8,128)S(1)}) fusion(f32[3,16,64,256]{3,2,1,0:T(8,128)} %v_ref.3), kind=kLoop, calls=%fused_computation.19 | loop fusion | bytes 393216 | tf_op jit(solution)/shard_map/slice | solution.py:548
  1.8 3.0 %collective-permute-start = (f32[3,4,16,256]{3,2,1,0:T(8,128)S(1)}, f32[3,4,16,256]{3,2,1,0:T(8,128)S(1)}, u32[]{:S(2)}, u32[]{:S(2)}) collective-permute-start(f32[3,4,16,256]{3,2,1,0:T(8,128)S(1)} %pad_maximum_fusion), channel_id=1, source_target_pairs={{0,4},{4,8},{8,12},{12,16},{16,20},{20,24},{24,28},{28,0},{1,5},{5... | collective-permute-start | bytes 589832 | tf_op jit(solution)/shard_map/ppermute | solution.py:23
  4.8 1.0 %slice.102 = f32[3,16,4,256]{3,2,1,0:T(4,128)S(1)} slice(f32[3,16,64,256]{3,2,1,0:T(8,128)} %v_ref.3), slice={[0:3], [0:16], [60:64], [0:256]} | slice | bytes 393216 | tf_op jit(solution)/shard_map/slice | solution.py:553
  5.9 0.1 collective-permute-start.2
  5.9 1.0 %slice.103 = f32[3,16,3,256]{3,2,1,0:T(4,128)S(1)} slice(f32[3,16,64,256]{3,2,1,0:T(8,128)} %v_ref.3), slice={[0:3], [0:16], [0:3], [0:256]} | slice | bytes 294912 | tf_op jit(solution)/shard_map/slice | solution.py:554
  6.9 1.8 %collective-permute-start.3 = (f32[3,16,3,256]{3,2,1,0:T(4,128)S(1)}, f32[3,16,3,256]{3,2,1,0:T(4,128)S(1)}, u32[]{:S(2)}, u32[]{:S(2)}) collective-permute-start(f32[3,16,3,256]{3,2,1,0:T(4,128)S(1)} %slice.103), channel_id=1, source_target_pairs={{0,3},{1,0},{2,1},{3,2},{4,7},{5,4},{6,5},{7,6},{8,11},{9,8},{10,9... | collective-permute-start | bytes 442376 | tf_op jit(solution)/shard_map/ppermute | solution.py:23
  8.7 1.0 %slice.105 = f32[3,3,48,256]{3,2,1,0:T(8,128)S(1)} slice(f32[3,16,64,256]{3,2,1,0:T(8,128)} %v_ref.3), slice={[0:3], [0:3], [8:56], [0:256]} | slice | bytes 884736 | tf_op jit(solution)/shard_map/slice | solution.py:552
  9.8 3.1 %collective-permute-start.5 = (f32[3,3,48,256]{3,2,1,0:T(8,128)S(1)}, f32[3,3,48,256]{3,2,1,0:T(8,128)S(1)}, u32[]{:S(2)}, u32[]{:S(2)}) collective-permute-start(f32[3,3,48,256]{3,2,1,0:T(8,128)S(1)} %slice.105), channel_id=1, source_target_pairs={{0,28},{4,0},{8,4},{12,8},{16,12},{20,16},{24,20},{28,24},{1,29},{... | collective-permute-start | bytes 1327112 | tf_op jit(solution)/shard_map/ppermute | solution.py:23
  12.9 1.1 %slice.104 = f32[3,4,48,256]{3,2,1,0:T(8,128)S(1)} slice(f32[3,16,64,256]{3,2,1,0:T(8,128)} %v_ref.3), slice={[0:3], [12:16], [8:56], [0:256]} | slice | bytes 1179648 | tf_op jit(solution)/shard_map/slice | solution.py:551
  14.0 0.1 collective-permute-start.4
  14.1 4.7 %collective-permute-start.1 = (f32[3,3,16,256]{3,2,1,0:T(8,128)S(1)}, f32[3,3,16,256]{3,2,1,0:T(8,128)S(1)}, u32[]{:S(2)}, u32[]{:S(2)}) collective-permute-start(f32[3,3,16,256]{3,2,1,0:T(8,128)S(1)} %pad_maximum_fusion.1), channel_id=1, source_target_pairs={{0,28},{4,0},{8,4},{12,8},{16,12},{20,16},{24,20},{28,24},{1,29},{... | collective-permute-start | bytes 442376 | tf_op jit(solution)/shard_map/ppermute | solution.py:23
  18.9 5.4 %local_pass.2 = (f32[9,8,32,128]{3,2,1,0:T(8,128)S(1)}, f32[3,9,8,32,128]{4,3,2,1,0:T(8,128)S(1)}) custom-call(f32[3,16,64,256]{3,2,1,0:T(8,128)S(1)} %copy-done, f32[3,16,4,256]{3,2,1,0:T(4,128)S(1)} %collective-permute-done.2.before_ref, f32[3,16,3,256]{3,2,1,0:T(4,128)S(1)} %collective-permute-done.3.after_ref, f32[256,256]{1,0:T(8,128)S(1)} %copy-done.1), custom_call_target="tpu_custom_call" | custom-call | flops 603979776 | bytes 7077888 | tf_op jit(solution)/shard_map/local_pass/pallas_call | solution.py:166
  24.3 13.7 %collective-permute-done.1.refs_5_.refs_6_ = f32[3,3,16,256]{3,2,1,0:T(8,128)S(1)} collective-permute-done((f32[3,3,16,256]{3,2,1,0:T(8,128)S(1)}, f32[3,3,16,256]{3,2,1,0:T(8,128)S(1)}, u32[]{:S(2)}, u32[]{:S(2)}) %collective-permute-start.1) | collective-permute-done | bytes 147488 | tf_op jit(solution)/shard_map/ppermute | solution.py:23
  38.0 0.0 collective-permute-done.refs_3_.refs_4_
  38.1 0.1 collective-permute-start.6
  38.2 1.8 %collective-permute-start.7 = (f32[3,7,3,256]{3,2,1,0:T(4,128)S(1)}, f32[3,7,3,256]{3,2,1,0:T(4,128)S(1)}, u32[]{:S(2)}, u32[]{:S(2)}) collective-permute-start(f32[3,7,3,256]{3,2,1,0:T(4,128)S(1)} %pad_maximum_fusion.5), channel_id=1, source_target_pairs={{0,3},{1,0},{2,1},{3,2},{4,7},{5,4},{6,5},{7,6},{8,11},{9,8},{10,9... | collective-permute-start | bytes 193544 | tf_op jit(solution)/shard_map/ppermute | solution.py:23
  40.0 5.4 %local_pass.3 = (f32[9,8,32,128]{3,2,1,0:T(8,128)S(1)}, f32[3,9,8,32,128]{4,3,2,1,0:T(8,128)S(1)}) custom-call(f32[3,16,64,256]{3,2,1,0:T(8,128)S(1)} %copy-done, f32[3,16,4,256]{3,2,1,0:T(4,128)S(1)} %collective-permute-done.2.before_ref, f32[3,16,3,256]{3,2,1,0:T(4,128)S(1)} %collective-permute-done.3.after_ref, f32[256,256]{1,0:T(8,128)S(1)} %copy-done.1), custom_call_target="tpu_custom_call" | custom-call | flops 603979776 | bytes 7077888 | tf_op jit(solution)/shard_map/local_pass/pallas_call | solution.py:166
  45.5 0.0 collective-permute-done.7.refs_8_.refs_9_
  45.5 0.0 collective-permute-done.6.refs_7_.refs_8_
  45.5 0.0 collective-permute-done.4.refs_4_.refs_5_
  45.5 4.2 %approx_pass.1 = (f32[9,8,32,128]{3,2,1,0:T(8,128)S(1)}, f32[9,8,32,128]{3,2,1,0:T(8,128)S(1)}, f32[6,8,32,128]{3,2,1,0:T(8,128)}, f32[9,2,32,128]{3,2,1,0:T(8,1...) custom-call(f32[9,8,32,128]{3,2,1,0:T(8,128)S(1)} %get-tuple-element, ...), custom_call_target="tpu_custom_call" | custom-call | tf_op jit(solution)/shard_map/approx_pass/pallas_call | solution.py:310
  49.7 0.0 collective-permute-start.10
  49.7 4.7 %collective-permute-start.11 = (f32[9,2,4,128]{3,2,1,0:T(4,128)S(1)}, f32[9,2,4,128]{3,2,1,0:T(4,128)S(1)}, u32[]{:S(2)}, u32[]{:S(2)}) collective-permute-start(f32[9,2,4,128]{3,2,1,0:T(4,128)S(1)} %get-tuple-element.53), channel_id=1, source_target_pairs={{0,28},{4,0},{8,4},{12,8},{16,12},{20,16},{24,20},{28,24},{1,29},{... | collective-permute-start | bytes 110600 | tf_op jit(solution)/shard_map/ppermute | solution.py:23
  54.4 4.7 %collective-permute-start.9 = (f32[9,2,32,128]{3,2,1,0:T(8,128)S(1)}, f32[9,2,32,128]{3,2,1,0:T(8,128)S(1)}, u32[]{:S(2)}, u32[]{:S(2)}) collective-permute-start(f32[9,2,32,128]{3,2,1,0:T(8,128)S(1)} %get-tuple-element.50), channel_id=1, source_target_pairs={{0,28},{4,0},{8,4},{12,8},{16,12},{20,16},{24,20},{28,24},{1,29},{... | collective-permute-start | bytes 884744 | tf_op jit(solution)/shard_map/ppermute | solution.py:23
  59.2 0.1 pad_maximum_fusion.2
  59.2 0.1 collective-permute-start.12
  59.3 0.1 pad_maximum_fusion.3
  59.4 1.8 %collective-permute-start.13 = (f32[9,12,2,128]{3,2,1,0:T(2,128)S(1)}, f32[9,12,2,128]{3,2,1,0:T(2,128)S(1)}, u32[]{:S(2)}, u32[]{:S(2)}) collective-permute-start(f32[9,12,2,128]{3,2,1,0:T(2,128)S(1)} %pad_maximum_fusion.3), channel_id=1, source_target_pairs={{0,3},{1,0},{2,1},{3,2},{4,7},{5,4},{6,5},{7,6},{8,11},{9,8},{10,9... | collective-permute-start | bytes 331784 | tf_op jit(solution)/shard_map/ppermute | solution.py:23
  61.1 6.4 %detail_pass.1 = f32[7,9,8,32,128]{4,3,2,1,0:T(8,128)} custom-call(f32[3,9,8,32,128]{4,3,2,1,0:T(8,128)S(1)} %get-tuple-element.43.refs_0_, f32[3,9,8,32,128]{4,3,2,1,0:T(8,128)S(1)} %get-tuple-element.44.refs_1_, f32[9,8,32,128]{3,2,1,0:T(8,128)S(1)} %get-tuple-element.45.refs_2_, f32[256,256]{1,0:T(8,128)S(1)} %copy-done.1, ...), custom_call_target="tpu_custom_call" | custom-call | flops 235929600 | bytes 18874368 | tf_op jit(solution)/shard_map/detail_pass/pallas_call | solution.py:376
  67.6 1.4 %collective-permute-done.9.refs_2_ = f32[9,2,32,128]{3,2,1,0:T(8,128)S(1)} collective-permute-done((f32[9,2,32,128]{3,2,1,0:T(8,128)S(1)}, f32[9,2,32,128]{3,2,1,0:T(8,128)S(1)}, u32[]{:S(2)}, u32[]{:S(2)}) %collective-permute-start.9) | collective-permute-done | bytes 294944 | tf_op jit(solution)/shard_map/ppermute | solution.py:23
  69.0 2.0 %shard_map.108 = (f32[9,4,16,64]{3,2,1,0:T(8,128)S(1)}, f32[6,4,16,64]{3,2,1,0:T(8,128)}, f32[9,2,16,64]{3,2,1,0:T(8,128)S(1)}, f32[9,2,16,64]{3,2,1,0:T(8,128)S...) custom-call(f32[9,8,32,128]{3,2,1,0:T(8,128)S(1)} %get-tuple-element.48.refs_0_, ...), custom_call_target="tpu_custom_call" | custom-call | tf_op jit(solution)/shard_map/pallas_call | solution.py:490
  71.0 0.7 collective-permute-start.14
  71.7 4.0 %collective-permute-start.15 = (f32[9,2,16,64]{3,2,1,0:T(8,128)S(1)}, f32[9,2,16,64]{3,2,1,0:T(8,128)S(1)}, u32[]{:S(2)}, u32[]{:S(2)}) collective-permute-start(f32[9,2,16,64]{3,2,1,0:T(8,128)S(1)} %get-tuple-element.56), channel_id=1, source_target_pairs={{0,28},{4,0},{8,4},{12,8},{16,12},{20,16},{24,20},{28,24},{1,29},{... | collective-permute-start | bytes 221192 | tf_op jit(solution)/shard_map/ppermute | solution.py:23
  75.7 2.9 %shard_map.109 = f32[7,9,4,16,64]{4,3,2,1,0:T(8,128)} custom-call(f32[9,8,32,128]{3,2,1,0:T(8,128)S(1)} %get-tuple-element.48.refs_0_, f32[9,2,32,128]{3,2,1,0:T(8,128)S(1)} %collective-permute-done.8.refs_1_, f32[9,2,32,128]{3,2,1,0:T(8,128)S(1)} %collective-permute-done.9.refs_2_, f32[9,12,2,128]{3,2,1,0:T(2,128)S(1)} %collective-permute-done.12.refs_3_, ...), custom_call_target="tpu_custom_call" | custom-call | tf_op jit(solution)/shard_map/pallas_call | solution.py:490
  78.6 0.3 collective-permute-done.14.refs_1_
  78.9 1.4 %collective-permute-done.15.refs_2_ = f32[9,2,16,64]{3,2,1,0:T(8,128)S(1)} collective-permute-done((f32[9,2,16,64]{3,2,1,0:T(8,128)S(1)}, f32[9,2,16,64]{3,2,1,0:T(8,128)S(1)}, u32[]{:S(2)}, u32[]{:S(2)}) %collective-permute-start.15) | collective-permute-done | bytes 73760 | tf_op jit(solution)/shard_map/ppermute | solution.py:23
  80.3 0.1 fusion.7
  80.4 0.1 fusion.1
  80.5 0.1 maximum_maximum_fusion
  80.6 0.1 collective-permute-start.16
  80.6 0.1 fusion.4
  80.7 0.1 maximum_maximum_fusion.1
  80.8 1.8 %collective-permute-start.17 = (f32[9,8,2,64]{3,2,1,0:T(2,128)S(1)}, f32[9,8,2,64]{3,2,1,0:T(2,128)S(1)}, u32[]{:S(2)}, u32[]{:S(2)}) collective-permute-start(f32[9,8,2,64]{3,2,1,0:T(2,128)S(1)} %maximum_maximum_fusion.1), channel_id=1, source_target_pairs={{0,3},{1,0},{2,1},{3,2},{4,7},{5,4},{6,5},{7,6},{8,11},{9,8},{10,9... | collective-permute-start | bytes 110600 | tf_op jit(solution)/shard_map/ppermute | solution.py:23
  82.6 1.8 %collective-permute-done.16.refs_3_ = f32[9,8,2,64]{3,2,1,0:T(2,128)S(1)} collective-permute-done((f32[9,8,2,64]{3,2,1,0:T(2,128)S(1)}, f32[9,8,2,64]{3,2,1,0:T(2,128)S(1)}, u32[]{:S(2)}, u32[]{:S(2)}) %collective-permute-start.16) | collective-permute-done | bytes 36896 | tf_op jit(solution)/shard_map/ppermute | solution.py:23
  84.4 0.1 collective-permute-done.17.refs_4_
  84.5 1.6 %shard_map.110 = (f32[7,9,2,8,32]{4,3,2,1,0:T(8,128)}, f32[6,2,8,32]{3,2,1,0:T(8,128)}, f32[3,2,8,32]{3,2,1,0:T(8,128)}) custom-call(f32[9,4,16,64]{3,2,1,0:T(8,128)S(1)} %get-tuple-element.59.refs_0_, f32[9,2,16,64]{3,2,1,0:T(8,128)S(1)} %collective-permute-done.14.refs_1_, f32[9,2,16,64]{3,2,1,0:T(8,128)S(1)} %collective-permute-done.15.refs_2_, ...), custom_call_target="tpu_custom_call" | custom-call | tf_op jit(solution)/shard_map/pallas_call | solution.py:490
  (26 shorter events, 0.2 us)
Async XLA Ops:
  0.6 18.3 %copy-start.1 = (f32[256,256]{1,0:T(8,128)S(1)}, f32[256,256]{1,0:T(8,128)}, u32[]{:S(2)}) copy-start(f32[256,256]{1,0:T(8,128)} %constant.10.clone.table_ref.refs_2_.refs_3_) | copy-start | bytes 786436
  0.6 13.4 %copy-start = (f32[3,16,64,256]{3,2,1,0:T(8,128)S(1)}, f32[3,16,64,256]{3,2,1,0:T(8,128)}, u32[]{:S(2)}) copy-start(f32[3,16,64,256]{3,2,1,0:T(8,128)} %v_ref.3) | copy-start | bytes 9437188
  1.8 36.2 %collective-permute-start = (f32[3,4,16,256]{3,2,1,0:T(8,128)S(1)}, f32[3,4,16,256]{3,2,1,0:T(8,128)S(1)}, u32[]{:S(2)}, u32[]{:S(2)}) collective-permute-start(f32[3,4,16,256]{3,2,1,0:T(8,128)S(1)} %pad_maximum_fusion), channel_id=1, source_target_pairs={{0,4},{4,8},{8,12},{12,16},{16,20},{20,24},{24,28},{28,0},{1,5},{5... | collective-permute-start | bytes 589832 | tf_op jit(solution)/shard_map/ppermute | solution.py:23
  5.9 13.0 %collective-permute-start.2 = (f32[3,16,4,256]{3,2,1,0:T(4,128)S(1)}, f32[3,16,4,256]{3,2,1,0:T(4,128)S(1)}, u32[]{:S(2)}, u32[]{:S(2)}) collective-permute-start(f32[3,16,4,256]{3,2,1,0:T(4,128)S(1)} %slice.102), channel_id=1, source_target_pairs={{0,1},{1,2},{2,3},{3,0},{4,5},{5,6},{6,7},{7,4},{8,9},{9,10},{10,1... | collective-permute-start | bytes 589832 | tf_op jit(solution)/shard_map/ppermute | solution.py:23
  6.9 7.2 %collective-permute-start.3 = (f32[3,16,3,256]{3,2,1,0:T(4,128)S(1)}, f32[3,16,3,256]{3,2,1,0:T(4,128)S(1)}, u32[]{:S(2)}, u32[]{:S(2)}) collective-permute-start(f32[3,16,3,256]{3,2,1,0:T(4,128)S(1)} %slice.103), channel_id=1, source_target_pairs={{0,3},{1,0},{2,1},{3,2},{4,7},{5,4},{6,5},{7,6},{8,11},{9,8},{10,9... | collective-permute-start | bytes 442376 | tf_op jit(solution)/shard_map/ppermute | solution.py:23
  9.8 35.7 %collective-permute-start.5 = (f32[3,3,48,256]{3,2,1,0:T(8,128)S(1)}, f32[3,3,48,256]{3,2,1,0:T(8,128)S(1)}, u32[]{:S(2)}, u32[]{:S(2)}) collective-permute-start(f32[3,3,48,256]{3,2,1,0:T(8,128)S(1)} %slice.105), channel_id=1, source_target_pairs={{0,28},{4,0},{8,4},{12,8},{16,12},{20,16},{24,20},{28,24},{1,29},{... | collective-permute-start | bytes 1327112 | tf_op jit(solution)/shard_map/ppermute | solution.py:23
  14.0 31.5 %collective-permute-start.4 = (f32[3,4,48,256]{3,2,1,0:T(8,128)S(1)}, f32[3,4,48,256]{3,2,1,0:T(8,128)S(1)}, u32[]{:S(2)}, u32[]{:S(2)}) collective-permute-start(f32[3,4,48,256]{3,2,1,0:T(8,128)S(1)} %slice.104), channel_id=1, source_target_pairs={{0,4},{4,8},{8,12},{12,16},{16,20},{20,24},{24,28},{28,0},{1,5},{5... | collective-permute-start | bytes 1769480 | tf_op jit(solution)/shard_map/ppermute | solution.py:23
  14.1 23.9 %collective-permute-start.1 = (f32[3,3,16,256]{3,2,1,0:T(8,128)S(1)}, f32[3,3,16,256]{3,2,1,0:T(8,128)S(1)}, u32[]{:S(2)}, u32[]{:S(2)}) collective-permute-start(f32[3,3,16,256]{3,2,1,0:T(8,128)S(1)} %pad_maximum_fusion.1), channel_id=1, source_target_pairs={{0,28},{4,0},{8,4},{12,8},{16,12},{20,16},{24,20},{28,24},{1,29},{... | collective-permute-start | bytes 442376 | tf_op jit(solution)/shard_map/ppermute | solution.py:23
  38.1 7.3 %collective-permute-start.6 = (f32[3,7,4,256]{3,2,1,0:T(4,128)S(1)}, f32[3,7,4,256]{3,2,1,0:T(4,128)S(1)}, u32[]{:S(2)}, u32[]{:S(2)}) collective-permute-start(f32[3,7,4,256]{3,2,1,0:T(4,128)S(1)} %pad_maximum_fusion.4), channel_id=1, source_target_pairs={{0,1},{1,2},{2,3},{3,0},{4,5},{5,6},{6,7},{7,4},{8,9},{9,10},{10,1... | collective-permute-start | bytes 258056 | tf_op jit(solution)/shard_map/ppermute | solution.py:23
  38.2 7.2 %collective-permute-start.7 = (f32[3,7,3,256]{3,2,1,0:T(4,128)S(1)}, f32[3,7,3,256]{3,2,1,0:T(4,128)S(1)}, u32[]{:S(2)}, u32[]{:S(2)}) collective-permute-start(f32[3,7,3,256]{3,2,1,0:T(4,128)S(1)} %pad_maximum_fusion.5), channel_id=1, source_target_pairs={{0,3},{1,0},{2,1},{3,2},{4,7},{5,4},{6,5},{7,6},{8,11},{9,8},{10,9... | collective-permute-start | bytes 193544 | tf_op jit(solution)/shard_map/ppermute | solution.py:23
  49.7 9.4 %collective-permute-start.10 = (f32[9,2,4,128]{3,2,1,0:T(4,128)S(1)}, f32[9,2,4,128]{3,2,1,0:T(4,128)S(1)}, u32[]{:S(2)}, u32[]{:S(2)}) collective-permute-start(f32[9,2,4,128]{3,2,1,0:T(4,128)S(1)} %get-tuple-element.52), channel_id=1, source_target_pairs={{0,4},{4,8},{8,12},{12,16},{16,20},{20,24},{24,28},{28,0},{1,5},{5... | collective-permute-start | bytes 110600 | tf_op jit(solution)/shard_map/ppermute | solution.py:23
  49.7 9.5 %collective-permute-start.11 = (f32[9,2,4,128]{3,2,1,0:T(4,128)S(1)}, f32[9,2,4,128]{3,2,1,0:T(4,128)S(1)}, u32[]{:S(2)}, u32[]{:S(2)}) collective-permute-start(f32[9,2,4,128]{3,2,1,0:T(4,128)S(1)} %get-tuple-element.53), channel_id=1, source_target_pairs={{0,28},{4,0},{8,4},{12,8},{16,12},{20,16},{24,20},{28,24},{1,29},{... | collective-permute-start | bytes 110600 | tf_op jit(solution)/shard_map/ppermute | solution.py:23
  54.4 13.1 %collective-permute-start.8 = (f32[9,2,32,128]{3,2,1,0:T(8,128)S(1)}, f32[9,2,32,128]{3,2,1,0:T(8,128)S(1)}, u32[]{:S(2)}, u32[]{:S(2)}) collective-permute-start(f32[9,2,32,128]{3,2,1,0:T(8,128)S(1)} %get-tuple-element.49), channel_id=1, source_target_pairs={{0,4},{4,8},{8,12},{12,16},{16,20},{20,24},{24,28},{28,0},{1,5},{5... | collective-permute-start | bytes 884744 | tf_op jit(solution)/shard_map/ppermute | solution.py:23
  54.4 14.6 %collective-permute-start.9 = (f32[9,2,32,128]{3,2,1,0:T(8,128)S(1)}, f32[9,2,32,128]{3,2,1,0:T(8,128)S(1)}, u32[]{:S(2)}, u32[]{:S(2)}) collective-permute-start(f32[9,2,32,128]{3,2,1,0:T(8,128)S(1)} %get-tuple-element.50), channel_id=1, source_target_pairs={{0,28},{4,0},{8,4},{12,8},{16,12},{20,16},{24,20},{28,24},{1,29},{... | collective-permute-start | bytes 884744 | tf_op jit(solution)/shard_map/ppermute | solution.py:23
  59.2 8.3 %collective-permute-start.12 = (f32[9,12,2,128]{3,2,1,0:T(2,128)S(1)}, f32[9,12,2,128]{3,2,1,0:T(2,128)S(1)}, u32[]{:S(2)}, u32[]{:S(2)}) collective-permute-start(f32[9,12,2,128]{3,2,1,0:T(2,128)S(1)} %pad_maximum_fusion.2), channel_id=1, source_target_pairs={{0,1},{1,2},{2,3},{3,0},{4,5},{5,6},{6,7},{7,4},{8,9},{9,10},{10,1... | collective-permute-start | bytes 331784 | tf_op jit(solution)/shard_map/ppermute | solution.py:23
  59.4 8.2 %collective-permute-start.13 = (f32[9,12,2,128]{3,2,1,0:T(2,128)S(1)}, f32[9,12,2,128]{3,2,1,0:T(2,128)S(1)}, u32[]{:S(2)}, u32[]{:S(2)}) collective-permute-start(f32[9,12,2,128]{3,2,1,0:T(2,128)S(1)} %pad_maximum_fusion.3), channel_id=1, source_target_pairs={{0,3},{1,0},{2,1},{3,2},{4,7},{5,4},{6,5},{7,6},{8,11},{9,8},{10,9... | collective-permute-start | bytes 331784 | tf_op jit(solution)/shard_map/ppermute | solution.py:23
  61.1 7.9 %copy-start.2 = (f32[128,128]{1,0:T(8,128)S(1)}, f32[128,128]{1,0:T(8,128)}, u32[]{:S(2)}) copy-start(f32[128,128]{1,0:T(8,128)} %constant.11.clone.refs_5_) | copy-start | bytes 196612
  67.5 17.0 %copy-start.3 = (f32[128,128]{1,0:T(8,128)S(1)}, f32[128,128]{1,0:T(8,128)}, u32[]{:S(2)}) copy-start(f32[128,128]{1,0:T(8,128)} %constant.12.clone.refs_5_) | copy-start | bytes 196612
  71.0 7.9 %collective-permute-start.14 = (f32[9,2,16,64]{3,2,1,0:T(8,128)S(1)}, f32[9,2,16,64]{3,2,1,0:T(8,128)S(1)}, u32[]{:S(2)}, u32[]{:S(2)}) collective-permute-start(f32[9,2,16,64]{3,2,1,0:T(8,128)S(1)} %get-tuple-element.55), channel_id=1, source_target_pairs={{0,4},{4,8},{8,12},{12,16},{16,20},{20,24},{24,28},{28,0},{1,5},{5... | collective-permute-start | bytes 221192 | tf_op jit(solution)/shard_map/ppermute | solution.py:23
  71.7 8.6 %collective-permute-start.15 = (f32[9,2,16,64]{3,2,1,0:T(8,128)S(1)}, f32[9,2,16,64]{3,2,1,0:T(8,128)S(1)}, u32[]{:S(2)}, u32[]{:S(2)}) collective-permute-start(f32[9,2,16,64]{3,2,1,0:T(8,128)S(1)} %get-tuple-element.56), channel_id=1, source_target_pairs={{0,28},{4,0},{8,4},{12,8},{16,12},{20,16},{24,20},{28,24},{1,29},{... | collective-permute-start | bytes 221192 | tf_op jit(solution)/shard_map/ppermute | solution.py:23
  80.6 3.8 %collective-permute-start.16 = (f32[9,8,2,64]{3,2,1,0:T(2,128)S(1)}, f32[9,8,2,64]{3,2,1,0:T(2,128)S(1)}, u32[]{:S(2)}, u32[]{:S(2)}) collective-permute-start(f32[9,8,2,64]{3,2,1,0:T(2,128)S(1)} %maximum_maximum_fusion), channel_id=1, source_target_pairs={{0,1},{1,2},{2,3},{3,0},{4,5},{5,6},{6,7},{7,4},{8,9},{9,10},{10,1... | collective-permute-start | bytes 110600 | tf_op jit(solution)/shard_map/ppermute | solution.py:23
  80.8 3.8 %collective-permute-start.17 = (f32[9,8,2,64]{3,2,1,0:T(2,128)S(1)}, f32[9,8,2,64]{3,2,1,0:T(2,128)S(1)}, u32[]{:S(2)}, u32[]{:S(2)}) collective-permute-start(f32[9,8,2,64]{3,2,1,0:T(2,128)S(1)} %maximum_maximum_fusion.1), channel_id=1, source_target_pairs={{0,3},{1,0},{2,1},{3,2},{4,7},{5,4},{6,5},{7,6},{8,11},{9,8},{10,9... | collective-permute-start | bytes 110600 | tf_op jit(solution)/shard_map/ppermute | solution.py:23

commit v6 on v5

--- a/solution.py
+++ b/solution.py
@@ -21,6 +21,21 @@
 def shifted(block, axis, distance):
     size = lax.axis_size(axis)
     return lax.ppermute(block, axis, [(i, (i + distance) % size) for i in range(size)])
+
+
+def swapped(block, axis, odd):
+    size = lax.axis_size(axis)
+    route = []
+    for i in range(size):
+        route.append((i, (i + 1) % size if i % 2 == odd else (i - 1) % size))
+    return lax.ppermute(block, axis, route)
+
+
+def neighbours(to_next, to_prev, axis):
+    even = lax.axis_index(axis) % 2 == 0
+    near = swapped(jnp.where(even, to_next, to_prev), axis, 0)
+    far = swapped(jnp.where(even, to_prev, to_next), axis, 1)
+    return jnp.where(even, far, near), jnp.where(even, near, far)
 
 
 def third_table(length, lanes):
@@ -406,7 +421,10 @@
             else:
                 source, at = after_ref, layer - nx - 2
             if nz < wide:
-                pad_ref[f, layer, :, :nz] = source[f, at]
+                if layer < nx:
+                    pad_ref[f, layer, :, :nz] = source[f, at]
+                else:
+                    pad_ref[f, layer, :, :nz] = source[f, :, at * nz : (at + 1) * nz]
                 source, at = pad_ref, layer
             e = source[f, at, pl.ds(0, half, stride=2), :]
             o = source[f, at, pl.ds(1, half, stride=2), :]
@@ -444,7 +462,9 @@
                     i, j = product_pairs[f - 3]
                     stress_ref[f - 3, x, rows, :] = approx[x] - kept_ref[i, x, rows, :] * kept_ref[j, x, rows, :]
                 approx_ref[f, x, rows, :] = approx[x]
-            send_layers(approx, f, r, sends[0], sends[1])
+            for ref, parts in zip(sends, (parts_for_next(approx), parts_for_previous(approx))):
+                for part, value in enumerate(parts):
+                    ref[f, rows, part * lanes : (part + 1) * lanes] = value
         send_rows(approx_ref, f, sends[2], sends[3])
 
 
@@ -506,7 +526,7 @@
     _, nx, ny, nz = approx.shape
     mx, half, lanes = nx // 2, ny // 2, nz // 2
     f32 = lambda *shape: jax.ShapeDtypeStruct(shape, jnp.float32)
-    sends = ((2, half, lanes), (2, half, lanes), (mx, 2, lanes), (mx, 2, lanes))
+    sends = ((half, 2 * lanes), (half, 2 * lanes), (mx, 2, lanes), (mx, 2, lanes))
     out = [f32(9, mx, half, lanes), f32(6, mx, half, lanes)] + [f32(9, *s) for s in sends]
     return level_call(lambda *refs: level_approx_kernel(nz, *refs), approx, halo, out, half)
 
@@ -522,23 +542,26 @@
 
 
 def halo_rows(before, after, down, up):
-    rows = before.shape[2]
-    cell = lambda at: jnp.concatenate([before[:, :, at : at + 1], after[:, :, at : at + 1]], axis=1)
+    rows, lanes = before.shape[1], down.shape[3]
+
+    def cell(at):
+        both = [t[:, at].reshape(9, 2, 1, lanes) for t in (before, after)]
+        return jnp.concatenate(both, axis=1)
+
     p, q = parts_for_next([cell(rows - 4 + i) for i in range(4)])
     down = jnp.concatenate([down, jnp.concatenate([q, p], axis=2)], axis=1)
     head = jnp.concatenate(parts_for_previous([cell(i) for i in range(3)]), axis=2)
     up = jnp.concatenate([up, head], axis=1)
-    return shifted(down, "gy", 1), shifted(up, "gy", -1)
+    return neighbours(down, up, "gy")
 
 
 def exchange(to_next, to_prev, edge_next, edge_prev, down, up):
-    from_prev_edge = shifted(edge_next, "gx", 1)
-    from_next_edge = shifted(edge_prev, "gx", -1)
     before = shifted(to_next, "gx", 1)
     after = shifted(to_prev, "gx", -1)
-    down = jnp.concatenate([down, from_prev_edge[:, :, 0:2], from_next_edge[:, :, 0:2]], axis=1)
-    up = jnp.concatenate([up, from_prev_edge[:, :, 2:4], from_next_edge[:, :, 2:4]], axis=1)
-    return before, after, shifted(down, "gy", 1), shifted(up, "gy", -1)
+    from_prev, from_next = neighbours(edge_next, edge_prev, "gx")
+    down = jnp.concatenate([down, from_prev[:, :, 0:2], from_next[:, :, 0:2]], axis=1)
+    up = jnp.concatenate([up, from_prev[:, :, 2:4], from_next[:, :, 2:4]], axis=1)
+    return (before, after) + neighbours(down, up, "gy")
 
 
 def body(velocity):
@@ -566,8 +589,7 @@
     approx, details_one = lax.optimization_barrier((approx, details_one))
     second = approx
     approx, stress_two, *sends = level_approx(second, second_halo)
-    before = shifted(sends[0], "gx", 1)
-    after = shifted(sends[1], "gx", -1)
+    before, after = neighbours(sends[0], sends[1], "gx")
     (details_two,) = level_details(second, second_halo, False)
     before, after, details_two = lax.optimization_barrier((before, after, details_two))
     third_halo = (before, after) + halo_rows(before, after, *sends[2:])

time: 87.4 us -> 101 us (1.16)
  local copies, waits for them, and re-layouts: 5.52 us -> 19.3 us
  starting transfers between devices: 32.5 us -> 22.4 us
  waiting for transfers between devices: 18.9 us -> 25.3 us
  Pallas kernels: 27.9 us -> 30.3 us
  other arithmetic: 0.46 us -> 1.8 us
    ppermute x18 -> x10, starting transfers between devices: 32.5 us -> 16.5 us  [shifted(): lax.ppermute(block, axis, [(i, (i + distance) % size) for i in range(size)])]
    unnamed x8 -> x36, local copies, waits for them, and re-layouts: 0.02 us -> 11.1 us
    ppermute x0 -> x8, waiting for transfers between devices: none -> 9.85 us  [swapped(): return lax.ppermute(block, axis, route)]
    ppermute x0 -> x8, starting transfers between devices: none -> 5.93 us  [swapped(): return lax.ppermute(block, axis, route)]
    ppermute x18 -> x10, waiting for transfers between devices: 18.9 us -> 15.5 us  [shifted(): lax.ppermute(block, axis, [(i, (i + distance) % size) for i in range(size)])]
    pallas_call x1, Pallas kernels: 4.18 us -> 5.47 us  [approx_pass(): pl.pallas_call(approx_kernel, grid=(9 // GROUP,), in_specs=[per_field((nx...]
    pallas_call x1, Pallas kernels: 6.39 us -> 7.46 us  [detail_pass(): pl.pallas_call(detail_kernel, grid=(9 // GROUP,), in_specs=[pl.BlockSpec(...]
  transfers between devices with their start and end apart: 18 -> 18, of which waited for: 6 -> 4; matrix products, arithmetic and copies ran while one was open for 5% -> 7% of each run, Pallas kernels for 23% -> 21%
where the time goes in v6:
time: 101 us; the launch traced here: 100 us
  Pallas kernels  30.3 us (30%)
  waiting for transfers between devices  25.3 us (25%)
  starting transfers between devices  22.4 us (22%)
  local copies, waits for them, and re-layouts  19.3 us (19%)
  other arithmetic  1.8 us (2%)
    ppermute x10, starting transfers between devices, shifted(): lax.ppermute(block, axis, [(i, (i + distance) % size) for i in range(size)])  16.5 us
    ppermute x10, waiting for transfers between devices, shifted(): lax.ppermute(block, axis, [(i, (i + distance) % size) for i in range(size)])  15.5 us
    unnamed x36, local copies, waits for them, and re-layouts  11.1 us
    pallas_call x2, Pallas kernels, local_pass(): pl.pallas_call(local_kernel, grid=(nx,), in_specs=[pl.BlockSpec((3, 1, ny...  10.9 us
    ppermute x8, waiting for transfers between devices, swapped(): return lax.ppermute(block, axis, route)  9.85 us
    pallas_call x1, Pallas kernels, detail_pass(): pl.pallas_call(detail_kernel, grid=(9 // GROUP,), in_specs=[pl.BlockSpec(...  7.46 us
    pallas_call x3, Pallas kernels, level_call(): pl.pallas_call(kernel, in_specs=[vmem] * 6, out_specs=[vmem] * len(out),...  6.48 us
    ppermute x8, starting transfers between devices, swapped(): return lax.ppermute(block, axis, route)  5.93 us
  transfers between devices with their start and end apart: 18, of which 4 were waited for; matrix products, arithmetic and copies ran while one was open for 7% of the time, Pallas kernels for 21%

profile of v6, /device:TPU:0, one launch (start us, length us, event | category | flops | bytes accessed | tf_op | source)
XLA Modules:
  0.0 100.0 jit_solution(8224669519359709806)
XLA Ops:
  0.7 1.1 %fusion.5 = (f32[3,4,8,256]{3,2,1,0:T(8,128)S(1)}, f32[3,4,8,256]{3,2,1,0:T(8,128)S(1)}) fusion(f32[3,16,64,256]{3,2,1,0:T(8,128)} %v_ref.3), kind=kLoop, calls=%fused_computation.52 | loop fusion | bytes 393216 | tf_op jit(solution)/shard_map/slice | solution.py:571
  1.8 3.0 %collective-permute-start = (f32[3,4,16,256]{3,2,1,0:T(8,128)S(1)}, f32[3,4,16,256]{3,2,1,0:T(8,128)S(1)}, u32[]{:S(2)}, u32[]{:S(2)}) collective-permute-start(f32[3,4,16,256]{3,2,1,0:T(8,128)S(1)} %pad_maximum_fusion), channel_id=1, source_target_pairs={{0,4},{4,8},{8,12},{12,16},{16,20},{20,24},{24,28},{28,0},{1,5},{5... | collective-permute-start | bytes 589832 | tf_op jit(solution)/shard_map/ppermute | solution.py:23
  4.8 1.0 %slice.102 = f32[3,16,4,256]{3,2,1,0:T(4,128)S(1)} slice(f32[3,16,64,256]{3,2,1,0:T(8,128)} %v_ref.3), slice={[0:3], [0:16], [60:64], [0:256]} | slice | bytes 393216 | tf_op jit(solution)/shard_map/slice | solution.py:576
  5.9 1.0 %slice.103 = f32[3,16,3,256]{3,2,1,0:T(4,128)S(1)} slice(f32[3,16,64,256]{3,2,1,0:T(8,128)} %v_ref.3), slice={[0:3], [0:16], [0:3], [0:256]} | slice | bytes 294912 | tf_op jit(solution)/shard_map/slice | solution.py:577
  6.9 1.8 %collective-permute-start.3 = (f32[3,16,3,256]{3,2,1,0:T(4,128)S(1)}, f32[3,16,3,256]{3,2,1,0:T(4,128)S(1)}, u32[]{:S(2)}, u32[]{:S(2)}) collective-permute-start(f32[3,16,3,256]{3,2,1,0:T(4,128)S(1)} %slice.103), channel_id=1, source_target_pairs={{0,3},{1,0},{2,1},{3,2},{4,7},{5,4},{6,5},{7,6},{8,11},{9,8},{10,9... | collective-permute-start | bytes 442376 | tf_op jit(solution)/shard_map/ppermute | solution.py:23
  8.7 1.9 %slice.104 = f32[3,4,48,256]{3,2,1,0:T(8,128)} slice(f32[3,16,64,256]{3,2,1,0:T(8,128)} %v_ref.3), slice={[0:3], [12:16], [8:56], [0:256]} | slice | bytes 1179648 | tf_op jit(solution)/shard_map/slice | solution.py:574
  10.6 1.5 %collective-permute-start.4 = (f32[3,4,48,256]{3,2,1,0:T(8,128)}, f32[3,4,48,256]{3,2,1,0:T(8,128)}, u32[]{:S(2)}, u32[]{:S(2)}) collective-permute-start(f32[3,4,48,256]{3,2,1,0:T(8,128)} %slice.104), channel_id=1, source_target_pairs={{0,4},{4,8},{8,12},{12,16},{16,20},{20,24},{24,28},{28,0},{1,5},{5... | collective-permute-start | bytes 1769480 | tf_op jit(solution)/shard_map/ppermute | solution.py:23
  12.2 1.8 %slice.105 = f32[3,3,48,256]{3,2,1,0:T(8,128)} slice(f32[3,16,64,256]{3,2,1,0:T(8,128)} %v_ref.3), slice={[0:3], [0:3], [8:56], [0:256]} | slice | bytes 884736 | tf_op jit(solution)/shard_map/slice | solution.py:575
  14.0 3.2 %collective-permute-start.5 = (f32[3,3,48,256]{3,2,1,0:T(8,128)}, f32[3,3,48,256]{3,2,1,0:T(8,128)}, u32[]{:S(2)}, u32[]{:S(2)}) collective-permute-start(f32[3,3,48,256]{3,2,1,0:T(8,128)} %slice.105), channel_id=1, source_target_pairs={{0,28},{4,0},{8,4},{12,8},{16,12},{20,16},{24,20},{28,24},{1,29},{... | collective-permute-start | bytes 1327112 | tf_op jit(solution)/shard_map/ppermute | solution.py:23
  17.2 0.4 collective-permute-start.1
  17.7 5.4 %local_pass.2 = (f32[9,8,32,128]{3,2,1,0:T(8,128)S(1)}, f32[3,9,8,32,128]{4,3,2,1,0:T(8,128)S(1)}) custom-call(f32[3,16,64,256]{3,2,1,0:T(8,128)S(1)} %copy-done, f32[3,16,4,256]{3,2,1,0:T(4,128)S(1)} %collective-permute-done.2.before_ref, f32[3,16,3,256]{3,2,1,0:T(4,128)S(1)} %collective-permute-done.3.after_ref, f32[256,256]{1,0:T(8,128)S(1)} %copy-done.1), custom_call_target="tpu_custom_call" | custom-call | flops 603979776 | bytes 7077888 | tf_op jit(solution)/shard_map/local_pass/pallas_call | solution.py:181
  23.1 1.8 %copy-done.2 = f32[3,9,8,32,128]{4,3,2,1,0:T(8,128)} copy-done((f32[3,9,8,32,128]{4,3,2,1,0:T(8,128)}, f32[3,9,8,32,128]{4,3,2,1,0:T(8,128)S(1)}, u32[]{:S(2)}) %copy-start.2) | copy-done | bytes 3538968
  24.9 1.0 %copy-done.9 = f32[9,8,32,128]{3,2,1,0:T(8,128)} copy-done((f32[9,8,32,128]{3,2,1,0:T(8,128)}, f32[9,8,32,128]{3,2,1,0:T(8,128)S(1)}, u32[]{:S(2)}) %copy-start.9) | copy-done | bytes 1179672
  25.9 15.4 %collective-permute-done.1.refs_5_.refs_6_ = f32[3,3,16,256]{3,2,1,0:T(8,128)S(1)} collective-permute-done((f32[3,3,16,256]{3,2,1,0:T(8,128)S(1)}, f32[3,3,16,256]{3,2,1,0:T(8,128)S(1)}, u32[]{:S(2)}, u32[]{:S(2)}) %collective-permute-start.1) | collective-permute-done | bytes 147488 | tf_op jit(solution)/shard_map/ppermute | solution.py:23
  41.4 0.6 copy-done.6
  42.0 0.6 pad_maximum_fusion.4
  42.7 0.6 pad_maximum_fusion.5
  43.3 1.7 %collective-permute-start.7 = (f32[3,7,3,256]{3,2,1,0:T(4,128)}, f32[3,7,3,256]{3,2,1,0:T(4,128)}, u32[]{:S(2)}, u32[]{:S(2)}) collective-permute-start(f32[3,7,3,256]{3,2,1,0:T(4,128)} %pad_maximum_fusion.5), channel_id=1, source_target_pairs={{0,3},{1,0},{2,1},{3,2},{4,7},{5,4},{6,5},{7,6},{8,11},{9,8},{10,9... | collective-permute-start | bytes 193544 | tf_op jit(solution)/shard_map/ppermute | solution.py:23
  45.1 0.9 copy-done.12
  46.0 0.9 copy-done.14
  46.9 5.4 %local_pass.3 = (f32[9,8,32,128]{3,2,1,0:T(8,128)S(1)}, f32[3,9,8,32,128]{4,3,2,1,0:T(8,128)S(1)}) custom-call(f32[3,16,64,256]{3,2,1,0:T(8,128)S(1)} %copy-done, f32[3,16,4,256]{3,2,1,0:T(4,128)S(1)} %copy-done.12, f32[3,16,3,256]{3,2,1,0:T(4,128)S(1)} %copy-done.14, f32[256,256]{1,0:T(8,128)S(1)} %copy-done.1), custom_call_target="tpu_custom_call" | custom-call | flops 603979776 | bytes 7077888 | tf_op jit(solution)/shard_map/local_pass/pallas_call | solution.py:181
  52.4 1.7 %copy-done.4 = f32[3,9,8,32,128]{4,3,2,1,0:T(8,128)} copy-done((f32[3,9,8,32,128]{4,3,2,1,0:T(8,128)}, f32[3,9,8,32,128]{4,3,2,1,0:T(8,128)S(1)}, u32[]{:S(2)}) %copy-start.4) | copy-done | bytes 3538968
  54.2 5.5 %approx_pass.1 = (f32[9,8,32,128]{3,2,1,0:T(8,128)S(1)}, f32[9,8,32,128]{3,2,1,0:T(8,128)S(1)}, f32[6,8,32,128]{3,2,1,0:T(8,128)}, f32[9,2,32,128]{3,2,1,0:T(8,1...) custom-call(f32[9,8,32,128]{3,2,1,0:T(8,128)S(1)} %copy-done.10, ...), custom_call_target="tpu_custom_call" | custom-call | tf_op jit(solution)/shard_map/approx_pass/pallas_call | solution.py:325
  59.7 0.9 collective-permute-start.10
  60.5 0.5 collective-permute-start.11
  61.0 5.4 %collective-permute-done.10 = f32[9,2,4,128]{3,2,1,0:T(4,128)S(1)} collective-permute-done((f32[9,2,4,128]{3,2,1,0:T(4,128)S(1)}, f32[9,2,4,128]{3,2,1,0:T(4,128)S(1)}, u32[]{:S(2)}, u32[]{:S(2)}) %collective-permute-start.10) | collective-permute-done | bytes 36896 | tf_op jit(solution)/shard_map/ppermute | solution.py:31
  66.4 0.1 broadcast_select_fusion.2
  66.6 0.6 collective-permute-start.12
  67.2 4.7 %collective-permute-start.9 = (f32[9,2,32,128]{3,2,1,0:T(8,128)}, f32[9,2,32,128]{3,2,1,0:T(8,128)S(1)}, u32[]{:S(2)}, u32[]{:S(2)}) collective-permute-start(f32[9,2,32,128]{3,2,1,0:T(8,128)} %get-tuple-element.50), channel_id=1, source_target_pairs={{0,28},{4,0},{8,4},{12,8},{16,12},{20,16},{24,20},{28,24},{1,29},{... | collective-permute-start | bytes 884744 | tf_op jit(solution)/shard_map/ppermute | solution.py:23
  72.0 2.0 %copy-done.3 = f32[3,9,8,32,128]{4,3,2,1,0:T(8,128)S(1)} copy-done((f32[3,9,8,32,128]{4,3,2,1,0:T(8,128)S(1)}, f32[3,9,8,32,128]{4,3,2,1,0:T(8,128)}, u32[]{:S(2)}) %copy-start.3) | copy-done | bytes 3538968
  74.0 2.0 %copy-done.5 = f32[3,9,8,32,128]{4,3,2,1,0:T(8,128)S(1)} copy-done((f32[3,9,8,32,128]{4,3,2,1,0:T(8,128)S(1)}, f32[3,9,8,32,128]{4,3,2,1,0:T(8,128)}, u32[]{:S(2)}) %copy-start.5) | copy-done | bytes 3538968
  76.0 7.5 %detail_pass.1 = f32[7,9,8,32,128]{4,3,2,1,0:T(8,128)} custom-call(f32[3,9,8,32,128]{4,3,2,1,0:T(8,128)S(1)} %copy-done.3, f32[3,9,8,32,128]{4,3,2,1,0:T(8,128)S(1)} %copy-done.5, f32[9,8,32,128]{3,2,1,0:T(8,128)S(1)} %get-tuple-element.45.refs_2_, f32[256,256]{1,0:T(8,128)S(1)} %copy-done.1, f32[3,4,16,256]{3,2,1,0:T(8,128)S(1)} %copy-done.8, ...), custom_call_target="tpu_custom_call" | custom-call | flops 235929600 | bytes 18874368 | tf_op jit(solution)/shard_map/detail_pass/pallas_call | solution.py:391
  83.5 2.0 %shard_map.108 = (f32[9,4,16,64]{3,2,1,0:T(8,128)S(1)}, f32[6,4,16,64]{3,2,1,0:T(8,128)}, f32[9,16,128]{2,1,0:T(8,128)S(1)}, f32[9,16,128]{2,1,0:T(8,128)S(1)}, ...) custom-call(f32[9,8,32,128]{3,2,1,0:T(8,128)S(1)} %get-tuple-element.48.refs_0_, ...), custom_call_target="tpu_custom_call" | custom-call | tf_op jit(solution)/shard_map/pallas_call | solution.py:510
  85.6 2.2 %collective-permute-start.14 = (f32[9,16,128]{2,1,0:T(8,128)S(1)}, f32[9,16,128]{2,1,0:T(8,128)S(1)}, u32[]{:S(2)}, u32[]{:S(2)}) collective-permute-start(f32[9,16,128]{2,1,0:T(8,128)S(1)} %get-tuple-element.96), channel_id=1, source_target_pairs={{0,28},{4,8},{8,4},{12,16},{16,12},{20,24},{24,20},{28,0},{1,29},{... | collective-permute-start | bytes 221192 | tf_op jit(solution)/shard_map/ppermute | solution.py:31
  87.8 2.9 %shard_map.109 = f32[7,9,4,16,64]{4,3,2,1,0:T(8,128)} custom-call(f32[9,8,32,128]{3,2,1,0:T(8,128)S(1)} %get-tuple-element.48.refs_0_, f32[9,2,32,128]{3,2,1,0:T(8,128)S(1)} %collective-permute-done.8.refs_1_, f32[9,2,32,128]{3,2,1,0:T(8,128)S(1)} %collective-permute-done.9.refs_2_, f32[9,12,2,128]{3,2,1,0:T(2,128)S(1)} %bitcast.19, ...), custom_call_target="tpu_custom_call" | custom-call | tf_op jit(solution)/shard_map/pallas_call | solution.py:510
  90.7 2.0 %collective-permute-done.14 = f32[9,16,128]{2,1,0:T(8,128)S(1)} collective-permute-done((f32[9,16,128]{2,1,0:T(8,128)S(1)}, f32[9,16,128]{2,1,0:T(8,128)S(1)}, u32[]{:S(2)}, u32[]{:S(2)}) %collective-permute-start.14) | collective-permute-done | bytes 73760 | tf_op jit(solution)/shard_map/ppermute | solution.py:31
  92.7 0.1 slice_reduce_fusion.9
  92.8 0.1 concatenate.162
  92.9 0.1 slice_reduce_fusion.8
  93.0 0.1 concatenate.163
  93.1 0.1 concatenate.166
  93.1 0.1 concatenate.165
  93.6 0.1 concatenate.154
  94.1 0.1 fusion.2
  94.2 0.1 broadcast_select_fusion.6
  94.4 1.6 %collective-permute-start.16 = (f32[9,8,2,64]{3,2,1,0:T(2,128)S(1)}, f32[9,8,2,64]{3,2,1,0:T(2,128)S(1)}, u32[]{:S(2)}, u32[]{:S(2)}) collective-permute-start(f32[9,8,2,64]{3,2,1,0:T(2,128)S(1)} %get-tuple-element.92), channel_id=1, source_target_pairs={{0,3},{1,2},{2,1},{3,0},{4,7},{5,6},{6,5},{7,4},{8,11},{9,10},{10,... | collective-permute-start | bytes 110600 | tf_op jit(solution)/shard_map/ppermute | solution.py:31
  96.0 2.4 %collective-permute-done.16 = f32[9,8,2,64]{3,2,1,0:T(2,128)S(1)} collective-permute-done((f32[9,8,2,64]{3,2,1,0:T(2,128)S(1)}, f32[9,8,2,64]{3,2,1,0:T(2,128)S(1)}, u32[]{:S(2)}, u32[]{:S(2)}) %collective-permute-start.16) | collective-permute-done | bytes 36896 | tf_op jit(solution)/shard_map/ppermute | solution.py:31
  98.5 1.6 %shard_map.110 = (f32[7,9,2,8,32]{4,3,2,1,0:T(8,128)}, f32[6,2,8,32]{3,2,1,0:T(8,128)}, f32[3,2,8,32]{3,2,1,0:T(8,128)}) custom-call(f32[9,4,16,64]{3,2,1,0:T(8,128)S(1)} %get-tuple-element.59.refs_0_, f32[9,16,128]{2,1,0:T(8,128)S(1)} %get-tuple-element.60.refs_1_, f32[9,16,128]{2,1,0:T(8,128)S(1)} %get-tuple-element.61.refs_2_, ...), custom_call_target="tpu_custom_call" | custom-call | tf_op jit(solution)/shard_map/pallas_call | solution.py:510
  (74 shorter events, 1.4 us)
Async XLA Ops:
  0.6 17.0 %copy-start.1 = (f32[256,256]{1,0:T(8,128)S(1)}, f32[256,256]{1,0:T(8,128)}, u32[]{:S(2)}) copy-start(f32[256,256]{1,0:T(8,128)} %constant.41.clone.table_ref.refs_2_.refs_3_) | copy-start | bytes 786436
  0.6 16.5 %copy-start = (f32[3,16,64,256]{3,2,1,0:T(8,128)S(1)}, f32[3,16,64,256]{3,2,1,0:T(8,128)}, u32[]{:S(2)}) copy-start(f32[3,16,64,256]{3,2,1,0:T(8,128)} %v_ref.3) | copy-start | bytes 9437188
  1.8 39.6 %collective-permute-start = (f32[3,4,16,256]{3,2,1,0:T(8,128)S(1)}, f32[3,4,16,256]{3,2,1,0:T(8,128)S(1)}, u32[]{:S(2)}, u32[]{:S(2)}) collective-permute-start(f32[3,4,16,256]{3,2,1,0:T(8,128)S(1)} %pad_maximum_fusion), channel_id=1, source_target_pairs={{0,4},{4,8},{8,12},{12,16},{16,20},{20,24},{24,28},{28,0},{1,5},{5... | collective-permute-start | bytes 589832 | tf_op jit(solution)/shard_map/ppermute | solution.py:23
  5.9 11.8 %collective-permute-start.2 = (f32[3,16,4,256]{3,2,1,0:T(4,128)S(1)}, f32[3,16,4,256]{3,2,1,0:T(4,128)S(1)}, u32[]{:S(2)}, u32[]{:S(2)}) collective-permute-start(f32[3,16,4,256]{3,2,1,0:T(4,128)S(1)} %slice.102), channel_id=1, source_target_pairs={{0,1},{1,2},{2,3},{3,0},{4,5},{5,6},{6,7},{7,4},{8,9},{9,10},{10,1... | collective-permute-start | bytes 589832 | tf_op jit(solution)/shard_map/ppermute | solution.py:23
  6.9 10.3 %collective-permute-start.3 = (f32[3,16,3,256]{3,2,1,0:T(4,128)S(1)}, f32[3,16,3,256]{3,2,1,0:T(4,128)S(1)}, u32[]{:S(2)}, u32[]{:S(2)}) collective-permute-start(f32[3,16,3,256]{3,2,1,0:T(4,128)S(1)} %slice.103), channel_id=1, source_target_pairs={{0,3},{1,0},{2,1},{3,2},{4,7},{5,4},{6,5},{7,6},{8,11},{9,8},{10,9... | collective-permute-start | bytes 442376 | tf_op jit(solution)/shard_map/ppermute | solution.py:23
  10.6 43.5 %collective-permute-start.4 = (f32[3,4,48,256]{3,2,1,0:T(8,128)}, f32[3,4,48,256]{3,2,1,0:T(8,128)}, u32[]{:S(2)}, u32[]{:S(2)}) collective-permute-start(f32[3,4,48,256]{3,2,1,0:T(8,128)} %slice.104), channel_id=1, source_target_pairs={{0,4},{4,8},{8,12},{12,16},{16,20},{20,24},{24,28},{28,0},{1,5},{5... | collective-permute-start | bytes 1769480 | tf_op jit(solution)/shard_map/ppermute | solution.py:23
  14.0 40.1 %collective-permute-start.5 = (f32[3,3,48,256]{3,2,1,0:T(8,128)}, f32[3,3,48,256]{3,2,1,0:T(8,128)}, u32[]{:S(2)}, u32[]{:S(2)}) collective-permute-start(f32[3,3,48,256]{3,2,1,0:T(8,128)} %slice.105), channel_id=1, source_target_pairs={{0,28},{4,0},{8,4},{12,8},{16,12},{20,16},{24,20},{28,24},{1,29},{... | collective-permute-start | bytes 1327112 | tf_op jit(solution)/shard_map/ppermute | solution.py:23
  17.2 25.5 %copy-start.13 = (f32[3,16,3,256]{3,2,1,0:T(4,128)}, f32[3,16,3,256]{3,2,1,0:T(4,128)S(1)}, u32[]{:S(2)}) copy-start(f32[3,16,3,256]{3,2,1,0:T(4,128)S(1)} %collective-permute-done.3.after_ref) | copy-start | bytes 442372
  17.2 24.1 %collective-permute-start.1 = (f32[3,3,16,256]{3,2,1,0:T(8,128)S(1)}, f32[3,3,16,256]{3,2,1,0:T(8,128)S(1)}, u32[]{:S(2)}, u32[]{:S(2)}) collective-permute-start(f32[3,3,16,256]{3,2,1,0:T(8,128)S(1)} %pad_maximum_fusion.1), channel_id=1, source_target_pairs={{0,28},{4,0},{8,4},{12,8},{16,12},{20,16},{24,20},{28,24},{1,29},{... | collective-permute-start | bytes 442376 | tf_op jit(solution)/shard_map/ppermute | solution.py:23
  17.7 24.4 %copy-start.11 = (f32[3,16,4,256]{3,2,1,0:T(4,128)}, f32[3,16,4,256]{3,2,1,0:T(4,128)S(1)}, u32[]{:S(2)}) copy-start(f32[3,16,4,256]{3,2,1,0:T(4,128)S(1)} %collective-permute-done.2.before_ref) | copy-start | bytes 589828
  23.1 1.8 %copy-start.2 = (f32[3,9,8,32,128]{4,3,2,1,0:T(8,128)}, f32[3,9,8,32,128]{4,3,2,1,0:T(8,128)S(1)}, u32[]{:S(2)}) copy-start(f32[3,9,8,32,128]{4,3,2,1,0:T(8,128)S(1)} %get-tuple-element.43.refs_0_) | copy-start | bytes 10616836
  24.9 1.0 %copy-start.9 = (f32[9,8,32,128]{3,2,1,0:T(8,128)}, f32[9,8,32,128]{3,2,1,0:T(8,128)S(1)}, u32[]{:S(2)}) copy-start(f32[9,8,32,128]{3,2,1,0:T(8,128)S(1)} %get-tuple-element.38.refs_0_) | copy-start | bytes 3538948
  41.3 0.7 copy-start.6
  42.7 11.5 %collective-permute-start.6 = (f32[3,7,4,256]{3,2,1,0:T(4,128)}, f32[3,7,4,256]{3,2,1,0:T(4,128)}, u32[]{:S(2)}, u32[]{:S(2)}) collective-permute-start(f32[3,7,4,256]{3,2,1,0:T(4,128)} %pad_maximum_fusion.4), channel_id=1, source_target_pairs={{0,1},{1,2},{2,3},{3,0},{4,5},{5,6},{6,7},{7,4},{8,9},{9,10},{10,1... | collective-permute-start | bytes 258056 | tf_op jit(solution)/shard_map/ppermute | solution.py:23
  43.3 10.8 %collective-permute-start.7 = (f32[3,7,3,256]{3,2,1,0:T(4,128)}, f32[3,7,3,256]{3,2,1,0:T(4,128)}, u32[]{:S(2)}, u32[]{:S(2)}) collective-permute-start(f32[3,7,3,256]{3,2,1,0:T(4,128)} %pad_maximum_fusion.5), channel_id=1, source_target_pairs={{0,3},{1,0},{2,1},{3,2},{4,7},{5,4},{6,5},{7,6},{8,11},{9,8},{10,9... | collective-permute-start | bytes 193544 | tf_op jit(solution)/shard_map/ppermute | solution.py:23
  45.1 0.9 copy-start.12
  46.0 0.9 copy-start.14
  46.9 7.2 %copy-start.7 = (f32[3,4,16,256]{3,2,1,0:T(8,128)S(1)}, f32[3,4,16,256]{3,2,1,0:T(8,128)}, u32[]{:S(2)}) copy-start(f32[3,4,16,256]{3,2,1,0:T(8,128)} %copy-done.6) | copy-start | bytes 589828
  46.9 7.2 %copy-start.10 = (f32[9,8,32,128]{3,2,1,0:T(8,128)S(1)}, f32[9,8,32,128]{3,2,1,0:T(8,128)}, u32[]{:S(2)}) copy-start(f32[9,8,32,128]{3,2,1,0:T(8,128)} %copy-done.9) | copy-start | bytes 3538948
  52.4 1.8 %copy-start.4 = (f32[3,9,8,32,128]{4,3,2,1,0:T(8,128)}, f32[3,9,8,32,128]{4,3,2,1,0:T(8,128)S(1)}, u32[]{:S(2)}) copy-start(f32[3,9,8,32,128]{4,3,2,1,0:T(8,128)S(1)} %get-tuple-element.44.refs_1_) | copy-start | bytes 10616836
  54.1 17.8 %copy-start.8 = (f32[3,4,16,256]{3,2,1,0:T(8,128)S(1)}, f32[3,4,16,256]{3,2,1,0:T(8,128)}, u32[]{:S(2)}) copy-start(f32[3,4,16,256]{3,2,1,0:T(8,128)} %copy-done.6) | copy-start | bytes 589828
  59.7 6.7 %collective-permute-start.10 = (f32[9,2,4,128]{3,2,1,0:T(4,128)S(1)}, f32[9,2,4,128]{3,2,1,0:T(4,128)S(1)}, u32[]{:S(2)}, u32[]{:S(2)}) collective-permute-start(f32[9,2,4,128]{3,2,1,0:T(4,128)S(1)} %bitcast.32), channel_id=1, source_target_pairs={{0,28},{4,8},{8,4},{12,16},{16,12},{20,24},{24,20},{28,0},{1,29},{... | collective-permute-start | bytes 110600 | tf_op jit(solution)/shard_map/ppermute | solution.py:31
  60.5 5.9 %collective-permute-start.11 = (f32[9,2,4,128]{3,2,1,0:T(4,128)S(1)}, f32[9,2,4,128]{3,2,1,0:T(4,128)S(1)}, u32[]{:S(2)}, u32[]{:S(2)}) collective-permute-start(f32[9,2,4,128]{3,2,1,0:T(4,128)S(1)} %bitcast.31), channel_id=1, source_target_pairs={{0,4},{4,0},{8,12},{12,8},{16,20},{20,16},{24,28},{28,24},{1,5},{5... | collective-permute-start | bytes 110600 | tf_op jit(solution)/shard_map/ppermute | solution.py:31
  66.6 16.9 %collective-permute-start.13 = (f32[9,12,2,128]{3,2,1,0:T(2,128)S(1)}, f32[9,12,2,128]{3,2,1,0:T(2,128)S(1)}, u32[]{:S(2)}, u32[]{:S(2)}) collective-permute-start(f32[9,12,2,128]{3,2,1,0:T(2,128)S(1)} %get-tuple-element.87), channel_id=1, source_target_pairs={{0,1},{1,0},{2,3},{3,2},{4,5},{5,4},{6,7},{7,6},{8,9},{9,8},{10,11... | collective-permute-start | bytes 331784 | tf_op jit(solution)/shard_map/ppermute | solution.py:31
  66.6 16.8 %collective-permute-start.12 = (f32[9,12,2,128]{3,2,1,0:T(2,128)S(1)}, f32[9,12,2,128]{3,2,1,0:T(2,128)S(1)}, u32[]{:S(2)}, u32[]{:S(2)}) collective-permute-start(f32[9,12,2,128]{3,2,1,0:T(2,128)S(1)} %get-tuple-element.88), channel_id=1, source_target_pairs={{0,3},{1,2},{2,1},{3,0},{4,7},{5,6},{6,5},{7,4},{8,11},{9,10},{10,... | collective-permute-start | bytes 331784 | tf_op jit(solution)/shard_map/ppermute | solution.py:31
  67.2 16.2 %collective-permute-start.8 = (f32[9,2,32,128]{3,2,1,0:T(8,128)}, f32[9,2,32,128]{3,2,1,0:T(8,128)S(1)}, u32[]{:S(2)}, u32[]{:S(2)}) collective-permute-start(f32[9,2,32,128]{3,2,1,0:T(8,128)} %get-tuple-element.49), channel_id=1, source_target_pairs={{0,4},{4,8},{8,12},{12,16},{16,20},{20,24},{24,28},{28,0},{1,5},{5... | collective-permute-start | bytes 884744 | tf_op jit(solution)/shard_map/ppermute | solution.py:23
  67.2 16.2 %collective-permute-start.9 = (f32[9,2,32,128]{3,2,1,0:T(8,128)}, f32[9,2,32,128]{3,2,1,0:T(8,128)S(1)}, u32[]{:S(2)}, u32[]{:S(2)}) collective-permute-start(f32[9,2,32,128]{3,2,1,0:T(8,128)} %get-tuple-element.50), channel_id=1, source_target_pairs={{0,28},{4,0},{8,4},{12,8},{16,12},{20,16},{24,20},{28,24},{1,29},{... | collective-permute-start | bytes 884744 | tf_op jit(solution)/shard_map/ppermute | solution.py:23
  72.0 2.0 %copy-start.3 = (f32[3,9,8,32,128]{4,3,2,1,0:T(8,128)S(1)}, f32[3,9,8,32,128]{4,3,2,1,0:T(8,128)}, u32[]{:S(2)}) copy-start(f32[3,9,8,32,128]{4,3,2,1,0:T(8,128)} %copy-done.2) | copy-start | bytes 10616836
  74.0 2.0 %copy-start.5 = (f32[3,9,8,32,128]{4,3,2,1,0:T(8,128)S(1)}, f32[3,9,8,32,128]{4,3,2,1,0:T(8,128)}, u32[]{:S(2)}) copy-start(f32[3,9,8,32,128]{4,3,2,1,0:T(8,128)} %copy-done.4) | copy-start | bytes 10616836
  76.0 7.5 %copy-start.15 = (f32[128,128]{1,0:T(8,128)S(1)}, f32[128,128]{1,0:T(8,128)}, u32[]{:S(2)}) copy-start(f32[128,128]{1,0:T(8,128)} %constant.42.clone.refs_5_) | copy-start | bytes 196612
  85.5 13.0 %copy-start.16 = (f32[128,128]{1,0:T(8,128)S(1)}, f32[128,128]{1,0:T(8,128)}, u32[]{:S(2)}) copy-start(f32[128,128]{1,0:T(8,128)} %constant.43.clone.refs_5_) | copy-start | bytes 196612
  85.5 5.2 %collective-permute-start.15 = (f32[9,16,128]{2,1,0:T(8,128)S(1)}, f32[9,16,128]{2,1,0:T(8,128)S(1)}, u32[]{:S(2)}, u32[]{:S(2)}) collective-permute-start(f32[9,16,128]{2,1,0:T(8,128)S(1)} %get-tuple-element.95), channel_id=1, source_target_pairs={{0,4},{4,0},{8,12},{12,8},{16,20},{20,16},{24,28},{28,24},{1,5},{5... | collective-permute-start | bytes 221192 | tf_op jit(solution)/shard_map/ppermute | solution.py:31
  85.6 7.1 %collective-permute-start.14 = (f32[9,16,128]{2,1,0:T(8,128)S(1)}, f32[9,16,128]{2,1,0:T(8,128)S(1)}, u32[]{:S(2)}, u32[]{:S(2)}) collective-permute-start(f32[9,16,128]{2,1,0:T(8,128)S(1)} %get-tuple-element.96), channel_id=1, source_target_pairs={{0,28},{4,8},{8,4},{12,16},{16,12},{20,24},{24,20},{28,0},{1,29},{... | collective-permute-start | bytes 221192 | tf_op jit(solution)/shard_map/ppermute | solution.py:31
  94.3 1.7 %collective-permute-start.17 = (f32[9,8,2,64]{3,2,1,0:T(2,128)S(1)}, f32[9,8,2,64]{3,2,1,0:T(2,128)S(1)}, u32[]{:S(2)}, u32[]{:S(2)}) collective-permute-start(f32[9,8,2,64]{3,2,1,0:T(2,128)S(1)} %get-tuple-element.91), channel_id=1, source_target_pairs={{0,1},{1,0},{2,3},{3,2},{4,5},{5,4},{6,7},{7,6},{8,9},{9,8},{10,11... | collective-permute-start | bytes 110600 | tf_op jit(solution)/shard_map/ppermute | solution.py:31
  94.4 4.0 %collective-permute-start.16 = (f32[9,8,2,64]{3,2,1,0:T(2,128)S(1)}, f32[9,8,2,64]{3,2,1,0:T(2,128)S(1)}, u32[]{:S(2)}, u32[]{:S(2)}) collective-permute-start(f32[9,8,2,64]{3,2,1,0:T(2,128)S(1)} %get-tuple-element.92), channel_id=1, source_target_pairs={{0,3},{1,2},{2,1},{3,0},{4,7},{5,6},{6,5},{7,4},{8,11},{9,10},{10,... | collective-permute-start | bytes 110600 | tf_op jit(solution)/shard_map/ppermute | solution.py:31

commit v7 on v5

--- a/solution.py
+++ b/solution.py
@@ -252,46 +252,32 @@
 def approx_kernel(*refs):
     low_refs, table_ref = refs[:2], refs[2]
     halo_refs = refs[3:9]
-    approx_ref, high_ref, stress_ref = refs[9:12]
-    next_ref, prev_ref, next_edge_ref, prev_edge_ref, down_ref, up_ref = refs[12:18]
-    rows_ref, even_ref, odd_ref, kept_ref, part_ref, stack_ref, out_ref = refs[18:]
-    f = pl.program_id(0)
+    approx_ref, high_ref, stress_ref, next_ref, prev_ref, down_ref, up_ref = refs[9:16]
+    rows_ref, even_ref, odd_ref, part_ref, stack_ref, out_ref = refs[16:]
     half, lanes = low_refs[0].shape[2:]
     mx = approx_ref.shape[1]
-
-    @pl.when(f == 0)
-    def _():
-        gather_rows(halo_refs, rows_ref, even_ref, odd_ref)
-
-    pairs = [pair_of(f * GROUP + n) for n in range(GROUP)]
-    halo_stack(pairs, False, even_ref, odd_ref, part_ref, stack_ref)
-    out_ref[...] = dot(stack_ref[...], table_ref[:, :lanes])
-    for n in range(GROUP):
-        for r in range(0, half, 8):
-            rows = slice(r, r + 8)
-            halo = [out_ref[(4 * n + k) * half + r : (4 * n + k) * half + r + 8, :] for k in range(4)]
-            e, o = lift_first(layer_list(low_refs, (n,), rows), halo)
-            e = [t * band_scale(0, 0) for t in e]
-            for x in range(mx):
-                approx_ref[n, x, rows, :] = e[x]
-                high_ref[n, x, rows, :] = o[x] * band_scale(0, 1)
-            send_layers(e, n, r, next_ref, prev_ref)
-        send_rows(approx_ref, n, down_ref, up_ref)
-        for ref, edge_ref in ((next_ref, next_edge_ref), (prev_ref, prev_edge_ref)):
-            for part in range(2):
-                tail, head = row_parts(lambda row: ref[n, part, row : row + 8, :], half)
-                edge_ref[n, part, 0:2, :] = tail
-                edge_ref[n, part, 2:4, :] = head
-
-    @pl.when(f == 0)
-    def _():
-        kept_ref[...] = approx_ref[...]
-
-    @pl.when(f > 0)
-    def _():
-        for n, (i, j) in enumerate(pairs):
-            for x in range(mx):
-                stress_ref[n, x] = approx_ref[n, x] - kept_ref[i, x] * kept_ref[j, x]
+    gather_rows(halo_refs, rows_ref, even_ref, odd_ref)
+
+    def group(g, carry):
+        halo_stack([pair_of(g * GROUP + n) for n in range(GROUP)], False, even_ref, odd_ref, part_ref, stack_ref)
+        out_ref[...] = dot(stack_ref[...], table_ref[:, :lanes])
+        for n in range(GROUP):
+            f = g * GROUP + n
+            for r in range(0, half, 8):
+                rows = slice(r, r + 8)
+                halo = [out_ref[(4 * n + k) * half + r : (4 * n + k) * half + r + 8, :] for k in range(4)]
+                e, o = lift_first(layer_list(low_refs, (f,), rows), halo)
+                e = [t * band_scale(0, 0) for t in e]
+                for x in range(mx):
+                    approx_ref[f, x, rows, :] = e[x]
+                    high_ref[f, x, rows, :] = o[x] * band_scale(0, 1)
+                send_layers(e, f, r, next_ref, prev_ref)
+            send_rows(approx_ref, f, down_ref, up_ref)
+        return carry
+
+    lax.fori_loop(0, 9 // GROUP, group, 0)
+    for k, (i, j) in enumerate(product_pairs):
+        stress_ref[k] = approx_ref[3 + k] - approx_ref[i] * approx_ref[j]
 
 
 def whole(shape):
@@ -303,24 +289,19 @@
 
 
 def approx_pass(lows, halo, table):
-    _, nx, half, lanes = lows[0].shape
-    nz, count, mx = 2 * lanes, half + 16, nx
+    _, mx, half, lanes = lows[0].shape
+    nz, count = 2 * lanes, half + 16
     f32 = lambda *shape: jax.ShapeDtypeStruct(shape, jnp.float32)
-    sends = [(2, half, lanes), (2, half, lanes), (2, 4, lanes), (2, 4, lanes), (mx, 2, lanes), (mx, 2, lanes)]
+    sends = [(2, half, lanes), (2, half, lanes), (mx, 2, lanes), (mx, 2, lanes)]
+    out = [f32(9, mx, half, lanes), f32(9, mx, half, lanes), f32(6, mx, half, lanes)] + [f32(9, *t) for t in sends]
+    vmem = pl.BlockSpec(memory_space=pltpu.VMEM)
     return pl.pallas_call(
         approx_kernel,
-        grid=(9 // GROUP,),
-        in_specs=[per_field((nx, half, lanes))] * 2 + [whole((nz, nz))] + [whole(h.shape) for h in halo],
-        out_specs=[
-            per_field((mx, half, lanes)),
-            per_field((mx, half, lanes)),
-            pl.BlockSpec((GROUP, mx, half, lanes), lambda f: (jnp.maximum(f - 1, 0), 0, 0, 0)),
-        ]
-        + [per_field(s) for s in sends],
-        out_shape=[f32(9, mx, half, lanes), f32(9, mx, half, lanes), f32(6, mx, half, lanes)] + [f32(9, *s) for s in sends],
+        in_specs=[vmem] * (3 + len(halo)),
+        out_specs=[vmem] * len(out),
+        out_shape=out,
         scratch_shapes=halo_scratch(half, lanes)
         + [
-            pltpu.VMEM((3, mx, half, lanes), jnp.float32),
             pltpu.VMEM((2, 4, count, lanes), jnp.float32),
             pltpu.VMEM((GROUP * 4 * half, nz), jnp.float32),
             pltpu.VMEM((GROUP * 4 * half, lanes), jnp.float32),
@@ -531,16 +512,6 @@
     return shifted(down, "gy", 1), shifted(up, "gy", -1)
 
 
-def exchange(to_next, to_prev, edge_next, edge_prev, down, up):
-    from_prev_edge = shifted(edge_next, "gx", 1)
-    from_next_edge = shifted(edge_prev, "gx", -1)
-    before = shifted(to_next, "gx", 1)
-    after = shifted(to_prev, "gx", -1)
-    down = jnp.concatenate([down, from_prev_edge[:, :, 0:2], from_next_edge[:, :, 0:2]], axis=1)
-    up = jnp.concatenate([up, from_prev_edge[:, :, 2:4], from_next_edge[:, :, 2:4]], axis=1)
-    return before, after, shifted(down, "gy", 1), shifted(up, "gy", -1)
-
-
 def body(velocity):
     _, nx, ny, nz = velocity.shape
     table = jnp.asarray(third_table(nz, nz))
@@ -561,9 +532,11 @@
     low_two, rest_two = local_pass(velocity, own_before, own_after, table, nx // 2)
     halo = (edge_before, mid_before, edge_after, mid_after, row_before, row_after)
     approx, high, stress_one, *sends = approx_pass((low_one, low_two), halo, table)
-    second_halo = exchange(*sends)
+    before = shifted(sends[0], "gx", 1)
+    after = shifted(sends[1], "gx", -1)
     details_one = detail_pass((rest_one, rest_two), high, halo, table)
-    approx, details_one = lax.optimization_barrier((approx, details_one))
+    before, after, details_one = lax.optimization_barrier((before, after, details_one))
+    second_halo = (before, after) + halo_rows(before, after, *sends[2:])
     second = approx
     approx, stress_two, *sends = level_approx(second, second_halo)
     before = shifted(sends[0], "gx", 1)

time: 87.4 us -> 88.9 us (1.017)
  the two profiles are of different devices: /device:TPU:0 before, /device:TPU:1 now
where the time goes in v7:
time: 88.9 us; the launch traced here: 88.6 us
  Pallas kernels  27.8 us (31%)
  waiting for transfers between devices  27.1 us (30%)
  starting transfers between devices  26.6 us (30%)
  local copies, waits for them, and re-layouts  5.58 us (6%)
  between operations  0.89 us (1%)
    ppermute x16, waiting for transfers between devices, shifted(): lax.ppermute(block, axis, [(i, (i + distance) % size) for i in range(size)])  27.1 us
    ppermute x16, starting transfers between devices, shifted(): lax.ppermute(block, axis, [(i, (i + distance) % size) for i in range(size)])  26.6 us
    pallas_call x2, Pallas kernels, local_pass(): pl.pallas_call(local_kernel, grid=(nx,), in_specs=[pl.BlockSpec((3, 1, ny...  10.9 us
    pallas_call x3, Pallas kernels, level_call(): pl.pallas_call(kernel, in_specs=[vmem] * 6, out_specs=[vmem] * len(out),...  6.47 us
    pallas_call x1, Pallas kernels, detail_pass(): pl.pallas_call(detail_kernel, grid=(9 // GROUP,), in_specs=[pl.BlockSpec(...  6.39 us
    pallas_call x1, Pallas kernels, approx_pass(): pl.pallas_call(approx_kernel, in_specs=[vmem] * (3 + len(halo)), out_spec...  4.03 us
  transfers between devices with their start and end apart: 16, of which 10 were waited for; matrix products, arithmetic and copies ran while one was open for 5% of the time, Pallas kernels for 23%

profile of v7, /device:TPU:1, one launch (start us, length us, event | category | flops | bytes accessed | tf_op | source)
XLA Modules:
  0.0 88.6 jit_solution(16058717756753300836)
XLA Ops:
  0.6 0.0 copy-start.1
  0.6 0.0 copy-start
  0.7 1.1 %fusion.11 = (f32[3,4,8,256]{3,2,1,0:T(8,128)S(1)}, f32[3,4,8,256]{3,2,1,0:T(8,128)S(1)}) fusion(f32[3,16,64,256]{3,2,1,0:T(8,128)} %v_ref.3), kind=kLoop, calls=%fused_computation.29 | loop fusion | bytes 393216 | tf_op jit(solution)/shard_map/slice | solution.py:519
  1.8 2.1 %collective-permute-start = (f32[3,4,16,256]{3,2,1,0:T(8,128)S(1)}, f32[3,4,16,256]{3,2,1,0:T(8,128)S(1)}, u32[]{:S(2)}, u32[]{:S(2)}) collective-permute-start(f32[3,4,16,256]{3,2,1,0:T(8,128)S(1)} %pad_maximum_fusion), channel_id=1, source_target_pairs={{0,4},{4,8},{8,12},{12,16},{16,20},{20,24},{24,28},{28,0},{1,5},{5... | collective-permute-start | bytes 589832 | tf_op jit(solution)/shard_map/ppermute | solution.py:23
  3.9 1.0 %slice.132 = f32[3,16,4,256]{3,2,1,0:T(4,128)S(1)} slice(f32[3,16,64,256]{3,2,1,0:T(8,128)} %v_ref.3), slice={[0:3], [0:16], [60:64], [0:256]} | slice | bytes 393216 | tf_op jit(solution)/shard_map/slice | solution.py:524
  4.9 2.1 %collective-permute-start.2 = (f32[3,16,4,256]{3,2,1,0:T(4,128)S(1)}, f32[3,16,4,256]{3,2,1,0:T(4,128)S(1)}, u32[]{:S(2)}, u32[]{:S(2)}) collective-permute-start(f32[3,16,4,256]{3,2,1,0:T(4,128)S(1)} %slice.132), channel_id=1, source_target_pairs={{0,1},{1,2},{2,3},{3,0},{4,5},{5,6},{6,7},{7,4},{8,9},{9,10},{10,1... | collective-permute-start | bytes 589832 | tf_op jit(solution)/shard_map/ppermute | solution.py:23
  7.1 1.0 %slice.133 = f32[3,16,3,256]{3,2,1,0:T(4,128)S(1)} slice(f32[3,16,64,256]{3,2,1,0:T(8,128)} %v_ref.3), slice={[0:3], [0:16], [0:3], [0:256]} | slice | bytes 294912 | tf_op jit(solution)/shard_map/slice | solution.py:525
  8.1 0.1 collective-permute-start.3
  8.1 1.1 %slice.135 = f32[3,3,48,256]{3,2,1,0:T(8,128)S(1)} slice(f32[3,16,64,256]{3,2,1,0:T(8,128)} %v_ref.3), slice={[0:3], [0:3], [8:56], [0:256]} | slice | bytes 884736 | tf_op jit(solution)/shard_map/slice | solution.py:523
  9.2 3.0 %collective-permute-start.5 = (f32[3,3,48,256]{3,2,1,0:T(8,128)S(1)}, f32[3,3,48,256]{3,2,1,0:T(8,128)S(1)}, u32[]{:S(2)}, u32[]{:S(2)}) collective-permute-start(f32[3,3,48,256]{3,2,1,0:T(8,128)S(1)} %slice.135), channel_id=1, source_target_pairs={{0,28},{4,0},{8,4},{12,8},{16,12},{20,16},{24,20},{28,24},{1,29},{... | collective-permute-start | bytes 1327112 | tf_op jit(solution)/shard_map/ppermute | solution.py:23
  12.2 1.1 %slice.134 = f32[3,4,48,256]{3,2,1,0:T(8,128)S(1)} slice(f32[3,16,64,256]{3,2,1,0:T(8,128)} %v_ref.3), slice={[0:3], [12:16], [8:56], [0:256]} | slice | bytes 1179648 | tf_op jit(solution)/shard_map/slice | solution.py:522
  13.3 0.1 collective-permute-start.4
  13.4 0.1 collective-permute-done.3.after_ref
  13.5 4.1 %collective-permute-start.1 = (f32[3,3,16,256]{3,2,1,0:T(8,128)S(1)}, f32[3,3,16,256]{3,2,1,0:T(8,128)S(1)}, u32[]{:S(2)}, u32[]{:S(2)}) collective-permute-start(f32[3,3,16,256]{3,2,1,0:T(8,128)S(1)} %pad_maximum_fusion.1), channel_id=1, source_target_pairs={{0,28},{4,0},{8,4},{12,8},{16,12},{20,16},{24,20},{28,24},{1,29},{... | collective-permute-start | bytes 442376 | tf_op jit(solution)/shard_map/ppermute | solution.py:23
  17.6 0.0 collective-permute-done.2.before_ref
  17.6 5.4 %local_pass.2 = (f32[9,8,32,128]{3,2,1,0:T(8,128)S(1)}, f32[3,9,8,32,128]{4,3,2,1,0:T(8,128)S(1)}) custom-call(f32[3,16,64,256]{3,2,1,0:T(8,128)S(1)} %copy-done, f32[3,16,4,256]{3,2,1,0:T(4,128)S(1)} %collective-permute-done.2.before_ref, f32[3,16,3,256]{3,2,1,0:T(4,128)S(1)} %collective-permute-done.3.after_ref, f32[256,256]{1,0:T(8,128)S(1)} %copy-done.1), custom_call_target="tpu_custom_call" | custom-call | flops 603979776 | bytes 7077888 | tf_op jit(solution)/shard_map/local_pass/pallas_call | solution.py:166
  23.1 14.0 %collective-permute-done.1.refs_5_.refs_6_ = f32[3,3,16,256]{3,2,1,0:T(8,128)S(1)} collective-permute-done((f32[3,3,16,256]{3,2,1,0:T(8,128)S(1)}, f32[3,3,16,256]{3,2,1,0:T(8,128)S(1)}, u32[]{:S(2)}, u32[]{:S(2)}) %collective-permute-start.1) | collective-permute-done | bytes 147488 | tf_op jit(solution)/shard_map/ppermute | solution.py:23
  37.1 2.2 %collective-permute-start.6 = (f32[3,7,4,256]{3,2,1,0:T(4,128)S(1)}, f32[3,7,4,256]{3,2,1,0:T(4,128)S(1)}, u32[]{:S(2)}, u32[]{:S(2)}) collective-permute-start(f32[3,7,4,256]{3,2,1,0:T(4,128)S(1)} %pad_maximum_fusion.2), channel_id=1, source_target_pairs={{0,1},{1,2},{2,3},{3,0},{4,5},{5,6},{6,7},{7,4},{8,9},{9,10},{10,1... | collective-permute-start | bytes 258056 | tf_op jit(solution)/shard_map/ppermute | solution.py:23
  39.4 0.1 collective-permute-start.7
  39.4 5.5 %local_pass.3 = (f32[9,8,32,128]{3,2,1,0:T(8,128)S(1)}, f32[3,9,8,32,128]{4,3,2,1,0:T(8,128)S(1)}) custom-call(f32[3,16,64,256]{3,2,1,0:T(8,128)S(1)} %copy-done, f32[3,16,4,256]{3,2,1,0:T(4,128)S(1)} %collective-permute-done.2.before_ref, f32[3,16,3,256]{3,2,1,0:T(4,128)S(1)} %collective-permute-done.3.after_ref, f32[256,256]{1,0:T(8,128)S(1)} %copy-done.1), custom_call_target="tpu_custom_call" | custom-call | flops 603979776 | bytes 7077888 | tf_op jit(solution)/shard_map/local_pass/pallas_call | solution.py:166
  44.9 0.0 collective-permute-done.5.refs_6_.refs_7_
  44.9 4.0 %approx_pass.1 = (f32[9,8,32,128]{3,2,1,0:T(8,128)S(1)}, f32[9,8,32,128]{3,2,1,0:T(8,128)S(1)}, f32[6,8,32,128]{3,2,1,0:T(8,128)}, f32[9,2,32,128]{3,2,1,0:T(8,1...) custom-call(f32[9,8,32,128]{3,2,1,0:T(8,128)S(1)} %get-tuple-element.37.refs_0_, ...), custom_call_target="tpu_custom_call" | custom-call | tf_op jit(solution)/shard_map/approx_pass/pallas_call | solution.py:298
  49.0 4.2 %collective-permute-start.9 = (f32[9,2,32,128]{3,2,1,0:T(8,128)S(1)}, f32[9,2,32,128]{3,2,1,0:T(8,128)S(1)}, u32[]{:S(2)}, u32[]{:S(2)}) collective-permute-start(f32[9,2,32,128]{3,2,1,0:T(8,128)S(1)} %get-tuple-element.42), channel_id=1, source_target_pairs={{0,28},{4,0},{8,4},{12,8},{16,12},{20,16},{24,20},{28,24},{1,29},{... | collective-permute-start | bytes 884744 | tf_op jit(solution)/shard_map/ppermute | solution.py:23
  53.1 6.4 %detail_pass.1 = f32[7,9,8,32,128]{4,3,2,1,0:T(8,128)} custom-call(f32[3,9,8,32,128]{4,3,2,1,0:T(8,128)S(1)} %get-tuple-element.43.refs_0_, f32[3,9,8,32,128]{4,3,2,1,0:T(8,128)S(1)} %get-tuple-element.44.refs_1_, f32[9,8,32,128]{3,2,1,0:T(8,128)S(1)} %get-tuple-element.45.refs_2_, f32[256,256]{1,0:T(8,128)S(1)} %copy-done.1, ...), custom_call_target="tpu_custom_call" | custom-call | flops 235929600 | bytes 18874368 | tf_op jit(solution)/shard_map/detail_pass/pallas_call | solution.py:357
  59.5 1.8 %collective-permute-done.8.refs_1_ = f32[9,2,32,128]{3,2,1,0:T(8,128)S(1)} collective-permute-done((f32[9,2,32,128]{3,2,1,0:T(8,128)S(1)}, f32[9,2,32,128]{3,2,1,0:T(8,128)S(1)}, u32[]{:S(2)}, u32[]{:S(2)}) %collective-permute-start.8) | collective-permute-done | bytes 294944 | tf_op jit(solution)/shard_map/ppermute | solution.py:23
  61.3 1.3 %collective-permute-done.9.refs_2_ = f32[9,2,32,128]{3,2,1,0:T(8,128)S(1)} collective-permute-done((f32[9,2,32,128]{3,2,1,0:T(8,128)S(1)}, f32[9,2,32,128]{3,2,1,0:T(8,128)S(1)}, u32[]{:S(2)}, u32[]{:S(2)}) %collective-permute-start.9) | collective-permute-done | bytes 294944 | tf_op jit(solution)/shard_map/ppermute | solution.py:23
  62.7 0.1 fusion.12
  62.8 0.1 fusion.1
  62.8 0.1 maximum_maximum_fusion
  62.9 2.8 %collective-permute-start.10 = (f32[9,12,2,128]{3,2,1,0:T(2,128)S(1)}, f32[9,12,2,128]{3,2,1,0:T(2,128)S(1)}, u32[]{:S(2)}, u32[]{:S(2)}) collective-permute-start(f32[9,12,2,128]{3,2,1,0:T(2,128)S(1)} %maximum_maximum_fusion), channel_id=1, source_target_pairs={{0,1},{1,2},{2,3},{3,0},{4,5},{5,6},{6,7},{7,4},{8,9},{9,10},{10,1... | collective-permute-start | bytes 331784 | tf_op jit(solution)/shard_map/ppermute | solution.py:23
  65.8 0.1 maximum_maximum_fusion.1
  65.8 0.1 collective-permute-start.11
  65.9 1.6 %collective-permute-done.10.refs_3_ = f32[9,12,2,128]{3,2,1,0:T(2,128)S(1)} collective-permute-done((f32[9,12,2,128]{3,2,1,0:T(2,128)S(1)}, f32[9,12,2,128]{3,2,1,0:T(2,128)S(1)}, u32[]{:S(2)}, u32[]{:S(2)}) %collective-permute-start.10) | collective-permute-done | bytes 110624 | tf_op jit(solution)/shard_map/ppermute | solution.py:23
  67.5 2.6 %collective-permute-done.11.refs_4_ = f32[9,12,2,128]{3,2,1,0:T(2,128)S(1)} collective-permute-done((f32[9,12,2,128]{3,2,1,0:T(2,128)S(1)}, f32[9,12,2,128]{3,2,1,0:T(2,128)S(1)}, u32[]{:S(2)}, u32[]{:S(2)}) %collective-permute-start.11) | collective-permute-done | bytes 110624 | tf_op jit(solution)/shard_map/ppermute | solution.py:23
  70.1 2.0 %shard_map.108 = (f32[9,4,16,64]{3,2,1,0:T(8,128)S(1)}, f32[6,4,16,64]{3,2,1,0:T(8,128)}, f32[9,2,16,64]{3,2,1,0:T(8,128)S(1)}, f32[9,2,16,64]{3,2,1,0:T(8,128)S...) custom-call(f32[9,8,32,128]{3,2,1,0:T(8,128)S(1)} %get-tuple-element.48.refs_0_, ...), custom_call_target="tpu_custom_call" | custom-call | tf_op jit(solution)/shard_map/pallas_call | solution.py:471
  72.1 4.2 %collective-permute-start.13 = (f32[9,2,16,64]{3,2,1,0:T(8,128)S(1)}, f32[9,2,16,64]{3,2,1,0:T(8,128)S(1)}, u32[]{:S(2)}, u32[]{:S(2)}) collective-permute-start(f32[9,2,16,64]{3,2,1,0:T(8,128)S(1)} %get-tuple-element.54), channel_id=1, source_target_pairs={{0,28},{4,0},{8,4},{12,8},{16,12},{20,16},{24,20},{28,24},{1,29},{... | collective-permute-start | bytes 221192 | tf_op jit(solution)/shard_map/ppermute | solution.py:23
  76.2 2.9 %shard_map.109 = f32[7,9,4,16,64]{4,3,2,1,0:T(8,128)} custom-call(f32[9,8,32,128]{3,2,1,0:T(8,128)S(1)} %get-tuple-element.48.refs_0_, f32[9,2,32,128]{3,2,1,0:T(8,128)S(1)} %collective-permute-done.8.refs_1_, f32[9,2,32,128]{3,2,1,0:T(8,128)S(1)} %collective-permute-done.9.refs_2_, f32[9,12,2,128]{3,2,1,0:T(2,128)S(1)} %collective-permute-done.10.refs_3_, ...), custom_call_target="tpu_custom_call" | custom-call | tf_op jit(solution)/shard_map/pallas_call | solution.py:471
  79.1 0.9 %collective-permute-done.12.refs_1_ = f32[9,2,16,64]{3,2,1,0:T(8,128)S(1)} collective-permute-done((f32[9,2,16,64]{3,2,1,0:T(8,128)S(1)}, f32[9,2,16,64]{3,2,1,0:T(8,128)S(1)}, u32[]{:S(2)}, u32[]{:S(2)}) %collective-permute-start.12) | collective-permute-done | bytes 73760 | tf_op jit(solution)/shard_map/ppermute | solution.py:23
  80.1 1.0 %collective-permute-done.13.refs_2_ = f32[9,2,16,64]{3,2,1,0:T(8,128)S(1)} collective-permute-done((f32[9,2,16,64]{3,2,1,0:T(8,128)S(1)}, f32[9,2,16,64]{3,2,1,0:T(8,128)S(1)}, u32[]{:S(2)}, u32[]{:S(2)}) %collective-permute-start.13) | collective-permute-done | bytes 73760 | tf_op jit(solution)/shard_map/ppermute | solution.py:23
  81.2 0.1 fusion.6
  81.3 0.1 maximum_maximum_fusion.2
  81.3 1.7 %collective-permute-start.14 = (f32[9,8,2,64]{3,2,1,0:T(2,128)S(1)}, f32[9,8,2,64]{3,2,1,0:T(2,128)S(1)}, u32[]{:S(2)}, u32[]{:S(2)}) collective-permute-start(f32[9,8,2,64]{3,2,1,0:T(2,128)S(1)} %maximum_maximum_fusion.2), channel_id=1, source_target_pairs={{0,1},{1,2},{2,3},{3,0},{4,5},{5,6},{6,7},{7,4},{8,9},{9,10},{10,1... | collective-permute-start | bytes 110600 | tf_op jit(solution)/shard_map/ppermute | solution.py:23
  83.0 0.1 fusion.9
  83.1 0.1 maximum_maximum_fusion.3
  83.2 0.1 collective-permute-start.15
  83.2 1.3 %collective-permute-done.14.refs_3_ = f32[9,8,2,64]{3,2,1,0:T(2,128)S(1)} collective-permute-done((f32[9,8,2,64]{3,2,1,0:T(2,128)S(1)}, f32[9,8,2,64]{3,2,1,0:T(2,128)S(1)}, u32[]{:S(2)}, u32[]{:S(2)}) %collective-permute-start.14) | collective-permute-done | bytes 36896 | tf_op jit(solution)/shard_map/ppermute | solution.py:23
  84.6 2.4 %collective-permute-done.15.refs_4_ = f32[9,8,2,64]{3,2,1,0:T(2,128)S(1)} collective-permute-done((f32[9,8,2,64]{3,2,1,0:T(2,128)S(1)}, f32[9,8,2,64]{3,2,1,0:T(2,128)S(1)}, u32[]{:S(2)}, u32[]{:S(2)}) %collective-permute-start.15) | collective-permute-done | bytes 36896 | tf_op jit(solution)/shard_map/ppermute | solution.py:23
  87.0 1.6 %shard_map.110 = (f32[7,9,2,8,32]{4,3,2,1,0:T(8,128)}, f32[6,2,8,32]{3,2,1,0:T(8,128)}, f32[3,2,8,32]{3,2,1,0:T(8,128)}) custom-call(f32[9,4,16,64]{3,2,1,0:T(8,128)S(1)} %get-tuple-element.57.refs_0_, f32[9,2,16,64]{3,2,1,0:T(8,128)S(1)} %collective-permute-done.12.refs_1_, f32[9,2,16,64]{3,2,1,0:T(8,128)S(1)} %collective-permute-done.13.refs_2_, ...), custom_call_target="tpu_custom_call" | custom-call | tf_op jit(solution)/shard_map/pallas_call | solution.py:471
  (24 shorter events, 0.3 us)
Async XLA Ops:
  0.6 17.0 %copy-start.1 = (f32[256,256]{1,0:T(8,128)S(1)}, f32[256,256]{1,0:T(8,128)}, u32[]{:S(2)}) copy-start(f32[256,256]{1,0:T(8,128)} %constant.3.clone.table_ref.refs_2_.refs_3_) | copy-start | bytes 786436
  0.6 12.7 %copy-start = (f32[3,16,64,256]{3,2,1,0:T(8,128)S(1)}, f32[3,16,64,256]{3,2,1,0:T(8,128)}, u32[]{:S(2)}) copy-start(f32[3,16,64,256]{3,2,1,0:T(8,128)} %v_ref.3) | copy-start | bytes 9437188
  1.8 35.2 %collective-permute-start = (f32[3,4,16,256]{3,2,1,0:T(8,128)S(1)}, f32[3,4,16,256]{3,2,1,0:T(8,128)S(1)}, u32[]{:S(2)}, u32[]{:S(2)}) collective-permute-start(f32[3,4,16,256]{3,2,1,0:T(8,128)S(1)} %pad_maximum_fusion), channel_id=1, source_target_pairs={{0,4},{4,8},{8,12},{12,16},{16,20},{20,24},{24,28},{28,0},{1,5},{5... | collective-permute-start | bytes 589832 | tf_op jit(solution)/shard_map/ppermute | solution.py:23
  4.9 12.7 %collective-permute-start.2 = (f32[3,16,4,256]{3,2,1,0:T(4,128)S(1)}, f32[3,16,4,256]{3,2,1,0:T(4,128)S(1)}, u32[]{:S(2)}, u32[]{:S(2)}) collective-permute-start(f32[3,16,4,256]{3,2,1,0:T(4,128)S(1)} %slice.132), channel_id=1, source_target_pairs={{0,1},{1,2},{2,3},{3,0},{4,5},{5,6},{6,7},{7,4},{8,9},{9,10},{10,1... | collective-permute-start | bytes 589832 | tf_op jit(solution)/shard_map/ppermute | solution.py:23
  8.1 5.4 %collective-permute-start.3 = (f32[3,16,3,256]{3,2,1,0:T(4,128)S(1)}, f32[3,16,3,256]{3,2,1,0:T(4,128)S(1)}, u32[]{:S(2)}, u32[]{:S(2)}) collective-permute-start(f32[3,16,3,256]{3,2,1,0:T(4,128)S(1)} %slice.133), channel_id=1, source_target_pairs={{0,3},{1,0},{2,1},{3,2},{4,7},{5,4},{6,5},{7,6},{8,11},{9,8},{10,9... | collective-permute-start | bytes 442376 | tf_op jit(solution)/shard_map/ppermute | solution.py:23
  9.2 35.7 %collective-permute-start.5 = (f32[3,3,48,256]{3,2,1,0:T(8,128)S(1)}, f32[3,3,48,256]{3,2,1,0:T(8,128)S(1)}, u32[]{:S(2)}, u32[]{:S(2)}) collective-permute-start(f32[3,3,48,256]{3,2,1,0:T(8,128)S(1)} %slice.135), channel_id=1, source_target_pairs={{0,28},{4,0},{8,4},{12,8},{16,12},{20,16},{24,20},{28,24},{1,29},{... | collective-permute-start | bytes 1327112 | tf_op jit(solution)/shard_map/ppermute | solution.py:23
  13.3 31.6 %collective-permute-start.4 = (f32[3,4,48,256]{3,2,1,0:T(8,128)S(1)}, f32[3,4,48,256]{3,2,1,0:T(8,128)S(1)}, u32[]{:S(2)}, u32[]{:S(2)}) collective-permute-start(f32[3,4,48,256]{3,2,1,0:T(8,128)S(1)} %slice.134), channel_id=1, source_target_pairs={{0,4},{4,8},{8,12},{12,16},{16,20},{20,24},{24,28},{28,0},{1,5},{5... | collective-permute-start | bytes 1769480 | tf_op jit(solution)/shard_map/ppermute | solution.py:23
  13.5 23.5 %collective-permute-start.1 = (f32[3,3,16,256]{3,2,1,0:T(8,128)S(1)}, f32[3,3,16,256]{3,2,1,0:T(8,128)S(1)}, u32[]{:S(2)}, u32[]{:S(2)}) collective-permute-start(f32[3,3,16,256]{3,2,1,0:T(8,128)S(1)} %pad_maximum_fusion.1), channel_id=1, source_target_pairs={{0,28},{4,0},{8,4},{12,8},{16,12},{20,16},{24,20},{28,24},{1,29},{... | collective-permute-start | bytes 442376 | tf_op jit(solution)/shard_map/ppermute | solution.py:23
  37.1 7.8 %collective-permute-start.6 = (f32[3,7,4,256]{3,2,1,0:T(4,128)S(1)}, f32[3,7,4,256]{3,2,1,0:T(4,128)S(1)}, u32[]{:S(2)}, u32[]{:S(2)}) collective-permute-start(f32[3,7,4,256]{3,2,1,0:T(4,128)S(1)} %pad_maximum_fusion.2), channel_id=1, source_target_pairs={{0,1},{1,2},{2,3},{3,0},{4,5},{5,6},{6,7},{7,4},{8,9},{9,10},{10,1... | collective-permute-start | bytes 258056 | tf_op jit(solution)/shard_map/ppermute | solution.py:23
  39.4 5.5 %collective-permute-start.7 = (f32[3,7,3,256]{3,2,1,0:T(4,128)S(1)}, f32[3,7,3,256]{3,2,1,0:T(4,128)S(1)}, u32[]{:S(2)}, u32[]{:S(2)}) collective-permute-start(f32[3,7,3,256]{3,2,1,0:T(4,128)S(1)} %pad_maximum_fusion.3), channel_id=1, source_target_pairs={{0,3},{1,0},{2,1},{3,2},{4,7},{5,4},{6,5},{7,6},{8,11},{9,8},{10,9... | collective-permute-start | bytes 193544 | tf_op jit(solution)/shard_map/ppermute | solution.py:23
  49.0 12.4 %collective-permute-start.8 = (f32[9,2,32,128]{3,2,1,0:T(8,128)S(1)}, f32[9,2,32,128]{3,2,1,0:T(8,128)S(1)}, u32[]{:S(2)}, u32[]{:S(2)}) collective-permute-start(f32[9,2,32,128]{3,2,1,0:T(8,128)S(1)} %get-tuple-element.41), channel_id=1, source_target_pairs={{0,4},{4,8},{8,12},{12,16},{16,20},{20,24},{24,28},{28,0},{1,5},{5... | collective-permute-start | bytes 884744 | tf_op jit(solution)/shard_map/ppermute | solution.py:23
  49.0 13.7 %collective-permute-start.9 = (f32[9,2,32,128]{3,2,1,0:T(8,128)S(1)}, f32[9,2,32,128]{3,2,1,0:T(8,128)S(1)}, u32[]{:S(2)}, u32[]{:S(2)}) collective-permute-start(f32[9,2,32,128]{3,2,1,0:T(8,128)S(1)} %get-tuple-element.42), channel_id=1, source_target_pairs={{0,28},{4,0},{8,4},{12,8},{16,12},{20,16},{24,20},{28,24},{1,29},{... | collective-permute-start | bytes 884744 | tf_op jit(solution)/shard_map/ppermute | solution.py:23
  53.1 17.0 %copy-start.2 = (f32[128,128]{1,0:T(8,128)S(1)}, f32[128,128]{1,0:T(8,128)}, u32[]{:S(2)}) copy-start(f32[128,128]{1,0:T(8,128)} %constant.4.clone.refs_5_) | copy-start | bytes 196612
  62.9 4.6 %collective-permute-start.10 = (f32[9,12,2,128]{3,2,1,0:T(2,128)S(1)}, f32[9,12,2,128]{3,2,1,0:T(2,128)S(1)}, u32[]{:S(2)}, u32[]{:S(2)}) collective-permute-start(f32[9,12,2,128]{3,2,1,0:T(2,128)S(1)} %maximum_maximum_fusion), channel_id=1, source_target_pairs={{0,1},{1,2},{2,3},{3,0},{4,5},{5,6},{6,7},{7,4},{8,9},{9,10},{10,1... | collective-permute-start | bytes 331784 | tf_op jit(solution)/shard_map/ppermute | solution.py:23
  65.8 4.2 %collective-permute-start.11 = (f32[9,12,2,128]{3,2,1,0:T(2,128)S(1)}, f32[9,12,2,128]{3,2,1,0:T(2,128)S(1)}, u32[]{:S(2)}, u32[]{:S(2)}) collective-permute-start(f32[9,12,2,128]{3,2,1,0:T(2,128)S(1)} %maximum_maximum_fusion.1), channel_id=1, source_target_pairs={{0,3},{1,0},{2,1},{3,2},{4,7},{5,4},{6,5},{7,6},{8,11},{9,8},{10,9... | collective-permute-start | bytes 331784 | tf_op jit(solution)/shard_map/ppermute | solution.py:23
  70.1 16.9 %copy-start.3 = (f32[128,128]{1,0:T(8,128)S(1)}, f32[128,128]{1,0:T(8,128)}, u32[]{:S(2)}) copy-start(f32[128,128]{1,0:T(8,128)} %constant.14.clone.refs_5_) | copy-start | bytes 196612
  72.1 8.0 %collective-permute-start.12 = (f32[9,2,16,64]{3,2,1,0:T(8,128)S(1)}, f32[9,2,16,64]{3,2,1,0:T(8,128)S(1)}, u32[]{:S(2)}, u32[]{:S(2)}) collective-permute-start(f32[9,2,16,64]{3,2,1,0:T(8,128)S(1)} %get-tuple-element.53), channel_id=1, source_target_pairs={{0,4},{4,8},{8,12},{12,16},{16,20},{20,24},{24,28},{28,0},{1,5},{5... | collective-permute-start | bytes 221192 | tf_op jit(solution)/shard_map/ppermute | solution.py:23
  72.1 9.0 %collective-permute-start.13 = (f32[9,2,16,64]{3,2,1,0:T(8,128)S(1)}, f32[9,2,16,64]{3,2,1,0:T(8,128)S(1)}, u32[]{:S(2)}, u32[]{:S(2)}) collective-permute-start(f32[9,2,16,64]{3,2,1,0:T(8,128)S(1)} %get-tuple-element.54), channel_id=1, source_target_pairs={{0,28},{4,0},{8,4},{12,8},{16,12},{20,16},{24,20},{28,24},{1,29},{... | collective-permute-start | bytes 221192 | tf_op jit(solution)/shard_map/ppermute | solution.py:23
  81.3 3.2 %collective-permute-start.14 = (f32[9,8,2,64]{3,2,1,0:T(2,128)S(1)}, f32[9,8,2,64]{3,2,1,0:T(2,128)S(1)}, u32[]{:S(2)}, u32[]{:S(2)}) collective-permute-start(f32[9,8,2,64]{3,2,1,0:T(2,128)S(1)} %maximum_maximum_fusion.2), channel_id=1, source_target_pairs={{0,1},{1,2},{2,3},{3,0},{4,5},{5,6},{6,7},{7,4},{8,9},{9,10},{10,1... | collective-permute-start | bytes 110600 | tf_op jit(solution)/shard_map/ppermute | solution.py:23
  83.2 3.8 %collective-permute-start.15 = (f32[9,8,2,64]{3,2,1,0:T(2,128)S(1)}, f32[9,8,2,64]{3,2,1,0:T(2,128)S(1)}, u32[]{:S(2)}, u32[]{:S(2)}) collective-permute-start(f32[9,8,2,64]{3,2,1,0:T(2,128)S(1)} %maximum_maximum_fusion.3), channel_id=1, source_target_pairs={{0,3},{1,0},{2,1},{3,2},{4,7},{5,4},{6,5},{7,6},{8,11},{9,8},{10,9... | collective-permute-start | bytes 110600 | tf_op jit(solution)/shard_map/ppermute | solution.py:23

commit v8 on v5

--- a/solution.py
+++ b/solution.py
@@ -194,27 +194,23 @@
     return jnp.where(f < 3, f, one), jnp.where(f < 3, 3, two)
 
 
-def gather_rows(refs, rows_ref, even_ref, odd_ref):
-    edge_before, mid_before, edge_after, mid_after, row_before, row_after = refs
-    mid = mid_before.shape[2]
+def gather_rows(refs, first, rows_ref, even_ref, odd_ref):
+    edge, middle, row_before, row_after = refs
+    layers, mid = middle.shape[1:3]
     ny = mid + 16
     lanes = rows_ref.shape[2]
     count = ny // 2 + 16
     even_ref[3] = jnp.ones(even_ref.shape[1:], jnp.float32)
     odd_ref[3] = jnp.ones(odd_ref.shape[1:], jnp.float32)
     for c in range(3):
-        for layer in range(BEFORE + AFTER):
-            if layer < BEFORE:
-                edge, middle, at = edge_before, mid_before, layer
-            else:
-                edge, middle, at = edge_after, mid_after, layer - BEFORE
+        for layer in range(layers):
             for h in range(2):
                 cut = pl.ds(h * lanes, lanes)
-                rows_ref[h, 12:16, :] = row_before[c, layer, :, cut]
-                rows_ref[h, 16:24, :] = edge[c, at, 0:8, cut]
-                rows_ref[h, 24 : 24 + mid, :] = middle[c, at, :, cut]
-                rows_ref[h, 24 + mid : 32 + mid, :] = edge[c, at, 8:16, cut]
-                rows_ref[h, 16 + ny : 16 + ny + AFTER, :] = row_after[c, layer, :, cut]
+                rows_ref[h, 12:16, :] = row_before[c, first + layer, :, cut]
+                rows_ref[h, 16:24, :] = edge[c, layer, 0:8, cut]
+                rows_ref[h, 24 : 24 + mid, :] = middle[c, layer, :, cut]
+                rows_ref[h, 24 + mid : 32 + mid, :] = edge[c, layer, 8:16, cut]
+                rows_ref[h, 16 + ny : 16 + ny + AFTER, :] = row_after[c, first + layer, :, cut]
                 even_ref[c, layer, :, cut] = rows_ref[h, pl.ds(0, count, stride=2), :]
                 odd_ref[c, layer, :, cut] = rows_ref[h, pl.ds(1, count, stride=2), :]
 
@@ -223,26 +219,65 @@
     return halo_lift_list(layers[0::2], layers[1::2], *halo)
 
 
-def halo_stack(pairs, both, even_ref, odd_ref, part_ref, stack_ref):
+def halo_stack(pairs, both, combine, even_ref, odd_ref, part_ref, stack_ref):
     count, nz = even_ref.shape[2:]
     half, lanes = count - 16, nz // 2
-    kinds = 8 if both else 4
+    kinds = 4 if both else 2
     for n, (i, j) in enumerate(pairs):
         for h in range(2):
             cut = slice(h * lanes, (h + 1) * lanes)
             for parity, ref in enumerate((even_ref, odd_ref)):
                 for r in range(0, count, 16):
                     rows = slice(r, r + 16)
-                    g = [ref[i, layer, rows, cut] * ref[j, layer, rows, cut] for layer in range(BEFORE + AFTER)]
-                    for k, value in enumerate(parts_for_next(g[:BEFORE]) + parts_for_previous(g[BEFORE:])):
+                    g = [ref[i, layer, rows, cut] * ref[j, layer, rows, cut] for layer in range(ref.shape[1])]
+                    for k, value in enumerate(combine(g)):
                         part_ref[parity, k, rows, :] = value
-            for k in range(4):
+            for k in range(2):
                 e, o = ring_lift(part_ref[0, k], part_ref[1, k])
                 at = (kinds * n + k) * half
                 stack_ref[at : at + half, cut] = e[8 : 8 + half]
                 if both:
-                    at += 4 * half
+                    at += 2 * half
                     stack_ref[at : at + half, cut] = o[8 : 8 + half]
+
+
+def halo_kernel(*refs):
+    table_ref, low_ref, rest_ref = refs[4:7]
+    rows_ref, even_ref, odd_ref, part_ref, stack_ref = refs[7:]
+    half, lanes = low_ref.shape[2:]
+    gather_rows(refs[:4], 0, rows_ref, even_ref, odd_ref)
+
+    def group(g, carry):
+        pairs = [pair_of(g * GROUP + n) for n in range(GROUP)]
+        halo_stack(pairs, True, parts_for_next, even_ref, odd_ref, part_ref, stack_ref)
+        stack_ref[...] = dot(stack_ref[...], table_ref[...])
+        for n in range(GROUP):
+            for k in range(2):
+                low, high = (slice((4 * n + k + m) * half, (4 * n + k + m + 1) * half) for m in (0, 2))
+                low_ref[g * GROUP + n, k] = stack_ref[low, :lanes]
+                rest_ref[0, g * GROUP + n, k] = stack_ref[high, :lanes]
+                rest_ref[1, g * GROUP + n, k] = stack_ref[low, lanes:]
+                rest_ref[2, g * GROUP + n, k] = stack_ref[high, lanes:]
+        return carry
+
+    lax.fori_loop(0, 9 // GROUP, group, 0)
+
+
+def halo_pass(halo, table):
+    half, lanes = (halo[1].shape[2] + 16) // 2, halo[1].shape[3] // 2
+    vmem = pl.BlockSpec(memory_space=pltpu.VMEM)
+    return pl.pallas_call(
+        halo_kernel,
+        in_specs=[vmem] * 5,
+        out_specs=[vmem] * 2,
+        out_shape=[
+            jax.ShapeDtypeStruct((9, 2, half, lanes), jnp.float32),
+            jax.ShapeDtypeStruct((3, 9, 2, half, lanes), jnp.float32),
+        ],
+        scratch_shapes=halo_scratch(half, lanes, BEFORE, True),
+        compiler_params=pltpu.CompilerParams(vmem_limit_bytes=24 * MIB),
+        name="halo_pass",
+    )(*halo, table)
 
 
 def layer_list(refs, index, rows):
@@ -250,26 +285,27 @@
 
 
 def approx_kernel(*refs):
-    low_refs, table_ref = refs[:2], refs[2]
-    halo_refs = refs[3:9]
-    approx_ref, high_ref, stress_ref = refs[9:12]
-    next_ref, prev_ref, next_edge_ref, prev_edge_ref, down_ref, up_ref = refs[12:18]
-    rows_ref, even_ref, odd_ref, kept_ref, part_ref, stack_ref, out_ref = refs[18:]
+    low_refs, before_ref, table_ref = refs[:2], refs[2], refs[3]
+    halo_refs = refs[4:8]
+    approx_ref, high_ref, stress_ref = refs[8:11]
+    next_ref, prev_ref, next_edge_ref, prev_edge_ref, down_ref, up_ref = refs[11:17]
+    rows_ref, even_ref, odd_ref, part_ref, stack_ref, kept_ref, out_ref = refs[17:]
     f = pl.program_id(0)
     half, lanes = low_refs[0].shape[2:]
     mx = approx_ref.shape[1]
 
     @pl.when(f == 0)
     def _():
-        gather_rows(halo_refs, rows_ref, even_ref, odd_ref)
+        gather_rows(halo_refs, BEFORE, rows_ref, even_ref, odd_ref)
 
     pairs = [pair_of(f * GROUP + n) for n in range(GROUP)]
-    halo_stack(pairs, False, even_ref, odd_ref, part_ref, stack_ref)
+    halo_stack(pairs, False, parts_for_previous, even_ref, odd_ref, part_ref, stack_ref)
     out_ref[...] = dot(stack_ref[...], table_ref[:, :lanes])
     for n in range(GROUP):
         for r in range(0, half, 8):
             rows = slice(r, r + 8)
-            halo = [out_ref[(4 * n + k) * half + r : (4 * n + k) * half + r + 8, :] for k in range(4)]
+            halo = [before_ref[n, k, rows, :] for k in range(2)]
+            halo += [out_ref[(2 * n + k) * half + r : (2 * n + k) * half + r + 8, :] for k in range(2)]
             e, o = lift_first(layer_list(low_refs, (n,), rows), halo)
             e = [t * band_scale(0, 0) for t in e]
             for x in range(mx):
@@ -302,15 +338,17 @@
     return pl.BlockSpec((GROUP,) + shape, lambda f: (f,) + (0,) * len(shape))
 
 
-def approx_pass(lows, halo, table):
+def approx_pass(lows, before, halo, table):
     _, nx, half, lanes = lows[0].shape
-    nz, count, mx = 2 * lanes, half + 16, nx
+    nz, mx = 2 * lanes, nx
     f32 = lambda *shape: jax.ShapeDtypeStruct(shape, jnp.float32)
     sends = [(2, half, lanes), (2, half, lanes), (2, 4, lanes), (2, 4, lanes), (mx, 2, lanes), (mx, 2, lanes)]
     return pl.pallas_call(
         approx_kernel,
         grid=(9 // GROUP,),
-        in_specs=[per_field((nx, half, lanes))] * 2 + [whole((nz, nz))] + [whole(h.shape) for h in halo],
+        in_specs=[per_field((nx, half, lanes))] * 2
+        + [per_field((2, half, lanes)), whole((nz, nz))]
+        + [whole(h.shape) for h in halo],
         out_specs=[
             per_field((mx, half, lanes)),
             per_field((mx, half, lanes)),
@@ -318,40 +356,40 @@
         ]
         + [per_field(s) for s in sends],
         out_shape=[f32(9, mx, half, lanes), f32(9, mx, half, lanes), f32(6, mx, half, lanes)] + [f32(9, *s) for s in sends],
-        scratch_shapes=halo_scratch(half, lanes)
+        scratch_shapes=halo_scratch(half, lanes, AFTER, False)
         + [
             pltpu.VMEM((3, mx, half, lanes), jnp.float32),
-            pltpu.VMEM((2, 4, count, lanes), jnp.float32),
-            pltpu.VMEM((GROUP * 4 * half, nz), jnp.float32),
-            pltpu.VMEM((GROUP * 4 * half, lanes), jnp.float32),
+            pltpu.VMEM((GROUP * 2 * half, lanes), jnp.float32),
         ],
         compiler_params=pltpu.CompilerParams(vmem_limit_bytes=24 * MIB),
         name="approx_pass",
-    )(*lows, table, *halo)
-
-
-def halo_scratch(half, lanes):
+    )(*lows, before, table, *halo)
+
+
+def halo_scratch(half, lanes, layers, both):
     return [
         pltpu.VMEM((2, 2 * half + 32, lanes), jnp.float32),
-        pltpu.VMEM((4, BEFORE + AFTER, half + 16, 2 * lanes), jnp.float32),
-        pltpu.VMEM((4, BEFORE + AFTER, half + 16, 2 * lanes), jnp.float32),
+        pltpu.VMEM((4, layers, half + 16, 2 * lanes), jnp.float32),
+        pltpu.VMEM((4, layers, half + 16, 2 * lanes), jnp.float32),
+        pltpu.VMEM((2, 2, half + 16, lanes), jnp.float32),
+        pltpu.VMEM((GROUP * (4 if both else 2) * half, 2 * lanes), jnp.float32),
     ]
 
 
 def detail_kernel(*refs):
-    rest_refs, high_ref, table_ref = refs[:2], refs[2], refs[3]
-    halo_refs = refs[4:10]
-    out_ref, rows_ref, even_ref, odd_ref, part_ref, stack_ref = refs[10:]
+    rest_refs, before_ref, high_ref, table_ref = refs[:2], refs[2], refs[3], refs[4]
+    halo_refs = refs[5:9]
+    out_ref, rows_ref, even_ref, odd_ref, part_ref, stack_ref = refs[9:]
     f = pl.program_id(0)
     half, lanes = high_ref.shape[2:]
     mx = high_ref.shape[1]
 
     @pl.when(f == 0)
     def _():
-        gather_rows(halo_refs, rows_ref, even_ref, odd_ref)
+        gather_rows(halo_refs, BEFORE, rows_ref, even_ref, odd_ref)
 
     pairs = [pair_of(f * GROUP + n) for n in range(GROUP)]
-    halo_stack(pairs, True, even_ref, odd_ref, part_ref, stack_ref)
+    halo_stack(pairs, True, parts_for_previous, even_ref, odd_ref, part_ref, stack_ref)
     stack_ref[...] = dot(stack_ref[...], table_ref[...])
     for n in range(GROUP):
         for x in range(mx):
@@ -360,9 +398,9 @@
             plane = 4 * bz + 2 * by - 1
             for r in range(0, half, 8):
                 rows = slice(r, r + 8)
-                halo = []
-                for k in range(4):
-                    at = (8 * n + 4 * by + k) * half + r
+                halo = [before_ref[band, n, k, rows, :] for k in range(2)]
+                for k in range(2):
+                    at = (4 * n + 2 * by + k) * half + r
                     halo.append(stack_ref[at : at + 8, bz * lanes : (bz + 1) * lanes])
                 e, o = lift_first(layer_list(rest_refs, (band, n), rows), halo)
                 for x in range(mx):
@@ -370,35 +408,34 @@
                     out_ref[plane + 1, n, x, rows, :] = o[x] * band_scale(by, 1)
 
 
-def detail_pass(rests, high, halo, table):
+def detail_pass(rests, before, high, halo, table):
     _, mx, half, lanes = high.shape
-    nz, count = 2 * lanes, half + 16
+    nz = 2 * lanes
     return pl.pallas_call(
         detail_kernel,
         grid=(9 // GROUP,),
         in_specs=[pl.BlockSpec((3, GROUP, mx, half, lanes), lambda f: (0, f, 0, 0, 0))] * 2
-        + [per_field((mx, half, lanes)), whole((nz, nz))]
+        + [pl.BlockSpec((3, GROUP, 2, half, lanes), lambda f: (0, f, 0, 0, 0)), per_field((mx, half, lanes)), whole((nz, nz))]
         + [whole(h.shape) for h in halo],
         out_specs=pl.BlockSpec((7, GROUP, mx, half, lanes), lambda f: (0, f, 0, 0, 0)),
         out_shape=jax.ShapeDtypeStruct((7, 9, mx, half, lanes), jnp.float32),
-        scratch_shapes=halo_scratch(half, lanes)
-        + [pltpu.VMEM((2, 4, count, lanes), jnp.float32), pltpu.VMEM((GROUP * 8 * half, nz), jnp.float32)],
+        scratch_shapes=halo_scratch(half, lanes, AFTER, True),
         compiler_params=pltpu.CompilerParams(vmem_limit_bytes=24 * MIB),
         cost_estimate=pl.CostEstimate(flops=18 * mx * half * nz * 200, bytes_accessed=18 * mx * half * nz * 16, transcendentals=0),
         name="detail_pass",
-    )(*rests, high, table, *halo)
-
-
-def level_rows(refs, nz, lows, pad_ref, stack_ref):
+    )(*rests, before, high, table, *halo)
+
+
+def level_rows(refs, nz, nx, span, lows, pad_ref, stack_ref):
     a_ref, before_ref, after_ref, down_ref, up_ref = refs
-    nx, ny = a_ref.shape[1:3]
+    ny = (before_ref if a_ref is None else a_ref).shape[2]
     half = ny // 2
     wide = stack_ref.shape[1]
     kept = half if lows else ny
     if nz < wide:
         pad_ref[...] = jnp.zeros_like(pad_ref)
     for f in range(9):
-        for layer in range(nx + 4):
+        for step, layer in enumerate(span):
             if layer < nx:
                 source, at = a_ref, layer
             elif layer < nx + 2:
@@ -414,28 +451,34 @@
             if nz < wide:
                 rows = [jnp.concatenate([row, jnp.zeros((1, wide - nz), jnp.float32)], axis=1) for row in rows]
             e, o = sublane_lift(e, o, *rows)
-            at = (f * (nx + 4) + layer) * kept
+            at = (f * len(span) + step) * kept
             stack_ref[at : at + half, :] = e
             if not lows:
                 stack_ref[at + half : at + ny, :] = o
 
 
+def level_own_kernel(nz, a_ref, down_ref, up_ref, table_ref, own_ref, stack_ref):
+    nx, _ = a_ref.shape[1:3]
+    level_rows((a_ref, None, None, down_ref, up_ref), nz, nx, range(nx), True, None, stack_ref)
+    own_ref[...] = dot(stack_ref[...], table_ref[...]).reshape(own_ref.shape)
+
+
 def level_approx_kernel(nz, *refs):
-    table_ref, approx_ref, stress_ref = refs[5:8]
-    sends, (pad_ref, stack_ref, out_ref, kept_ref) = refs[8:-4], refs[-4:]
-    nx, ny = refs[0].shape[1:3]
-    half, lanes = ny // 2, nz // 2
-    level_rows(refs[:5], nz, True, pad_ref, stack_ref)
+    own_ref, table_ref, approx_ref, stress_ref = refs[0], refs[5], refs[6], refs[7]
+    sends, (stack_ref, out_ref, kept_ref) = refs[8:-3], refs[-3:]
+    nx, half = own_ref.shape[1:3]
+    lanes = nz // 2
+    level_rows((None,) + refs[1:5], nz, nx, range(nx, nx + 4), True, None, stack_ref)
     out_ref[...] = dot(stack_ref[...], table_ref[...])
     mx = nx // 2
     for f in range(9):
         for r in range(0, half, 8):
             rows = slice(r, r + 8)
-            layers = []
-            for layer in range(nx + 4):
-                at = (f * (nx + 4) + layer) * half + r
-                layers.append(out_ref[at : at + 8, :])
-            low, _ = lift_first(layers[:nx], layers[nx:])
+            halo = []
+            for k in range(4):
+                at = (f * 4 + k) * half + r
+                halo.append(out_ref[at : at + 8, :])
+            low, _ = lift_first([own_ref[f, x, rows, :] for x in range(nx)], halo)
             approx = [(t * band_scale(0, 0))[:, :lanes] for t in low]
             for x in range(mx):
                 if f < 3:
@@ -454,7 +497,7 @@
     nx, ny = refs[0].shape[1:3]
     half, lanes = ny // 2, nz // 2
     wide = stack_ref.shape[1]
-    level_rows(refs[:5], nz, False, pad_ref, stack_ref)
+    level_rows(refs[:5], nz, nx, range(nx + 4), False, pad_ref, stack_ref)
     out_ref[...] = dot(stack_ref[...], table_ref[...])
     for f in range(9):
         for by in range(2):
@@ -506,9 +549,33 @@
     _, nx, ny, nz = approx.shape
     mx, half, lanes = nx // 2, ny // 2, nz // 2
     f32 = lambda *shape: jax.ShapeDtypeStruct(shape, jnp.float32)
+    vmem = pl.BlockSpec(memory_space=pltpu.VMEM)
+    params = pltpu.CompilerParams(vmem_limit_bytes=24 * MIB)
+    table = jnp.asarray(third_table(nz, nz))
+    own = pl.pallas_call(
+        lambda *refs: level_own_kernel(nz, *refs),
+        in_specs=[vmem] * 4,
+        out_specs=vmem,
+        out_shape=f32(9, nx, half, nz),
+        scratch_shapes=[pltpu.VMEM((9 * nx * half, nz), jnp.float32)],
+        compiler_params=params,
+        name="level_own",
+    )(approx, *halo[2:], table)
     sends = ((2, half, lanes), (2, half, lanes), (mx, 2, lanes), (mx, 2, lanes))
     out = [f32(9, mx, half, lanes), f32(6, mx, half, lanes)] + [f32(9, *s) for s in sends]
-    return level_call(lambda *refs: level_approx_kernel(nz, *refs), approx, halo, out, half)
+    return pl.pallas_call(
+        lambda *refs: level_approx_kernel(nz, *refs),
+        in_specs=[vmem] * 6,
+        out_specs=[vmem] * len(out),
+        out_shape=out,
+        scratch_shapes=[
+            pltpu.VMEM((9 * 4 * half, nz), jnp.float32),
+            pltpu.VMEM((9 * 4 * half, nz), jnp.float32),
+            pltpu.VMEM((3, mx, half, lanes), jnp.float32),
+        ],
+        compiler_params=params,
+        name="level_approx",
+    )(own, *halo, table)
 
 
 def level_details(approx, halo, last):
@@ -559,10 +626,11 @@
     row_before = shifted(down, "gy", 1)
     row_after = shifted(up, "gy", -1)
     low_two, rest_two = local_pass(velocity, own_before, own_after, table, nx // 2)
-    halo = (edge_before, mid_before, edge_after, mid_after, row_before, row_after)
-    approx, high, stress_one, *sends = approx_pass((low_one, low_two), halo, table)
+    low_before, rest_before = halo_pass((edge_before, mid_before, row_before, row_after), table)
+    halo = (edge_after, mid_after, row_before, row_after)
+    approx, high, stress_one, *sends = approx_pass((low_one, low_two), low_before, halo, table)
     second_halo = exchange(*sends)
-    details_one = detail_pass((rest_one, rest_two), high, halo, table)
+    details_one = detail_pass((rest_one, rest_two), rest_before, high, halo, table)
     approx, details_one = lax.optimization_barrier((approx, details_one))
     second = approx
     approx, stress_two, *sends = level_approx(second, second_halo)

time: 87.4 us -> 87.7 us (level)
    pallas_call x0 -> x3, Pallas kernels: none -> 4.07 us  [the longest x1 1.91 us: halo_pass(): pl.pallas_call(halo_kernel, in_specs=[vmem] * 5, out_specs=[vmem] * 2, ou...]
    pallas_call x3 -> x2, Pallas kernels: 6.46 us -> 4.49 us  [level_call(): pl.pallas_call(kernel, in_specs=[vmem] * 6, out_specs=[vmem] * len(out),...]
    pallas_call x1, Pallas kernels: 4.18 us -> 3.24 us  [approx_pass(): pl.pallas_call(approx_kernel, grid=(9 // GROUP,), in_specs=[per_field((nx...]
  transfers between devices with their start and end apart: 18 -> 18, of which waited for: 6 -> 6; matrix products, arithmetic and copies ran while one was open for 5% -> 5% of each run, Pallas kernels for 23% -> 26%
where the time goes in v8:
time: 87.7 us; the launch traced here: 86.5 us
  starting transfers between devices  32.5 us (37%)
  Pallas kernels  28.2 us (32%)
  waiting for transfers between devices  18.9 us (22%)
  local copies, waits for them, and re-layouts  5.52 us (6%)
  between operations  0.95 us (1%)
    ppermute x18, starting transfers between devices, shifted(): lax.ppermute(block, axis, [(i, (i + distance) % size) for i in range(size)])  32.5 us
    ppermute x18, waiting for transfers between devices, shifted(): lax.ppermute(block, axis, [(i, (i + distance) % size) for i in range(size)])  18.9 us
    pallas_call x2, Pallas kernels, local_pass(): pl.pallas_call(local_kernel, grid=(nx,), in_specs=[pl.BlockSpec((3, 1, ny...  10.9 us
    pallas_call x1, Pallas kernels, detail_pass(): pl.pallas_call(detail_kernel, grid=(9 // GROUP,), in_specs=[pl.BlockSpec(...  5.58 us
    pallas_call x2, Pallas kernels, level_call(): pl.pallas_call(kernel, in_specs=[vmem] * 6, out_specs=[vmem] * len(out),...  4.49 us
    pallas_call x1, Pallas kernels, approx_pass(): pl.pallas_call(approx_kernel, grid=(9 // GROUP,), in_specs=[per_field((nx...  3.24 us
    pallas_call x1, Pallas kernels, halo_pass(): pl.pallas_call(halo_kernel, in_specs=[vmem] * 5, out_specs=[vmem] * 2, ou...  1.91 us
  transfers between devices with their start and end apart: 18, of which 6 were waited for; matrix products, arithmetic and copies ran while one was open for 5% of the time, Pallas kernels for 26%

profile of v8, /device:TPU:0, one launch (start us, length us, event | category | flops | bytes accessed | tf_op | source)
XLA Modules:
  0.0 86.5 jit_solution(15842066390272757478)
XLA Ops:
  0.6 0.0 copy-start.1
  0.6 0.0 copy-start
  0.7 1.1 %fusion.6 = (f32[3,4,8,256]{3,2,1,0:T(8,128)S(1)}, f32[3,4,8,256]{3,2,1,0:T(8,128)S(1)}) fusion(f32[3,16,64,256]{3,2,1,0:T(8,128)} %v_ref.3), kind=kLoop, calls=%fused_computation.19 | loop fusion | bytes 393216 | tf_op jit(solution)/shard_map/slice | solution.py:615
  1.8 3.0 %collective-permute-start = (f32[3,4,16,256]{3,2,1,0:T(8,128)S(1)}, f32[3,4,16,256]{3,2,1,0:T(8,128)S(1)}, u32[]{:S(2)}, u32[]{:S(2)}) collective-permute-start(f32[3,4,16,256]{3,2,1,0:T(8,128)S(1)} %pad_maximum_fusion), channel_id=1, source_target_pairs={{0,4},{4,8},{8,12},{12,16},{16,20},{20,24},{24,28},{28,0},{1,5},{5... | collective-permute-start | bytes 589832 | tf_op jit(solution)/shard_map/ppermute | solution.py:23
  4.8 1.0 %slice.102 = f32[3,16,4,256]{3,2,1,0:T(4,128)S(1)} slice(f32[3,16,64,256]{3,2,1,0:T(8,128)} %v_ref.3), slice={[0:3], [0:16], [60:64], [0:256]} | slice | bytes 393216 | tf_op jit(solution)/shard_map/slice | solution.py:620
  5.9 0.1 collective-permute-start.2
  5.9 1.0 %slice.103 = f32[3,16,3,256]{3,2,1,0:T(4,128)S(1)} slice(f32[3,16,64,256]{3,2,1,0:T(8,128)} %v_ref.3), slice={[0:3], [0:16], [0:3], [0:256]} | slice | bytes 294912 | tf_op jit(solution)/shard_map/slice | solution.py:621
  6.9 1.8 %collective-permute-start.3 = (f32[3,16,3,256]{3,2,1,0:T(4,128)S(1)}, f32[3,16,3,256]{3,2,1,0:T(4,128)S(1)}, u32[]{:S(2)}, u32[]{:S(2)}) collective-permute-start(f32[3,16,3,256]{3,2,1,0:T(4,128)S(1)} %slice.103), channel_id=1, source_target_pairs={{0,3},{1,0},{2,1},{3,2},{4,7},{5,4},{6,5},{7,6},{8,11},{9,8},{10,9... | collective-permute-start | bytes 442376 | tf_op jit(solution)/shard_map/ppermute | solution.py:23
  8.7 1.0 %slice.109 = f32[3,3,48,256]{3,2,1,0:T(8,128)S(1)} slice(f32[3,16,64,256]{3,2,1,0:T(8,128)} %v_ref.3), slice={[0:3], [0:3], [8:56], [0:256]} | slice | bytes 884736 | tf_op jit(solution)/shard_map/slice | solution.py:619
  9.8 3.1 %collective-permute-start.7 = (f32[3,3,48,256]{3,2,1,0:T(8,128)S(1)}, f32[3,3,48,256]{3,2,1,0:T(8,128)S(1)}, u32[]{:S(2)}, u32[]{:S(2)}) collective-permute-start(f32[3,3,48,256]{3,2,1,0:T(8,128)S(1)} %slice.109), channel_id=1, source_target_pairs={{0,28},{4,0},{8,4},{12,8},{16,12},{20,16},{24,20},{28,24},{1,29},{... | collective-permute-start | bytes 1327112 | tf_op jit(solution)/shard_map/ppermute | solution.py:23
  12.9 1.1 %slice.104 = f32[3,4,48,256]{3,2,1,0:T(8,128)S(1)} slice(f32[3,16,64,256]{3,2,1,0:T(8,128)} %v_ref.3), slice={[0:3], [12:16], [8:56], [0:256]} | slice | bytes 1179648 | tf_op jit(solution)/shard_map/slice | solution.py:618
  14.0 0.1 collective-permute-start.4
  14.1 4.7 %collective-permute-start.1 = (f32[3,3,16,256]{3,2,1,0:T(8,128)S(1)}, f32[3,3,16,256]{3,2,1,0:T(8,128)S(1)}, u32[]{:S(2)}, u32[]{:S(2)}) collective-permute-start(f32[3,3,16,256]{3,2,1,0:T(8,128)S(1)} %pad_maximum_fusion.1), channel_id=1, source_target_pairs={{0,28},{4,0},{8,4},{12,8},{16,12},{20,16},{24,20},{28,24},{1,29},{... | collective-permute-start | bytes 442376 | tf_op jit(solution)/shard_map/ppermute | solution.py:23
  18.9 5.4 %local_pass.2 = (f32[9,8,32,128]{3,2,1,0:T(8,128)S(1)}, f32[3,9,8,32,128]{4,3,2,1,0:T(8,128)S(1)}) custom-call(f32[3,16,64,256]{3,2,1,0:T(8,128)S(1)} %copy-done, f32[3,16,4,256]{3,2,1,0:T(4,128)S(1)} %collective-permute-done.2.before_ref, f32[3,16,3,256]{3,2,1,0:T(4,128)S(1)} %collective-permute-done.3.after_ref, f32[256,256]{1,0:T(8,128)S(1)} %copy-done.1), custom_call_target="tpu_custom_call" | custom-call | flops 603979776 | bytes 7077888 | tf_op jit(solution)/shard_map/local_pass/pallas_call | solution.py:166
  24.3 13.7 %collective-permute-done.1.refs_4_.refs_5_ = f32[3,3,16,256]{3,2,1,0:T(8,128)S(1)} collective-permute-done((f32[3,3,16,256]{3,2,1,0:T(8,128)S(1)}, f32[3,3,16,256]{3,2,1,0:T(8,128)S(1)}, u32[]{:S(2)}, u32[]{:S(2)}) %collective-permute-start.1) | collective-permute-done | bytes 147488 | tf_op jit(solution)/shard_map/ppermute | solution.py:23
  38.0 0.0 collective-permute-done.refs_0_
  38.1 0.1 collective-permute-start.5
  38.2 1.8 %collective-permute-start.6 = (f32[3,7,3,256]{3,2,1,0:T(4,128)S(1)}, f32[3,7,3,256]{3,2,1,0:T(4,128)S(1)}, u32[]{:S(2)}, u32[]{:S(2)}) collective-permute-start(f32[3,7,3,256]{3,2,1,0:T(4,128)S(1)} %pad_maximum_fusion.5), channel_id=1, source_target_pairs={{0,3},{1,0},{2,1},{3,2},{4,7},{5,4},{6,5},{7,6},{8,11},{9,8},{10,9... | collective-permute-start | bytes 193544 | tf_op jit(solution)/shard_map/ppermute | solution.py:23
  40.0 5.4 %local_pass.3 = (f32[9,8,32,128]{3,2,1,0:T(8,128)S(1)}, f32[3,9,8,32,128]{4,3,2,1,0:T(8,128)S(1)}) custom-call(f32[3,16,64,256]{3,2,1,0:T(8,128)S(1)} %copy-done, f32[3,16,4,256]{3,2,1,0:T(4,128)S(1)} %collective-permute-done.2.before_ref, f32[3,16,3,256]{3,2,1,0:T(4,128)S(1)} %collective-permute-done.3.after_ref, f32[256,256]{1,0:T(8,128)S(1)} %copy-done.1), custom_call_target="tpu_custom_call" | custom-call | flops 603979776 | bytes 7077888 | tf_op jit(solution)/shard_map/local_pass/pallas_call | solution.py:166
  45.5 0.0 collective-permute-done.6.refs_3_.refs_7_.refs_8_
  45.5 1.9 %halo_pass.1 = (f32[9,2,32,128]{3,2,1,0:T(8,128)S(1)}, f32[3,9,2,32,128]{4,3,2,1,0:T(8,128)S(1)}) custom-call(f32[3,4,16,256]{3,2,1,0:T(8,128)S(1)} %collective-permute-done.refs_0_, f32[3,4,48,256]{3,2,1,0:T(8,128)S(1)} %collective-permute-done.4.refs_1_, f32[3,7,4,256]{3,2,1,0:T(4,128)S(1)} %collective-permute-done.5.refs_2_.refs_6_.refs_7_, ...), custom_call_target="tpu_custom_call" | custom-call | tf_op jit(solution)/shard_map/halo_pass/pallas_call | solution.py:269
  47.4 3.2 %approx_pass.1 = (f32[9,8,32,128]{3,2,1,0:T(8,128)S(1)}, f32[9,8,32,128]{3,2,1,0:T(8,128)S(1)}, f32[6,8,32,128]{3,2,1,0:T(8,128)}, f32[9,2,32,128]{3,2,1,0:T(8,1...) custom-call(f32[9,8,32,128]{3,2,1,0:T(8,128)S(1)} %get-tuple-element, ...), custom_call_target="tpu_custom_call" | custom-call | tf_op jit(solution)/shard_map/approx_pass/pallas_call | solution.py:346
  50.7 4.7 %collective-permute-start.9 = (f32[9,2,4,128]{3,2,1,0:T(4,128)S(1)}, f32[9,2,4,128]{3,2,1,0:T(4,128)S(1)}, u32[]{:S(2)}, u32[]{:S(2)}) collective-permute-start(f32[9,2,4,128]{3,2,1,0:T(4,128)S(1)} %get-tuple-element.55), channel_id=1, source_target_pairs={{0,28},{4,0},{8,4},{12,8},{16,12},{20,16},{24,20},{28,24},{1,29},{... | collective-permute-start | bytes 110600 | tf_op jit(solution)/shard_map/ppermute | solution.py:23
  55.4 4.7 %collective-permute-start.13 = (f32[9,2,32,128]{3,2,1,0:T(8,128)S(1)}, f32[9,2,32,128]{3,2,1,0:T(8,128)S(1)}, u32[]{:S(2)}, u32[]{:S(2)}) collective-permute-start(f32[9,2,32,128]{3,2,1,0:T(8,128)S(1)} %get-tuple-element.58), channel_id=1, source_target_pairs={{0,28},{4,0},{8,4},{12,8},{16,12},{20,16},{24,20},{28,24},{1,29},{... | collective-permute-start | bytes 884744 | tf_op jit(solution)/shard_map/ppermute | solution.py:23
  60.2 0.1 pad_maximum_fusion.2
  60.2 0.1 collective-permute-start.10
  60.3 0.1 pad_maximum_fusion.3
  60.3 1.8 %collective-permute-start.11 = (f32[9,12,2,128]{3,2,1,0:T(2,128)S(1)}, f32[9,12,2,128]{3,2,1,0:T(2,128)S(1)}, u32[]{:S(2)}, u32[]{:S(2)}) collective-permute-start(f32[9,12,2,128]{3,2,1,0:T(2,128)S(1)} %pad_maximum_fusion.3), channel_id=1, source_target_pairs={{0,3},{1,0},{2,1},{3,2},{4,7},{5,4},{6,5},{7,6},{8,11},{9,8},{10,9... | collective-permute-start | bytes 331784 | tf_op jit(solution)/shard_map/ppermute | solution.py:23
  62.1 5.6 %detail_pass.1 = f32[7,9,8,32,128]{4,3,2,1,0:T(8,128)} custom-call(f32[3,9,8,32,128]{4,3,2,1,0:T(8,128)S(1)} %get-tuple-element.46.refs_0_, f32[3,9,8,32,128]{4,3,2,1,0:T(8,128)S(1)} %get-tuple-element.47.refs_1_, f32[3,9,2,32,128]{4,3,2,1,0:T(8,128)S(1)} %get-tuple-element.48.refs_2_, f32[9,8,32,128]{3,2,1,0:T(8,128)S(1)} %get-tuple-element.49.refs_3_, ...), custom_call_target="tpu_custom_call" | custom-call | flops 235929600 | bytes 18874368 | tf_op jit(solution)/shard_map/detail_pass/pallas_call | solution.py:414
  67.7 0.8 level_own.1.refs_0_
  68.6 0.0 copy-start.3
  68.6 1.4 %collective-permute-done.13.refs_2_ = f32[9,2,32,128]{3,2,1,0:T(8,128)S(1)} collective-permute-done((f32[9,2,32,128]{3,2,1,0:T(8,128)S(1)}, f32[9,2,32,128]{3,2,1,0:T(8,128)S(1)}, u32[]{:S(2)}, u32[]{:S(2)}) %collective-permute-start.13) | collective-permute-done | bytes 294944 | tf_op jit(solution)/shard_map/ppermute | solution.py:23
  70.0 1.3 %level_approx.1 = (f32[9,4,16,64]{3,2,1,0:T(8,128)S(1)}, f32[6,4,16,64]{3,2,1,0:T(8,128)}, f32[9,2,16,64]{3,2,1,0:T(8,128)S(1)}, f32[9,2,16,64]{3,2,1,0:T(8,128)...) custom-call(f32[9,8,16,128]{3,2,1,0:T(8,128)S(1)} %level_own.1.refs_0_, ...), custom_call_target="tpu_custom_call" | custom-call | tf_op jit(solution)/shard_map/level_approx/pallas_call | solution.py:566
  71.3 0.7 collective-permute-start.14
  72.0 4.0 %collective-permute-start.15 = (f32[9,2,16,64]{3,2,1,0:T(8,128)S(1)}, f32[9,2,16,64]{3,2,1,0:T(8,128)S(1)}, u32[]{:S(2)}, u32[]{:S(2)}) collective-permute-start(f32[9,2,16,64]{3,2,1,0:T(8,128)S(1)} %get-tuple-element.60), channel_id=1, source_target_pairs={{0,28},{4,0},{8,4},{12,8},{16,12},{20,16},{24,20},{28,24},{1,29},{... | collective-permute-start | bytes 221192 | tf_op jit(solution)/shard_map/ppermute | solution.py:23
  76.0 2.9 %shard_map.108 = f32[7,9,4,16,64]{4,3,2,1,0:T(8,128)} custom-call(f32[9,8,32,128]{3,2,1,0:T(8,128)S(1)} %get-tuple-element.52.refs_0_, f32[9,2,32,128]{3,2,1,0:T(8,128)S(1)} %collective-permute-done.12.refs_1_, f32[9,2,32,128]{3,2,1,0:T(8,128)S(1)} %collective-permute-done.13.refs_2_, f32[9,12,2,128]{3,2,1,0:T(2,128)S(1)} %collective-permute-done.10.refs_1_.refs_3_, ...), custom_call_target="tpu_custom_call" | custom-call | tf_op jit(solution)/shard_map/pallas_call | solution.py:533
  78.9 0.3 collective-permute-done.14.refs_1_
  79.2 1.4 %collective-permute-done.15.refs_2_ = f32[9,2,16,64]{3,2,1,0:T(8,128)S(1)} collective-permute-done((f32[9,2,16,64]{3,2,1,0:T(8,128)S(1)}, f32[9,2,16,64]{3,2,1,0:T(8,128)S(1)}, u32[]{:S(2)}, u32[]{:S(2)}) %collective-permute-start.15) | collective-permute-done | bytes 73760 | tf_op jit(solution)/shard_map/ppermute | solution.py:23
  80.7 0.1 fusion.7
  80.8 0.1 fusion.1
  80.9 0.1 maximum_maximum_fusion
  80.9 0.1 collective-permute-start.16
  81.0 0.1 fusion.4
  81.1 0.1 maximum_maximum_fusion.1
  81.1 1.8 %collective-permute-start.17 = (f32[9,8,2,64]{3,2,1,0:T(2,128)S(1)}, f32[9,8,2,64]{3,2,1,0:T(2,128)S(1)}, u32[]{:S(2)}, u32[]{:S(2)}) collective-permute-start(f32[9,8,2,64]{3,2,1,0:T(2,128)S(1)} %maximum_maximum_fusion.1), channel_id=1, source_target_pairs={{0,3},{1,0},{2,1},{3,2},{4,7},{5,4},{6,5},{7,6},{8,11},{9,8},{10,9... | collective-permute-start | bytes 110600 | tf_op jit(solution)/shard_map/ppermute | solution.py:23
  82.9 1.8 %collective-permute-done.16.refs_3_ = f32[9,8,2,64]{3,2,1,0:T(2,128)S(1)} collective-permute-done((f32[9,8,2,64]{3,2,1,0:T(2,128)S(1)}, f32[9,8,2,64]{3,2,1,0:T(2,128)S(1)}, u32[]{:S(2)}, u32[]{:S(2)}) %collective-permute-start.16) | collective-permute-done | bytes 36896 | tf_op jit(solution)/shard_map/ppermute | solution.py:23
  84.8 0.1 collective-permute-done.17.refs_4_
  84.9 1.6 %shard_map.109 = (f32[7,9,2,8,32]{4,3,2,1,0:T(8,128)}, f32[6,2,8,32]{3,2,1,0:T(8,128)}, f32[3,2,8,32]{3,2,1,0:T(8,128)}) custom-call(f32[9,4,16,64]{3,2,1,0:T(8,128)S(1)} %get-tuple-element.63.refs_0_, f32[9,2,16,64]{3,2,1,0:T(8,128)S(1)} %collective-permute-done.14.refs_1_, f32[9,2,16,64]{3,2,1,0:T(8,128)S(1)} %collective-permute-done.15.refs_2_, ...), custom_call_target="tpu_custom_call" | custom-call | tf_op jit(solution)/shard_map/pallas_call | solution.py:533
  (28 shorter events, 0.2 us)
Async XLA Ops:
  0.6 18.3 %copy-start.1 = (f32[256,256]{1,0:T(8,128)S(1)}, f32[256,256]{1,0:T(8,128)}, u32[]{:S(2)}) copy-start(f32[256,256]{1,0:T(8,128)} %constant.10.clone.table_ref.refs_4_.refs_3_) | copy-start | bytes 786436
  0.6 13.4 %copy-start = (f32[3,16,64,256]{3,2,1,0:T(8,128)S(1)}, f32[3,16,64,256]{3,2,1,0:T(8,128)}, u32[]{:S(2)}) copy-start(f32[3,16,64,256]{3,2,1,0:T(8,128)} %v_ref.3) | copy-start | bytes 9437188
  1.8 36.2 %collective-permute-start = (f32[3,4,16,256]{3,2,1,0:T(8,128)S(1)}, f32[3,4,16,256]{3,2,1,0:T(8,128)S(1)}, u32[]{:S(2)}, u32[]{:S(2)}) collective-permute-start(f32[3,4,16,256]{3,2,1,0:T(8,128)S(1)} %pad_maximum_fusion), channel_id=1, source_target_pairs={{0,4},{4,8},{8,12},{12,16},{16,20},{20,24},{24,28},{28,0},{1,5},{5... | collective-permute-start | bytes 589832 | tf_op jit(solution)/shard_map/ppermute | solution.py:23
  5.9 13.0 %collective-permute-start.2 = (f32[3,16,4,256]{3,2,1,0:T(4,128)S(1)}, f32[3,16,4,256]{3,2,1,0:T(4,128)S(1)}, u32[]{:S(2)}, u32[]{:S(2)}) collective-permute-start(f32[3,16,4,256]{3,2,1,0:T(4,128)S(1)} %slice.102), channel_id=1, source_target_pairs={{0,1},{1,2},{2,3},{3,0},{4,5},{5,6},{6,7},{7,4},{8,9},{9,10},{10,1... | collective-permute-start | bytes 589832 | tf_op jit(solution)/shard_map/ppermute | solution.py:23
  6.9 7.2 %collective-permute-start.3 = (f32[3,16,3,256]{3,2,1,0:T(4,128)S(1)}, f32[3,16,3,256]{3,2,1,0:T(4,128)S(1)}, u32[]{:S(2)}, u32[]{:S(2)}) collective-permute-start(f32[3,16,3,256]{3,2,1,0:T(4,128)S(1)} %slice.103), channel_id=1, source_target_pairs={{0,3},{1,0},{2,1},{3,2},{4,7},{5,4},{6,5},{7,6},{8,11},{9,8},{10,9... | collective-permute-start | bytes 442376 | tf_op jit(solution)/shard_map/ppermute | solution.py:23
  9.8 37.6 %collective-permute-start.7 = (f32[3,3,48,256]{3,2,1,0:T(8,128)S(1)}, f32[3,3,48,256]{3,2,1,0:T(8,128)S(1)}, u32[]{:S(2)}, u32[]{:S(2)}) collective-permute-start(f32[3,3,48,256]{3,2,1,0:T(8,128)S(1)} %slice.109), channel_id=1, source_target_pairs={{0,28},{4,0},{8,4},{12,8},{16,12},{20,16},{24,20},{28,24},{1,29},{... | collective-permute-start | bytes 1327112 | tf_op jit(solution)/shard_map/ppermute | solution.py:23
  14.0 31.5 %collective-permute-start.4 = (f32[3,4,48,256]{3,2,1,0:T(8,128)S(1)}, f32[3,4,48,256]{3,2,1,0:T(8,128)S(1)}, u32[]{:S(2)}, u32[]{:S(2)}) collective-permute-start(f32[3,4,48,256]{3,2,1,0:T(8,128)S(1)} %slice.104), channel_id=1, source_target_pairs={{0,4},{4,8},{8,12},{12,16},{16,20},{20,24},{24,28},{28,0},{1,5},{5... | collective-permute-start | bytes 1769480 | tf_op jit(solution)/shard_map/ppermute | solution.py:23
  14.1 23.9 %collective-permute-start.1 = (f32[3,3,16,256]{3,2,1,0:T(8,128)S(1)}, f32[3,3,16,256]{3,2,1,0:T(8,128)S(1)}, u32[]{:S(2)}, u32[]{:S(2)}) collective-permute-start(f32[3,3,16,256]{3,2,1,0:T(8,128)S(1)} %pad_maximum_fusion.1), channel_id=1, source_target_pairs={{0,28},{4,0},{8,4},{12,8},{16,12},{20,16},{24,20},{28,24},{1,29},{... | collective-permute-start | bytes 442376 | tf_op jit(solution)/shard_map/ppermute | solution.py:23
  38.1 7.3 %collective-permute-start.5 = (f32[3,7,4,256]{3,2,1,0:T(4,128)S(1)}, f32[3,7,4,256]{3,2,1,0:T(4,128)S(1)}, u32[]{:S(2)}, u32[]{:S(2)}) collective-permute-start(f32[3,7,4,256]{3,2,1,0:T(4,128)S(1)} %pad_maximum_fusion.4), channel_id=1, source_target_pairs={{0,1},{1,2},{2,3},{3,0},{4,5},{5,6},{6,7},{7,4},{8,9},{9,10},{10,1... | collective-permute-start | bytes 258056 | tf_op jit(solution)/shard_map/ppermute | solution.py:23
  38.2 7.2 %collective-permute-start.6 = (f32[3,7,3,256]{3,2,1,0:T(4,128)S(1)}, f32[3,7,3,256]{3,2,1,0:T(4,128)S(1)}, u32[]{:S(2)}, u32[]{:S(2)}) collective-permute-start(f32[3,7,3,256]{3,2,1,0:T(4,128)S(1)} %pad_maximum_fusion.5), channel_id=1, source_target_pairs={{0,3},{1,0},{2,1},{3,2},{4,7},{5,4},{6,5},{7,6},{8,11},{9,8},{10,9... | collective-permute-start | bytes 193544 | tf_op jit(solution)/shard_map/ppermute | solution.py:23
  50.6 9.4 %collective-permute-start.8 = (f32[9,2,4,128]{3,2,1,0:T(4,128)S(1)}, f32[9,2,4,128]{3,2,1,0:T(4,128)S(1)}, u32[]{:S(2)}, u32[]{:S(2)}) collective-permute-start(f32[9,2,4,128]{3,2,1,0:T(4,128)S(1)} %get-tuple-element.54), channel_id=1, source_target_pairs={{0,4},{4,8},{8,12},{12,16},{16,20},{20,24},{24,28},{28,0},{1,5},{5... | collective-permute-start | bytes 110600 | tf_op jit(solution)/shard_map/ppermute | solution.py:23
  50.7 9.5 %collective-permute-start.9 = (f32[9,2,4,128]{3,2,1,0:T(4,128)S(1)}, f32[9,2,4,128]{3,2,1,0:T(4,128)S(1)}, u32[]{:S(2)}, u32[]{:S(2)}) collective-permute-start(f32[9,2,4,128]{3,2,1,0:T(4,128)S(1)} %get-tuple-element.55), channel_id=1, source_target_pairs={{0,28},{4,0},{8,4},{12,8},{16,12},{20,16},{24,20},{28,24},{1,29},{... | collective-permute-start | bytes 110600 | tf_op jit(solution)/shard_map/ppermute | solution.py:23
  55.4 13.2 %collective-permute-start.12 = (f32[9,2,32,128]{3,2,1,0:T(8,128)S(1)}, f32[9,2,32,128]{3,2,1,0:T(8,128)S(1)}, u32[]{:S(2)}, u32[]{:S(2)}) collective-permute-start(f32[9,2,32,128]{3,2,1,0:T(8,128)S(1)} %get-tuple-element.57), channel_id=1, source_target_pairs={{0,4},{4,8},{8,12},{12,16},{16,20},{20,24},{24,28},{28,0},{1,5},{5... | collective-permute-start | bytes 884744 | tf_op jit(solution)/shard_map/ppermute | solution.py:23
  55.4 14.6 %collective-permute-start.13 = (f32[9,2,32,128]{3,2,1,0:T(8,128)S(1)}, f32[9,2,32,128]{3,2,1,0:T(8,128)S(1)}, u32[]{:S(2)}, u32[]{:S(2)}) collective-permute-start(f32[9,2,32,128]{3,2,1,0:T(8,128)S(1)} %get-tuple-element.58), channel_id=1, source_target_pairs={{0,28},{4,0},{8,4},{12,8},{16,12},{20,16},{24,20},{28,24},{1,29},{... | collective-permute-start | bytes 884744 | tf_op jit(solution)/shard_map/ppermute | solution.py:23
  60.2 7.5 %collective-permute-start.10 = (f32[9,12,2,128]{3,2,1,0:T(2,128)S(1)}, f32[9,12,2,128]{3,2,1,0:T(2,128)S(1)}, u32[]{:S(2)}, u32[]{:S(2)}) collective-permute-start(f32[9,12,2,128]{3,2,1,0:T(2,128)S(1)} %pad_maximum_fusion.2), channel_id=1, source_target_pairs={{0,1},{1,2},{2,3},{3,0},{4,5},{5,6},{6,7},{7,4},{8,9},{9,10},{10,1... | collective-permute-start | bytes 331784 | tf_op jit(solution)/shard_map/ppermute | solution.py:23
  60.3 7.4 %collective-permute-start.11 = (f32[9,12,2,128]{3,2,1,0:T(2,128)S(1)}, f32[9,12,2,128]{3,2,1,0:T(2,128)S(1)}, u32[]{:S(2)}, u32[]{:S(2)}) collective-permute-start(f32[9,12,2,128]{3,2,1,0:T(2,128)S(1)} %pad_maximum_fusion.3), channel_id=1, source_target_pairs={{0,3},{1,0},{2,1},{3,2},{4,7},{5,4},{6,5},{7,6},{8,11},{9,8},{10,9... | collective-permute-start | bytes 331784 | tf_op jit(solution)/shard_map/ppermute | solution.py:23
  62.1 5.6 %copy-start.2 = (f32[128,128]{1,0:T(8,128)S(1)}, f32[128,128]{1,0:T(8,128)}, u32[]{:S(2)}) copy-start(f32[128,128]{1,0:T(8,128)} %constant.11.clone.refs_3_.refs_5_) | copy-start | bytes 196612
  68.6 16.3 %copy-start.3 = (f32[128,128]{1,0:T(8,128)S(1)}, f32[128,128]{1,0:T(8,128)}, u32[]{:S(2)}) copy-start(f32[128,128]{1,0:T(8,128)} %constant.12.clone.refs_5_) | copy-start | bytes 196612
  71.3 7.9 %collective-permute-start.14 = (f32[9,2,16,64]{3,2,1,0:T(8,128)S(1)}, f32[9,2,16,64]{3,2,1,0:T(8,128)S(1)}, u32[]{:S(2)}, u32[]{:S(2)}) collective-permute-start(f32[9,2,16,64]{3,2,1,0:T(8,128)S(1)} %get-tuple-element.59), channel_id=1, source_target_pairs={{0,4},{4,8},{8,12},{12,16},{16,20},{20,24},{24,28},{28,0},{1,5},{5... | collective-permute-start | bytes 221192 | tf_op jit(solution)/shard_map/ppermute | solution.py:23
  72.0 8.7 %collective-permute-start.15 = (f32[9,2,16,64]{3,2,1,0:T(8,128)S(1)}, f32[9,2,16,64]{3,2,1,0:T(8,128)S(1)}, u32[]{:S(2)}, u32[]{:S(2)}) collective-permute-start(f32[9,2,16,64]{3,2,1,0:T(8,128)S(1)} %get-tuple-element.60), channel_id=1, source_target_pairs={{0,28},{4,0},{8,4},{12,8},{16,12},{20,16},{24,20},{28,24},{1,29},{... | collective-permute-start | bytes 221192 | tf_op jit(solution)/shard_map/ppermute | solution.py:23
  80.9 3.8 %collective-permute-start.16 = (f32[9,8,2,64]{3,2,1,0:T(2,128)S(1)}, f32[9,8,2,64]{3,2,1,0:T(2,128)S(1)}, u32[]{:S(2)}, u32[]{:S(2)}) collective-permute-start(f32[9,8,2,64]{3,2,1,0:T(2,128)S(1)} %maximum_maximum_fusion), channel_id=1, source_target_pairs={{0,1},{1,2},{2,3},{3,0},{4,5},{5,6},{6,7},{7,4},{8,9},{9,10},{10,1... | collective-permute-start | bytes 110600 | tf_op jit(solution)/shard_map/ppermute | solution.py:23
  81.1 3.8 %collective-permute-start.17 = (f32[9,8,2,64]{3,2,1,0:T(2,128)S(1)}, f32[9,8,2,64]{3,2,1,0:T(2,128)S(1)}, u32[]{:S(2)}, u32[]{:S(2)}) collective-permute-start(f32[9,8,2,64]{3,2,1,0:T(2,128)S(1)} %maximum_maximum_fusion.1), channel_id=1, source_target_pairs={{0,3},{1,0},{2,1},{3,2},{4,7},{5,4},{6,5},{7,6},{8,11},{9,8},{10,9... | collective-permute-start | bytes 110600 | tf_op jit(solution)/shard_map/ppermute | solution.py:23

commit v9 on v8

--- a/solution.py
+++ b/solution.py
@@ -598,14 +598,15 @@
     return shifted(down, "gy", 1), shifted(up, "gy", -1)
 
 
-def exchange(to_next, to_prev, edge_next, edge_prev, down, up):
-    from_prev_edge = shifted(edge_next, "gx", 1)
-    from_next_edge = shifted(edge_prev, "gx", -1)
+def exchange(to_next, to_prev, edge_next, edge_prev, down, up, meanwhile):
+    from_prev = shifted(edge_next, "gx", 1)
+    from_next = shifted(edge_prev, "gx", -1)
     before = shifted(to_next, "gx", 1)
     after = shifted(to_prev, "gx", -1)
-    down = jnp.concatenate([down, from_prev_edge[:, :, 0:2], from_next_edge[:, :, 0:2]], axis=1)
-    up = jnp.concatenate([up, from_prev_edge[:, :, 2:4], from_next_edge[:, :, 2:4]], axis=1)
-    return before, after, shifted(down, "gy", 1), shifted(up, "gy", -1)
+    from_prev, from_next, result = lax.optimization_barrier((from_prev, from_next, meanwhile()))
+    down = jnp.concatenate([down, from_prev[:, :, 0:2], from_next[:, :, 0:2]], axis=1)
+    up = jnp.concatenate([up, from_prev[:, :, 2:4], from_next[:, :, 2:4]], axis=1)
+    return (before, after, shifted(down, "gy", 1), shifted(up, "gy", -1)), result
 
 
 def body(velocity):
@@ -620,18 +621,18 @@
     own_before = shifted(velocity[:, :, ny - BEFORE :], "gy", 1)
     own_after = shifted(velocity[:, :, :AFTER], "gy", -1)
     low_one, rest_one = local_pass(velocity, own_before, own_after, table, 0)
-    edge_before, edge_after, low_one = lax.optimization_barrier((edge_before, edge_after, low_one))
+    low_two, rest_two = local_pass(velocity, own_before, own_after, table, nx // 2)
+    edge_before, edge_after, low_one, low_two = lax.optimization_barrier((edge_before, edge_after, low_one, low_two))
     down = jnp.concatenate([edge_before[:, :, 12:], edge_after[:, :, 12:]], axis=1)
     up = jnp.concatenate([edge_before[:, :, :AFTER], edge_after[:, :, :AFTER]], axis=1)
     row_before = shifted(down, "gy", 1)
     row_after = shifted(up, "gy", -1)
-    low_two, rest_two = local_pass(velocity, own_before, own_after, table, nx // 2)
     low_before, rest_before = halo_pass((edge_before, mid_before, row_before, row_after), table)
     halo = (edge_after, mid_after, row_before, row_after)
     approx, high, stress_one, *sends = approx_pass((low_one, low_two), low_before, halo, table)
-    second_halo = exchange(*sends)
-    details_one = detail_pass((rest_one, rest_two), rest_before, high, halo, table)
-    approx, details_one = lax.optimization_barrier((approx, details_one))
+    second_halo, details_one = exchange(
+        *sends, lambda: detail_pass((rest_one, rest_two), rest_before, high, halo, table)
+    )
     second = approx
     approx, stress_two, *sends = level_approx(second, second_halo)
     before = shifted(sends[0], "gx", 1)

time: 87.7 us -> 86.1 us (0.982)
  waiting for transfers between devices: 18.9 us -> 17.2 us
    ppermute x18, waiting for transfers between devices: 18.9 us -> 17.2 us  [shifted(): lax.ppermute(block, axis, [(i, (i + distance) % size) for i in range(size)])]
  transfers between devices with their start and end apart: 18 -> 18, of which waited for: 6 -> 9; matrix products, arithmetic and copies ran while one was open for 5% -> 5% of each run, Pallas kernels for 26% -> 26%
where the time goes in v9:
time: 86.1 us; the launch traced here: 84.8 us
  starting transfers between devices  32.5 us (38%)
  Pallas kernels  28.3 us (33%)
  waiting for transfers between devices  17.2 us (20%)
  local copies, waits for them, and re-layouts  5.52 us (6%)
  between operations  0.9 us (1%)
    ppermute x18, starting transfers between devices, shifted(): lax.ppermute(block, axis, [(i, (i + distance) % size) for i in range(size)])  32.5 us
    ppermute x18, waiting for transfers between devices, shifted(): lax.ppermute(block, axis, [(i, (i + distance) % size) for i in range(size)])  17.2 us
    pallas_call x2, Pallas kernels, local_pass(): pl.pallas_call(local_kernel, grid=(nx,), in_specs=[pl.BlockSpec((3, 1, ny...  10.9 us
    pallas_call x1, Pallas kernels, detail_pass(): pl.pallas_call(detail_kernel, grid=(9 // GROUP,), in_specs=[pl.BlockSpec(...  5.59 us
    pallas_call x2, Pallas kernels, level_call(): pl.pallas_call(kernel, in_specs=[vmem] * 6, out_specs=[vmem] * len(out),...  4.5 us
    pallas_call x1, Pallas kernels, approx_pass(): pl.pallas_call(approx_kernel, grid=(9 // GROUP,), in_specs=[per_field((nx...  3.24 us
    pallas_call x1, Pallas kernels, halo_pass(): pl.pallas_call(halo_kernel, in_specs=[vmem] * 5, out_specs=[vmem] * 2, ou...  1.9 us
  transfers between devices with their start and end apart: 18, of which 9 were waited for; matrix products, arithmetic and copies ran while one was open for 5% of the time, Pallas kernels for 26%

profile of v9, /device:TPU:0, one launch (start us, length us, event | category | flops | bytes accessed | tf_op | source)
XLA Modules:
  0.0 84.8 jit_solution(12074115580817931169)
XLA Ops:
  0.6 0.0 copy-start.1
  0.6 0.0 copy-start
  0.7 1.1 %fusion.6 = (f32[3,4,8,256]{3,2,1,0:T(8,128)S(1)}, f32[3,4,8,256]{3,2,1,0:T(8,128)S(1)}) fusion(f32[3,16,64,256]{3,2,1,0:T(8,128)} %v_ref.3), kind=kLoop, calls=%fused_computation.19 | loop fusion | bytes 393216 | tf_op jit(solution)/shard_map/slice | solution.py:616
  1.8 3.0 %collective-permute-start = (f32[3,4,16,256]{3,2,1,0:T(8,128)S(1)}, f32[3,4,16,256]{3,2,1,0:T(8,128)S(1)}, u32[]{:S(2)}, u32[]{:S(2)}) collective-permute-start(f32[3,4,16,256]{3,2,1,0:T(8,128)S(1)} %pad_maximum_fusion), channel_id=1, source_target_pairs={{0,4},{4,8},{8,12},{12,16},{16,20},{20,24},{24,28},{28,0},{1,5},{5... | collective-permute-start | bytes 589832 | tf_op jit(solution)/shard_map/ppermute | solution.py:23
  4.8 1.0 %slice.102 = f32[3,16,4,256]{3,2,1,0:T(4,128)S(1)} slice(f32[3,16,64,256]{3,2,1,0:T(8,128)} %v_ref.3), slice={[0:3], [0:16], [60:64], [0:256]} | slice | bytes 393216 | tf_op jit(solution)/shard_map/slice | solution.py:621
  5.9 0.1 collective-permute-start.2
  5.9 1.0 %slice.103 = f32[3,16,3,256]{3,2,1,0:T(4,128)S(1)} slice(f32[3,16,64,256]{3,2,1,0:T(8,128)} %v_ref.3), slice={[0:3], [0:16], [0:3], [0:256]} | slice | bytes 294912 | tf_op jit(solution)/shard_map/slice | solution.py:622
  6.9 1.8 %collective-permute-start.3 = (f32[3,16,3,256]{3,2,1,0:T(4,128)S(1)}, f32[3,16,3,256]{3,2,1,0:T(4,128)S(1)}, u32[]{:S(2)}, u32[]{:S(2)}) collective-permute-start(f32[3,16,3,256]{3,2,1,0:T(4,128)S(1)} %slice.103), channel_id=1, source_target_pairs={{0,3},{1,0},{2,1},{3,2},{4,7},{5,4},{6,5},{7,6},{8,11},{9,8},{10,9... | collective-permute-start | bytes 442376 | tf_op jit(solution)/shard_map/ppermute | solution.py:23
  8.7 1.0 %slice.109 = f32[3,3,48,256]{3,2,1,0:T(8,128)S(1)} slice(f32[3,16,64,256]{3,2,1,0:T(8,128)} %v_ref.3), slice={[0:3], [0:3], [8:56], [0:256]} | slice | bytes 884736 | tf_op jit(solution)/shard_map/slice | solution.py:620
  9.8 3.1 %collective-permute-start.7 = (f32[3,3,48,256]{3,2,1,0:T(8,128)S(1)}, f32[3,3,48,256]{3,2,1,0:T(8,128)S(1)}, u32[]{:S(2)}, u32[]{:S(2)}) collective-permute-start(f32[3,3,48,256]{3,2,1,0:T(8,128)S(1)} %slice.109), channel_id=1, source_target_pairs={{0,28},{4,0},{8,4},{12,8},{16,12},{20,16},{24,20},{28,24},{1,29},{... | collective-permute-start | bytes 1327112 | tf_op jit(solution)/shard_map/ppermute | solution.py:23
  12.9 1.1 %slice.104 = f32[3,4,48,256]{3,2,1,0:T(8,128)S(1)} slice(f32[3,16,64,256]{3,2,1,0:T(8,128)} %v_ref.3), slice={[0:3], [12:16], [8:56], [0:256]} | slice | bytes 1179648 | tf_op jit(solution)/shard_map/slice | solution.py:619
  14.0 0.1 collective-permute-start.4
  14.1 4.7 %collective-permute-start.1 = (f32[3,3,16,256]{3,2,1,0:T(8,128)S(1)}, f32[3,3,16,256]{3,2,1,0:T(8,128)S(1)}, u32[]{:S(2)}, u32[]{:S(2)}) collective-permute-start(f32[3,3,16,256]{3,2,1,0:T(8,128)S(1)} %pad_maximum_fusion.1), channel_id=1, source_target_pairs={{0,28},{4,0},{8,4},{12,8},{16,12},{20,16},{24,20},{28,24},{1,29},{... | collective-permute-start | bytes 442376 | tf_op jit(solution)/shard_map/ppermute | solution.py:23
  18.9 5.4 %local_pass.3 = (f32[9,8,32,128]{3,2,1,0:T(8,128)S(1)}, f32[3,9,8,32,128]{4,3,2,1,0:T(8,128)S(1)}) custom-call(f32[3,16,64,256]{3,2,1,0:T(8,128)S(1)} %copy-done, f32[3,16,4,256]{3,2,1,0:T(4,128)S(1)} %collective-permute-done.2.before_ref, f32[3,16,3,256]{3,2,1,0:T(4,128)S(1)} %collective-permute-done.3.after_ref, f32[256,256]{1,0:T(8,128)S(1)} %copy-done.1), custom_call_target="tpu_custom_call" | custom-call | flops 603979776 | bytes 7077888 | tf_op jit(solution)/shard_map/local_pass/pallas_call | solution.py:166
  24.3 5.4 %local_pass.2 = (f32[9,8,32,128]{3,2,1,0:T(8,128)S(1)}, f32[3,9,8,32,128]{4,3,2,1,0:T(8,128)S(1)}) custom-call(f32[3,16,64,256]{3,2,1,0:T(8,128)S(1)} %copy-done, f32[3,16,4,256]{3,2,1,0:T(4,128)S(1)} %collective-permute-done.2.before_ref, f32[3,16,3,256]{3,2,1,0:T(4,128)S(1)} %collective-permute-done.3.after_ref, f32[256,256]{1,0:T(8,128)S(1)} %copy-done.1), custom_call_target="tpu_custom_call" | custom-call | flops 603979776 | bytes 7077888 | tf_op jit(solution)/shard_map/local_pass/pallas_call | solution.py:166
  29.8 8.3 %collective-permute-done.1.refs_4_.refs_5_ = f32[3,3,16,256]{3,2,1,0:T(8,128)S(1)} collective-permute-done((f32[3,3,16,256]{3,2,1,0:T(8,128)S(1)}, f32[3,3,16,256]{3,2,1,0:T(8,128)S(1)}, u32[]{:S(2)}, u32[]{:S(2)}) %collective-permute-start.1) | collective-permute-done | bytes 147488 | tf_op jit(solution)/shard_map/ppermute | solution.py:23
  38.0 0.0 collective-permute-done.refs_0_
  38.1 0.1 collective-permute-start.5
  38.2 1.8 %collective-permute-start.6 = (f32[3,7,3,256]{3,2,1,0:T(4,128)S(1)}, f32[3,7,3,256]{3,2,1,0:T(4,128)S(1)}, u32[]{:S(2)}, u32[]{:S(2)}) collective-permute-start(f32[3,7,3,256]{3,2,1,0:T(4,128)S(1)} %pad_maximum_fusion.5), channel_id=1, source_target_pairs={{0,3},{1,0},{2,1},{3,2},{4,7},{5,4},{6,5},{7,6},{8,11},{9,8},{10,9... | collective-permute-start | bytes 193544 | tf_op jit(solution)/shard_map/ppermute | solution.py:23
  40.0 2.1 %collective-permute-done.6.refs_3_.refs_7_.refs_8_ = f32[3,7,3,256]{3,2,1,0:T(4,128)S(1)} collective-permute-done((f32[3,7,3,256]{3,2,1,0:T(4,128)S(1)}, f32[3,7,3,256]{3,2,1,0:T(4,128)S(1)}, u32[]{:S(2)}, u32[]{:S(2)}) %collective-permute-start.6) | collective-permute-done | bytes 64544 | tf_op jit(solution)/shard_map/ppermute | solution.py:23
  42.1 1.9 %halo_pass.1 = (f32[9,2,32,128]{3,2,1,0:T(8,128)S(1)}, f32[3,9,2,32,128]{4,3,2,1,0:T(8,128)S(1)}) custom-call(f32[3,4,16,256]{3,2,1,0:T(8,128)S(1)} %collective-permute-done.refs_0_, f32[3,4,48,256]{3,2,1,0:T(8,128)S(1)} %collective-permute-done.4.refs_1_, f32[3,7,4,256]{3,2,1,0:T(4,128)S(1)} %collective-permute-done.5.refs_2_.refs_6_.refs_7_, ...), custom_call_target="tpu_custom_call" | custom-call | tf_op jit(solution)/shard_map/halo_pass/pallas_call | solution.py:269
  44.0 0.0 collective-permute-done.7.refs_5_.refs_6_
  44.0 3.2 %approx_pass.1 = (f32[9,8,32,128]{3,2,1,0:T(8,128)S(1)}, f32[9,8,32,128]{3,2,1,0:T(8,128)S(1)}, f32[6,8,32,128]{3,2,1,0:T(8,128)}, f32[9,2,32,128]{3,2,1,0:T(8,1...) custom-call(f32[9,8,32,128]{3,2,1,0:T(8,128)S(1)} %get-tuple-element, ...), custom_call_target="tpu_custom_call" | custom-call | tf_op jit(solution)/shard_map/approx_pass/pallas_call | solution.py:346
  47.3 4.7 %collective-permute-start.9 = (f32[9,2,4,128]{3,2,1,0:T(4,128)S(1)}, f32[9,2,4,128]{3,2,1,0:T(4,128)S(1)}, u32[]{:S(2)}, u32[]{:S(2)}) collective-permute-start(f32[9,2,4,128]{3,2,1,0:T(4,128)S(1)} %get-tuple-element.49), channel_id=1, source_target_pairs={{0,28},{4,0},{8,4},{12,8},{16,12},{20,16},{24,20},{28,24},{1,29},{... | collective-permute-start | bytes 110600 | tf_op jit(solution)/shard_map/ppermute | solution.py:23
  52.0 4.7 %collective-permute-start.13 = (f32[9,2,32,128]{3,2,1,0:T(8,128)S(1)}, f32[9,2,32,128]{3,2,1,0:T(8,128)S(1)}, u32[]{:S(2)}, u32[]{:S(2)}) collective-permute-start(f32[9,2,32,128]{3,2,1,0:T(8,128)S(1)} %get-tuple-element.62), channel_id=1, source_target_pairs={{0,28},{4,0},{8,4},{12,8},{16,12},{20,16},{24,20},{28,24},{1,29},{... | collective-permute-start | bytes 884744 | tf_op jit(solution)/shard_map/ppermute | solution.py:23
  56.7 5.6 %detail_pass.1 = f32[7,9,8,32,128]{4,3,2,1,0:T(8,128)} custom-call(f32[3,9,8,32,128]{4,3,2,1,0:T(8,128)S(1)} %get-tuple-element.50.refs_0_, f32[3,9,8,32,128]{4,3,2,1,0:T(8,128)S(1)} %get-tuple-element.51.refs_1_, f32[3,9,2,32,128]{4,3,2,1,0:T(8,128)S(1)} %get-tuple-element.52.refs_2_, f32[9,8,32,128]{3,2,1,0:T(8,128)S(1)} %get-tuple-element.53.refs_3_, ...), custom_call_target="tpu_custom_call" | custom-call | flops 235929600 | bytes 18874368 | tf_op jit(solution)/shard_map/detail_pass/pallas_call | solution.py:414
  62.4 0.1 pad_maximum_fusion.2
  62.4 0.6 collective-permute-start.10
  63.1 1.2 %collective-permute-start.11 = (f32[9,12,2,128]{3,2,1,0:T(2,128)S(1)}, f32[9,12,2,128]{3,2,1,0:T(2,128)S(1)}, u32[]{:S(2)}, u32[]{:S(2)}) collective-permute-start(f32[9,12,2,128]{3,2,1,0:T(2,128)S(1)} %pad_maximum_fusion.3), channel_id=1, source_target_pairs={{0,3},{1,0},{2,1},{3,2},{4,7},{5,4},{6,5},{7,6},{8,11},{9,8},{10,9... | collective-permute-start | bytes 331784 | tf_op jit(solution)/shard_map/ppermute | solution.py:23
  64.3 2.3 %collective-permute-done.10.refs_1_.refs_3_ = f32[9,12,2,128]{3,2,1,0:T(2,128)S(1)} collective-permute-done((f32[9,12,2,128]{3,2,1,0:T(2,128)S(1)}, f32[9,12,2,128]{3,2,1,0:T(2,128)S(1)}, u32[]{:S(2)}, u32[]{:S(2)}) %collective-permute-start.10) | collective-permute-done | bytes 110624 | tf_op jit(solution)/shard_map/ppermute | solution.py:23
  66.6 0.2 collective-permute-done.11.refs_2_.refs_4_
  66.9 0.8 level_own.1.refs_0_
  67.7 0.0 copy-start.3
  67.8 0.3 collective-permute-done.13.refs_2_
  68.0 1.3 %level_approx.1 = (f32[9,4,16,64]{3,2,1,0:T(8,128)S(1)}, f32[6,4,16,64]{3,2,1,0:T(8,128)}, f32[9,2,16,64]{3,2,1,0:T(8,128)S(1)}, f32[9,2,16,64]{3,2,1,0:T(8,128)...) custom-call(f32[9,8,16,128]{3,2,1,0:T(8,128)S(1)} %level_own.1.refs_0_, ...), custom_call_target="tpu_custom_call" | custom-call | tf_op jit(solution)/shard_map/level_approx/pallas_call | solution.py:566
  69.4 4.7 %collective-permute-start.15 = (f32[9,2,16,64]{3,2,1,0:T(8,128)S(1)}, f32[9,2,16,64]{3,2,1,0:T(8,128)S(1)}, u32[]{:S(2)}, u32[]{:S(2)}) collective-permute-start(f32[9,2,16,64]{3,2,1,0:T(8,128)S(1)} %get-tuple-element.64), channel_id=1, source_target_pairs={{0,28},{4,0},{8,4},{12,8},{16,12},{20,16},{24,20},{28,24},{1,29},{... | collective-permute-start | bytes 221192 | tf_op jit(solution)/shard_map/ppermute | solution.py:23
  74.1 2.9 %shard_map.108 = f32[7,9,4,16,64]{4,3,2,1,0:T(8,128)} custom-call(f32[9,8,32,128]{3,2,1,0:T(8,128)S(1)} %get-tuple-element.56.refs_0_, f32[9,2,32,128]{3,2,1,0:T(8,128)S(1)} %collective-permute-done.12.refs_1_, f32[9,2,32,128]{3,2,1,0:T(8,128)S(1)} %collective-permute-done.13.refs_2_, f32[9,12,2,128]{3,2,1,0:T(2,128)S(1)} %collective-permute-done.10.refs_1_.refs_3_, ...), custom_call_target="tpu_custom_call" | custom-call | tf_op jit(solution)/shard_map/pallas_call | solution.py:533
  77.0 1.6 %collective-permute-done.14.refs_1_ = f32[9,2,16,64]{3,2,1,0:T(8,128)S(1)} collective-permute-done((f32[9,2,16,64]{3,2,1,0:T(8,128)S(1)}, f32[9,2,16,64]{3,2,1,0:T(8,128)S(1)}, u32[]{:S(2)}, u32[]{:S(2)}) %collective-permute-start.14) | collective-permute-done | bytes 73760 | tf_op jit(solution)/shard_map/ppermute | solution.py:23
  78.6 0.4 collective-permute-done.15.refs_2_
  79.1 0.1 fusion.1
  79.2 0.1 maximum_maximum_fusion
  79.2 0.2 collective-permute-start.16
  79.4 0.1 fusion.4
  79.5 0.1 maximum_maximum_fusion.1
  79.5 1.7 %collective-permute-start.17 = (f32[9,8,2,64]{3,2,1,0:T(2,128)S(1)}, f32[9,8,2,64]{3,2,1,0:T(2,128)S(1)}, u32[]{:S(2)}, u32[]{:S(2)}) collective-permute-start(f32[9,8,2,64]{3,2,1,0:T(2,128)S(1)} %maximum_maximum_fusion.1), channel_id=1, source_target_pairs={{0,3},{1,0},{2,1},{3,2},{4,7},{5,4},{6,5},{7,6},{8,11},{9,8},{10,9... | collective-permute-start | bytes 110600 | tf_op jit(solution)/shard_map/ppermute | solution.py:23
  81.2 1.8 %collective-permute-done.16.refs_3_ = f32[9,8,2,64]{3,2,1,0:T(2,128)S(1)} collective-permute-done((f32[9,8,2,64]{3,2,1,0:T(2,128)S(1)}, f32[9,8,2,64]{3,2,1,0:T(2,128)S(1)}, u32[]{:S(2)}, u32[]{:S(2)}) %collective-permute-start.16) | collective-permute-done | bytes 36896 | tf_op jit(solution)/shard_map/ppermute | solution.py:23
  83.1 0.1 collective-permute-done.17.refs_4_
  83.2 1.6 %shard_map.109 = (f32[7,9,2,8,32]{4,3,2,1,0:T(8,128)}, f32[6,2,8,32]{3,2,1,0:T(8,128)}, f32[3,2,8,32]{3,2,1,0:T(8,128)}) custom-call(f32[9,4,16,64]{3,2,1,0:T(8,128)S(1)} %get-tuple-element.67.refs_0_, f32[9,2,16,64]{3,2,1,0:T(8,128)S(1)} %collective-permute-done.14.refs_1_, f32[9,2,16,64]{3,2,1,0:T(8,128)S(1)} %collective-permute-done.15.refs_2_, ...), custom_call_target="tpu_custom_call" | custom-call | tf_op jit(solution)/shard_map/pallas_call | solution.py:533
  (28 shorter events, 0.3 us)
Async XLA Ops:
  0.6 18.2 %copy-start.1 = (f32[256,256]{1,0:T(8,128)S(1)}, f32[256,256]{1,0:T(8,128)}, u32[]{:S(2)}) copy-start(f32[256,256]{1,0:T(8,128)} %constant.10.clone.table_ref.refs_4_.refs_3_) | copy-start | bytes 786436
  0.6 13.4 %copy-start = (f32[3,16,64,256]{3,2,1,0:T(8,128)S(1)}, f32[3,16,64,256]{3,2,1,0:T(8,128)}, u32[]{:S(2)}) copy-start(f32[3,16,64,256]{3,2,1,0:T(8,128)} %v_ref.3) | copy-start | bytes 9437188
  1.8 36.2 %collective-permute-start = (f32[3,4,16,256]{3,2,1,0:T(8,128)S(1)}, f32[3,4,16,256]{3,2,1,0:T(8,128)S(1)}, u32[]{:S(2)}, u32[]{:S(2)}) collective-permute-start(f32[3,4,16,256]{3,2,1,0:T(8,128)S(1)} %pad_maximum_fusion), channel_id=1, source_target_pairs={{0,4},{4,8},{8,12},{12,16},{16,20},{20,24},{24,28},{28,0},{1,5},{5... | collective-permute-start | bytes 589832 | tf_op jit(solution)/shard_map/ppermute | solution.py:23
  5.9 13.0 %collective-permute-start.2 = (f32[3,16,4,256]{3,2,1,0:T(4,128)S(1)}, f32[3,16,4,256]{3,2,1,0:T(4,128)S(1)}, u32[]{:S(2)}, u32[]{:S(2)}) collective-permute-start(f32[3,16,4,256]{3,2,1,0:T(4,128)S(1)} %slice.102), channel_id=1, source_target_pairs={{0,1},{1,2},{2,3},{3,0},{4,5},{5,6},{6,7},{7,4},{8,9},{9,10},{10,1... | collective-permute-start | bytes 589832 | tf_op jit(solution)/shard_map/ppermute | solution.py:23
  6.9 7.2 %collective-permute-start.3 = (f32[3,16,3,256]{3,2,1,0:T(4,128)S(1)}, f32[3,16,3,256]{3,2,1,0:T(4,128)S(1)}, u32[]{:S(2)}, u32[]{:S(2)}) collective-permute-start(f32[3,16,3,256]{3,2,1,0:T(4,128)S(1)} %slice.103), channel_id=1, source_target_pairs={{0,3},{1,0},{2,1},{3,2},{4,7},{5,4},{6,5},{7,6},{8,11},{9,8},{10,9... | collective-permute-start | bytes 442376 | tf_op jit(solution)/shard_map/ppermute | solution.py:23
  9.8 34.3 %collective-permute-start.7 = (f32[3,3,48,256]{3,2,1,0:T(8,128)S(1)}, f32[3,3,48,256]{3,2,1,0:T(8,128)S(1)}, u32[]{:S(2)}, u32[]{:S(2)}) collective-permute-start(f32[3,3,48,256]{3,2,1,0:T(8,128)S(1)} %slice.109), channel_id=1, source_target_pairs={{0,28},{4,0},{8,4},{12,8},{16,12},{20,16},{24,20},{28,24},{1,29},{... | collective-permute-start | bytes 1327112 | tf_op jit(solution)/shard_map/ppermute | solution.py:23
  14.0 28.1 %collective-permute-start.4 = (f32[3,4,48,256]{3,2,1,0:T(8,128)S(1)}, f32[3,4,48,256]{3,2,1,0:T(8,128)S(1)}, u32[]{:S(2)}, u32[]{:S(2)}) collective-permute-start(f32[3,4,48,256]{3,2,1,0:T(8,128)S(1)} %slice.104), channel_id=1, source_target_pairs={{0,4},{4,8},{8,12},{12,16},{16,20},{20,24},{24,28},{28,0},{1,5},{5... | collective-permute-start | bytes 1769480 | tf_op jit(solution)/shard_map/ppermute | solution.py:23
  14.1 23.9 %collective-permute-start.1 = (f32[3,3,16,256]{3,2,1,0:T(8,128)S(1)}, f32[3,3,16,256]{3,2,1,0:T(8,128)S(1)}, u32[]{:S(2)}, u32[]{:S(2)}) collective-permute-start(f32[3,3,16,256]{3,2,1,0:T(8,128)S(1)} %pad_maximum_fusion.1), channel_id=1, source_target_pairs={{0,28},{4,0},{8,4},{12,8},{16,12},{20,16},{24,20},{28,24},{1,29},{... | collective-permute-start | bytes 442376 | tf_op jit(solution)/shard_map/ppermute | solution.py:23
  38.1 4.0 %collective-permute-start.5 = (f32[3,7,4,256]{3,2,1,0:T(4,128)S(1)}, f32[3,7,4,256]{3,2,1,0:T(4,128)S(1)}, u32[]{:S(2)}, u32[]{:S(2)}) collective-permute-start(f32[3,7,4,256]{3,2,1,0:T(4,128)S(1)} %pad_maximum_fusion.4), channel_id=1, source_target_pairs={{0,1},{1,2},{2,3},{3,0},{4,5},{5,6},{6,7},{7,4},{8,9},{9,10},{10,1... | collective-permute-start | bytes 258056 | tf_op jit(solution)/shard_map/ppermute | solution.py:23
  38.2 3.9 %collective-permute-start.6 = (f32[3,7,3,256]{3,2,1,0:T(4,128)S(1)}, f32[3,7,3,256]{3,2,1,0:T(4,128)S(1)}, u32[]{:S(2)}, u32[]{:S(2)}) collective-permute-start(f32[3,7,3,256]{3,2,1,0:T(4,128)S(1)} %pad_maximum_fusion.5), channel_id=1, source_target_pairs={{0,3},{1,0},{2,1},{3,2},{4,7},{5,4},{6,5},{7,6},{8,11},{9,8},{10,9... | collective-permute-start | bytes 193544 | tf_op jit(solution)/shard_map/ppermute | solution.py:23
  47.3 15.0 %collective-permute-start.8 = (f32[9,2,4,128]{3,2,1,0:T(4,128)S(1)}, f32[9,2,4,128]{3,2,1,0:T(4,128)S(1)}, u32[]{:S(2)}, u32[]{:S(2)}) collective-permute-start(f32[9,2,4,128]{3,2,1,0:T(4,128)S(1)} %get-tuple-element.48), channel_id=1, source_target_pairs={{0,4},{4,8},{8,12},{12,16},{16,20},{20,24},{24,28},{28,0},{1,5},{5... | collective-permute-start | bytes 110600 | tf_op jit(solution)/shard_map/ppermute | solution.py:23
  47.3 15.0 %collective-permute-start.9 = (f32[9,2,4,128]{3,2,1,0:T(4,128)S(1)}, f32[9,2,4,128]{3,2,1,0:T(4,128)S(1)}, u32[]{:S(2)}, u32[]{:S(2)}) collective-permute-start(f32[9,2,4,128]{3,2,1,0:T(4,128)S(1)} %get-tuple-element.49), channel_id=1, source_target_pairs={{0,28},{4,0},{8,4},{12,8},{16,12},{20,16},{24,20},{28,24},{1,29},{... | collective-permute-start | bytes 110600 | tf_op jit(solution)/shard_map/ppermute | solution.py:23
  52.0 15.8 %collective-permute-start.12 = (f32[9,2,32,128]{3,2,1,0:T(8,128)S(1)}, f32[9,2,32,128]{3,2,1,0:T(8,128)S(1)}, u32[]{:S(2)}, u32[]{:S(2)}) collective-permute-start(f32[9,2,32,128]{3,2,1,0:T(8,128)S(1)} %get-tuple-element.61), channel_id=1, source_target_pairs={{0,4},{4,8},{8,12},{12,16},{16,20},{20,24},{24,28},{28,0},{1,5},{5... | collective-permute-start | bytes 884744 | tf_op jit(solution)/shard_map/ppermute | solution.py:23
  52.0 16.0 %collective-permute-start.13 = (f32[9,2,32,128]{3,2,1,0:T(8,128)S(1)}, f32[9,2,32,128]{3,2,1,0:T(8,128)S(1)}, u32[]{:S(2)}, u32[]{:S(2)}) collective-permute-start(f32[9,2,32,128]{3,2,1,0:T(8,128)S(1)} %get-tuple-element.62), channel_id=1, source_target_pairs={{0,28},{4,0},{8,4},{12,8},{16,12},{20,16},{24,20},{28,24},{1,29},{... | collective-permute-start | bytes 884744 | tf_op jit(solution)/shard_map/ppermute | solution.py:23
  56.7 10.2 %copy-start.2 = (f32[128,128]{1,0:T(8,128)S(1)}, f32[128,128]{1,0:T(8,128)}, u32[]{:S(2)}) copy-start(f32[128,128]{1,0:T(8,128)} %constant.11.clone.refs_3_.refs_5_) | copy-start | bytes 196612
  62.4 4.2 %collective-permute-start.10 = (f32[9,12,2,128]{3,2,1,0:T(2,128)S(1)}, f32[9,12,2,128]{3,2,1,0:T(2,128)S(1)}, u32[]{:S(2)}, u32[]{:S(2)}) collective-permute-start(f32[9,12,2,128]{3,2,1,0:T(2,128)S(1)} %pad_maximum_fusion.2), channel_id=1, source_target_pairs={{0,1},{1,2},{2,3},{3,0},{4,5},{5,6},{6,7},{7,4},{8,9},{9,10},{10,1... | collective-permute-start | bytes 331784 | tf_op jit(solution)/shard_map/ppermute | solution.py:23
  63.1 3.8 %collective-permute-start.11 = (f32[9,12,2,128]{3,2,1,0:T(2,128)S(1)}, f32[9,12,2,128]{3,2,1,0:T(2,128)S(1)}, u32[]{:S(2)}, u32[]{:S(2)}) collective-permute-start(f32[9,12,2,128]{3,2,1,0:T(2,128)S(1)} %pad_maximum_fusion.3), channel_id=1, source_target_pairs={{0,3},{1,0},{2,1},{3,2},{4,7},{5,4},{6,5},{7,6},{8,11},{9,8},{10,9... | collective-permute-start | bytes 331784 | tf_op jit(solution)/shard_map/ppermute | solution.py:23
  67.7 15.5 %copy-start.3 = (f32[128,128]{1,0:T(8,128)S(1)}, f32[128,128]{1,0:T(8,128)}, u32[]{:S(2)}) copy-start(f32[128,128]{1,0:T(8,128)} %constant.12.clone.refs_5_) | copy-start | bytes 196612
  69.4 9.2 %collective-permute-start.14 = (f32[9,2,16,64]{3,2,1,0:T(8,128)S(1)}, f32[9,2,16,64]{3,2,1,0:T(8,128)S(1)}, u32[]{:S(2)}, u32[]{:S(2)}) collective-permute-start(f32[9,2,16,64]{3,2,1,0:T(8,128)S(1)} %get-tuple-element.63), channel_id=1, source_target_pairs={{0,4},{4,8},{8,12},{12,16},{16,20},{20,24},{24,28},{28,0},{1,5},{5... | collective-permute-start | bytes 221192 | tf_op jit(solution)/shard_map/ppermute | solution.py:23
  69.4 9.6 %collective-permute-start.15 = (f32[9,2,16,64]{3,2,1,0:T(8,128)S(1)}, f32[9,2,16,64]{3,2,1,0:T(8,128)S(1)}, u32[]{:S(2)}, u32[]{:S(2)}) collective-permute-start(f32[9,2,16,64]{3,2,1,0:T(8,128)S(1)} %get-tuple-element.64), channel_id=1, source_target_pairs={{0,28},{4,0},{8,4},{12,8},{16,12},{20,16},{24,20},{28,24},{1,29},{... | collective-permute-start | bytes 221192 | tf_op jit(solution)/shard_map/ppermute | solution.py:23
  79.2 3.8 %collective-permute-start.16 = (f32[9,8,2,64]{3,2,1,0:T(2,128)S(1)}, f32[9,8,2,64]{3,2,1,0:T(2,128)S(1)}, u32[]{:S(2)}, u32[]{:S(2)}) collective-permute-start(f32[9,8,2,64]{3,2,1,0:T(2,128)S(1)} %maximum_maximum_fusion), channel_id=1, source_target_pairs={{0,1},{1,2},{2,3},{3,0},{4,5},{5,6},{6,7},{7,4},{8,9},{9,10},{10,1... | collective-permute-start | bytes 110600 | tf_op jit(solution)/shard_map/ppermute | solution.py:23
  79.5 3.7 %collective-permute-start.17 = (f32[9,8,2,64]{3,2,1,0:T(2,128)S(1)}, f32[9,8,2,64]{3,2,1,0:T(2,128)S(1)}, u32[]{:S(2)}, u32[]{:S(2)}) collective-permute-start(f32[9,8,2,64]{3,2,1,0:T(2,128)S(1)} %maximum_maximum_fusion.1), channel_id=1, source_target_pairs={{0,3},{1,0},{2,1},{3,2},{4,7},{5,4},{6,5},{7,6},{8,11},{9,8},{10,9... | collective-permute-start | bytes 110600 | tf_op jit(solution)/shard_map/ppermute | solution.py:23

commit v10 on v9

--- a/solution.py
+++ b/solution.py
@@ -376,7 +376,9 @@
     ]
 
 
-def detail_kernel(*refs):
+def detail_kernel(start, *refs):
+    if start:
+        refs = refs[:9] + refs[10:]
     rest_refs, before_ref, high_ref, table_ref = refs[:2], refs[2], refs[3], refs[4]
     halo_refs = refs[5:9]
     out_ref, rows_ref, even_ref, odd_ref, part_ref, stack_ref = refs[9:]
@@ -388,7 +390,7 @@
     def _():
         gather_rows(halo_refs, BEFORE, rows_ref, even_ref, odd_ref)
 
-    pairs = [pair_of(f * GROUP + n) for n in range(GROUP)]
+    pairs = [pair_of((f + start) * GROUP + n) for n in range(GROUP)]
     halo_stack(pairs, True, parts_for_previous, even_ref, odd_ref, part_ref, stack_ref)
     stack_ref[...] = dot(stack_ref[...], table_ref[...])
     for n in range(GROUP):
@@ -408,22 +410,34 @@
                     out_ref[plane + 1, n, x, rows, :] = o[x] * band_scale(by, 1)
 
 
-def detail_pass(rests, before, high, halo, table):
+def detail_pass(rests, before, high, halo, table, start, stop, details=None):
     _, mx, half, lanes = high.shape
     nz = 2 * lanes
+    aliased = [] if details is None else [details]
+    band = lambda count, *shape: pl.BlockSpec((count, GROUP) + shape, lambda f: (0, f + start) + (0,) * len(shape))
     return pl.pallas_call(
-        detail_kernel,
-        grid=(9 // GROUP,),
-        in_specs=[pl.BlockSpec((3, GROUP, mx, half, lanes), lambda f: (0, f, 0, 0, 0))] * 2
-        + [pl.BlockSpec((3, GROUP, 2, half, lanes), lambda f: (0, f, 0, 0, 0)), per_field((mx, half, lanes)), whole((nz, nz))]
-        + [whole(h.shape) for h in halo],
-        out_specs=pl.BlockSpec((7, GROUP, mx, half, lanes), lambda f: (0, f, 0, 0, 0)),
+        lambda *refs: detail_kernel(start, *refs),
+        grid=(stop - start,),
+        in_specs=[band(3, mx, half, lanes)] * 2
+        + [
+            band(3, 2, half, lanes),
+            pl.BlockSpec((GROUP, mx, half, lanes), lambda f: (f + start, 0, 0, 0)),
+            whole((nz, nz)),
+        ]
+        + [whole(h.shape) for h in halo]
+        + [pl.BlockSpec(memory_space=pl.ANY)] * len(aliased),
+        out_specs=band(7, mx, half, lanes),
         out_shape=jax.ShapeDtypeStruct((7, 9, mx, half, lanes), jnp.float32),
+        input_output_aliases={9: 0} if aliased else {},
         scratch_shapes=halo_scratch(half, lanes, AFTER, True),
         compiler_params=pltpu.CompilerParams(vmem_limit_bytes=24 * MIB),
-        cost_estimate=pl.CostEstimate(flops=18 * mx * half * nz * 200, bytes_accessed=18 * mx * half * nz * 16, transcendentals=0),
+        cost_estimate=pl.CostEstimate(
+            flops=2 * (stop - start) * GROUP * mx * half * nz * 200,
+            bytes_accessed=2 * (stop - start) * GROUP * mx * half * nz * 16,
+            transcendentals=0,
+        ),
         name="detail_pass",
-    )(*rests, before, high, table, *halo)
+    )(*rests, before, high, table, *halo, *aliased)
 
 
 def level_rows(refs, nz, nx, span, lows, pad_ref, stack_ref):
@@ -630,9 +644,10 @@
     low_before, rest_before = halo_pass((edge_before, mid_before, row_before, row_after), table)
     halo = (edge_after, mid_after, row_before, row_after)
     approx, high, stress_one, *sends = approx_pass((low_one, low_two), low_before, halo, table)
-    second_halo, details_one = exchange(
-        *sends, lambda: detail_pass((rest_one, rest_two), rest_before, high, halo, table)
-    )
+    details = lambda *span: detail_pass((rest_one, rest_two), rest_before, high, halo, table, *span)
+    second_halo, details_one = exchange(*sends, lambda: details(0, 2))
+    details_one = details(2, 3, details_one)
+    approx, details_one = lax.optimization_barrier((approx, details_one))
     second = approx
     approx, stress_two, *sends = level_approx(second, second_halo)
     before = shifted(sends[0], "gx", 1)

time: 86.1 us -> 84.8 us (0.985)
  waiting for transfers between devices: 17.2 us -> 15.5 us
  Pallas kernels: 28.3 us -> 29.3 us
    ppermute x18, waiting for transfers between devices: 17.2 us -> 15.5 us  [shifted(): lax.ppermute(block, axis, [(i, (i + distance) % size) for i in range(size)])]
    pallas_call x1 -> x2, Pallas kernels: 5.59 us -> 6.65 us  [detail_pass(): pl.pallas_call(lambda *refs: detail_kernel(start, *refs), grid=(stop - st...]
  transfers between devices with their start and end apart: 18 -> 18, of which waited for: 9 -> 7; matrix products, arithmetic and copies ran while one was open for 5% -> 5% of each run, Pallas kernels for 26% -> 28%
where the time goes in v10:
time: 84.8 us; the launch traced here: 84.2 us
  starting transfers between devices  32.5 us (38%)
  Pallas kernels  29.3 us (35%)
  waiting for transfers between devices  15.5 us (18%)
  local copies, waits for them, and re-layouts  5.52 us (7%)
  between operations  0.91 us (1%)
    ppermute x18, starting transfers between devices, shifted(): lax.ppermute(block, axis, [(i, (i + distance) % size) for i in range(size)])  32.5 us
    ppermute x18, waiting for transfers between devices, shifted(): lax.ppermute(block, axis, [(i, (i + distance) % size) for i in range(size)])  15.5 us
    pallas_call x2, Pallas kernels, local_pass(): pl.pallas_call(local_kernel, grid=(nx,), in_specs=[pl.BlockSpec((3, 1, ny...  10.9 us
    pallas_call x2, Pallas kernels, detail_pass(): pl.pallas_call(lambda *refs: detail_kernel(start, *refs), grid=(stop - st...  6.65 us
    pallas_call x2, Pallas kernels, level_call(): pl.pallas_call(kernel, in_specs=[vmem] * 6, out_specs=[vmem] * len(out),...  4.48 us
    pallas_call x1, Pallas kernels, approx_pass(): pl.pallas_call(approx_kernel, grid=(9 // GROUP,), in_specs=[per_field((nx...  3.2 us
    pallas_call x1, Pallas kernels, halo_pass(): pl.pallas_call(halo_kernel, in_specs=[vmem] * 5, out_specs=[vmem] * 2, ou...  1.9 us
  transfers between devices with their start and end apart: 18, of which 7 were waited for; matrix products, arithmetic and copies ran while one was open for 5% of the time, Pallas kernels for 28%

profile of v10, /device:TPU:0, one launch (start us, length us, event | category | flops | bytes accessed | tf_op | source)
XLA Modules:
  0.0 84.2 jit_solution(3612346840935992129)
XLA Ops:
  0.6 0.0 copy-start.1
  0.6 0.0 copy-start
  0.7 1.1 %fusion.6 = (f32[3,4,8,256]{3,2,1,0:T(8,128)S(1)}, f32[3,4,8,256]{3,2,1,0:T(8,128)S(1)}) fusion(f32[3,16,64,256]{3,2,1,0:T(8,128)} %v_ref.3), kind=kLoop, calls=%fused_computation.19 | loop fusion | bytes 393216 | tf_op jit(solution)/shard_map/slice | solution.py:630
  1.8 3.0 %collective-permute-start = (f32[3,4,16,256]{3,2,1,0:T(8,128)S(1)}, f32[3,4,16,256]{3,2,1,0:T(8,128)S(1)}, u32[]{:S(2)}, u32[]{:S(2)}) collective-permute-start(f32[3,4,16,256]{3,2,1,0:T(8,128)S(1)} %pad_maximum_fusion), channel_id=1, source_target_pairs={{0,4},{4,8},{8,12},{12,16},{16,20},{20,24},{24,28},{28,0},{1,5},{5... | collective-permute-start | bytes 589832 | tf_op jit(solution)/shard_map/ppermute | solution.py:23
  4.8 1.0 %slice.102 = f32[3,16,4,256]{3,2,1,0:T(4,128)S(1)} slice(f32[3,16,64,256]{3,2,1,0:T(8,128)} %v_ref.3), slice={[0:3], [0:16], [60:64], [0:256]} | slice | bytes 393216 | tf_op jit(solution)/shard_map/slice | solution.py:635
  5.9 0.1 collective-permute-start.2
  5.9 1.0 %slice.103 = f32[3,16,3,256]{3,2,1,0:T(4,128)S(1)} slice(f32[3,16,64,256]{3,2,1,0:T(8,128)} %v_ref.3), slice={[0:3], [0:16], [0:3], [0:256]} | slice | bytes 294912 | tf_op jit(solution)/shard_map/slice | solution.py:636
  6.9 1.8 %collective-permute-start.3 = (f32[3,16,3,256]{3,2,1,0:T(4,128)S(1)}, f32[3,16,3,256]{3,2,1,0:T(4,128)S(1)}, u32[]{:S(2)}, u32[]{:S(2)}) collective-permute-start(f32[3,16,3,256]{3,2,1,0:T(4,128)S(1)} %slice.103), channel_id=1, source_target_pairs={{0,3},{1,0},{2,1},{3,2},{4,7},{5,4},{6,5},{7,6},{8,11},{9,8},{10,9... | collective-permute-start | bytes 442376 | tf_op jit(solution)/shard_map/ppermute | solution.py:23
  8.7 1.0 %slice.109 = f32[3,3,48,256]{3,2,1,0:T(8,128)S(1)} slice(f32[3,16,64,256]{3,2,1,0:T(8,128)} %v_ref.3), slice={[0:3], [0:3], [8:56], [0:256]} | slice | bytes 884736 | tf_op jit(solution)/shard_map/slice | solution.py:634
  9.8 3.1 %collective-permute-start.7 = (f32[3,3,48,256]{3,2,1,0:T(8,128)S(1)}, f32[3,3,48,256]{3,2,1,0:T(8,128)S(1)}, u32[]{:S(2)}, u32[]{:S(2)}) collective-permute-start(f32[3,3,48,256]{3,2,1,0:T(8,128)S(1)} %slice.109), channel_id=1, source_target_pairs={{0,28},{4,0},{8,4},{12,8},{16,12},{20,16},{24,20},{28,24},{1,29},{... | collective-permute-start | bytes 1327112 | tf_op jit(solution)/shard_map/ppermute | solution.py:23
  12.9 1.1 %slice.104 = f32[3,4,48,256]{3,2,1,0:T(8,128)S(1)} slice(f32[3,16,64,256]{3,2,1,0:T(8,128)} %v_ref.3), slice={[0:3], [12:16], [8:56], [0:256]} | slice | bytes 1179648 | tf_op jit(solution)/shard_map/slice | solution.py:633
  14.0 0.1 collective-permute-start.4
  14.1 4.7 %collective-permute-start.1 = (f32[3,3,16,256]{3,2,1,0:T(8,128)S(1)}, f32[3,3,16,256]{3,2,1,0:T(8,128)S(1)}, u32[]{:S(2)}, u32[]{:S(2)}) collective-permute-start(f32[3,3,16,256]{3,2,1,0:T(8,128)S(1)} %pad_maximum_fusion.1), channel_id=1, source_target_pairs={{0,28},{4,0},{8,4},{12,8},{16,12},{20,16},{24,20},{28,24},{1,29},{... | collective-permute-start | bytes 442376 | tf_op jit(solution)/shard_map/ppermute | solution.py:23
  18.9 5.4 %local_pass.3 = (f32[9,8,32,128]{3,2,1,0:T(8,128)S(1)}, f32[3,9,8,32,128]{4,3,2,1,0:T(8,128)S(1)}) custom-call(f32[3,16,64,256]{3,2,1,0:T(8,128)S(1)} %copy-done, f32[3,16,4,256]{3,2,1,0:T(4,128)S(1)} %collective-permute-done.2.before_ref, f32[3,16,3,256]{3,2,1,0:T(4,128)S(1)} %collective-permute-done.3.after_ref, f32[256,256]{1,0:T(8,128)S(1)} %copy-done.1), custom_call_target="tpu_custom_call" | custom-call | flops 603979776 | bytes 7077888 | tf_op jit(solution)/shard_map/local_pass/pallas_call | solution.py:166
  24.3 5.4 %local_pass.2 = (f32[9,8,32,128]{3,2,1,0:T(8,128)S(1)}, f32[3,9,8,32,128]{4,3,2,1,0:T(8,128)S(1)}) custom-call(f32[3,16,64,256]{3,2,1,0:T(8,128)S(1)} %copy-done, f32[3,16,4,256]{3,2,1,0:T(4,128)S(1)} %collective-permute-done.2.before_ref, f32[3,16,3,256]{3,2,1,0:T(4,128)S(1)} %collective-permute-done.3.after_ref, f32[256,256]{1,0:T(8,128)S(1)} %copy-done.1), custom_call_target="tpu_custom_call" | custom-call | flops 603979776 | bytes 7077888 | tf_op jit(solution)/shard_map/local_pass/pallas_call | solution.py:166
  29.8 8.3 %collective-permute-done.1.refs_4_.refs_5_ = f32[3,3,16,256]{3,2,1,0:T(8,128)S(1)} collective-permute-done((f32[3,3,16,256]{3,2,1,0:T(8,128)S(1)}, f32[3,3,16,256]{3,2,1,0:T(8,128)S(1)}, u32[]{:S(2)}, u32[]{:S(2)}) %collective-permute-start.1) | collective-permute-done | bytes 147488 | tf_op jit(solution)/shard_map/ppermute | solution.py:23
  38.0 0.0 collective-permute-done.refs_0_
  38.1 0.1 collective-permute-start.5
  38.2 1.8 %collective-permute-start.6 = (f32[3,7,3,256]{3,2,1,0:T(4,128)S(1)}, f32[3,7,3,256]{3,2,1,0:T(4,128)S(1)}, u32[]{:S(2)}, u32[]{:S(2)}) collective-permute-start(f32[3,7,3,256]{3,2,1,0:T(4,128)S(1)} %pad_maximum_fusion.5), channel_id=1, source_target_pairs={{0,3},{1,0},{2,1},{3,2},{4,7},{5,4},{6,5},{7,6},{8,11},{9,8},{10,9... | collective-permute-start | bytes 193544 | tf_op jit(solution)/shard_map/ppermute | solution.py:23
  40.0 2.1 %collective-permute-done.6.refs_3_.refs_7_.refs_8_ = f32[3,7,3,256]{3,2,1,0:T(4,128)S(1)} collective-permute-done((f32[3,7,3,256]{3,2,1,0:T(4,128)S(1)}, f32[3,7,3,256]{3,2,1,0:T(4,128)S(1)}, u32[]{:S(2)}, u32[]{:S(2)}) %collective-permute-start.6) | collective-permute-done | bytes 64544 | tf_op jit(solution)/shard_map/ppermute | solution.py:23
  42.1 1.9 %halo_pass.1 = (f32[9,2,32,128]{3,2,1,0:T(8,128)S(1)}, f32[3,9,2,32,128]{4,3,2,1,0:T(8,128)S(1)}) custom-call(f32[3,4,16,256]{3,2,1,0:T(8,128)S(1)} %collective-permute-done.refs_0_, f32[3,4,48,256]{3,2,1,0:T(8,128)S(1)} %collective-permute-done.4.refs_1_, f32[3,7,4,256]{3,2,1,0:T(4,128)S(1)} %collective-permute-done.5.refs_2_.refs_6_.refs_7_, ...), custom_call_target="tpu_custom_call" | custom-call | tf_op jit(solution)/shard_map/halo_pass/pallas_call | solution.py:269
  44.0 0.0 collective-permute-done.7.refs_5_.refs_6_
  44.0 3.2 %approx_pass.1 = (f32[9,8,32,128]{3,2,1,0:T(8,128)S(1)}, f32[9,8,32,128]{3,2,1,0:T(8,128)S(1)}, f32[6,8,32,128]{3,2,1,0:T(8,128)}, f32[9,2,32,128]{3,2,1,0:T(8,1...) custom-call(f32[9,8,32,128]{3,2,1,0:T(8,128)S(1)} %get-tuple-element, ...), custom_call_target="tpu_custom_call" | custom-call | tf_op jit(solution)/shard_map/approx_pass/pallas_call | solution.py:346
  47.2 4.7 %collective-permute-start.9 = (f32[9,2,4,128]{3,2,1,0:T(4,128)S(1)}, f32[9,2,4,128]{3,2,1,0:T(4,128)S(1)}, u32[]{:S(2)}, u32[]{:S(2)}) collective-permute-start(f32[9,2,4,128]{3,2,1,0:T(4,128)S(1)} %get-tuple-element.56), channel_id=1, source_target_pairs={{0,28},{4,0},{8,4},{12,8},{16,12},{20,16},{24,20},{28,24},{1,29},{... | collective-permute-start | bytes 110600 | tf_op jit(solution)/shard_map/ppermute | solution.py:23
  52.0 4.7 %collective-permute-start.13 = (f32[9,2,32,128]{3,2,1,0:T(8,128)S(1)}, f32[9,2,32,128]{3,2,1,0:T(8,128)S(1)}, u32[]{:S(2)}, u32[]{:S(2)}) collective-permute-start(f32[9,2,32,128]{3,2,1,0:T(8,128)S(1)} %get-tuple-element.66), channel_id=1, source_target_pairs={{0,28},{4,0},{8,4},{12,8},{16,12},{20,16},{24,20},{28,24},{1,29},{... | collective-permute-start | bytes 884744 | tf_op jit(solution)/shard_map/ppermute | solution.py:23
  56.7 4.1 %detail_pass.2.refs_9_ = f32[7,9,8,32,128]{4,3,2,1,0:T(8,128)} custom-call(f32[3,9,8,32,128]{4,3,2,1,0:T(8,128)S(1)} %get-tuple-element.51.refs_0_, f32[3,9,8,32,128]{4,3,2,1,0:T(8,128)S(1)} %get-tuple-element.52.refs_1_, f32[3,9,2,32,128]{4,3,2,1,0:T(8,128)S(1)} %get-tuple-element.53.refs_2_, f32[9,8,32,128]{3,2,1,0:T(8,128)S(1)} %get-tuple-element.54.refs_3_, ...), custom_call_target="tpu_custom_call" | custom-call | flops 157286400 | bytes 12582912 | tf_op jit(solution)/shard_map/detail_pass/pallas_call | solution.py:418
  60.8 0.1 pad_maximum_fusion.2
  60.9 0.6 collective-permute-start.10
  61.5 0.0 copy-start.2
  61.6 1.2 %collective-permute-start.11 = (f32[9,12,2,128]{3,2,1,0:T(2,128)S(1)}, f32[9,12,2,128]{3,2,1,0:T(2,128)S(1)}, u32[]{:S(2)}, u32[]{:S(2)}) collective-permute-start(f32[9,12,2,128]{3,2,1,0:T(2,128)S(1)} %pad_maximum_fusion.3), channel_id=1, source_target_pairs={{0,3},{1,0},{2,1},{3,2},{4,7},{5,4},{6,5},{7,6},{8,11},{9,8},{10,9... | collective-permute-start | bytes 331784 | tf_op jit(solution)/shard_map/ppermute | solution.py:23
  62.8 2.6 %detail_pass.3 = f32[7,9,8,32,128]{4,3,2,1,0:T(8,128)} custom-call(f32[3,9,8,32,128]{4,3,2,1,0:T(8,128)S(1)} %get-tuple-element.51.refs_0_, f32[3,9,8,32,128]{4,3,2,1,0:T(8,128)S(1)} %get-tuple-element.52.refs_1_, f32[3,9,2,32,128]{4,3,2,1,0:T(8,128)S(1)} %get-tuple-element.53.refs_2_, ...), custom_call_target="tpu_custom_call", output_to_operand_aliasing={{}: (9, {})} | custom-call | flops 78643200 | bytes 6291456 | tf_op jit(solution)/shard_map/detail_pass/pallas_call | solution.py:418
  65.4 0.8 level_own.1.refs_0_
  66.2 0.0 copy-start.3
  66.2 1.8 %collective-permute-done.13.refs_2_ = f32[9,2,32,128]{3,2,1,0:T(8,128)S(1)} collective-permute-done((f32[9,2,32,128]{3,2,1,0:T(8,128)S(1)}, f32[9,2,32,128]{3,2,1,0:T(8,128)S(1)}, u32[]{:S(2)}, u32[]{:S(2)}) %collective-permute-start.13) | collective-permute-done | bytes 294944 | tf_op jit(solution)/shard_map/ppermute | solution.py:23
  68.0 1.3 %level_approx.1 = (f32[9,4,16,64]{3,2,1,0:T(8,128)S(1)}, f32[6,4,16,64]{3,2,1,0:T(8,128)}, f32[9,2,16,64]{3,2,1,0:T(8,128)S(1)}, f32[9,2,16,64]{3,2,1,0:T(8,128)...) custom-call(f32[9,8,16,128]{3,2,1,0:T(8,128)S(1)} %level_own.1.refs_0_, ...), custom_call_target="tpu_custom_call" | custom-call | tf_op jit(solution)/shard_map/level_approx/pallas_call | solution.py:580
  69.3 4.7 %collective-permute-start.15 = (f32[9,2,16,64]{3,2,1,0:T(8,128)S(1)}, f32[9,2,16,64]{3,2,1,0:T(8,128)S(1)}, u32[]{:S(2)}, u32[]{:S(2)}) collective-permute-start(f32[9,2,16,64]{3,2,1,0:T(8,128)S(1)} %get-tuple-element.68), channel_id=1, source_target_pairs={{0,28},{4,0},{8,4},{12,8},{16,12},{20,16},{24,20},{28,24},{1,29},{... | collective-permute-start | bytes 221192 | tf_op jit(solution)/shard_map/ppermute | solution.py:23
  74.0 2.9 %shard_map.108 = f32[7,9,4,16,64]{4,3,2,1,0:T(8,128)} custom-call(f32[9,8,32,128]{3,2,1,0:T(8,128)S(1)} %get-tuple-element.60.refs_0_, f32[9,2,32,128]{3,2,1,0:T(8,128)S(1)} %collective-permute-done.12.refs_1_, f32[9,2,32,128]{3,2,1,0:T(8,128)S(1)} %collective-permute-done.13.refs_2_, f32[9,12,2,128]{3,2,1,0:T(2,128)S(1)} %collective-permute-done.10.refs_1_.refs_3_, ...), custom_call_target="tpu_custom_call" | custom-call | tf_op jit(solution)/shard_map/pallas_call | solution.py:547
  76.9 1.0 %collective-permute-done.14.refs_1_ = f32[9,2,16,64]{3,2,1,0:T(8,128)S(1)} collective-permute-done((f32[9,2,16,64]{3,2,1,0:T(8,128)S(1)}, f32[9,2,16,64]{3,2,1,0:T(8,128)S(1)}, u32[]{:S(2)}, u32[]{:S(2)}) %collective-permute-start.14) | collective-permute-done | bytes 73760 | tf_op jit(solution)/shard_map/ppermute | solution.py:23
  78.0 0.4 collective-permute-done.15.refs_2_
  78.4 0.1 fusion.1
  78.5 0.1 maximum_maximum_fusion
  78.6 0.1 collective-permute-start.16
  78.7 0.1 fusion.4
  78.8 0.1 maximum_maximum_fusion.1
  78.8 1.8 %collective-permute-start.17 = (f32[9,8,2,64]{3,2,1,0:T(2,128)S(1)}, f32[9,8,2,64]{3,2,1,0:T(2,128)S(1)}, u32[]{:S(2)}, u32[]{:S(2)}) collective-permute-start(f32[9,8,2,64]{3,2,1,0:T(2,128)S(1)} %maximum_maximum_fusion.1), channel_id=1, source_target_pairs={{0,3},{1,0},{2,1},{3,2},{4,7},{5,4},{6,5},{7,6},{8,11},{9,8},{10,9... | collective-permute-start | bytes 110600 | tf_op jit(solution)/shard_map/ppermute | solution.py:23
  80.6 1.8 %collective-permute-done.16.refs_3_ = f32[9,8,2,64]{3,2,1,0:T(2,128)S(1)} collective-permute-done((f32[9,8,2,64]{3,2,1,0:T(2,128)S(1)}, f32[9,8,2,64]{3,2,1,0:T(2,128)S(1)}, u32[]{:S(2)}, u32[]{:S(2)}) %collective-permute-start.16) | collective-permute-done | bytes 36896 | tf_op jit(solution)/shard_map/ppermute | solution.py:23
  82.5 0.1 collective-permute-done.17.refs_4_
  82.6 1.6 %shard_map.109 = (f32[7,9,2,8,32]{4,3,2,1,0:T(8,128)}, f32[6,2,8,32]{3,2,1,0:T(8,128)}, f32[3,2,8,32]{3,2,1,0:T(8,128)}) custom-call(f32[9,4,16,64]{3,2,1,0:T(8,128)S(1)} %get-tuple-element.71.refs_0_, f32[9,2,16,64]{3,2,1,0:T(8,128)S(1)} %collective-permute-done.14.refs_1_, f32[9,2,16,64]{3,2,1,0:T(8,128)S(1)} %collective-permute-done.15.refs_2_, ...), custom_call_target="tpu_custom_call" | custom-call | tf_op jit(solution)/shard_map/pallas_call | solution.py:547
  (29 shorter events, 0.3 us)
Async XLA Ops:
  0.6 18.2 %copy-start.1 = (f32[256,256]{1,0:T(8,128)S(1)}, f32[256,256]{1,0:T(8,128)}, u32[]{:S(2)}) copy-start(f32[256,256]{1,0:T(8,128)} %constant.10.clone.table_ref.refs_4_.refs_3_) | copy-start | bytes 786436
  0.6 13.4 %copy-start = (f32[3,16,64,256]{3,2,1,0:T(8,128)S(1)}, f32[3,16,64,256]{3,2,1,0:T(8,128)}, u32[]{:S(2)}) copy-start(f32[3,16,64,256]{3,2,1,0:T(8,128)} %v_ref.3) | copy-start | bytes 9437188
  1.8 36.2 %collective-permute-start = (f32[3,4,16,256]{3,2,1,0:T(8,128)S(1)}, f32[3,4,16,256]{3,2,1,0:T(8,128)S(1)}, u32[]{:S(2)}, u32[]{:S(2)}) collective-permute-start(f32[3,4,16,256]{3,2,1,0:T(8,128)S(1)} %pad_maximum_fusion), channel_id=1, source_target_pairs={{0,4},{4,8},{8,12},{12,16},{16,20},{20,24},{24,28},{28,0},{1,5},{5... | collective-permute-start | bytes 589832 | tf_op jit(solution)/shard_map/ppermute | solution.py:23
  5.9 13.0 %collective-permute-start.2 = (f32[3,16,4,256]{3,2,1,0:T(4,128)S(1)}, f32[3,16,4,256]{3,2,1,0:T(4,128)S(1)}, u32[]{:S(2)}, u32[]{:S(2)}) collective-permute-start(f32[3,16,4,256]{3,2,1,0:T(4,128)S(1)} %slice.102), channel_id=1, source_target_pairs={{0,1},{1,2},{2,3},{3,0},{4,5},{5,6},{6,7},{7,4},{8,9},{9,10},{10,1... | collective-permute-start | bytes 589832 | tf_op jit(solution)/shard_map/ppermute | solution.py:23
  6.9 7.2 %collective-permute-start.3 = (f32[3,16,3,256]{3,2,1,0:T(4,128)S(1)}, f32[3,16,3,256]{3,2,1,0:T(4,128)S(1)}, u32[]{:S(2)}, u32[]{:S(2)}) collective-permute-start(f32[3,16,3,256]{3,2,1,0:T(4,128)S(1)} %slice.103), channel_id=1, source_target_pairs={{0,3},{1,0},{2,1},{3,2},{4,7},{5,4},{6,5},{7,6},{8,11},{9,8},{10,9... | collective-permute-start | bytes 442376 | tf_op jit(solution)/shard_map/ppermute | solution.py:23
  9.8 34.3 %collective-permute-start.7 = (f32[3,3,48,256]{3,2,1,0:T(8,128)S(1)}, f32[3,3,48,256]{3,2,1,0:T(8,128)S(1)}, u32[]{:S(2)}, u32[]{:S(2)}) collective-permute-start(f32[3,3,48,256]{3,2,1,0:T(8,128)S(1)} %slice.109), channel_id=1, source_target_pairs={{0,28},{4,0},{8,4},{12,8},{16,12},{20,16},{24,20},{28,24},{1,29},{... | collective-permute-start | bytes 1327112 | tf_op jit(solution)/shard_map/ppermute | solution.py:23
  14.0 28.1 %collective-permute-start.4 = (f32[3,4,48,256]{3,2,1,0:T(8,128)S(1)}, f32[3,4,48,256]{3,2,1,0:T(8,128)S(1)}, u32[]{:S(2)}, u32[]{:S(2)}) collective-permute-start(f32[3,4,48,256]{3,2,1,0:T(8,128)S(1)} %slice.104), channel_id=1, source_target_pairs={{0,4},{4,8},{8,12},{12,16},{16,20},{20,24},{24,28},{28,0},{1,5},{5... | collective-permute-start | bytes 1769480 | tf_op jit(solution)/shard_map/ppermute | solution.py:23
  14.1 23.9 %collective-permute-start.1 = (f32[3,3,16,256]{3,2,1,0:T(8,128)S(1)}, f32[3,3,16,256]{3,2,1,0:T(8,128)S(1)}, u32[]{:S(2)}, u32[]{:S(2)}) collective-permute-start(f32[3,3,16,256]{3,2,1,0:T(8,128)S(1)} %pad_maximum_fusion.1), channel_id=1, source_target_pairs={{0,28},{4,0},{8,4},{12,8},{16,12},{20,16},{24,20},{28,24},{1,29},{... | collective-permute-start | bytes 442376 | tf_op jit(solution)/shard_map/ppermute | solution.py:23
  38.1 4.0 %collective-permute-start.5 = (f32[3,7,4,256]{3,2,1,0:T(4,128)S(1)}, f32[3,7,4,256]{3,2,1,0:T(4,128)S(1)}, u32[]{:S(2)}, u32[]{:S(2)}) collective-permute-start(f32[3,7,4,256]{3,2,1,0:T(4,128)S(1)} %pad_maximum_fusion.4), channel_id=1, source_target_pairs={{0,1},{1,2},{2,3},{3,0},{4,5},{5,6},{6,7},{7,4},{8,9},{9,10},{10,1... | collective-permute-start | bytes 258056 | tf_op jit(solution)/shard_map/ppermute | solution.py:23
  38.2 3.9 %collective-permute-start.6 = (f32[3,7,3,256]{3,2,1,0:T(4,128)S(1)}, f32[3,7,3,256]{3,2,1,0:T(4,128)S(1)}, u32[]{:S(2)}, u32[]{:S(2)}) collective-permute-start(f32[3,7,3,256]{3,2,1,0:T(4,128)S(1)} %pad_maximum_fusion.5), channel_id=1, source_target_pairs={{0,3},{1,0},{2,1},{3,2},{4,7},{5,4},{6,5},{7,6},{8,11},{9,8},{10,9... | collective-permute-start | bytes 193544 | tf_op jit(solution)/shard_map/ppermute | solution.py:23
  47.2 13.5 %collective-permute-start.8 = (f32[9,2,4,128]{3,2,1,0:T(4,128)S(1)}, f32[9,2,4,128]{3,2,1,0:T(4,128)S(1)}, u32[]{:S(2)}, u32[]{:S(2)}) collective-permute-start(f32[9,2,4,128]{3,2,1,0:T(4,128)S(1)} %get-tuple-element.55), channel_id=1, source_target_pairs={{0,4},{4,8},{8,12},{12,16},{16,20},{20,24},{24,28},{28,0},{1,5},{5... | collective-permute-start | bytes 110600 | tf_op jit(solution)/shard_map/ppermute | solution.py:23
  47.2 13.5 %collective-permute-start.9 = (f32[9,2,4,128]{3,2,1,0:T(4,128)S(1)}, f32[9,2,4,128]{3,2,1,0:T(4,128)S(1)}, u32[]{:S(2)}, u32[]{:S(2)}) collective-permute-start(f32[9,2,4,128]{3,2,1,0:T(4,128)S(1)} %get-tuple-element.56), channel_id=1, source_target_pairs={{0,28},{4,0},{8,4},{12,8},{16,12},{20,16},{24,20},{28,24},{1,29},{... | collective-permute-start | bytes 110600 | tf_op jit(solution)/shard_map/ppermute | solution.py:23
  52.0 14.3 %collective-permute-start.12 = (f32[9,2,32,128]{3,2,1,0:T(8,128)S(1)}, f32[9,2,32,128]{3,2,1,0:T(8,128)S(1)}, u32[]{:S(2)}, u32[]{:S(2)}) collective-permute-start(f32[9,2,32,128]{3,2,1,0:T(8,128)S(1)} %get-tuple-element.65), channel_id=1, source_target_pairs={{0,4},{4,8},{8,12},{12,16},{16,20},{20,24},{24,28},{28,0},{1,5},{5... | collective-permute-start | bytes 884744 | tf_op jit(solution)/shard_map/ppermute | solution.py:23
  52.0 16.0 %collective-permute-start.13 = (f32[9,2,32,128]{3,2,1,0:T(8,128)S(1)}, f32[9,2,32,128]{3,2,1,0:T(8,128)S(1)}, u32[]{:S(2)}, u32[]{:S(2)}) collective-permute-start(f32[9,2,32,128]{3,2,1,0:T(8,128)S(1)} %get-tuple-element.66), channel_id=1, source_target_pairs={{0,28},{4,0},{8,4},{12,8},{16,12},{20,16},{24,20},{28,24},{1,29},{... | collective-permute-start | bytes 884744 | tf_op jit(solution)/shard_map/ppermute | solution.py:23
  60.9 4.5 %collective-permute-start.10 = (f32[9,12,2,128]{3,2,1,0:T(2,128)S(1)}, f32[9,12,2,128]{3,2,1,0:T(2,128)S(1)}, u32[]{:S(2)}, u32[]{:S(2)}) collective-permute-start(f32[9,12,2,128]{3,2,1,0:T(2,128)S(1)} %pad_maximum_fusion.2), channel_id=1, source_target_pairs={{0,1},{1,2},{2,3},{3,0},{4,5},{5,6},{6,7},{7,4},{8,9},{9,10},{10,1... | collective-permute-start | bytes 331784 | tf_op jit(solution)/shard_map/ppermute | solution.py:23
  61.5 3.8 %copy-start.2 = (f32[128,128]{1,0:T(8,128)S(1)}, f32[128,128]{1,0:T(8,128)}, u32[]{:S(2)}) copy-start(f32[128,128]{1,0:T(8,128)} %constant.11.clone.refs_3_.refs_5_) | copy-start | bytes 196612
  61.6 3.8 %collective-permute-start.11 = (f32[9,12,2,128]{3,2,1,0:T(2,128)S(1)}, f32[9,12,2,128]{3,2,1,0:T(2,128)S(1)}, u32[]{:S(2)}, u32[]{:S(2)}) collective-permute-start(f32[9,12,2,128]{3,2,1,0:T(2,128)S(1)} %pad_maximum_fusion.3), channel_id=1, source_target_pairs={{0,3},{1,0},{2,1},{3,2},{4,7},{5,4},{6,5},{7,6},{8,11},{9,8},{10,9... | collective-permute-start | bytes 331784 | tf_op jit(solution)/shard_map/ppermute | solution.py:23
  66.2 16.4 %copy-start.3 = (f32[128,128]{1,0:T(8,128)S(1)}, f32[128,128]{1,0:T(8,128)}, u32[]{:S(2)}) copy-start(f32[128,128]{1,0:T(8,128)} %constant.12.clone.refs_5_) | copy-start | bytes 196612
  69.3 8.7 %collective-permute-start.14 = (f32[9,2,16,64]{3,2,1,0:T(8,128)S(1)}, f32[9,2,16,64]{3,2,1,0:T(8,128)S(1)}, u32[]{:S(2)}, u32[]{:S(2)}) collective-permute-start(f32[9,2,16,64]{3,2,1,0:T(8,128)S(1)} %get-tuple-element.67), channel_id=1, source_target_pairs={{0,4},{4,8},{8,12},{12,16},{16,20},{20,24},{24,28},{28,0},{1,5},{5... | collective-permute-start | bytes 221192 | tf_op jit(solution)/shard_map/ppermute | solution.py:23
  69.3 9.0 %collective-permute-start.15 = (f32[9,2,16,64]{3,2,1,0:T(8,128)S(1)}, f32[9,2,16,64]{3,2,1,0:T(8,128)S(1)}, u32[]{:S(2)}, u32[]{:S(2)}) collective-permute-start(f32[9,2,16,64]{3,2,1,0:T(8,128)S(1)} %get-tuple-element.68), channel_id=1, source_target_pairs={{0,28},{4,0},{8,4},{12,8},{16,12},{20,16},{24,20},{28,24},{1,29},{... | collective-permute-start | bytes 221192 | tf_op jit(solution)/shard_map/ppermute | solution.py:23
  78.6 3.8 %collective-permute-start.16 = (f32[9,8,2,64]{3,2,1,0:T(2,128)S(1)}, f32[9,8,2,64]{3,2,1,0:T(2,128)S(1)}, u32[]{:S(2)}, u32[]{:S(2)}) collective-permute-start(f32[9,8,2,64]{3,2,1,0:T(2,128)S(1)} %maximum_maximum_fusion), channel_id=1, source_target_pairs={{0,1},{1,2},{2,3},{3,0},{4,5},{5,6},{6,7},{7,4},{8,9},{9,10},{10,1... | collective-permute-start | bytes 110600 | tf_op jit(solution)/shard_map/ppermute | solution.py:23
  78.8 3.8 %collective-permute-start.17 = (f32[9,8,2,64]{3,2,1,0:T(2,128)S(1)}, f32[9,8,2,64]{3,2,1,0:T(2,128)S(1)}, u32[]{:S(2)}, u32[]{:S(2)}) collective-permute-start(f32[9,8,2,64]{3,2,1,0:T(2,128)S(1)} %maximum_maximum_fusion.1), channel_id=1, source_target_pairs={{0,3},{1,0},{2,1},{3,2},{4,7},{5,4},{6,5},{7,6},{8,11},{9,8},{10,9... | collective-permute-start | bytes 110600 | tf_op jit(solution)/shard_map/ppermute | solution.py:23

commit v11 on v10

--- a/solution.py
+++ b/solution.py
@@ -21,6 +21,21 @@
 def shifted(block, axis, distance):
     size = lax.axis_size(axis)
     return lax.ppermute(block, axis, [(i, (i + distance) % size) for i in range(size)])
+
+
+def swapped(block, axis, odd):
+    size = lax.axis_size(axis)
+    route = []
+    for i in range(size):
+        route.append((i, (i + 1) % size if i % 2 == odd else (i - 1) % size))
+    return lax.ppermute(block, axis, route)
+
+
+def neighbours(to_next, to_prev, axis):
+    even = lax.axis_index(axis) % 2 == 0
+    far = swapped(jnp.where(even, to_prev, to_next), axis, 1)
+    near = swapped(jnp.where(even, to_next, to_prev), axis, 0)
+    return jnp.where(even, far, near), jnp.where(even, near, far)
 
 
 def third_table(length, lanes):
@@ -613,10 +628,8 @@
 
 
 def exchange(to_next, to_prev, edge_next, edge_prev, down, up, meanwhile):
-    from_prev = shifted(edge_next, "gx", 1)
-    from_next = shifted(edge_prev, "gx", -1)
-    before = shifted(to_next, "gx", 1)
-    after = shifted(to_prev, "gx", -1)
+    from_prev, from_next = neighbours(edge_next, edge_prev, "gx")
+    before, after = neighbours(to_next, to_prev, "gx")
     from_prev, from_next, result = lax.optimization_barrier((from_prev, from_next, meanwhile()))
     down = jnp.concatenate([down, from_prev[:, :, 0:2], from_next[:, :, 0:2]], axis=1)
     up = jnp.concatenate([up, from_prev[:, :, 2:4], from_next[:, :, 2:4]], axis=1)
@@ -650,8 +663,7 @@
     approx, details_one = lax.optimization_barrier((approx, details_one))
     second = approx
     approx, stress_two, *sends = level_approx(second, second_halo)
-    before = shifted(sends[0], "gx", 1)
-    after = shifted(sends[1], "gx", -1)
+    before, after = neighbours(sends[0], sends[1], "gx")
     (details_two,) = level_details(second, second_halo, False)
     before, after, details_two = lax.optimization_barrier((before, after, details_two))
     third_halo = (before, after) + halo_rows(before, after, *sends[2:])

time: 84.8 us -> 97.3 us (1.15)
  the two profiles are of different devices: /device:TPU:0 before, /device:TPU:1 now
where the time goes in v11:
time: 97.3 us; the launch traced here: 96.8 us
  Pallas kernels  33.6 us (35%)
  starting transfers between devices  26.2 us (27%)
  local copies, waits for them, and re-layouts  18.6 us (19%)
  waiting for transfers between devices  15.6 us (16%)
  other arithmetic  1.88 us (2%)
    ppermute x12, starting transfers between devices, shifted(): lax.ppermute(block, axis, [(i, (i + distance) % size) for i in range(size)])  18.8 us
    ppermute x12, waiting for transfers between devices, shifted(): lax.ppermute(block, axis, [(i, (i + distance) % size) for i in range(size)])  12 us
    unnamed x32, local copies, waits for them, and re-layouts  11.5 us
    pallas_call x2, Pallas kernels, local_pass(): pl.pallas_call(local_kernel, grid=(nx,), in_specs=[pl.BlockSpec((3, 1, ny...  10.9 us
    pallas_call x2, Pallas kernels, detail_pass(): pl.pallas_call(lambda *refs: detail_kernel(start, *refs), grid=(stop - st...  8.88 us
    ppermute x6, starting transfers between devices, swapped(): return lax.ppermute(block, axis, route)  7.44 us
    pallas_call x2, Pallas kernels, level_call(): pl.pallas_call(kernel, in_specs=[vmem] * 6, out_specs=[vmem] * len(out),...  4.46 us
    pallas_call x1, Pallas kernels, approx_pass(): pl.pallas_call(approx_kernel, grid=(9 // GROUP,), in_specs=[per_field((nx...  4.22 us
  transfers between devices with their start and end apart: 18, of which 7 were waited for; matrix products, arithmetic and copies ran while one was open for 8% of the time, Pallas kernels for 27%

profile of v11, /device:TPU:1, one launch (start us, length us, event | category | flops | bytes accessed | tf_op | source)
XLA Modules:
  0.0 96.8 jit_solution(883735661897299057)
XLA Ops:
  0.7 1.1 %fusion.6 = (f32[3,4,8,256]{3,2,1,0:T(8,128)S(1)}, f32[3,4,8,256]{3,2,1,0:T(8,128)S(1)}) fusion(f32[3,16,64,256]{3,2,1,0:T(8,128)} %v_ref.3), kind=kLoop, calls=%fused_computation.31 | loop fusion | bytes 393216 | tf_op jit(solution)/shard_map/slice | solution.py:643
  1.8 2.1 %collective-permute-start = (f32[3,4,16,256]{3,2,1,0:T(8,128)S(1)}, f32[3,4,16,256]{3,2,1,0:T(8,128)S(1)}, u32[]{:S(2)}, u32[]{:S(2)}) collective-permute-start(f32[3,4,16,256]{3,2,1,0:T(8,128)S(1)} %pad_maximum_fusion), channel_id=1, source_target_pairs={{0,4},{4,8},{8,12},{12,16},{16,20},{20,24},{24,28},{28,0},{1,5},{5... | collective-permute-start | bytes 589832 | tf_op jit(solution)/shard_map/ppermute | solution.py:23
  3.9 1.0 %slice.102 = f32[3,16,4,256]{3,2,1,0:T(4,128)S(1)} slice(f32[3,16,64,256]{3,2,1,0:T(8,128)} %v_ref.3), slice={[0:3], [0:16], [60:64], [0:256]} | slice | bytes 393216 | tf_op jit(solution)/shard_map/slice | solution.py:648
  4.9 2.1 %collective-permute-start.2 = (f32[3,16,4,256]{3,2,1,0:T(4,128)S(1)}, f32[3,16,4,256]{3,2,1,0:T(4,128)S(1)}, u32[]{:S(2)}, u32[]{:S(2)}) collective-permute-start(f32[3,16,4,256]{3,2,1,0:T(4,128)S(1)} %slice.102), channel_id=1, source_target_pairs={{0,1},{1,2},{2,3},{3,0},{4,5},{5,6},{6,7},{7,4},{8,9},{9,10},{10,1... | collective-permute-start | bytes 589832 | tf_op jit(solution)/shard_map/ppermute | solution.py:23
  7.1 1.0 %slice.103 = f32[3,16,3,256]{3,2,1,0:T(4,128)S(1)} slice(f32[3,16,64,256]{3,2,1,0:T(8,128)} %v_ref.3), slice={[0:3], [0:16], [0:3], [0:256]} | slice | bytes 294912 | tf_op jit(solution)/shard_map/slice | solution.py:649
  8.1 1.8 %slice.109 = f32[3,3,48,256]{3,2,1,0:T(8,128)} slice(f32[3,16,64,256]{3,2,1,0:T(8,128)} %v_ref.3), slice={[0:3], [0:3], [8:56], [0:256]} | slice | bytes 884736 | tf_op jit(solution)/shard_map/slice | solution.py:647
  10.0 3.0 %collective-permute-start.7 = (f32[3,3,48,256]{3,2,1,0:T(8,128)}, f32[3,3,48,256]{3,2,1,0:T(8,128)}, u32[]{:S(2)}, u32[]{:S(2)}) collective-permute-start(f32[3,3,48,256]{3,2,1,0:T(8,128)} %slice.109), channel_id=1, source_target_pairs={{0,28},{4,0},{8,4},{12,8},{16,12},{20,16},{24,20},{28,24},{1,29},{... | collective-permute-start | bytes 1327112 | tf_op jit(solution)/shard_map/ppermute | solution.py:23
  12.9 1.9 %slice.104 = f32[3,4,48,256]{3,2,1,0:T(8,128)} slice(f32[3,16,64,256]{3,2,1,0:T(8,128)} %v_ref.3), slice={[0:3], [12:16], [8:56], [0:256]} | slice | bytes 1179648 | tf_op jit(solution)/shard_map/slice | solution.py:646
  14.9 4.2 %collective-permute-start.1 = (f32[3,3,16,256]{3,2,1,0:T(8,128)S(1)}, f32[3,3,16,256]{3,2,1,0:T(8,128)S(1)}, u32[]{:S(2)}, u32[]{:S(2)}) collective-permute-start(f32[3,3,16,256]{3,2,1,0:T(8,128)S(1)} %pad_maximum_fusion.1), channel_id=1, source_target_pairs={{0,28},{4,0},{8,4},{12,8},{16,12},{20,16},{24,20},{28,24},{1,29},{... | collective-permute-start | bytes 442376 | tf_op jit(solution)/shard_map/ppermute | solution.py:23
  19.1 5.4 %local_pass.3 = (f32[9,8,32,128]{3,2,1,0:T(8,128)S(1)}, f32[3,9,8,32,128]{4,3,2,1,0:T(8,128)S(1)}) custom-call(f32[3,16,64,256]{3,2,1,0:T(8,128)S(1)} %copy-done, f32[3,16,4,256]{3,2,1,0:T(4,128)S(1)} %collective-permute-done.2.before_ref, f32[3,16,3,256]{3,2,1,0:T(4,128)S(1)} %collective-permute-done.3.after_ref, f32[256,256]{1,0:T(8,128)S(1)} %copy-done.3), custom_call_target="tpu_custom_call" | custom-call | flops 603979776 | bytes 7077888 | tf_op jit(solution)/shard_map/local_pass/pallas_call | solution.py:181
  24.6 1.1 %copy-done.8 = f32[9,8,32,128]{3,2,1,0:T(8,128)} copy-done((f32[9,8,32,128]{3,2,1,0:T(8,128)}, f32[9,8,32,128]{3,2,1,0:T(8,128)S(1)}, u32[]{:S(2)}) %copy-start.8) | copy-done | bytes 1179672
  25.6 5.4 %local_pass.2 = (f32[9,8,32,128]{3,2,1,0:T(8,128)S(1)}, f32[3,9,8,32,128]{4,3,2,1,0:T(8,128)S(1)}) custom-call(f32[3,16,64,256]{3,2,1,0:T(8,128)S(1)} %copy-done, f32[3,16,4,256]{3,2,1,0:T(4,128)S(1)} %collective-permute-done.2.before_ref, f32[3,16,3,256]{3,2,1,0:T(4,128)S(1)} %collective-permute-done.3.after_ref, f32[256,256]{1,0:T(8,128)S(1)} %copy-done.3), custom_call_target="tpu_custom_call" | custom-call | flops 603979776 | bytes 7077888 | tf_op jit(solution)/shard_map/local_pass/pallas_call | solution.py:181
  31.0 1.8 %copy-done.1 = f32[3,9,8,32,128]{4,3,2,1,0:T(8,128)} copy-done((f32[3,9,8,32,128]{4,3,2,1,0:T(8,128)}, f32[3,9,8,32,128]{4,3,2,1,0:T(8,128)S(1)}, u32[]{:S(2)}) %copy-start.1) | copy-done | bytes 3538968
  32.8 1.0 %copy-done.10 = f32[9,8,32,128]{3,2,1,0:T(8,128)} copy-done((f32[9,8,32,128]{3,2,1,0:T(8,128)}, f32[9,8,32,128]{3,2,1,0:T(8,128)S(1)}, u32[]{:S(2)}) %copy-start.10) | copy-done | bytes 1179672
  33.8 3.3 %collective-permute-done.1.refs_4_.refs_5_ = f32[3,3,16,256]{3,2,1,0:T(8,128)S(1)} collective-permute-done((f32[3,3,16,256]{3,2,1,0:T(8,128)S(1)}, f32[3,3,16,256]{3,2,1,0:T(8,128)S(1)}, u32[]{:S(2)}, u32[]{:S(2)}) %collective-permute-start.1) | collective-permute-done | bytes 147488 | tf_op jit(solution)/shard_map/ppermute | solution.py:23
  37.1 0.7 copy-done.6
  37.8 0.7 copy-done.13
  38.5 0.7 pad_maximum_fusion.4
  39.2 2.1 %collective-permute-start.5 = (f32[3,7,4,256]{3,2,1,0:T(4,128)}, f32[3,7,4,256]{3,2,1,0:T(4,128)}, u32[]{:S(2)}, u32[]{:S(2)}) collective-permute-start(f32[3,7,4,256]{3,2,1,0:T(4,128)} %pad_maximum_fusion.4), channel_id=1, source_target_pairs={{0,1},{1,2},{2,3},{3,0},{4,5},{5,6},{6,7},{7,4},{8,9},{9,10},{10,1... | collective-permute-start | bytes 258056 | tf_op jit(solution)/shard_map/ppermute | solution.py:23
  41.2 0.6 pad_maximum_fusion.5
  41.9 4.2 %collective-permute-done.6.refs_3_.refs_7_.refs_8_ = f32[3,7,3,256]{3,2,1,0:T(4,128)} collective-permute-done((f32[3,7,3,256]{3,2,1,0:T(4,128)}, f32[3,7,3,256]{3,2,1,0:T(4,128)}, u32[]{:S(2)}, u32[]{:S(2)}) %collective-permute-start.6) | collective-permute-done | bytes 64544 | tf_op jit(solution)/shard_map/ppermute | solution.py:23
  46.1 0.9 copy-done.4
  47.1 0.9 copy-done.14
  48.0 3.0 %halo_pass.1 = (f32[9,2,32,128]{3,2,1,0:T(8,128)S(1)}, f32[3,9,2,32,128]{4,3,2,1,0:T(8,128)S(1)}) custom-call(f32[3,4,16,256]{3,2,1,0:T(8,128)S(1)} %copy-done.14, f32[3,4,48,256]{3,2,1,0:T(8,128)} %collective-permute-done.4.refs_1_, f32[3,7,4,256]{3,2,1,0:T(4,128)} %collective-permute-done.5.refs_2_.refs_6_.refs_7_, ...), custom_call_target="tpu_custom_call" | custom-call | tf_op jit(solution)/shard_map/halo_pass/pallas_call | solution.py:284
  51.0 0.9 copy-done.5
  52.0 0.9 copy-done.7
  52.9 1.3 %copy-done.9 = f32[9,8,32,128]{3,2,1,0:T(8,128)S(1)} copy-done((f32[9,8,32,128]{3,2,1,0:T(8,128)S(1)}, f32[9,8,32,128]{3,2,1,0:T(8,128)}, u32[]{:S(2)}) %copy-start.9) | copy-done | bytes 1179672
  54.2 1.3 %copy-done.11 = f32[9,8,32,128]{3,2,1,0:T(8,128)S(1)} copy-done((f32[9,8,32,128]{3,2,1,0:T(8,128)S(1)}, f32[9,8,32,128]{3,2,1,0:T(8,128)}, u32[]{:S(2)}) %copy-start.11) | copy-done | bytes 1179672
  55.4 4.2 %approx_pass.1 = (f32[9,8,32,128]{3,2,1,0:T(8,128)S(1)}, f32[9,8,32,128]{3,2,1,0:T(8,128)S(1)}, f32[6,8,32,128]{3,2,1,0:T(8,128)}, f32[9,2,32,128]{3,2,1,0:T(8,1...) custom-call(f32[9,8,32,128]{3,2,1,0:T(8,128)S(1)} %copy-done.11, ...), custom_call_target="tpu_custom_call" | custom-call | tf_op jit(solution)/shard_map/approx_pass/pallas_call | solution.py:361
  59.7 0.1 collective-permute-start.9
  59.7 4.0 %collective-permute-start.8 = (f32[9,2,4,128]{3,2,1,0:T(4,128)S(1)}, f32[9,2,4,128]{3,2,1,0:T(4,128)S(1)}, u32[]{:S(2)}, u32[]{:S(2)}) collective-permute-start(f32[9,2,4,128]{3,2,1,0:T(4,128)S(1)} %bitcast.13), channel_id=1, source_target_pairs={{0,28},{4,8},{8,4},{12,16},{16,12},{20,24},{24,20},{28,0},{1,29},{... | collective-permute-start | bytes 110600 | tf_op jit(solution)/shard_map/ppermute | solution.py:31
  63.9 1.3 %collective-permute-start.12 = (f32[9,2,32,128]{3,2,1,0:T(8,128)S(1)}, f32[9,2,32,128]{3,2,1,0:T(8,128)S(1)}, u32[]{:S(2)}, u32[]{:S(2)}) collective-permute-start(f32[9,2,32,128]{3,2,1,0:T(8,128)S(1)} %get-tuple-element.86), channel_id=1, source_target_pairs={{0,28},{4,8},{8,4},{12,16},{16,12},{20,24},{24,20},{28,0},{1,29},{... | collective-permute-start | bytes 884744 | tf_op jit(solution)/shard_map/ppermute | solution.py:31
  65.2 5.0 %detail_pass.2.refs_9_ = f32[7,9,8,32,128]{4,3,2,1,0:T(8,128)} custom-call(f32[3,9,8,32,128]{4,3,2,1,0:T(8,128)S(1)} %copy-done.2, f32[3,9,8,32,128]{4,3,2,1,0:T(8,128)S(1)} %get-tuple-element.52.refs_1_, f32[3,9,2,32,128]{4,3,2,1,0:T(8,128)S(1)} %get-tuple-element.53.refs_2_, f32[9,8,32,128]{3,2,1,0:T(8,128)S(1)} %get-tuple-element.54.refs_3_, ...), custom_call_target="tpu_custom_call" | custom-call | flops 157286400 | bytes 12582912 | tf_op jit(solution)/shard_map/detail_pass/pallas_call | solution.py:433
  70.3 1.1 %collective-permute-start.10 = (f32[9,12,2,128]{3,2,1,0:T(2,128)S(1)}, f32[9,12,2,128]{3,2,1,0:T(2,128)S(1)}, u32[]{:S(2)}, u32[]{:S(2)}) collective-permute-start(f32[9,12,2,128]{3,2,1,0:T(2,128)S(1)} %pad_maximum_fusion.2), channel_id=1, source_target_pairs={{0,1},{1,2},{2,3},{3,0},{4,5},{5,6},{6,7},{7,4},{8,9},{9,10},{10,1... | collective-permute-start | bytes 331784 | tf_op jit(solution)/shard_map/ppermute | solution.py:23
  71.5 3.9 %detail_pass.3 = f32[7,9,8,32,128]{4,3,2,1,0:T(8,128)} custom-call(f32[3,9,8,32,128]{4,3,2,1,0:T(8,128)S(1)} %copy-done.2, f32[3,9,8,32,128]{4,3,2,1,0:T(8,128)S(1)} %get-tuple-element.52.refs_1_, f32[3,9,2,32,128]{4,3,2,1,0:T(8,128)S(1)} %get-tuple-element.53.refs_2_, ...), custom_call_target="tpu_custom_call", output_to_operand_aliasing={{}: (9, {})} | custom-call | flops 78643200 | bytes 6291456 | tf_op jit(solution)/shard_map/detail_pass/pallas_call | solution.py:433
  75.4 0.8 collective-permute-done.11.refs_2_.refs_4_
  76.2 0.8 level_own.1.refs_0_
  77.1 1.3 %collective-permute-done.13 = f32[9,2,32,128]{3,2,1,0:T(8,128)S(1)} collective-permute-done((f32[9,2,32,128]{3,2,1,0:T(8,128)S(1)}, f32[9,2,32,128]{3,2,1,0:T(8,128)S(1)}, u32[]{:S(2)}, u32[]{:S(2)}) %collective-permute-start.13) | collective-permute-done | bytes 294944 | tf_op jit(solution)/shard_map/ppermute | solution.py:31
  78.4 1.3 %level_approx.1 = (f32[9,4,16,64]{3,2,1,0:T(8,128)S(1)}, f32[6,4,16,64]{3,2,1,0:T(8,128)}, f32[9,2,16,64]{3,2,1,0:T(8,128)S(1)}, f32[9,2,16,64]{3,2,1,0:T(8,128)...) custom-call(f32[9,8,16,128]{3,2,1,0:T(8,128)S(1)} %level_own.1.refs_0_, ...), custom_call_target="tpu_custom_call" | custom-call | tf_op jit(solution)/shard_map/level_approx/pallas_call | solution.py:595
  79.8 0.4 collective-permute-start.15
  80.1 1.6 %collective-permute-start.14 = (f32[9,2,16,64]{3,2,1,0:T(8,128)S(1)}, f32[9,2,16,64]{3,2,1,0:T(8,128)S(1)}, u32[]{:S(2)}, u32[]{:S(2)}) collective-permute-start(f32[9,2,16,64]{3,2,1,0:T(8,128)S(1)} %get-tuple-element.90), channel_id=1, source_target_pairs={{0,28},{4,8},{8,4},{12,16},{16,12},{20,24},{24,20},{28,0},{1,29},{... | collective-permute-start | bytes 221192 | tf_op jit(solution)/shard_map/ppermute | solution.py:31
  81.8 2.9 %shard_map.108 = f32[7,9,4,16,64]{4,3,2,1,0:T(8,128)} custom-call(f32[9,8,32,128]{3,2,1,0:T(8,128)S(1)} %get-tuple-element.60.refs_0_, f32[9,2,32,128]{3,2,1,0:T(8,128)S(1)} %get-tuple-element.84.refs_1_, f32[9,2,32,128]{3,2,1,0:T(8,128)S(1)} %get-tuple-element.83.refs_2_, f32[9,12,2,128]{3,2,1,0:T(2,128)S(1)} %collective-permute-done.10.refs_1_.refs_3_, ...), custom_call_target="tpu_custom_call" | custom-call | tf_op jit(solution)/shard_map/pallas_call | solution.py:562
  84.7 2.3 %collective-permute-done.14 = f32[9,2,16,64]{3,2,1,0:T(8,128)S(1)} collective-permute-done((f32[9,2,16,64]{3,2,1,0:T(8,128)S(1)}, f32[9,2,16,64]{3,2,1,0:T(8,128)S(1)}, u32[]{:S(2)}, u32[]{:S(2)}) %collective-permute-start.14) | collective-permute-done | bytes 73760 | tf_op jit(solution)/shard_map/ppermute | solution.py:31
  87.1 0.1 fusion.1
  87.2 4.0 %collective-permute-start.16 = (f32[9,8,2,64]{3,2,1,0:T(2,128)S(1)}, f32[9,8,2,64]{3,2,1,0:T(2,128)S(1)}, u32[]{:S(2)}, u32[]{:S(2)}) collective-permute-start(f32[9,8,2,64]{3,2,1,0:T(2,128)S(1)} %maximum_maximum_fusion), channel_id=1, source_target_pairs={{0,1},{1,2},{2,3},{3,0},{4,5},{5,6},{6,7},{7,4},{8,9},{9,10},{10,1... | collective-permute-start | bytes 110600 | tf_op jit(solution)/shard_map/ppermute | solution.py:23
  91.5 1.2 %collective-permute-done.16.refs_3_ = f32[9,8,2,64]{3,2,1,0:T(2,128)S(1)} collective-permute-done((f32[9,8,2,64]{3,2,1,0:T(2,128)S(1)}, f32[9,8,2,64]{3,2,1,0:T(2,128)S(1)}, u32[]{:S(2)}, u32[]{:S(2)}) %collective-permute-start.16) | collective-permute-done | bytes 36896 | tf_op jit(solution)/shard_map/ppermute | solution.py:23
  92.7 2.6 %collective-permute-done.17.refs_4_ = f32[9,8,2,64]{3,2,1,0:T(2,128)S(1)} collective-permute-done((f32[9,8,2,64]{3,2,1,0:T(2,128)S(1)}, f32[9,8,2,64]{3,2,1,0:T(2,128)S(1)}, u32[]{:S(2)}, u32[]{:S(2)}) %collective-permute-start.17) | collective-permute-done | bytes 36896 | tf_op jit(solution)/shard_map/ppermute | solution.py:23
  95.2 1.6 %shard_map.109 = (f32[7,9,2,8,32]{4,3,2,1,0:T(8,128)}, f32[6,2,8,32]{3,2,1,0:T(8,128)}, f32[3,2,8,32]{3,2,1,0:T(8,128)}) custom-call(f32[9,4,16,64]{3,2,1,0:T(8,128)S(1)} %get-tuple-element.71.refs_0_, f32[9,2,16,64]{3,2,1,0:T(8,128)S(1)} %get-tuple-element.72.refs_1_, f32[9,2,16,64]{3,2,1,0:T(8,128)S(1)} %get-tuple-element.73.refs_2_, ...), custom_call_target="tpu_custom_call" | custom-call | tf_op jit(solution)/shard_map/pallas_call | solution.py:562
  (59 shorter events, 1.0 us)
Async XLA Ops:
  0.6 18.5 %copy-start.3 = (f32[256,256]{1,0:T(8,128)S(1)}, f32[256,256]{1,0:T(8,128)}, u32[]{:S(2)}) copy-start(f32[256,256]{1,0:T(8,128)} %constant.34.clone.table_ref.refs_4_.refs_3_) | copy-start | bytes 786436
  0.6 14.2 %copy-start = (f32[3,16,64,256]{3,2,1,0:T(8,128)S(1)}, f32[3,16,64,256]{3,2,1,0:T(8,128)}, u32[]{:S(2)}) copy-start(f32[3,16,64,256]{3,2,1,0:T(8,128)} %v_ref.3) | copy-start | bytes 9437188
  1.8 35.3 %collective-permute-start = (f32[3,4,16,256]{3,2,1,0:T(8,128)S(1)}, f32[3,4,16,256]{3,2,1,0:T(8,128)S(1)}, u32[]{:S(2)}, u32[]{:S(2)}) collective-permute-start(f32[3,4,16,256]{3,2,1,0:T(8,128)S(1)} %pad_maximum_fusion), channel_id=1, source_target_pairs={{0,4},{4,8},{8,12},{12,16},{16,20},{20,24},{24,28},{28,0},{1,5},{5... | collective-permute-start | bytes 589832 | tf_op jit(solution)/shard_map/ppermute | solution.py:23
  4.9 14.2 %collective-permute-start.2 = (f32[3,16,4,256]{3,2,1,0:T(4,128)S(1)}, f32[3,16,4,256]{3,2,1,0:T(4,128)S(1)}, u32[]{:S(2)}, u32[]{:S(2)}) collective-permute-start(f32[3,16,4,256]{3,2,1,0:T(4,128)S(1)} %slice.102), channel_id=1, source_target_pairs={{0,1},{1,2},{2,3},{3,0},{4,5},{5,6},{6,7},{7,4},{8,9},{9,10},{10,1... | collective-permute-start | bytes 589832 | tf_op jit(solution)/shard_map/ppermute | solution.py:23
  8.1 6.8 %collective-permute-start.3 = (f32[3,16,3,256]{3,2,1,0:T(4,128)S(1)}, f32[3,16,3,256]{3,2,1,0:T(4,128)S(1)}, u32[]{:S(2)}, u32[]{:S(2)}) collective-permute-start(f32[3,16,3,256]{3,2,1,0:T(4,128)S(1)} %slice.103), channel_id=1, source_target_pairs={{0,3},{1,0},{2,1},{3,2},{4,7},{5,4},{6,5},{7,6},{8,11},{9,8},{10,9... | collective-permute-start | bytes 442376 | tf_op jit(solution)/shard_map/ppermute | solution.py:23
  10.0 41.1 %collective-permute-start.7 = (f32[3,3,48,256]{3,2,1,0:T(8,128)}, f32[3,3,48,256]{3,2,1,0:T(8,128)}, u32[]{:S(2)}, u32[]{:S(2)}) collective-permute-start(f32[3,3,48,256]{3,2,1,0:T(8,128)} %slice.109), channel_id=1, source_target_pairs={{0,28},{4,0},{8,4},{12,8},{16,12},{20,16},{24,20},{28,24},{1,29},{... | collective-permute-start | bytes 1327112 | tf_op jit(solution)/shard_map/ppermute | solution.py:23
  14.8 31.3 %collective-permute-start.4 = (f32[3,4,48,256]{3,2,1,0:T(8,128)}, f32[3,4,48,256]{3,2,1,0:T(8,128)}, u32[]{:S(2)}, u32[]{:S(2)}) collective-permute-start(f32[3,4,48,256]{3,2,1,0:T(8,128)} %slice.104), channel_id=1, source_target_pairs={{0,4},{4,8},{8,12},{12,16},{16,20},{20,24},{24,28},{28,0},{1,5},{5... | collective-permute-start | bytes 1769480 | tf_op jit(solution)/shard_map/ppermute | solution.py:23
  14.9 22.2 %collective-permute-start.1 = (f32[3,3,16,256]{3,2,1,0:T(8,128)S(1)}, f32[3,3,16,256]{3,2,1,0:T(8,128)S(1)}, u32[]{:S(2)}, u32[]{:S(2)}) collective-permute-start(f32[3,3,16,256]{3,2,1,0:T(8,128)S(1)} %pad_maximum_fusion.1), channel_id=1, source_target_pairs={{0,28},{4,0},{8,4},{12,8},{16,12},{20,16},{24,20},{28,24},{1,29},{... | collective-permute-start | bytes 442376 | tf_op jit(solution)/shard_map/ppermute | solution.py:23
  24.5 1.1 %copy-start.8 = (f32[9,8,32,128]{3,2,1,0:T(8,128)}, f32[9,8,32,128]{3,2,1,0:T(8,128)S(1)}, u32[]{:S(2)}) copy-start(f32[9,8,32,128]{3,2,1,0:T(8,128)S(1)} %get-tuple-element.46.refs_1_) | copy-start | bytes 3538948
  31.0 1.8 %copy-start.1 = (f32[3,9,8,32,128]{4,3,2,1,0:T(8,128)}, f32[3,9,8,32,128]{4,3,2,1,0:T(8,128)S(1)}, u32[]{:S(2)}) copy-start(f32[3,9,8,32,128]{4,3,2,1,0:T(8,128)S(1)} %get-tuple-element.51.refs_0_) | copy-start | bytes 10616836
  32.8 1.0 %copy-start.10 = (f32[9,8,32,128]{3,2,1,0:T(8,128)}, f32[9,8,32,128]{3,2,1,0:T(8,128)S(1)}, u32[]{:S(2)}) copy-start(f32[9,8,32,128]{3,2,1,0:T(8,128)S(1)} %get-tuple-element.45.refs_0_) | copy-start | bytes 3538948
  37.1 0.7 copy-start.6
  37.8 0.7 copy-start.13
  39.2 7.0 %collective-permute-start.5 = (f32[3,7,4,256]{3,2,1,0:T(4,128)}, f32[3,7,4,256]{3,2,1,0:T(4,128)}, u32[]{:S(2)}, u32[]{:S(2)}) collective-permute-start(f32[3,7,4,256]{3,2,1,0:T(4,128)} %pad_maximum_fusion.4), channel_id=1, source_target_pairs={{0,1},{1,2},{2,3},{3,0},{4,5},{5,6},{6,7},{7,4},{8,9},{9,10},{10,1... | collective-permute-start | bytes 258056 | tf_op jit(solution)/shard_map/ppermute | solution.py:23
  41.9 4.2 %collective-permute-start.6 = (f32[3,7,3,256]{3,2,1,0:T(4,128)}, f32[3,7,3,256]{3,2,1,0:T(4,128)}, u32[]{:S(2)}, u32[]{:S(2)}) collective-permute-start(f32[3,7,3,256]{3,2,1,0:T(4,128)} %pad_maximum_fusion.5), channel_id=1, source_target_pairs={{0,3},{1,0},{2,1},{3,2},{4,7},{5,4},{6,5},{7,6},{8,11},{9,8},{10,9... | collective-permute-start | bytes 193544 | tf_op jit(solution)/shard_map/ppermute | solution.py:23
  41.9 23.3 %copy-start.2 = (f32[3,9,8,32,128]{4,3,2,1,0:T(8,128)S(1)}, f32[3,9,8,32,128]{4,3,2,1,0:T(8,128)}, u32[]{:S(2)}) copy-start(f32[3,9,8,32,128]{4,3,2,1,0:T(8,128)} %copy-done.1) | copy-start | bytes 10616836
  46.1 1.0 copy-start.4
  47.1 0.9 copy-start.14
  51.0 1.0 copy-start.5
  52.0 0.9 copy-start.7
  52.9 1.3 %copy-start.9 = (f32[9,8,32,128]{3,2,1,0:T(8,128)S(1)}, f32[9,8,32,128]{3,2,1,0:T(8,128)}, u32[]{:S(2)}) copy-start(f32[9,8,32,128]{3,2,1,0:T(8,128)} %copy-done.8) | copy-start | bytes 3538948
  54.2 1.3 %copy-start.11 = (f32[9,8,32,128]{3,2,1,0:T(8,128)S(1)}, f32[9,8,32,128]{3,2,1,0:T(8,128)}, u32[]{:S(2)}) copy-start(f32[9,8,32,128]{3,2,1,0:T(8,128)} %copy-done.10) | copy-start | bytes 3538948
  59.7 10.5 %collective-permute-start.9 = (f32[9,2,4,128]{3,2,1,0:T(4,128)S(1)}, f32[9,2,4,128]{3,2,1,0:T(4,128)S(1)}, u32[]{:S(2)}, u32[]{:S(2)}) collective-permute-start(f32[9,2,4,128]{3,2,1,0:T(4,128)S(1)} %bitcast.14), channel_id=1, source_target_pairs={{0,4},{4,0},{8,12},{12,8},{16,20},{20,16},{24,28},{28,24},{1,5},{5... | collective-permute-start | bytes 110600 | tf_op jit(solution)/shard_map/ppermute | solution.py:31
  59.7 10.4 %collective-permute-start.8 = (f32[9,2,4,128]{3,2,1,0:T(4,128)S(1)}, f32[9,2,4,128]{3,2,1,0:T(4,128)S(1)}, u32[]{:S(2)}, u32[]{:S(2)}) collective-permute-start(f32[9,2,4,128]{3,2,1,0:T(4,128)S(1)} %bitcast.13), channel_id=1, source_target_pairs={{0,28},{4,8},{8,4},{12,16},{16,12},{20,24},{24,20},{28,0},{1,29},{... | collective-permute-start | bytes 110600 | tf_op jit(solution)/shard_map/ppermute | solution.py:31
  63.8 14.6 %collective-permute-start.13 = (f32[9,2,32,128]{3,2,1,0:T(8,128)S(1)}, f32[9,2,32,128]{3,2,1,0:T(8,128)S(1)}, u32[]{:S(2)}, u32[]{:S(2)}) collective-permute-start(f32[9,2,32,128]{3,2,1,0:T(8,128)S(1)} %get-tuple-element.85), channel_id=1, source_target_pairs={{0,4},{4,0},{8,12},{12,8},{16,20},{20,16},{24,28},{28,24},{1,5},{5... | collective-permute-start | bytes 884744 | tf_op jit(solution)/shard_map/ppermute | solution.py:31
  63.9 14.5 %collective-permute-start.12 = (f32[9,2,32,128]{3,2,1,0:T(8,128)S(1)}, f32[9,2,32,128]{3,2,1,0:T(8,128)S(1)}, u32[]{:S(2)}, u32[]{:S(2)}) collective-permute-start(f32[9,2,32,128]{3,2,1,0:T(8,128)S(1)} %get-tuple-element.86), channel_id=1, source_target_pairs={{0,28},{4,8},{8,4},{12,16},{16,12},{20,24},{24,20},{28,0},{1,29},{... | collective-permute-start | bytes 884744 | tf_op jit(solution)/shard_map/ppermute | solution.py:31
  70.3 5.2 %collective-permute-start.10 = (f32[9,12,2,128]{3,2,1,0:T(2,128)S(1)}, f32[9,12,2,128]{3,2,1,0:T(2,128)S(1)}, u32[]{:S(2)}, u32[]{:S(2)}) collective-permute-start(f32[9,12,2,128]{3,2,1,0:T(2,128)S(1)} %pad_maximum_fusion.2), channel_id=1, source_target_pairs={{0,1},{1,2},{2,3},{3,0},{4,5},{5,6},{6,7},{7,4},{8,9},{9,10},{10,1... | collective-permute-start | bytes 331784 | tf_op jit(solution)/shard_map/ppermute | solution.py:23
  71.4 4.8 %copy-start.12 = (f32[128,128]{1,0:T(8,128)S(1)}, f32[128,128]{1,0:T(8,128)}, u32[]{:S(2)}) copy-start(f32[128,128]{1,0:T(8,128)} %constant.35.clone.refs_3_.refs_5_) | copy-start | bytes 196612
  71.4 4.8 %collective-permute-start.11 = (f32[9,12,2,128]{3,2,1,0:T(2,128)S(1)}, f32[9,12,2,128]{3,2,1,0:T(2,128)S(1)}, u32[]{:S(2)}, u32[]{:S(2)}) collective-permute-start(f32[9,12,2,128]{3,2,1,0:T(2,128)S(1)} %pad_maximum_fusion.3), channel_id=1, source_target_pairs={{0,3},{1,0},{2,1},{3,2},{4,7},{5,4},{6,5},{7,6},{8,11},{9,8},{10,9... | collective-permute-start | bytes 331784 | tf_op jit(solution)/shard_map/ppermute | solution.py:23
  79.7 15.5 %copy-start.15 = (f32[128,128]{1,0:T(8,128)S(1)}, f32[128,128]{1,0:T(8,128)}, u32[]{:S(2)}) copy-start(f32[128,128]{1,0:T(8,128)} %constant.36.clone.refs_5_) | copy-start | bytes 196612
  79.8 4.9 %collective-permute-start.15 = (f32[9,2,16,64]{3,2,1,0:T(8,128)S(1)}, f32[9,2,16,64]{3,2,1,0:T(8,128)S(1)}, u32[]{:S(2)}, u32[]{:S(2)}) collective-permute-start(f32[9,2,16,64]{3,2,1,0:T(8,128)S(1)} %get-tuple-element.89), channel_id=1, source_target_pairs={{0,4},{4,0},{8,12},{12,8},{16,20},{20,16},{24,28},{28,24},{1,5},{5... | collective-permute-start | bytes 221192 | tf_op jit(solution)/shard_map/ppermute | solution.py:31
  80.1 6.8 %collective-permute-start.14 = (f32[9,2,16,64]{3,2,1,0:T(8,128)S(1)}, f32[9,2,16,64]{3,2,1,0:T(8,128)S(1)}, u32[]{:S(2)}, u32[]{:S(2)}) collective-permute-start(f32[9,2,16,64]{3,2,1,0:T(8,128)S(1)} %get-tuple-element.90), channel_id=1, source_target_pairs={{0,28},{4,8},{8,4},{12,16},{16,12},{20,24},{24,20},{28,0},{1,29},{... | collective-permute-start | bytes 221192 | tf_op jit(solution)/shard_map/ppermute | solution.py:31
  87.2 5.4 %collective-permute-start.16 = (f32[9,8,2,64]{3,2,1,0:T(2,128)S(1)}, f32[9,8,2,64]{3,2,1,0:T(2,128)S(1)}, u32[]{:S(2)}, u32[]{:S(2)}) collective-permute-start(f32[9,8,2,64]{3,2,1,0:T(2,128)S(1)} %maximum_maximum_fusion), channel_id=1, source_target_pairs={{0,1},{1,2},{2,3},{3,0},{4,5},{5,6},{6,7},{7,4},{8,9},{9,10},{10,1... | collective-permute-start | bytes 110600 | tf_op jit(solution)/shard_map/ppermute | solution.py:23
  91.4 3.8 %collective-permute-start.17 = (f32[9,8,2,64]{3,2,1,0:T(2,128)S(1)}, f32[9,8,2,64]{3,2,1,0:T(2,128)S(1)}, u32[]{:S(2)}, u32[]{:S(2)}) collective-permute-start(f32[9,8,2,64]{3,2,1,0:T(2,128)S(1)} %maximum_maximum_fusion.1), channel_id=1, source_target_pairs={{0,3},{1,0},{2,1},{3,2},{4,7},{5,4},{6,5},{7,6},{8,11},{9,8},{10,9... | collective-permute-start | bytes 110600 | tf_op jit(solution)/shard_map/ppermute | solution.py:23
